TPU v7x, 128 devices: a whole 4x4x4 slice. The times are simulated.
128 devices in a mesh: seq: 32 (over z, x, core), batch: 4 (over y).
Axes of the slice: x: 4, y: 4, z: 4, core: 2. Of those that a mesh axis runs over, the one named last changes fastest.
Arguments:
- sequence_input: bfloat16 [32768, 1536], P(('batch', 'seq')), parts along dimension 0, may hold values from -6 to 6
- conv_first: bfloat16 [5, 1536, 768], replicated, may hold values from -0.0625 to 0.0625
- conv_second: bfloat16 [5, 768, 768], replicated, may hold values from -0.09375 to 0.09375
- qkv_weight: bfloat16 [768, 1536], replicated, may hold values from -0.21875 to 0.21875
- out_weight: bfloat16 [512, 768], replicated, may hold values from -0.25 to 0.25
- logit_scale: float32 [4], replicated, may hold values from 2.5 to 30, as said below
Outputs:
- block_output: bfloat16 [32768, 768], P(('batch', 'seq')), parts along dimension 0
There are 4 independent parts, one for each index of `batch`. A program takes and returns all parts, laid end to end along the dimension named above; an argument that names none is the same for every part. Nothing has to cross between parts.
Inputs may be any that keep to these rules, and one draw needn't show every extreme that they name: `logit_scale`: one positive scale a head.
All inputs are finite; a program needn't handle non-finite values.
Results may differ from a plain program's by a relative error of at most 0.023.
Values may be sent and summed in bfloat16 or wider, within the bound.
A program may use at most 256 MiB of HBM per device.

v0:
```python
import math

import jax
import jax.numpy as jnp
from jax import lax
from jax.sharding import PartitionSpec as P


def padded_2(block, sides, width):
    for axis, dim in sides:
        count = lax.axis_size(axis)
        forward = [(i, i + 1) for i in range(count - 1)]
        backward = [(target, source) for source, target in forward]
        low = lax.ppermute(
            lax.slice_in_dim(block, block.shape[dim] - width, None, axis=dim), axis, forward
        )
        high = lax.ppermute(lax.slice_in_dim(block, 0, width, axis=dim), axis, backward)
        block = jnp.concatenate([low, block, high], axis=dim)
    return block


def convolve(padded, weight, row_count):
    conv_sum = jnp.dot(padded[0:row_count], weight[0], preferred_element_type=jnp.float32)
    for offset in range(1, weight.shape[0]):
        conv_sum = conv_sum + jnp.dot(
            padded[offset : offset + row_count], weight[offset], preferred_element_type=jnp.float32
        )
    return conv_sum


def head_rms(tensor):
    return tensor * lax.rsqrt(jnp.mean(tensor * tensor, axis=-1, keepdims=True) + 1e-06)


def attend_block(state_now, queries, key_block, value_block):
    running_max, running_sum, running_out = state_now
    scores = jnp.einsum("thd,shd->hts", queries, key_block, preferred_element_type=jnp.float32)
    new_max = jnp.maximum(running_max, jnp.max(scores, axis=2))
    weights = jnp.exp(scores - new_max[:, :, None])
    running_sum = jnp.sum(weights, axis=2)
    running_out = jnp.einsum(
        "hts,shd->htd",
        weights.astype(jnp.bfloat16),
        value_block,
        preferred_element_type=jnp.float32,
    )
    return (new_max, running_sum, running_out)


def body(sequence_input, conv_first, conv_second, qkv_weight, out_weight, logit_scale):
    row_count = sequence_input.shape[0]
    padded_input = padded_2(sequence_input, (("seq", 0),), 2)
    first_out = jax.nn.gelu(convolve(padded_input, conv_first, row_count)).astype(jnp.bfloat16)
    padded_first = padded_2(first_out, (("seq", 0),), 2)
    second = convolve(padded_first, conv_second, row_count)
    hidden = (first_out.astype(jnp.float32) + second).astype(jnp.bfloat16)
    head_count = logit_scale.shape[0]
    width_all = qkv_weight.shape[1] // 3
    head_size = width_all // head_count
    query_part = jnp.dot(hidden, qkv_weight[:, :width_all], preferred_element_type=jnp.float32)
    query_part = query_part.reshape(row_count, head_count, head_size)
    queries = (head_rms(query_part) * (logit_scale / math.sqrt(head_size))[None, :, None]).astype(
        jnp.bfloat16
    )
    kv_weight = qkv_weight[:, width_all:]
    start_state = (
        jnp.full((head_count, row_count), -1e30, jnp.float32),
        jnp.zeros((head_count, row_count), jnp.float32),
        jnp.zeros((head_count, row_count, head_size), jnp.float32),
    )
    piece_rows = hidden.shape[0]
    paired = jnp.dot(hidden, kv_weight, preferred_element_type=jnp.float32)
    key_block = head_rms(paired[:, :width_all].reshape(piece_rows, head_count, head_size)).astype(
        jnp.bfloat16
    )
    value_block = (
        paired[:, width_all:].reshape(piece_rows, head_count, head_size).astype(jnp.bfloat16)
    )
    own_keys = key_block
    own_values = value_block
    flat_keys = own_keys.reshape(row_count, width_all)
    flat_values = own_values.reshape(row_count, width_all)
    piece_pair = (
        lax.all_gather(flat_keys, "seq", axis=0, tiled=True),
        lax.all_gather(flat_values, "seq", axis=0, tiled=True),
    )
    piece_rows = piece_pair[0].shape[0]
    key_block = piece_pair[0].reshape(piece_rows, head_count, head_size)
    value_block = piece_pair[1].reshape(piece_rows, head_count, head_size)
    final_state = attend_block(start_state, queries, key_block, value_block)
    running_max, running_sum, running_out = final_state
    attended = (
        (running_out / running_sum[:, :, None])
        .transpose(1, 0, 2)
        .reshape(row_count, width_all)
        .astype(jnp.bfloat16)
    )
    return (
        hidden.astype(jnp.float32)
        + jnp.dot(attended, out_weight, preferred_element_type=jnp.float32)
    ).astype(jnp.bfloat16)


def solution(mesh):
    in_specs = (P(("batch", "seq"), None), P(), P(), P(), P(), P())
    out_specs = P(("batch", "seq"), None)
    return jax.shard_map(body, mesh=mesh, in_specs=in_specs, out_specs=out_specs, check_vma=False)
```

profile of v0, /device:TPU:1, one launch (start us, length us, event | category | flops | bytes accessed | tf_op | source)
XLA Modules:
  0.0 185.4 jit_solution(1731052009252895028)
XLA Ops:
  6.5 0.0 copy-start
  6.5 0.8 fusion.101
  7.4 3.3 %collective-permute-start.1 = (bf16[2,1536]{1,0:T(2,128)(2,1)S(1)}, bf16[2,1536]{1,0:T(2,128)(2,1)S(1)}, u32[]{:S(2)}, u32[]{:S(2)}) collective-permute-start(bf16[2,1536]{1,0:T(2,128)(2,1)S(1)} %get-tuple-element.6), channel_id=1, source_target_pairs={{4,0},{8,4},{12,8},{16,12},{20,16},{24,20},{28,24},{32,28},{36,32}... | collective-permute-start | bytes 18440 | tf_op jit(solution)/shard_map/ppermute | solution.py:17
  10.7 0.0 copy-start.3
  10.7 3.5 %collective-permute-start = (bf16[2,1536]{1,0:T(2,128)(2,1)S(1)}, bf16[2,1536]{1,0:T(2,128)(2,1)S(1)}, u32[]{:S(2)}, u32[]{:S(2)}) collective-permute-start(bf16[2,1536]{1,0:T(2,128)(2,1)S(1)} %get-tuple-element.5), channel_id=1, source_target_pairs={{0,4},{4,8},{8,12},{12,16},{16,20},{20,24},{24,28},{28,32},{32,36}... | collective-permute-start | bytes 18440 | tf_op jit(solution)/shard_map/ppermute | solution.py:14
  14.2 2.7 %fusion.12 = f32[256,768]{1,0:T(8,128)S(1)} fusion(bf16[256,1536]{1,0:T(8,128)(2,1)} %param.6, bf16[5,1536,768]{2,1,0:T(8,128)(2,1)} %param.7), kind=kOutput, calls=%fused_computation.12 | convolution fusion | flops 603979776 | bytes 3932160 | tf_op jit(solution)/shard_map/dot_general | solution.py:25
  16.9 1.2 constant_dynamic-update-slice_fusion.1
  18.1 0.0 copy-start.2
  18.1 0.0 collective-permute-done.1
  18.2 2.5 %fusion.8 = f32[256,768]{1,0:T(8,128)S(1)} fusion(bf16[5,1536,768]{2,1,0:T(8,128)(2,1)} %param.7, bf16[258,1536]{1,0:T(8,128)(2,1)S(1)} %constant_dynamic-update-slice_fusion), kind=kOutput, calls=%fused_computation.8 | convolution fusion | flops 603979776 | bytes 3932160 | tf_op jit(solution)/shard_map/dot_general | solution.py:25
  20.7 0.8 fusion.10
  21.5 0.0 slice-start
  21.5 0.0 collective-permute-done
  21.5 0.0 copy-done.2
  21.5 0.8 fusion.14
  22.4 0.0 slice-start.1
  22.4 1.0 fusion.77
  23.4 2.9 %collective-permute-start.2 = (bf16[2,768]{1,0:T(2,128)(2,1)S(1)}, bf16[2,768]{1,0:T(2,128)(2,1)S(1)}, u32[]{:S(2)}, u32[]{:S(2)}) collective-permute-start(bf16[2,768]{1,0:T(2,128)(2,1)S(1)} %get-tuple-element.7), channel_id=1, source_target_pairs={{0,4},{4,8},{8,12},{12,16},{16,20},{20,24},{24,28},{28,32},{32,36}... | collective-permute-start | bytes 9224 | tf_op jit(solution)/shard_map/ppermute | solution.py:14
  26.4 0.5 fusion.54
  26.8 1.9 %collective-permute-start.3 = (bf16[2,768]{1,0:T(2,128)(2,1)S(1)}, bf16[2,768]{1,0:T(2,128)(2,1)S(1)}, u32[]{:S(2)}, u32[]{:S(2)}) collective-permute-start(bf16[2,768]{1,0:T(2,128)(2,1)S(1)} %get-tuple-element.8), channel_id=1, source_target_pairs={{4,0},{8,4},{12,8},{16,12},{20,16},{24,20},{28,24},{32,28},{36,32}... | collective-permute-start | bytes 9224 | tf_op jit(solution)/shard_map/ppermute | solution.py:17
  28.8 0.0 collective-permute-done.2
  28.8 0.5 fusion.56
  29.3 0.0 copy-start.1
  29.3 2.5 %collective-permute-done.3 = bf16[2,768]{1,0:T(2,128)(2,1)S(1)} collective-permute-done((bf16[2,768]{1,0:T(2,128)(2,1)S(1)}, bf16[2,768]{1,0:T(2,128)(2,1)S(1)}, u32[]{:S(2)}, u32[]{:S(2)}) %collective-permute-start.3) | collective-permute-done | bytes 3104 | tf_op jit(solution)/shard_map/ppermute | solution.py:17
  31.8 0.5 fusion.51
  32.2 0.5 fusion.33
  32.8 0.0 copy-start.4
  32.8 0.5 fusion.40
  33.3 0.6 fusion.23
  33.9 0.2 mul.70
  34.1 0.3 reduce_sum.28
  34.5 0.3 mul.71
  34.9 0.8 fusion.87
  35.6 0.0 all-gather.3.cloned.1.call-update
  35.7 0.2 all-gather.5.cloned.1.call-start
  35.9 0.7 slice.220
  36.6 0.0 all-gather.5.cloned.1.call-update
  36.7 1.5 fusion.85
  38.2 0.2 reshape.38
  38.4 0.3 multiply_reduce_fusion
  38.8 0.3 multiply_convert_fusion
  39.1 55.5 %all-gather.3.cloned.1.call-done = bf16[8192,512]{1,0:T(8,128)(2,1)} async-done(((bf16[256,512]{1,0:T(8,128)(2,1)}), bf16[8192,512]{1,0:T(8,128)(2,1)}) %all-gather.3.cloned.1.call-update) | async-done | bytes 8388624 | tf_op jit(solution)/shard_map/all_gather | solution.py:84
  94.6 16.8 %fusion.103 = (f32[4,256]{1,0:T(4,128)S(1)}, f32[4,256,8192]{2,1,0:T(8,128)}) fusion(bf16[256,4,128]{2,1,0:T(4,128)(2,1)S(1)} %multiply_convert_fusion, bf16[8192,512]{1,0:T(8,128)(2,1)} %all-gather.3.cloned.1.call-done), kind=kOutput, calls=%fused_computation.102 | convolution fusion | flops 2155871232 | bytes 42209280 | tf_op jit(solution)/shard_map/thd,shd->hts/dot_general | solution.py:37
  111.4 13.7 %fusion = f32[4,256]{1,0:T(4,128)S(1)} fusion(f32[4,256,8192]{2,1,0:T(8,128)} %get-tuple-element.10, f32[4,256]{1,0:T(4,128)S(1)} %broadcast_maximum_fusion), kind=kLoop, calls=%fused_computation.1 | loop fusion | flops 16776192 | bytes 33562624 | tf_op jit(solution)/shard_map/reduce_sum | solution.py:40
  125.2 24.3 %all-gather.5.cloned.1.call-done = bf16[8192,512]{1,0:T(8,128)(2,1)} async-done(((bf16[256,512]{1,0:T(8,128)(2,1)}), bf16[8192,512]{1,0:T(8,128)(2,1)}) %all-gather.5.cloned.1.call-update) | async-done | bytes 8388624 | tf_op jit(solution)/shard_map/all_gather | solution.py:85
  149.4 12.0 %copy.21 = bf16[8192,512]{0,1:T(8,128)(2,1)} copy(bf16[8192,512]{1,0:T(8,128)(2,1)} %all-gather.5.cloned.1.call-done) | data formatting | bytes 16777216 | tf_op jit(solution)/shard_map/reshape | solution.py:89
  161.4 16.0 %fusion.48 = bf16[256,4,128]{0,2,1:T(8,128)(2,1)S(1)} fusion(bf16[8192,4,128]{0,2,1:T(8,128)(2,1)} %bitcast.72, f32[4,256,8192]{2,1,0:T(8,128)} %get-tuple-element.10, f32[4,256]{1,0:T(4,128)S(1)} %broadcast_maximum_fusion, f32[256,4]{0,1:T(4,128)S(1)} %bitcast.77), kind=kOutput, calls=%fused_computation.39 | convolution fusion | flops 2164523008 | bytes 42213376 | tf_op jit(solution)/shard_map/hts,shd->htd/dot_general | solution.py:41
  177.5 1.1 fusion.41
  (15 shorter events, 0.1 us)
Async XLA Ops:
  6.5 170.9 %copy-start = (bf16[512,768]{1,0:T(8,128)(2,1)S(1)}, bf16[512,768]{1,0:T(8,128)(2,1)}, u32[]{:S(2)}) copy-start(bf16[512,768]{1,0:T(8,128)(2,1)} %param.10) | copy-start | bytes 2359300
  6.5 88.1 %all-gather.3.cloned.1.call-start = ((), (), s32[]{:S(2)}) async-start(), calls=%async_computation | async-start | bytes 8650752 | tf_op jit(solution)/shard_map/all_gather | solution.py:84
  7.4 10.8 %collective-permute-start.1 = (bf16[2,1536]{1,0:T(2,128)(2,1)S(1)}, bf16[2,1536]{1,0:T(2,128)(2,1)S(1)}, u32[]{:S(2)}, u32[]{:S(2)}) collective-permute-start(bf16[2,1536]{1,0:T(2,128)(2,1)S(1)} %get-tuple-element.6), channel_id=1, source_target_pairs={{4,0},{8,4},{12,8},{16,12},{20,16},{24,20},{28,24},{32,28},{36,32}... | collective-permute-start | bytes 18440 | tf_op jit(solution)/shard_map/ppermute | solution.py:17
  10.7 10.0 %copy-start.3 = (bf16[5,1536,768]{2,1,0:T(8,128)(2,1)S(1)}, bf16[5,1536,768]{2,1,0:T(8,128)(2,1)}, u32[]{:S(2)}) copy-start(bf16[5,1536,768]{2,1,0:T(8,128)(2,1)} %param.7) | copy-start | bytes 35389444
  10.7 10.8 %collective-permute-start = (bf16[2,1536]{1,0:T(2,128)(2,1)S(1)}, bf16[2,1536]{1,0:T(2,128)(2,1)S(1)}, u32[]{:S(2)}, u32[]{:S(2)}) collective-permute-start(bf16[2,1536]{1,0:T(2,128)(2,1)S(1)} %get-tuple-element.5), channel_id=1, source_target_pairs={{0,4},{4,8},{8,12},{12,16},{16,20},{20,24},{24,28},{28,32},{32,36}... | collective-permute-start | bytes 18440 | tf_op jit(solution)/shard_map/ppermute | solution.py:14
  18.1 3.4 %copy-start.2 = (bf16[256,1536]{1,0:T(8,128)(2,1)S(1)}, bf16[256,1536]{1,0:T(8,128)(2,1)}, u32[]{:S(2)}) copy-start(bf16[256,1536]{1,0:T(8,128)(2,1)} %param.6) | copy-start | bytes 2359300
  21.5 4.8 %slice-start = ((s8[5898240]{0:T(1024)(128)(4,1)}), s8[4194304]{0:T(1024)(128)(4,1)S(1)}, s32[]{:S(2)}) async-start(s8[5898240]{0:T(1024)(128)(4,1)} %bitcast.73), calls=%async_computation.2 | async-start | bytes 8388608
  22.4 4.0 %slice-start.1 = ((s8[5898240]{0:T(1024)(128)(4,1)}), s8[1703936]{0:T(1024)(128)(4,1)S(1)}, s32[]{:S(2)}) async-start(s8[5898240]{0:T(1024)(128)(4,1)} %bitcast.73), calls=%async_computation.3 | async-start | bytes 3407872
  23.4 5.4 %collective-permute-start.2 = (bf16[2,768]{1,0:T(2,128)(2,1)S(1)}, bf16[2,768]{1,0:T(2,128)(2,1)S(1)}, u32[]{:S(2)}, u32[]{:S(2)}) collective-permute-start(bf16[2,768]{1,0:T(2,128)(2,1)S(1)} %get-tuple-element.7), channel_id=1, source_target_pairs={{0,4},{4,8},{8,12},{12,16},{16,20},{20,24},{24,28},{28,32},{32,36}... | collective-permute-start | bytes 9224 | tf_op jit(solution)/shard_map/ppermute | solution.py:14
  26.8 4.9 %collective-permute-start.3 = (bf16[2,768]{1,0:T(2,128)(2,1)S(1)}, bf16[2,768]{1,0:T(2,128)(2,1)S(1)}, u32[]{:S(2)}, u32[]{:S(2)}) collective-permute-start(bf16[2,768]{1,0:T(2,128)(2,1)S(1)} %get-tuple-element.8), channel_id=1, source_target_pairs={{4,0},{8,4},{12,8},{16,12},{20,16},{24,20},{28,24},{32,28},{36,32}... | collective-permute-start | bytes 9224 | tf_op jit(solution)/shard_map/ppermute | solution.py:17
  29.3 4.0 %copy-start.1 = (bf16[768,1536]{1,0:T(8,128)(2,1)S(1)}, bf16[768,1536]{1,0:T(8,128)(2,1)}, u32[]{:S(2)}) copy-start(bf16[768,1536]{1,0:T(8,128)(2,1)} %param.9) | copy-start | bytes 7077892
  32.8 3.9 %copy-start.4 = (f32[4]{0:T(128)S(1)}, f32[4]{0:T(128)}, u32[]{:S(2)}) copy-start(f32[4]{0:T(128)} %param.11) | copy-start | bytes 52
  35.7 113.8 %all-gather.5.cloned.1.call-start = ((), (), s32[]{:S(2)}) async-start(), calls=%async_computation.1 | async-start | bytes 8650752 | tf_op jit(solution)/shard_map/all_gather | solution.py:85
Sparse Core Ops, SparseCore 0:
  35.8 58.7 all-gather.2
  96.9 52.5 all-gather.4
where the time goes:
time: 186 us; the launch traced here: 185 us
  waiting for transfers between devices  82.3 us (44%)
  matrix products  46.4 us (25%)
  other arithmetic  15.6 us (8%)
  local copies, waits for them, and re-layouts  15.5 us (8%)
  between operations  13.8 us (7%)
  starting transfers between devices  11.9 us (6%)
    all_gather x1, waiting for transfers between devices, body(): lax.all_gather(flat_keys, 'seq', axis=0, tiled=True)  55.5 us
    all_gather x1, waiting for transfers between devices, body(): lax.all_gather(flat_values, 'seq', axis=0, tiled=True)  24.3 us
    dot_general x1, matrix products, attend_block(): jnp.einsum('thd,shd->hts', queries, key_block, preferred_element_type=jnp...  16.8 us
    dot_general x1, matrix products, attend_block(): jnp.einsum('hts,shd->htd', weights.astype(jnp.bfloat16), value_block, pre...  16 us
    reduce_sum x1, other arithmetic, attend_block(): running_sum = jnp.sum(weights, axis=2)  13.7 us
    reshape x1, local copies, waits for them, and re-layouts, body(): value_block = piece_pair[1].reshape(piece_rows, head_count, head_size)  12 us
    dot_general x8, matrix products, convolve(): jnp.dot(padded[offset:offset + row_count], weight[offset], preferred_elem...  8.8 us
    ppermute x2, starting transfers between devices, padded_2(): lax.ppermute(lax.slice_in_dim(block, block.shape[dim] - width, None, axis...  6.42 us
  transfers between devices with their start and end apart: 6, of which 3 were waited for; matrix products, arithmetic and copies ran while one was open for 23% of the time, Pallas kernels for 0%

commit v1 on v0

v1 whole, which is shorter than its diff:
```python
import functools
import math

import jax
import jax.numpy as jnp
import numpy as np
from jax import lax
from jax.experimental import pallas as pl
from jax.experimental.pallas import tpu as pltpu
from jax.sharding import Mesh
from jax.sharding import PartitionSpec as P

SEQ_AXES = ("zx", "core")


def padded_2(block, width):
    count = lax.axis_size(SEQ_AXES)
    forward = [(i, i + 1) for i in range(count - 1)]
    backward = [(target, source) for source, target in forward]
    low = lax.ppermute(lax.slice_in_dim(block, block.shape[0] - width, None, axis=0), SEQ_AXES, forward)
    high = lax.ppermute(lax.slice_in_dim(block, 0, width, axis=0), SEQ_AXES, backward)
    return jnp.concatenate([low, block, high], axis=0)


def convolve(padded, weight, row_count):
    conv_sum = jnp.dot(padded[0:row_count], weight[0], preferred_element_type=jnp.float32)
    for offset in range(1, weight.shape[0]):
        conv_sum = conv_sum + jnp.dot(
            padded[offset : offset + row_count], weight[offset], preferred_element_type=jnp.float32
        )
    return conv_sum


def head_rms(tensor):
    return tensor * lax.rsqrt(jnp.mean(tensor * tensor, axis=-1, keepdims=True) + 1e-06)


def flash_kernel(nk, q_ref, k_ref, v_ref, o_ref, m_ref, l_ref, m_sc, l_sc, acc_sc):
    kb = pl.program_id(2)

    @pl.when(kb == 0)
    def _():
        m_sc[...] = jnp.full(m_sc.shape, -jnp.inf, jnp.float32)
        l_sc[...] = jnp.zeros(l_sc.shape, jnp.float32)
        acc_sc[...] = jnp.zeros(acc_sc.shape, jnp.float32)

    s = lax.dot_general(
        q_ref[...], k_ref[...], (((1,), (1,)), ((), ())), preferred_element_type=jnp.float32
    )
    m_prev = m_sc[...]
    m_new = jnp.maximum(m_prev, jnp.max(s, axis=1, keepdims=True))
    alpha = jnp.exp(m_prev - m_new)
    p = jnp.exp(s - m_new)
    l_sc[...] = alpha * l_sc[...] + jnp.sum(p, axis=1, keepdims=True)
    acc_sc[...] = alpha * acc_sc[...] + jnp.dot(
        p.astype(jnp.bfloat16), v_ref[...], preferred_element_type=jnp.float32
    )
    m_sc[...] = m_new

    @pl.when(kb == nk - 1)
    def _():
        o_ref[...] = acc_sc[...]
        m_ref[...] = m_sc[...]
        l_ref[...] = l_sc[...]


def flash_partial(queries, kv, heads, head_size, tq=256, tk=1024):
    q_rows = queries.shape[0]
    k_rows = kv.shape[0]
    nq, nk = q_rows // tq, k_rows // tk
    return pl.pallas_call(
        functools.partial(flash_kernel, nk),
        grid=(heads, nq, nk),
        in_specs=[
            pl.BlockSpec((tq, head_size), lambda h, i, j: (i, h)),
            pl.BlockSpec((tk, head_size), lambda h, i, j: (j, h)),
            pl.BlockSpec((tk, head_size), lambda h, i, j: (j, heads + h)),
        ],
        out_specs=[
            pl.BlockSpec((tq, head_size), lambda h, i, j: (i, h)),
            pl.BlockSpec((None, tq, 1), lambda h, i, j: (h, i, 0)),
            pl.BlockSpec((None, tq, 1), lambda h, i, j: (h, i, 0)),
        ],
        out_shape=[
            jax.ShapeDtypeStruct((q_rows, heads * head_size), jnp.float32),
            jax.ShapeDtypeStruct((heads, q_rows, 1), jnp.float32),
            jax.ShapeDtypeStruct((heads, q_rows, 1), jnp.float32),
        ],
        scratch_shapes=[
            pltpu.VMEM((tq, 1), jnp.float32),
            pltpu.VMEM((tq, 1), jnp.float32),
            pltpu.VMEM((tq, head_size), jnp.float32),
        ],
        compiler_params=pltpu.CompilerParams(
            dimension_semantics=("arbitrary", "arbitrary", "arbitrary")
        ),
        cost_estimate=pl.CostEstimate(
            flops=4 * q_rows * k_rows * heads * head_size,
            transcendentals=q_rows * k_rows * heads,
            bytes_accessed=(k_rows * 2 * heads * head_size * 2) * nq + q_rows * heads * head_size * 6,
        ),
    )(queries, kv, kv)


def body(sequence_input, conv_first, conv_second, qkv_weight, out_weight, logit_scale):
    row_count = sequence_input.shape[0]
    padded_input = padded_2(sequence_input, 2)
    first_out = jax.nn.gelu(convolve(padded_input, conv_first, row_count)).astype(jnp.bfloat16)
    padded_first = padded_2(first_out, 2)
    second = convolve(padded_first, conv_second, row_count)
    hidden = (first_out.astype(jnp.float32) + second).astype(jnp.bfloat16)
    head_count = logit_scale.shape[0]
    width_all = qkv_weight.shape[1] // 3
    head_size = width_all // head_count
    projected = jnp.dot(hidden, qkv_weight, preferred_element_type=jnp.float32)
    query_part = projected[:, :width_all].reshape(row_count, head_count, head_size)
    queries = (head_rms(query_part) * (logit_scale / math.sqrt(head_size))[None, :, None]).astype(
        jnp.bfloat16
    ).reshape(row_count, width_all)
    key_part = projected[:, width_all : 2 * width_all].reshape(row_count, head_count, head_size)
    keys = head_rms(key_part).astype(jnp.bfloat16).reshape(row_count, width_all)
    values = projected[:, 2 * width_all :].astype(jnp.bfloat16)
    kv_local = jnp.concatenate([keys, values], axis=1)

    kv_all = lax.all_gather(kv_local, "zx", axis=0, tiled=True)
    pair_queries = lax.all_gather(queries, "core", axis=0, tiled=True)
    o_part, m_part, l_part = flash_partial(pair_queries, kv_all, head_count, head_size)

    core = lax.axis_index("core")
    other = 1 - core
    send_o = lax.dynamic_slice_in_dim(o_part, other * row_count, row_count, axis=0)
    send_m = lax.dynamic_slice_in_dim(m_part, other * row_count, row_count, axis=1)
    send_l = lax.dynamic_slice_in_dim(l_part, other * row_count, row_count, axis=1)
    own_o = lax.dynamic_slice_in_dim(o_part, core * row_count, row_count, axis=0)
    own_m = lax.dynamic_slice_in_dim(m_part, core * row_count, row_count, axis=1)
    own_l = lax.dynamic_slice_in_dim(l_part, core * row_count, row_count, axis=1)
    swap = [(0, 1), (1, 0)]
    got_o, got_m, got_l = lax.ppermute((send_o, send_m, send_l), "core", swap)

    m_all = jnp.maximum(own_m, got_m)
    w_own = jnp.exp(own_m - m_all)
    w_got = jnp.exp(got_m - m_all)
    denom = own_l * w_own + got_l * w_got
    w_own_t = w_own[:, :, 0].T[:, :, None]
    w_got_t = w_got[:, :, 0].T[:, :, None]
    denom_t = denom[:, :, 0].T[:, :, None]
    mixed = (
        own_o.reshape(row_count, head_count, head_size) * w_own_t
        + got_o.reshape(row_count, head_count, head_size) * w_got_t
    )
    attended = (mixed / denom_t).reshape(row_count, width_all).astype(jnp.bfloat16)
    return (
        hidden.astype(jnp.float32)
        + jnp.dot(attended, out_weight, preferred_element_type=jnp.float32)
    ).astype(jnp.bfloat16)


def solution(mesh):
    devices = np.asarray(mesh.devices)
    seq_size = mesh.shape["seq"]
    batch_size = mesh.shape["batch"]
    order = [mesh.axis_names.index("seq"), mesh.axis_names.index("batch")]
    devices = devices.transpose(order).reshape(seq_size // 2, 2, batch_size)
    split_mesh = Mesh(devices, ("zx", "core", "batch"))
    rows = P(("batch", "zx", "core"), None)
    in_specs = (rows, P(), P(), P(), P(), P())
    return jax.shard_map(body, mesh=split_mesh, in_specs=in_specs, out_specs=rows, check_vma=False)
```

time: 186 us -> 182 us (0.978)
  matrix products: 46.4 us -> 13.6 us
  Pallas kernels: 0 us -> 32.7 us
  other arithmetic: 15.6 us -> 10.9 us
  waiting for transfers between devices: 82.3 us -> 78.2 us
  blocking collectives: 0 us -> 2.31 us
  local copies, waits for them, and re-layouts: 15.5 us -> 17.8 us
    dot_general x4 -> x1, matrix products: 34.9 us -> 0.77 us  [body(): projected = jnp.dot(hidden, qkv_weight, preferred_element_type=jnp.float32)]
    pallas_call x0 -> x1, Pallas kernels: none -> 32.7 us  [flash_partial(): pl.pallas_call(functools.partial(flash_kernel, nk), grid=(heads, nq, nk),...]
    reduce_sum x1 -> x0, other arithmetic: 13.7 us -> none  [attend_block(): running_sum = jnp.sum(weights, axis=2)]
    reshape x2 -> x0, local copies, waits for them, and re-layouts: 12.1 us -> none  [the longest x1 12 us: body(): value_block = piece_pair[1].reshape(piece_rows, head_count, head_size)]
    all_gather x2 -> x1, waiting for transfers between devices: 79.8 us -> 73.8 us  [body(): kv_all = lax.all_gather(kv_local, 'zx', axis=0, tiled=True)]
    dynamic_slice x0 -> x3, local copies, waits for them, and re-layouts: none -> 4.65 us  [the longest x1 1.94 us: body(): lax.dynamic_slice_in_dim(o_part, other * row_count, row_count, axis=0)]
    mul x0 -> x3, local copies, waits for them, and re-layouts: none -> 2.54 us  [the longest x1 1.24 us: body(): got_o.reshape(row_count, head_count, head_size) * w_got_t]
    rsqrt x2, other arithmetic: 0.05 us -> 2.51 us  [head_rms(): lax.rsqrt(jnp.mean(tensor * tensor, axis=-1, keepdims=True) + 1e-06)]
  transfers between devices with their start and end apart: 6 -> 8, of which waited for: 3 -> 4; matrix products, arithmetic and copies ran while one was open for 23% -> 9% of each run, Pallas kernels for 0% -> 0%
where the time goes in v1:
time: 182 us; the launch traced here: 181 us
  waiting for transfers between devices  78.2 us (43%)
  Pallas kernels  32.7 us (18%)
  local copies, waits for them, and re-layouts  17.8 us (10%)
  between operations  13.7 us (8%)
  matrix products  13.6 us (7%)
  starting transfers between devices  11.9 us (7%)
  other arithmetic  10.9 us (6%)
  blocking collectives  2.31 us (1%)
    all_gather x1, waiting for transfers between devices, body(): kv_all = lax.all_gather(kv_local, 'zx', axis=0, tiled=True)  73.8 us
    pallas_call x1, Pallas kernels, flash_partial(): pl.pallas_call(functools.partial(flash_kernel, nk), grid=(heads, nq, nk),...  32.7 us
    dot_general x8, matrix products, convolve(): jnp.dot(padded[offset:offset + row_count], weight[offset], preferred_elem...  8.95 us
    ppermute x2, starting transfers between devices, padded_2(): lax.ppermute(lax.slice_in_dim(block, block.shape[0] - width, None, axis=0...  5.5 us
    ppermute x2, starting transfers between devices, padded_2(): lax.ppermute(lax.slice_in_dim(block, 0, width, axis=0), SEQ_AXES, backward)  5.25 us
  transfers between devices with their start and end apart: 8, of which 4 were waited for; matrix products, arithmetic and copies ran while one was open for 9% of the time, Pallas kernels for 0%

profile of v1, /device:TPU:1, one launch (start us, length us, event | category | flops | bytes accessed | tf_op | source)
XLA Modules:
  0.0 181.1 jit_solution(2301667064528853389)
XLA Ops:
  6.5 0.9 fusion.89
  7.5 3.3 %collective-permute-start.1 = (bf16[2,1536]{1,0:T(2,128)(2,1)S(1)}, bf16[2,1536]{1,0:T(2,128)(2,1)S(1)}, u32[]{:S(2)}, u32[]{:S(2)}) collective-permute-start(bf16[2,1536]{1,0:T(2,128)(2,1)S(1)} %get-tuple-element.19), channel_id=1, source_target_pairs={{4,0},{8,4},{12,8},{16,12},{20,16},{24,20},{28,24},{32,28},{36,32}... | collective-permute-start | bytes 18440 | tf_op jit(solution)/shard_map/ppermute | solution.py:21
  10.8 3.1 %collective-permute-start = (bf16[2,1536]{1,0:T(2,128)(2,1)S(1)}, bf16[2,1536]{1,0:T(2,128)(2,1)S(1)}, u32[]{:S(2)}, u32[]{:S(2)}) collective-permute-start(bf16[2,1536]{1,0:T(2,128)(2,1)S(1)} %get-tuple-element.18), channel_id=1, source_target_pairs={{0,4},{4,8},{8,12},{12,16},{16,20},{20,24},{24,28},{28,32},{32,36}... | collective-permute-start | bytes 18440 | tf_op jit(solution)/shard_map/ppermute | solution.py:20
  13.9 1.3 constant_dynamic-update-slice_fusion.1
  15.3 2.9 %fusion.4 = f32[256,768]{1,0:T(8,128)S(1)} fusion(bf16[256,1536]{1,0:T(8,128)(2,1)} %param.6, bf16[5,1536,768]{2,1,0:T(8,128)(2,1)} %param.7), kind=kOutput, calls=%fused_computation.4 | convolution fusion | flops 603979776 | bytes 3932160 | tf_op jit(solution)/shard_map/dot_general | solution.py:28
  18.2 0.9 broadcast_multiply_fusion
  19.2 2.5 %fusion = f32[256,768]{1,0:T(8,128)S(1)} fusion(bf16[5,1536,768]{2,1,0:T(8,128)(2,1)} %param.7, bf16[258,1536]{1,0:T(8,128)(2,1)S(1)} %constant_dynamic-update-slice_fusion), kind=kOutput, calls=%fused_computation | convolution fusion | flops 603979776 | bytes 3932160 | tf_op jit(solution)/shard_map/dot_general | solution.py:28
  21.7 0.8 fusion.2
  22.8 0.8 fusion.6
  23.6 1.0 fusion.58
  24.6 2.4 %collective-permute-start.2 = (bf16[2,768]{1,0:T(2,128)(2,1)S(1)}, bf16[2,768]{1,0:T(2,128)(2,1)S(1)}, u32[]{:S(2)}, u32[]{:S(2)}) collective-permute-start(bf16[2,768]{1,0:T(2,128)(2,1)S(1)} %get-tuple-element.20), channel_id=1, source_target_pairs={{0,4},{4,8},{8,12},{12,16},{16,20},{20,24},{24,28},{28,32},{32,36}... | collective-permute-start | bytes 9224 | tf_op jit(solution)/shard_map/ppermute | solution.py:20
  27.1 0.5 fusion.35
  27.6 1.9 %collective-permute-start.3 = (bf16[2,768]{1,0:T(2,128)(2,1)S(1)}, bf16[2,768]{1,0:T(2,128)(2,1)S(1)}, u32[]{:S(2)}, u32[]{:S(2)}) collective-permute-start(bf16[2,768]{1,0:T(2,128)(2,1)S(1)} %get-tuple-element.21), channel_id=1, source_target_pairs={{4,0},{8,4},{12,8},{16,12},{20,16},{24,20},{28,24},{32,28},{36,32}... | collective-permute-start | bytes 9224 | tf_op jit(solution)/shard_map/ppermute | solution.py:21
  29.5 0.5 fusion.37
  30.0 2.5 %collective-permute-done.3 = bf16[2,768]{1,0:T(2,128)(2,1)S(1)} collective-permute-done((bf16[2,768]{1,0:T(2,128)(2,1)S(1)}, bf16[2,768]{1,0:T(2,128)(2,1)S(1)}, u32[]{:S(2)}, u32[]{:S(2)}) %collective-permute-start.3) | collective-permute-done | bytes 3104 | tf_op jit(solution)/shard_map/ppermute | solution.py:21
  32.5 0.5 fusion.32
  33.0 0.5 fusion.23
  33.5 0.5 fusion.30
  34.0 0.8 fusion.91
  34.8 1.1 slice_multiply_fusion
  36.0 0.3 copy-done.1
  36.3 1.2 mul.114
  37.6 1.0 reduce_sum.18
  38.6 1.6 add_rsqrt_fusion.1
  40.1 1.2 mul.123
  41.4 1.0 reduce_sum.19
  42.4 0.9 add_rsqrt_fusion
  43.3 1.2 mul.115
  44.9 1.4 fusion.70
  46.3 0.9 pad_maximum_fusion.2
  47.2 2.3 %all_gather.6.q_ref = bf16[512,512]{1,0:T(8,128)(2,1)} all-gather(bf16[256,512]{1,0:T(8,128)(2,1)S(1)} %get-tuple-element.15), channel_id=1, replica_groups=mesh['zx'=16,'core'=2,'batch'=4] {'core'}, dimensions={0}, use_global_device_ids=true | all-gather | bytes 786432 | tf_op jit(solution)/shard_map/all_gather | solution.py:126
  49.5 73.8 %all-gather.2.cloned.1.call-done.k_ref.v_ref = bf16[4096,1024]{1,0:T(8,128)(2,1)} async-done(((bf16[256,1024]{1,0:T(8,128)(2,1)}), bf16[4096,1024]{1,0:T(8,128)(2,1)}) %all-gather.2.cloned.1.call-update) | async-done | bytes 8388624 | tf_op jit(solution)/shard_map/all_gather | solution.py:125
  123.4 32.7 %shard_map.64 = (f32[512,512]{1,0:T(8,128)}, f32[4,512,1]{2,1,0:T(8,128)}, f32[4,512,1]{2,1,0:T(8,128)}) custom-call(bf16[512,512]{1,0:T(8,128)(2,1)} %all_gather.6.q_ref, bf16[4096,1024]{1,0:T(8,128)(2,1)} %all-gather.2.cloned.1.call-done.k_ref.v_ref, bf16[4096,1024]{1,0:T(8,128)(2,1)} %all-gather.2.cloned.1.call-done.k_ref.v_ref), custom_call_target="tpu_custom_call" | custom-call | flops 4294967296 | bytes 18350080 | tf_op jit(solution)/shard_map/pallas_call | solution.py:71
  156.0 1.9 %constant_dynamic-slice_fusion.1 = f32[256,512]{1,0:T(8,128)} fusion(f32[512,512]{1,0:T(8,128)} %get-tuple-element.8, s32[]{:T(128)S(6)} %select_n.5), kind=kLoop, calls=%fused_computation.92 | loop fusion | bytes 1048580 | tf_op jit(solution)/shard_map/dynamic_slice | solution.py:131
  158.0 0.7 collective-permute-start.5
  158.7 1.9 %constant_dynamic-slice_fusion = f32[4,256,1]{2,1,0:T(8,128)} fusion(f32[4,512,1]{2,1,0:T(8,128)} %get-tuple-element.10, s32[]{:T(128)S(6)} %select_n.5), kind=kLoop, calls=%fused_computation.91 | loop fusion | bytes 8196 | tf_op jit(solution)/shard_map/dynamic_slice | solution.py:133
  160.5 0.8 constant_dynamic-slice_fusion.2
  161.4 0.5 collective-permute-start.4
  161.9 0.9 collective-permute-done.6
  162.8 1.0 collective-permute-done.4
  163.8 2.0 %fusion.81 = (f32[4,256]{1,0:T(4,128)S(1)}, f32[4,256]{1,0:T(4,128)S(1)}, f32[4,256]{1,0:T(4,128)S(1)}) fusion(f32[4,256,1]{2,1,0:T(8,128)} %collective-permute-done.4, f32[4,512,1]{2,1,0:T(8,128)} %get-tuple-element.9, s32[]{:T(128)S(6)} %select_n.4, f32[4,256,1]{2,1,0:T(8,128)} %collective-permute-done.6, f32[4,512,1]{2,1,0:T(8,128)} %get-tuple-element.10), kind=kLoop, calls=%fused_computation.86 | loop fusion | flops 6144 | bytes 28676 | tf_op jit(solution)/shard_map/exp | solution.py:141
  165.8 0.8 copy.22
  166.6 0.8 copy.23
  167.4 0.8 copy.24
  168.2 1.2 mul.129
  169.4 1.2 mul.132
  170.6 1.2 div.23
  171.9 2.4 %fusion.31 = bf16[256,768]{1,0:T(8,128)(2,1)} fusion(bf16[512,768]{1,0:T(8,128)(2,1)S(1)} %copy-done.4, bf16[256,768]{1,0:T(8,128)(2,1)S(1)} %fusion.30, f32[32,8,4,128]{3,2,1,0:T(4,128)S(1)} %bitcast.88, f32[256,512]{1,0:T(8,128)} %collective-permute-done.5, f32[32,8,4,128]{3,2,1,0:T(4,128)S(1)} %bitcast.87, f32[32,8,4,128]{3,2,1,0:T(4,128)S(1)} %bitcast.86, ...), kind=kOutput, calls=%fused_computation.26 | convolution fusion | flops 202571776 | bytes 4194308 | tf_op jit(solution)/shard_map/dot_general | solution.py:154
  (28 shorter events, 0.8 us)
Async XLA Ops:
  6.5 27.5 %copy-start = (bf16[768,1536]{1,0:T(8,128)(2,1)S(1)}, bf16[768,1536]{1,0:T(8,128)(2,1)}, u32[]{:S(2)}) copy-start(bf16[768,1536]{1,0:T(8,128)(2,1)} %param.9) | copy-start | bytes 7077892
  6.5 116.8 %all-gather.2.cloned.1.call-start = ((), (), s32[]{:S(2)}) async-start(), calls=%async_computation | async-start | bytes 8912896 | tf_op jit(solution)/shard_map/all_gather | solution.py:125
  7.5 11.7 %collective-permute-start.1 = (bf16[2,1536]{1,0:T(2,128)(2,1)S(1)}, bf16[2,1536]{1,0:T(2,128)(2,1)S(1)}, u32[]{:S(2)}, u32[]{:S(2)}) collective-permute-start(bf16[2,1536]{1,0:T(2,128)(2,1)S(1)} %get-tuple-element.19), channel_id=1, source_target_pairs={{4,0},{8,4},{12,8},{16,12},{20,16},{24,20},{28,24},{32,28},{36,32}... | collective-permute-start | bytes 18440 | tf_op jit(solution)/shard_map/ppermute | solution.py:21
  10.8 11.7 %collective-permute-start = (bf16[2,1536]{1,0:T(2,128)(2,1)S(1)}, bf16[2,1536]{1,0:T(2,128)(2,1)S(1)}, u32[]{:S(2)}, u32[]{:S(2)}) collective-permute-start(bf16[2,1536]{1,0:T(2,128)(2,1)S(1)} %get-tuple-element.18), channel_id=1, source_target_pairs={{0,4},{4,8},{8,12},{12,16},{16,20},{20,24},{24,28},{28,32},{32,36}... | collective-permute-start | bytes 18440 | tf_op jit(solution)/shard_map/ppermute | solution.py:20
  13.9 7.8 %copy-start.5 = (bf16[5,1536,768]{2,1,0:T(8,128)(2,1)S(1)}, bf16[5,1536,768]{2,1,0:T(8,128)(2,1)}, u32[]{:S(2)}) copy-start(bf16[5,1536,768]{2,1,0:T(8,128)(2,1)} %param.7) | copy-start | bytes 35389444
  21.7 1.1 copy-start.3
  22.8 4.2 %slice-start = ((s8[5898240]{0:T(1024)(128)(4,1)}), s8[4194304]{0:T(1024)(128)(4,1)S(1)}, s32[]{:S(2)}) async-start(s8[5898240]{0:T(1024)(128)(4,1)} %bitcast.84), calls=%async_computation.1 | async-start | bytes 8388608
  23.6 3.5 %slice-start.1 = ((s8[5898240]{0:T(1024)(128)(4,1)}), s8[1703936]{0:T(1024)(128)(4,1)S(1)}, s32[]{:S(2)}) async-start(s8[5898240]{0:T(1024)(128)(4,1)} %bitcast.84), calls=%async_computation.2 | async-start | bytes 3407872
  24.6 4.9 %collective-permute-start.2 = (bf16[2,768]{1,0:T(2,128)(2,1)S(1)}, bf16[2,768]{1,0:T(2,128)(2,1)S(1)}, u32[]{:S(2)}, u32[]{:S(2)}) collective-permute-start(bf16[2,768]{1,0:T(2,128)(2,1)S(1)} %get-tuple-element.20), channel_id=1, source_target_pairs={{0,4},{4,8},{8,12},{12,16},{16,20},{20,24},{24,28},{28,32},{32,36}... | collective-permute-start | bytes 9224 | tf_op jit(solution)/shard_map/ppermute | solution.py:20
  27.6 4.9 %collective-permute-start.3 = (bf16[2,768]{1,0:T(2,128)(2,1)S(1)}, bf16[2,768]{1,0:T(2,128)(2,1)S(1)}, u32[]{:S(2)}, u32[]{:S(2)}) collective-permute-start(bf16[2,768]{1,0:T(2,128)(2,1)S(1)} %get-tuple-element.21), channel_id=1, source_target_pairs={{4,0},{8,4},{12,8},{16,12},{20,16},{24,20},{28,24},{32,28},{36,32}... | collective-permute-start | bytes 9224 | tf_op jit(solution)/shard_map/ppermute | solution.py:21
  34.8 1.5 copy-start.1
  156.0 4.5 %copy-start.2 = (f32[4,512,1]{2,1,0:T(8,128)S(1)}, f32[4,512,1]{2,1,0:T(8,128)}, u32[]{:S(2)}) copy-start(f32[4,512,1]{2,1,0:T(8,128)} %get-tuple-element.9) | copy-start | bytes 24580
  158.0 10.2 %collective-permute-start.5 = (f32[256,512]{1,0:T(8,128)}, f32[256,512]{1,0:T(8,128)}, u32[]{:S(2)}, u32[]{:S(2)}) collective-permute-start(f32[256,512]{1,0:T(8,128)} %constant_dynamic-slice_fusion.1), channel_id=1, source_target_pairs={{0,4},{4,0},{1,5},{5,1},{2,6},{6,2},{3,7},{7,3},{8,12},{12,8},{9,1... | collective-permute-start | bytes 1572872 | tf_op jit(solution)/shard_map/ppermute | solution.py:138
  160.5 2.3 %collective-permute-start.6 = (f32[4,256,1]{2,1,0:T(8,128)}, f32[4,256,1]{2,1,0:T(8,128)}, u32[]{:S(2)}, u32[]{:S(2)}) collective-permute-start(f32[4,256,1]{2,1,0:T(8,128)} %constant_dynamic-slice_fusion), channel_id=1, source_target_pairs={{0,4},{4,0},{1,5},{5,1},{2,6},{6,2},{3,7},{7,3},{8,12},{12,8},{9,1... | collective-permute-start | bytes 12296 | tf_op jit(solution)/shard_map/ppermute | solution.py:138
  161.4 10.5 %copy-start.4 = (bf16[512,768]{1,0:T(8,128)(2,1)S(1)}, bf16[512,768]{1,0:T(8,128)(2,1)}, u32[]{:S(2)}) copy-start(bf16[512,768]{1,0:T(8,128)(2,1)} %param.10) | copy-start | bytes 2359300
  161.4 2.4 %collective-permute-start.4 = (f32[4,256,1]{2,1,0:T(8,128)}, f32[4,256,1]{2,1,0:T(8,128)}, u32[]{:S(2)}, u32[]{:S(2)}) collective-permute-start(f32[4,256,1]{2,1,0:T(8,128)} %constant_dynamic-slice_fusion.2), channel_id=1, source_target_pairs={{0,4},{4,0},{1,5},{5,1},{2,6},{6,2},{3,7},{7,3},{8,12},{12,8},{9,1... | collective-permute-start | bytes 12296 | tf_op jit(solution)/shard_map/ppermute | solution.py:138
Sparse Core Ops, SparseCore 0:
  47.3 75.9 all-gather.1

commit v2 on v1

v2 whole, which is shorter than its diff:
```python
import functools
import math

import jax
import jax.numpy as jnp
import numpy as np
from jax import lax
from jax.experimental import pallas as pl
from jax.experimental.pallas import tpu as pltpu
from jax.sharding import Mesh
from jax.sharding import PartitionSpec as P

SEQ_AXES = ("zx", "core")


def padded_2(block, width):
    count = lax.axis_size(SEQ_AXES)
    forward = [(i, i + 1) for i in range(count - 1)]
    backward = [(target, source) for source, target in forward]
    low = lax.ppermute(lax.slice_in_dim(block, block.shape[0] - width, None, axis=0), SEQ_AXES, forward)
    high = lax.ppermute(lax.slice_in_dim(block, 0, width, axis=0), SEQ_AXES, backward)
    return jnp.concatenate([low, block, high], axis=0)


def convolve(padded, weight, row_count):
    conv_sum = jnp.dot(padded[0:row_count], weight[0], preferred_element_type=jnp.float32)
    for offset in range(1, weight.shape[0]):
        conv_sum = conv_sum + jnp.dot(
            padded[offset : offset + row_count], weight[offset], preferred_element_type=jnp.float32
        )
    return conv_sum


def head_rms(tensor):
    return tensor * lax.rsqrt(jnp.mean(tensor * tensor, axis=-1, keepdims=True) + 1e-06)


def head_norm(block, heads, head_size):
    parts = []
    for h in range(heads):
        part = block[:, h * head_size : (h + 1) * head_size]
        mean_sq = jnp.mean(part * part, axis=1, keepdims=True)
        parts.append(part * lax.rsqrt(mean_sq + 1e-06))
    return parts


def attend_kernel(heads, head_size, nk, hq_ref, hkv_ref, wq_ref, wkv_ref, scale_ref,
                  o_ref, st_ref, q_sc, m_sc, l_sc, acc_sc):
    j = pl.program_id(0)
    width = heads * head_size

    @pl.when(j == 0)
    def _():
        proj = jnp.dot(hq_ref[...], wq_ref[...], preferred_element_type=jnp.float32)
        normed = head_norm(proj, heads, head_size)
        scale = scale_ref[...]
        for h in range(heads):
            cols = slice(h * head_size, (h + 1) * head_size)
            q_sc[:, cols] = (normed[h] * scale[:, cols]).astype(jnp.bfloat16)
        m_sc[...] = jnp.full(m_sc.shape, -jnp.inf, jnp.float32)
        l_sc[...] = jnp.zeros(l_sc.shape, jnp.float32)
        acc_sc[...] = jnp.zeros(acc_sc.shape, jnp.float32)

    kv = jnp.dot(hkv_ref[...], wkv_ref[...], preferred_element_type=jnp.float32)
    keys = head_norm(kv[:, :width], heads, head_size)
    for h in range(heads):
        cols = slice(h * head_size, (h + 1) * head_size)
        k_h = keys[h].astype(jnp.bfloat16)
        v_h = kv[:, width + h * head_size : width + (h + 1) * head_size].astype(jnp.bfloat16)
        s = lax.dot_general(
            q_sc[:, cols], k_h, (((1,), (1,)), ((), ())), preferred_element_type=jnp.float32
        )
        m_prev = m_sc[h]
        m_next = jnp.maximum(m_prev, jnp.max(s, axis=1, keepdims=True))
        alpha = jnp.exp(m_prev - m_next)
        p = jnp.exp(s - m_next[:, 0:1])
        l_sc[h] = alpha * l_sc[h] + jnp.sum(p, axis=1, keepdims=True)
        acc_sc[:, cols] = alpha[:, 0:1] * acc_sc[:, cols] + jnp.dot(
            p.astype(jnp.bfloat16), v_h, preferred_element_type=jnp.float32
        )
        m_sc[h] = m_next

    @pl.when(j == nk - 1)
    def _():
        o_ref[...] = acc_sc[...]
        lane = lax.broadcasted_iota(jnp.int32, st_ref.shape, 1)
        packed = jnp.zeros(st_ref.shape, jnp.float32)
        for h in range(heads):
            packed = jnp.where(lane == h, m_sc[h], packed)
            packed = jnp.where(lane == 64 + h, l_sc[h], packed)
        st_ref[...] = packed


def attend_partial(hidden_q, hidden_kv, wq, wkv, scale_row, heads, head_size, tk=512):
    q_rows, channels = hidden_q.shape
    k_rows = hidden_kv.shape[0]
    width = heads * head_size
    nk = k_rows // tk
    whole = lambda j: (0, 0)
    return pl.pallas_call(
        functools.partial(attend_kernel, heads, head_size, nk),
        grid=(nk,),
        in_specs=[
            pl.BlockSpec((q_rows, channels), whole),
            pl.BlockSpec((tk, channels), lambda j: (j, 0)),
            pl.BlockSpec((channels, width), whole),
            pl.BlockSpec((channels, 2 * width), whole),
            pl.BlockSpec((1, width), whole),
        ],
        out_specs=[
            pl.BlockSpec((q_rows, width), whole),
            pl.BlockSpec((q_rows, 128), whole),
        ],
        out_shape=[
            jax.ShapeDtypeStruct((q_rows, width), jnp.float32),
            jax.ShapeDtypeStruct((q_rows, 128), jnp.float32),
        ],
        scratch_shapes=[
            pltpu.VMEM((q_rows, width), jnp.bfloat16),
            pltpu.VMEM((heads, q_rows, 128), jnp.float32),
            pltpu.VMEM((heads, q_rows, 128), jnp.float32),
            pltpu.VMEM((q_rows, width), jnp.float32),
        ],
        compiler_params=pltpu.CompilerParams(dimension_semantics=("arbitrary",)),
        cost_estimate=pl.CostEstimate(
            flops=4 * q_rows * k_rows * width + 2 * k_rows * channels * 2 * width,
            transcendentals=q_rows * k_rows * heads,
            bytes_accessed=k_rows * channels * 2 + q_rows * width * 8,
        ),
    )(hidden_q, hidden_kv, wq, wkv, scale_row)


def finish_kernel(heads, head_size, o_ref, st_ref, og_ref, sg_ref, hid_ref, wo_ref, out_ref):
    st_own = st_ref[...]
    st_got = sg_ref[...]
    mixed = []
    for h in range(heads):
        cols = slice(h * head_size, (h + 1) * head_size)
        m_own = st_own[:, h : h + 1]
        m_got = st_got[:, h : h + 1]
        m_all = jnp.maximum(m_own, m_got)
        w_own = jnp.exp(m_own - m_all)
        w_got = jnp.exp(m_got - m_all)
        denom = st_own[:, 64 + h : 65 + h] * w_own + st_got[:, 64 + h : 65 + h] * w_got
        part = (o_ref[:, cols] * w_own + og_ref[:, cols] * w_got) / denom
        mixed.append(part.astype(jnp.bfloat16))
    attended = jnp.concatenate(mixed, axis=1)
    out = hid_ref[...].astype(jnp.float32) + jnp.dot(
        attended, wo_ref[...], preferred_element_type=jnp.float32
    )
    out_ref[...] = out.astype(out_ref.dtype)


def finish(o_part, st_part, o_got, st_got, hidden, out_weight, heads, head_size):
    rows, width_out = hidden.shape
    width = heads * head_size
    whole = lambda i: (0, 0)
    return pl.pallas_call(
        functools.partial(finish_kernel, heads, head_size),
        grid=(1,),
        in_specs=[
            pl.BlockSpec((rows, width), whole),
            pl.BlockSpec((rows, 128), whole),
            pl.BlockSpec((rows, width), whole),
            pl.BlockSpec((rows, 128), whole),
            pl.BlockSpec((rows, width_out), whole),
            pl.BlockSpec((width, width_out), whole),
        ],
        out_specs=pl.BlockSpec((rows, width_out), whole),
        out_shape=jax.ShapeDtypeStruct((rows, width_out), jnp.bfloat16),
    )(o_part, st_part, o_got, st_got, hidden, out_weight)


def body(sequence_input, conv_first, conv_second, qkv_weight, out_weight, logit_scale):
    row_count = sequence_input.shape[0]
    padded_input = padded_2(sequence_input, 2)
    first_out = jax.nn.gelu(convolve(padded_input, conv_first, row_count)).astype(jnp.bfloat16)
    padded_first = padded_2(first_out, 2)
    second = convolve(padded_first, conv_second, row_count)
    hidden = (first_out.astype(jnp.float32) + second).astype(jnp.bfloat16)
    head_count = logit_scale.shape[0]
    width_all = qkv_weight.shape[1] // 3
    head_size = width_all // head_count
    scale_row = jnp.repeat(logit_scale / math.sqrt(head_size), head_size)[None, :]
    wq = qkv_weight[:, :width_all]
    wkv = qkv_weight[:, width_all:]

    swap = [(0, 1), (1, 0)]
    hidden_all = lax.all_gather(hidden, "zx", axis=0, tiled=True)
    hidden_other = lax.ppermute(hidden, "core", swap)
    hidden_q = jnp.concatenate([hidden, hidden_other], axis=0)
    o_part, st_part = attend_partial(hidden_q, hidden_all, wq, wkv, scale_row, head_count, head_size)
    o_got, st_got = lax.ppermute((o_part[row_count:], st_part[row_count:]), "core", swap)
    return finish(o_part, st_part, o_got, st_got, hidden, out_weight, head_count, head_size)


def solution(mesh):
    devices = np.asarray(mesh.devices)
    seq_size = mesh.shape["seq"]
    batch_size = mesh.shape["batch"]
    order = [mesh.axis_names.index("seq"), mesh.axis_names.index("batch")]
    devices = devices.transpose(order).reshape(seq_size // 2, 2, batch_size)
    split_mesh = Mesh(devices, ("zx", "core", "batch"))
    rows = P(("batch", "zx", "core"), None)
    in_specs = (rows, P(), P(), P(), P(), P())
    return jax.shard_map(body, mesh=split_mesh, in_specs=in_specs, out_specs=rows, check_vma=False)
```

time: 182 us -> 172 us (0.945)
  Pallas kernels: 32.7 us -> 52.3 us
  waiting for transfers between devices: 78.2 us -> 67.5 us
  local copies, waits for them, and re-layouts: 17.8 us -> 7.72 us
  other arithmetic: 10.9 us -> 0.93 us
  matrix products: 13.6 us -> 16.2 us
  blocking collectives: 2.31 us -> 0 us
    pallas_call x1 -> x2, Pallas kernels: 32.7 us -> 52.3 us  [the longest x1 49 us: attend_partial(): pl.pallas_call(functools.partial(attend_kernel, heads, head_size, nk), gr...]
    all_gather x1, waiting for transfers between devices: 73.8 us -> 63.4 us  [body(): hidden_all = lax.all_gather(hidden, 'zx', axis=0, tiled=True)]
    mul x7 -> x0, local copies, waits for them, and re-layouts: 6.53 us -> none  [the longest x2 2.42 us: head_rms(): tensor * tensor]
    dynamic_slice x3 -> x0, local copies, waits for them, and re-layouts: 4.65 us -> none  [the longest x1 1.94 us: body(): lax.dynamic_slice_in_dim(o_part, other * row_count, row_count, axis=0)]
    slice x1 -> x4, local copies, waits for them, and re-layouts: 0.03 us -> 4.35 us  [the longest x1 1.4 us: body(): wkv = qkv_weight[:, width_all:]]
    dot_general x8, matrix products: 8.95 us -> 12.9 us  [convolve(): jnp.dot(padded[offset:offset + row_count], weight[offset], preferred_elem...]
    dot_general x2 -> x0, matrix products: 3.16 us -> none  [the longest x1 2.4 us: body(): jnp.dot(attended, out_weight, preferred_element_type=jnp.float32)]
    rsqrt x2 -> x0, other arithmetic: 2.51 us -> none  [head_rms(): lax.rsqrt(jnp.mean(tensor * tensor, axis=-1, keepdims=True) + 1e-06)]
  transfers between devices with their start and end apart: 8 -> 8, of which waited for: 4 -> 4; matrix products, arithmetic and copies ran while one was open for 9% -> 7% of each run, Pallas kernels for 0% -> 0%
where the time goes in v2:
time: 172 us; the launch traced here: 171 us
  waiting for transfers between devices  67.5 us (39%)
  Pallas kernels  52.3 us (30%)
  matrix products  16.2 us (9%)
  between operations  13.6 us (8%)
  starting transfers between devices  12.8 us (7%)
  local copies, waits for them, and re-layouts  7.72 us (4%)
    all_gather x1, waiting for transfers between devices, body(): hidden_all = lax.all_gather(hidden, 'zx', axis=0, tiled=True)  63.4 us
    pallas_call x1, Pallas kernels, attend_partial(): pl.pallas_call(functools.partial(attend_kernel, heads, head_size, nk), gr...  49 us
    dot_general x8, matrix products, convolve(): jnp.dot(padded[offset:offset + row_count], weight[offset], preferred_elem...  12.9 us
    ppermute x2, starting transfers between devices, padded_2(): lax.ppermute(lax.slice_in_dim(block, block.shape[0] - width, None, axis=0...  7.92 us
    ppermute x2, starting transfers between devices, padded_2(): lax.ppermute(lax.slice_in_dim(block, 0, width, axis=0), SEQ_AXES, backward)  3.97 us
  transfers between devices with their start and end apart: 8, of which 4 were waited for; matrix products, arithmetic and copies ran while one was open for 7% of the time, Pallas kernels for 0%

profile of v2, /device:TPU:1, one launch (start us, length us, event | category | flops | bytes accessed | tf_op | source)
XLA Modules:
  0.0 171.2 jit_solution(4426562260365878947)
XLA Ops:
  6.5 0.0 all-gather.2.cloned.1.call-start
  6.5 0.8 fusion.77
  7.3 4.5 %collective-permute-start = (bf16[2,1536]{1,0:T(2,128)(2,1)S(1)}, bf16[2,1536]{1,0:T(2,128)(2,1)S(1)}, u32[]{:S(2)}, u32[]{:S(2)}) collective-permute-start(bf16[2,1536]{1,0:T(2,128)(2,1)S(1)} %get-tuple-element.9), channel_id=1, source_target_pairs={{0,4},{4,8},{8,12},{12,16},{16,20},{20,24},{24,28},{28,32},{32,36}... | collective-permute-start | bytes 18440 | tf_op jit(solution)/shard_map/ppermute | solution.py:20
  11.8 0.0 copy-start.2
  11.8 2.1 %collective-permute-start.1 = (bf16[2,1536]{1,0:T(2,128)(2,1)S(1)}, bf16[2,1536]{1,0:T(2,128)(2,1)S(1)}, u32[]{:S(2)}, u32[]{:S(2)}) collective-permute-start(bf16[2,1536]{1,0:T(2,128)(2,1)S(1)} %get-tuple-element.10), channel_id=1, source_target_pairs={{4,0},{8,4},{12,8},{16,12},{20,16},{24,20},{28,24},{32,28},{36,32}... | collective-permute-start | bytes 18440 | tf_op jit(solution)/shard_map/ppermute | solution.py:21
  13.9 2.7 %fusion.4 = f32[256,768]{1,0:T(8,128)S(1)} fusion(bf16[256,1536]{1,0:T(8,128)(2,1)} %param.6, bf16[5,1536,768]{2,1,0:T(8,128)(2,1)} %param.7), kind=kOutput, calls=%fused_computation.4 | convolution fusion | flops 603979776 | bytes 3932160 | tf_op jit(solution)/shard_map/dot_general | solution.py:28
  16.6 0.0 copy-done.2
  16.6 0.1 constant_dynamic-update-slice_fusion.1
  16.7 0.2 collective-permute-done.1
  16.9 2.5 %fusion = f32[256,768]{1,0:T(8,128)S(1)} fusion(bf16[5,1536,768]{2,1,0:T(8,128)(2,1)} %param.7, bf16[258,1536]{1,0:T(8,128)(2,1)S(1)} %constant_dynamic-update-slice_fusion), kind=kOutput, calls=%fused_computation | convolution fusion | flops 603979776 | bytes 3932160 | tf_op jit(solution)/shard_map/dot_general | solution.py:28
  19.4 2.5 %fusion.2 = f32[256,768]{1,0:T(8,128)S(1)} fusion(bf16[5,1536,768]{2,1,0:T(8,128)(2,1)} %param.7, bf16[258,1536]{1,0:T(8,128)(2,1)S(1)} %constant_dynamic-update-slice_fusion), kind=kOutput, calls=%fused_computation.2 | convolution fusion | flops 603979776 | bytes 3932160 | tf_op jit(solution)/shard_map/dot_general | solution.py:28
  21.9 0.0 collective-permute-done
  21.9 0.0 slice-start
  21.9 2.6 %fusion.6 = f32[256,768]{1,0:T(8,128)S(1)} fusion(bf16[5,1536,768]{2,1,0:T(8,128)(2,1)} %param.7, bf16[256,1536]{1,0:T(8,128)(2,1)S(1)} %copy-done.2, bf16[2,1536]{1,0:T(2,128)(2,1)S(1)} %collective-permute-done), kind=kOutput, calls=%fused_computation.6 | convolution fusion | flops 605552640 | bytes 3938304 | tf_op jit(solution)/shard_map/dot_general | solution.py:28
  24.5 0.0 slice-start.1
  24.5 2.8 %fusion.57 = bf16[256,768]{1,0:T(8,128)(2,1)S(1)} fusion(f32[256,768]{1,0:T(8,128)S(1)} %fusion, f32[256,768]{1,0:T(8,128)S(1)} %fusion.2, f32[256,768]{1,0:T(8,128)S(1)} %fusion.4, f32[256,768]{1,0:T(8,128)S(1)} %fusion.6, bf16[5,1536,768]{2,1,0:T(8,128)(2,1)} %param.7, bf16[2,1536]{1,0:T(2,128)(2,1)S(1)} %collective-permute-done, ...), kind=kOutput, calls=%fused_computation.49 | convolution fusion | flops 608108544 | bytes 6690816 | tf_op jit(solution)/shard_map/dot_general | solution.py:26
  27.3 3.4 %collective-permute-start.2 = (bf16[2,768]{1,0:T(2,128)(2,1)S(1)}, bf16[2,768]{1,0:T(2,128)(2,1)S(1)}, u32[]{:S(2)}, u32[]{:S(2)}) collective-permute-start(bf16[2,768]{1,0:T(2,128)(2,1)S(1)} %get-tuple-element.11), channel_id=1, source_target_pairs={{0,4},{4,8},{8,12},{12,16},{16,20},{20,24},{24,28},{28,32},{32,36}... | collective-permute-start | bytes 9224 | tf_op jit(solution)/shard_map/ppermute | solution.py:20
  30.7 1.9 %collective-permute-start.3 = (bf16[2,768]{1,0:T(2,128)(2,1)S(1)}, bf16[2,768]{1,0:T(2,128)(2,1)S(1)}, u32[]{:S(2)}, u32[]{:S(2)}) collective-permute-start(bf16[2,768]{1,0:T(2,128)(2,1)S(1)} %get-tuple-element.12), channel_id=1, source_target_pairs={{4,0},{8,4},{12,8},{16,12},{20,16},{24,20},{28,24},{32,28},{36,32}... | collective-permute-start | bytes 9224 | tf_op jit(solution)/shard_map/ppermute | solution.py:21
  32.7 0.0 slice-done
  32.7 0.0 slice-done.1
  32.7 0.5 fusion.34
  33.2 2.5 %collective-permute-done.3 = bf16[2,768]{1,0:T(2,128)(2,1)S(1)} collective-permute-done((bf16[2,768]{1,0:T(2,128)(2,1)S(1)}, bf16[2,768]{1,0:T(2,128)(2,1)S(1)}, u32[]{:S(2)}, u32[]{:S(2)}) %collective-permute-start.3) | collective-permute-done | bytes 3104 | tf_op jit(solution)/shard_map/ppermute | solution.py:21
  35.6 0.5 fusion.31
  36.1 0.0 collective-permute-done.2
  36.2 0.5 fusion.36
  36.6 0.5 fusion.23
  37.1 0.0 copy-start.1
  37.2 1.3 fusion.30.hid_ref
  38.4 0.0 all-gather.2.cloned.1.call-update
  38.5 0.0 copy-start.5
  38.5 0.1 collective-permute-start.4
  38.6 0.4 copy-done.1
  39.0 1.0 slice.108.wq_ref
  39.9 1.4 slice.109.wkv_ref
  41.3 0.0 collective-permute-done.4
  41.3 0.9 pad_maximum_fusion.2.hq_ref
  42.3 63.4 %all-gather.2.cloned.1.call-done.hkv_ref = bf16[4096,768]{1,0:T(8,128)(2,1)} async-done(((bf16[256,768]{1,0:T(8,128)(2,1)}), bf16[4096,768]{1,0:T(8,128)(2,1)}) %all-gather.2.cloned.1.call-update) | async-done | bytes 6291472 | tf_op jit(solution)/shard_map/all_gather | solution.py:189
  105.7 0.6 broadcast_in_dim.3
  106.4 49.0 %shard_map.64 = (f32[512,512]{1,0:T(8,128)}, f32[512,128]{1,0:T(8,128)}) custom-call(bf16[512,768]{1,0:T(8,128)(2,1)} %pad_maximum_fusion.2.hq_ref, bf16[4096,768]{1,0:T(8,128)(2,1)} %all-gather.2.cloned.1.call-done.hkv_ref, bf16[768,512]{1,0:T(8,128)(2,1)} %slice.108.wq_ref, bf16[768,1024]{1,0:T(8,128)(2,1)} %slice.109.wkv_ref, f32[1,512]{1,0:T(1,128)} %bitcast.47), custom_call_target="tpu_custom_call" | custom-call | flops 10737418240 | bytes 8388608 | tf_op jit(solution)/shard_map/pallas_call | solution.py:100
  155.3 1.1 slice.110
  156.4 0.8 collective-permute-start.5
  157.1 0.9 slice.111
  158.1 0.1 collective-permute-start.6
  158.2 1.3 collective-permute-done.6.sg_ref
  159.5 0.0 collective-permute-done.5.og_ref
  159.5 0.7 copy-done.4
  160.1 0.8 copy-done.3
  161.0 3.4 %shard_map.65 = bf16[256,768]{1,0:T(8,128)(2,1)} custom-call(f32[512,512]{1,0:T(8,128)} %get-tuple-element.7.o_ref, f32[512,128]{1,0:T(8,128)} %get-tuple-element.8.st_ref, f32[256,512]{1,0:T(8,128)} %copy-done.3, f32[256,128]{1,0:T(8,128)} %copy-done.4, bf16[256,768]{1,0:T(8,128)(2,1)} %fusion.30.hid_ref, bf16[512,768]{1,0:T(8,128)(2,1)} %wo_ref.1), custom_call_target="tpu_custom_call" | custom-call | tf_op jit(solution)/shard_map/pallas_call | solution.py:158
  (9 shorter events, 0.0 us)
Async XLA Ops:
  6.5 99.2 %all-gather.2.cloned.1.call-start = ((), (), s32[]{:S(2)}) async-start(), calls=%async_computation | async-start | bytes 6684672 | tf_op jit(solution)/shard_map/all_gather | solution.py:189
  7.3 14.6 %collective-permute-start = (bf16[2,1536]{1,0:T(2,128)(2,1)S(1)}, bf16[2,1536]{1,0:T(2,128)(2,1)S(1)}, u32[]{:S(2)}, u32[]{:S(2)}) collective-permute-start(bf16[2,1536]{1,0:T(2,128)(2,1)S(1)} %get-tuple-element.9), channel_id=1, source_target_pairs={{0,4},{4,8},{8,12},{12,16},{16,20},{20,24},{24,28},{28,32},{32,36}... | collective-permute-start | bytes 18440 | tf_op jit(solution)/shard_map/ppermute | solution.py:20
  11.8 4.8 %copy-start.2 = (bf16[256,1536]{1,0:T(8,128)(2,1)S(1)}, bf16[256,1536]{1,0:T(8,128)(2,1)}, u32[]{:S(2)}) copy-start(bf16[256,1536]{1,0:T(8,128)(2,1)} %param.6) | copy-start | bytes 2359300
  11.8 5.1 %collective-permute-start.1 = (bf16[2,1536]{1,0:T(2,128)(2,1)S(1)}, bf16[2,1536]{1,0:T(2,128)(2,1)S(1)}, u32[]{:S(2)}, u32[]{:S(2)}) collective-permute-start(bf16[2,1536]{1,0:T(2,128)(2,1)S(1)} %get-tuple-element.10), channel_id=1, source_target_pairs={{4,0},{8,4},{12,8},{16,12},{20,16},{24,20},{28,24},{32,28},{36,32}... | collective-permute-start | bytes 18440 | tf_op jit(solution)/shard_map/ppermute | solution.py:21
  21.9 10.8 %slice-start = ((s8[5898240]{0:T(1024)(128)(4,1)}), s8[4194304]{0:T(1024)(128)(4,1)S(1)}, s32[]{:S(2)}) async-start(s8[5898240]{0:T(1024)(128)(4,1)} %bitcast.45), calls=%async_computation.1 | async-start | bytes 8388608
  24.5 8.2 %slice-start.1 = ((s8[5898240]{0:T(1024)(128)(4,1)}), s8[1703936]{0:T(1024)(128)(4,1)S(1)}, s32[]{:S(2)}) async-start(s8[5898240]{0:T(1024)(128)(4,1)} %bitcast.45), calls=%async_computation.2 | async-start | bytes 3407872
  27.3 8.8 %collective-permute-start.2 = (bf16[2,768]{1,0:T(2,128)(2,1)S(1)}, bf16[2,768]{1,0:T(2,128)(2,1)S(1)}, u32[]{:S(2)}, u32[]{:S(2)}) collective-permute-start(bf16[2,768]{1,0:T(2,128)(2,1)S(1)} %get-tuple-element.11), channel_id=1, source_target_pairs={{0,4},{4,8},{8,12},{12,16},{16,20},{20,24},{24,28},{28,32},{32,36}... | collective-permute-start | bytes 9224 | tf_op jit(solution)/shard_map/ppermute | solution.py:20
  30.7 4.9 %collective-permute-start.3 = (bf16[2,768]{1,0:T(2,128)(2,1)S(1)}, bf16[2,768]{1,0:T(2,128)(2,1)S(1)}, u32[]{:S(2)}, u32[]{:S(2)}) collective-permute-start(bf16[2,768]{1,0:T(2,128)(2,1)S(1)} %get-tuple-element.12), channel_id=1, source_target_pairs={{4,0},{8,4},{12,8},{16,12},{20,16},{24,20},{28,24},{32,28},{36,32}... | collective-permute-start | bytes 9224 | tf_op jit(solution)/shard_map/ppermute | solution.py:21
  37.1 1.8 %copy-start.1 = (bf16[768,1536]{1,0:T(8,128)(2,1)S(1)}, bf16[768,1536]{1,0:T(8,128)(2,1)}, u32[]{:S(2)}) copy-start(bf16[768,1536]{1,0:T(8,128)(2,1)} %param.9) | copy-start | bytes 7077892
  38.5 2.9 %copy-start.5 = (f32[4]{0:T(128)S(1)}, f32[4]{0:T(128)}, u32[]{:S(2)}) copy-start(f32[4]{0:T(128)} %param.11) | copy-start | bytes 52
  38.5 2.9 %copy-start = (bf16[256,768]{1,0:T(8,128)(2,1)S(1)}, bf16[256,768]{1,0:T(8,128)(2,1)}, u32[]{:S(2)}) copy-start(bf16[256,768]{1,0:T(8,128)(2,1)} %fusion.30.hid_ref) | copy-start | bytes 1179652
  38.5 2.9 %collective-permute-start.4 = (bf16[256,768]{1,0:T(8,128)(2,1)}, bf16[256,768]{1,0:T(8,128)(2,1)S(1)}, u32[]{:S(2)}, u32[]{:S(2)}) collective-permute-start(bf16[256,768]{1,0:T(8,128)(2,1)} %fusion.30.hid_ref), channel_id=1, source_target_pairs={{0,4},{4,0},{1,5},{5,1},{2,6},{6,2},{3,7},{7,3},{8,12},{12,8},{9,1... | collective-permute-start | bytes 1179656 | tf_op jit(solution)/shard_map/ppermute | solution.py:190
  156.4 3.1 %collective-permute-start.5 = (f32[256,512]{1,0:T(8,128)S(1)}, f32[256,512]{1,0:T(8,128)S(1)}, u32[]{:S(2)}, u32[]{:S(2)}) collective-permute-start(f32[256,512]{1,0:T(8,128)S(1)} %slice.110), channel_id=1, source_target_pairs={{0,4},{4,0},{1,5},{5,1},{2,6},{6,2},{3,7},{7,3},{8,12},{12,8},{9,1... | collective-permute-start | bytes 1572872 | tf_op jit(solution)/shard_map/ppermute | solution.py:193
  158.1 1.4 collective-permute-start.6
  159.5 0.7 copy-start.4
  160.1 0.8 copy-start.3
Sparse Core Ops, SparseCore 0:
  38.6 67.0 all-gather.1

commit v3 on v2

--- a/solution.py
+++ b/solution.py
@@ -44,22 +44,35 @@
     return parts
 
 
-def attend_kernel(heads, head_size, nk, hq_ref, hkv_ref, wq_ref, wkv_ref, scale_ref,
-                  o_ref, st_ref, q_sc, m_sc, l_sc, acc_sc):
+def attend_kernel(first, heads, head_size, nk, *refs):
+    if first:
+        hq_ref, hkv_ref, wq_ref, wkv_ref, scale_ref, q_out, o_ref, st_ref = refs[:8]
+    else:
+        q_in, hkv_ref, wkv_ref, o_in, st_in, o_ref, st_ref = refs[:7]
+    q_sc, m_sc, l_sc, acc_sc = refs[-4:]
     j = pl.program_id(0)
     width = heads * head_size
 
     @pl.when(j == 0)
     def _():
-        proj = jnp.dot(hq_ref[...], wq_ref[...], preferred_element_type=jnp.float32)
-        normed = head_norm(proj, heads, head_size)
-        scale = scale_ref[...]
-        for h in range(heads):
-            cols = slice(h * head_size, (h + 1) * head_size)
-            q_sc[:, cols] = (normed[h] * scale[:, cols]).astype(jnp.bfloat16)
-        m_sc[...] = jnp.full(m_sc.shape, -jnp.inf, jnp.float32)
-        l_sc[...] = jnp.zeros(l_sc.shape, jnp.float32)
-        acc_sc[...] = jnp.zeros(acc_sc.shape, jnp.float32)
+        if first:
+            proj = jnp.dot(hq_ref[...], wq_ref[...], preferred_element_type=jnp.float32)
+            normed = head_norm(proj, heads, head_size)
+            scale = scale_ref[...]
+            for h in range(heads):
+                cols = slice(h * head_size, (h + 1) * head_size)
+                q_sc[:, cols] = (normed[h] * scale[:, cols]).astype(jnp.bfloat16)
+            q_out[...] = q_sc[...]
+            m_sc[...] = jnp.full(m_sc.shape, -jnp.inf, jnp.float32)
+            l_sc[...] = jnp.zeros(l_sc.shape, jnp.float32)
+            acc_sc[...] = jnp.zeros(acc_sc.shape, jnp.float32)
+        else:
+            q_sc[...] = q_in[...]
+            acc_sc[...] = o_in[...]
+            st = st_in[...]
+            for h in range(heads):
+                m_sc[h] = jnp.broadcast_to(st[:, h : h + 1], m_sc.shape[1:])
+                l_sc[h] = jnp.broadcast_to(st[:, 64 + h : 65 + h], l_sc.shape[1:])
 
     kv = jnp.dot(hkv_ref[...], wkv_ref[...], preferred_element_type=jnp.float32)
     keys = head_norm(kv[:, :width], heads, head_size)
@@ -91,30 +104,50 @@
         st_ref[...] = packed
 
 
-def attend_partial(hidden_q, hidden_kv, wq, wkv, scale_row, heads, head_size, tk=512):
-    q_rows, channels = hidden_q.shape
-    k_rows = hidden_kv.shape[0]
+def attend_chunk(state, hidden_kv, wkv, heads, head_size, tk=512, first=None):
+    k_rows, channels = hidden_kv.shape
     width = heads * head_size
     nk = k_rows // tk
     whole = lambda j: (0, 0)
-    return pl.pallas_call(
-        functools.partial(attend_kernel, heads, head_size, nk),
-        grid=(nk,),
-        in_specs=[
+    if state is None:
+        hidden_q, wq, scale_row = first
+        q_rows = hidden_q.shape[0]
+        args = (hidden_q, hidden_kv, wq, wkv, scale_row)
+        in_specs = [
             pl.BlockSpec((q_rows, channels), whole),
             pl.BlockSpec((tk, channels), lambda j: (j, 0)),
             pl.BlockSpec((channels, width), whole),
             pl.BlockSpec((channels, 2 * width), whole),
             pl.BlockSpec((1, width), whole),
-        ],
-        out_specs=[
+        ]
+        out_specs = [pl.BlockSpec((q_rows, width), whole)]
+        out_shape = [jax.ShapeDtypeStruct((q_rows, width), jnp.bfloat16)]
+        aliases = {}
+    else:
+        queries, o_prev, st_prev = state
+        q_rows = queries.shape[0]
+        args = (queries, hidden_kv, wkv, o_prev, st_prev)
+        in_specs = [
+            pl.BlockSpec((q_rows, width), whole),
+            pl.BlockSpec((tk, channels), lambda j: (j, 0)),
+            pl.BlockSpec((channels, 2 * width), whole),
             pl.BlockSpec((q_rows, width), whole),
             pl.BlockSpec((q_rows, 128), whole),
-        ],
-        out_shape=[
-            jax.ShapeDtypeStruct((q_rows, width), jnp.float32),
-            jax.ShapeDtypeStruct((q_rows, 128), jnp.float32),
-        ],
+        ]
+        out_specs, out_shape = [], []
+        aliases = {3: 0, 4: 1}
+    out_specs += [pl.BlockSpec((q_rows, width), whole), pl.BlockSpec((q_rows, 128), whole)]
+    out_shape += [
+        jax.ShapeDtypeStruct((q_rows, width), jnp.float32),
+        jax.ShapeDtypeStruct((q_rows, 128), jnp.float32),
+    ]
+    outs = pl.pallas_call(
+        functools.partial(attend_kernel, state is None, heads, head_size, nk),
+        grid=(nk,),
+        in_specs=in_specs,
+        out_specs=out_specs,
+        out_shape=out_shape,
+        input_output_aliases=aliases,
         scratch_shapes=[
             pltpu.VMEM((q_rows, width), jnp.bfloat16),
             pltpu.VMEM((heads, q_rows, 128), jnp.float32),
@@ -127,7 +160,10 @@
             transcendentals=q_rows * k_rows * heads,
             bytes_accessed=k_rows * channels * 2 + q_rows * width * 8,
         ),
-    )(hidden_q, hidden_kv, wq, wkv, scale_row)
+    )(*args)
+    if state is None:
+        return tuple(outs)
+    return (queries,) + tuple(outs)
 
 
 def finish_kernel(heads, head_size, o_ref, st_ref, og_ref, sg_ref, hid_ref, wo_ref, out_ref):
@@ -186,10 +222,15 @@
     wkv = qkv_weight[:, width_all:]
 
     swap = [(0, 1), (1, 0)]
-    hidden_all = lax.all_gather(hidden, "zx", axis=0, tiled=True)
     hidden_other = lax.ppermute(hidden, "core", swap)
     hidden_q = jnp.concatenate([hidden, hidden_other], axis=0)
-    o_part, st_part = attend_partial(hidden_q, hidden_all, wq, wkv, scale_row, head_count, head_size)
+    chunks = 4
+    piece = row_count // chunks
+    state = None
+    for c in range(chunks):
+        gathered = lax.all_gather(hidden[c * piece : (c + 1) * piece], "zx", axis=0, tiled=True)
+        state = attend_chunk(state, gathered, wkv, head_count, head_size, first=(hidden_q, wq, scale_row))
+    _, o_part, st_part = state
     o_got, st_got = lax.ppermute((o_part[row_count:], st_part[row_count:]), "core", swap)
     return finish(o_part, st_part, o_got, st_got, hidden, out_weight, head_count, head_size)
 

time: 172 us -> 254 us (1.48)
  waiting for transfers between devices: 67.5 us -> 138 us
  Pallas kernels: 52.3 us -> 64.3 us
    all_gather x1 -> x4, waiting for transfers between devices: 63.4 us -> 133 us  [body(): lax.all_gather(hidden[c * piece:(c + 1) * piece], 'zx', axis=0, tiled=True)]
    pallas_call x1 -> x4, Pallas kernels: 49 us -> 60.9 us  [attend_chunk(): pl.pallas_call(functools.partial(attend_kernel, state is None, heads, hea...]
  transfers between devices with their start and end apart: 8 -> 11, of which waited for: 4 -> 6; matrix products, arithmetic and copies ran while one was open for 7% -> 5% of each run, Pallas kernels for 0% -> 18%
where the time goes in v3:
time: 254 us
  waiting for transfers between devices  138 us (54%)
  Pallas kernels  64.3 us (25%)
  matrix products  15.5 us (6%)
  between operations  13.4 us (5%)
  starting transfers between devices  13.1 us (5%)
  local copies, waits for them, and re-layouts  7.97 us (3%)
    all_gather x4, waiting for transfers between devices, body(): lax.all_gather(hidden[c * piece:(c + 1) * piece], 'zx', axis=0, tiled=True)  133 us
    pallas_call x4, Pallas kernels, attend_chunk(): pl.pallas_call(functools.partial(attend_kernel, state is None, heads, hea...  60.9 us
    dot_general x8, matrix products, convolve(): jnp.dot(padded[offset:offset + row_count], weight[offset], preferred_elem...  12.2 us
    ppermute x2, starting transfers between devices, padded_2(): lax.ppermute(lax.slice_in_dim(block, block.shape[0] - width, None, axis=0...  5.63 us
    ppermute x2, starting transfers between devices, padded_2(): lax.ppermute(lax.slice_in_dim(block, 0, width, axis=0), SEQ_AXES, backward)  5.25 us
  transfers between devices with their start and end apart: 11, of which 6 were waited for; matrix products, arithmetic and copies ran while one was open for 5% of the time, Pallas kernels for 18%

profile of v3, /device:TPU:1, one launch (start us, length us, event | category | flops | bytes accessed | tf_op | source)
XLA Modules:
  0.0 253.5 jit_solution(655013124187374563)
XLA Ops:
  6.5 0.8 fusion.77
  7.3 3.3 %collective-permute-start.1 = (bf16[2,1536]{1,0:T(2,128)(2,1)S(1)}, bf16[2,1536]{1,0:T(2,128)(2,1)S(1)}, u32[]{:S(2)}, u32[]{:S(2)}) collective-permute-start(bf16[2,1536]{1,0:T(2,128)(2,1)S(1)} %get-tuple-element.24), channel_id=1, source_target_pairs={{4,0},{8,4},{12,8},{16,12},{20,16},{24,20},{28,24},{32,28},{36,32}... | collective-permute-start | bytes 18440 | tf_op jit(solution)/shard_map/ppermute | solution.py:21
  10.7 3.2 %collective-permute-start = (bf16[2,1536]{1,0:T(2,128)(2,1)S(1)}, bf16[2,1536]{1,0:T(2,128)(2,1)S(1)}, u32[]{:S(2)}, u32[]{:S(2)}) collective-permute-start(bf16[2,1536]{1,0:T(2,128)(2,1)S(1)} %get-tuple-element.23), channel_id=1, source_target_pairs={{0,4},{4,8},{8,12},{12,16},{16,20},{20,24},{24,28},{28,32},{32,36}... | collective-permute-start | bytes 18440 | tf_op jit(solution)/shard_map/ppermute | solution.py:20
  13.9 2.7 %fusion.4 = f32[256,768]{1,0:T(8,128)S(1)} fusion(bf16[256,1536]{1,0:T(8,128)(2,1)} %param.6, bf16[5,1536,768]{2,1,0:T(8,128)(2,1)} %param.7), kind=kOutput, calls=%fused_computation.4 | convolution fusion | flops 603979776 | bytes 3932160 | tf_op jit(solution)/shard_map/dot_general | solution.py:28
  16.6 0.1 constant_dynamic-update-slice_fusion.1
  16.7 2.5 fusion
  19.2 2.5 fusion.2
  21.7 0.0 slice-start
  21.7 2.6 %fusion.6 = f32[256,768]{1,0:T(8,128)S(1)} fusion(bf16[5,1536,768]{2,1,0:T(8,128)(2,1)} %param.7, bf16[256,1536]{1,0:T(8,128)(2,1)S(1)} %copy-done.2, bf16[2,1536]{1,0:T(2,128)(2,1)S(1)} %collective-permute-done), kind=kOutput, calls=%fused_computation.6 | convolution fusion | flops 605552640 | bytes 3938304 | tf_op jit(solution)/shard_map/dot_general | solution.py:28
  24.3 0.0 slice-start.1
  24.3 2.8 %fusion.57 = bf16[256,768]{1,0:T(8,128)(2,1)S(1)} fusion(f32[256,768]{1,0:T(8,128)S(1)} %fusion, f32[256,768]{1,0:T(8,128)S(1)} %fusion.2, f32[256,768]{1,0:T(8,128)S(1)} %fusion.4, f32[256,768]{1,0:T(8,128)S(1)} %fusion.6, bf16[5,1536,768]{2,1,0:T(8,128)(2,1)} %param.7, bf16[2,1536]{1,0:T(2,128)(2,1)S(1)} %collective-permute-done, ...), kind=kOutput, calls=%fused_computation.49 | convolution fusion | flops 608108544 | bytes 6690816 | tf_op jit(solution)/shard_map/dot_general | solution.py:26
  27.1 2.4 collective-permute-start.2
  29.5 0.5 fusion.34
  30.0 1.9 collective-permute-start.3
  31.9 0.5 fusion.36
  32.4 2.5 collective-permute-done.3
  34.9 0.5 fusion.31
  35.4 0.5 fusion.23
  36.0 0.5 fusion.30.hid_ref
  36.5 0.7 fusion.78
  37.2 0.0 all-gather.5.cloned.1.call-update
  37.2 0.0 all-gather.11.cloned.1.call-start
  37.3 0.7 all-gather.11.cloned.1.call-update
  38.0 0.0 all-gather.9.cloned.1.call-start
  38.0 0.7 all-gather.9.cloned.1.call-update
  38.7 0.0 all-gather.7.cloned.1.call-start
  38.8 0.5 all-gather.7.cloned.1.call-update
  39.3 0.3 collective-permute-start.4
  39.6 1.4 slice.122.refs_3_.refs_2_
  41.0 1.0 slice.121.refs_2_
  42.0 0.9 pad_maximum_fusion.2.refs_0_
  42.9 42.7 %all-gather.5.cloned.1.call-done.refs_1_ = bf16[1024,768]{1,0:T(8,128)(2,1)} async-done(((bf16[64,768]{1,0:T(8,128)(2,1)}), bf16[1024,768]{1,0:T(8,128)(2,1)}) %all-gather.5.cloned.1.call-update) | async-done | bytes 1572880 | tf_op jit(solution)/shard_map/all_gather | solution.py:231
  85.6 0.6 broadcast_in_dim.3
  86.2 15.7 %shard_map.64 = (bf16[512,512]{1,0:T(8,128)(2,1)}, f32[512,512]{1,0:T(8,128)}, f32[512,128]{1,0:T(8,128)}) custom-call(bf16[512,768]{1,0:T(8,128)(2,1)} %pad_maximum_fusion.2.refs_0_, bf16[1024,768]{1,0:T(8,128)(2,1)} %all-gather.5.cloned.1.call-done.refs_1_, bf16[768,512]{1,0:T(8,128)(2,1)} %slice.121.refs_2_, bf16[768,1024]{1,0:T(8,128)(2,1)} %slice.122.refs_3_.refs_2_, ...), custom_call_target="tpu_custom_call" | custom-call | flops 2684354560 | bytes 3670016 | tf_op jit(solution)/shard_map/pallas_call | solution.py:144
  101.9 29.2 %all-gather.11.cloned.1.call-done.refs_1_ = bf16[1024,768]{1,0:T(8,128)(2,1)} async-done(((bf16[64,768]{1,0:T(8,128)(2,1)}), bf16[1024,768]{1,0:T(8,128)(2,1)}) %all-gather.11.cloned.1.call-update) | async-done | bytes 1572880 | tf_op jit(solution)/shard_map/all_gather | solution.py:231
  131.1 15.1 %shard_map.65 = (f32[512,512]{1,0:T(8,128)}, f32[512,128]{1,0:T(8,128)}) custom-call(bf16[512,512]{1,0:T(8,128)(2,1)} %get-tuple-element.14.refs_0_, bf16[1024,768]{1,0:T(8,128)(2,1)} %all-gather.11.cloned.1.call-done.refs_1_, bf16[768,1024]{1,0:T(8,128)(2,1)} %slice.122.refs_3_.refs_2_, ...), custom_call_target="tpu_custom_call", output_to_operand_aliasing={{0}: (3, {}), {1}: (4, {})} | custom-call | flops 2684354560 | bytes 3670016 | tf_op jit(solution)/shard_map/pallas_call | solution.py:144
  146.2 30.4 %all-gather.9.cloned.1.call-done.refs_1_ = bf16[1024,768]{1,0:T(8,128)(2,1)} async-done(((bf16[64,768]{1,0:T(8,128)(2,1)}), bf16[1024,768]{1,0:T(8,128)(2,1)}) %all-gather.9.cloned.1.call-update) | async-done | bytes 1572880 | tf_op jit(solution)/shard_map/all_gather | solution.py:231
  176.6 15.1 %shard_map.66 = (f32[512,512]{1,0:T(8,128)}, f32[512,128]{1,0:T(8,128)}) custom-call(bf16[512,512]{1,0:T(8,128)(2,1)} %get-tuple-element.14.refs_0_, bf16[1024,768]{1,0:T(8,128)(2,1)} %all-gather.9.cloned.1.call-done.refs_1_, bf16[768,1024]{1,0:T(8,128)(2,1)} %slice.122.refs_3_.refs_2_, ...), custom_call_target="tpu_custom_call", output_to_operand_aliasing={{0}: (3, {}), {1}: (4, {})} | custom-call | flops 2684354560 | bytes 3670016 | tf_op jit(solution)/shard_map/pallas_call | solution.py:144
  191.7 30.3 %all-gather.7.cloned.1.call-done.refs_1_ = bf16[1024,768]{1,0:T(8,128)(2,1)} async-done(((bf16[64,768]{1,0:T(8,128)(2,1)}), bf16[1024,768]{1,0:T(8,128)(2,1)}) %all-gather.7.cloned.1.call-update) | async-done | bytes 1572880 | tf_op jit(solution)/shard_map/all_gather | solution.py:231
  222.0 15.1 %shard_map.67 = (f32[512,512]{1,0:T(8,128)}, f32[512,128]{1,0:T(8,128)}) custom-call(bf16[512,512]{1,0:T(8,128)(2,1)} %get-tuple-element.14.refs_0_, bf16[1024,768]{1,0:T(8,128)(2,1)} %all-gather.7.cloned.1.call-done.refs_1_, bf16[768,1024]{1,0:T(8,128)(2,1)} %slice.122.refs_3_.refs_2_, ...), custom_call_target="tpu_custom_call", output_to_operand_aliasing={{0}: (3, {}), {1}: (4, {})} | custom-call | flops 2684354560 | bytes 3670016 | tf_op jit(solution)/shard_map/pallas_call | solution.py:144
  237.0 1.1 slice.126
  238.1 1.7 collective-permute-start.5
  239.8 0.9 slice.127
  240.7 0.1 collective-permute-start.6
  240.8 1.3 collective-permute-done.6.sg_ref
  242.2 0.6 copy-done.4
  242.8 0.8 copy-done.3
  243.6 3.4 %shard_map.68 = bf16[256,768]{1,0:T(8,128)(2,1)} custom-call(f32[512,512]{1,0:T(8,128)} %get-tuple-element.21.o_ref, f32[512,128]{1,0:T(8,128)} %get-tuple-element.22.st_ref, f32[256,512]{1,0:T(8,128)} %copy-done.3, f32[256,128]{1,0:T(8,128)} %copy-done.4, bf16[256,768]{1,0:T(8,128)(2,1)} %copy-done, bf16[512,768]{1,0:T(8,128)(2,1)} %wo_ref.1), custom_call_target="tpu_custom_call" | custom-call | tf_op jit(solution)/shard_map/pallas_call | solution.py:194
  (22 shorter events, 0.1 us)
Async XLA Ops:
  6.5 79.1 %all-gather.5.cloned.1.call-start = ((), (), s32[]{:S(2)}) async-start(), calls=%async_computation | async-start | bytes 1671168 | tf_op jit(solution)/shard_map/all_gather | solution.py:231
  7.3 9.4 %collective-permute-start.1 = (bf16[2,1536]{1,0:T(2,128)(2,1)S(1)}, bf16[2,1536]{1,0:T(2,128)(2,1)S(1)}, u32[]{:S(2)}, u32[]{:S(2)}) collective-permute-start(bf16[2,1536]{1,0:T(2,128)(2,1)S(1)} %get-tuple-element.24), channel_id=1, source_target_pairs={{4,0},{8,4},{12,8},{16,12},{20,16},{24,20},{28,24},{32,28},{36,32}... | collective-permute-start | bytes 18440 | tf_op jit(solution)/shard_map/ppermute | solution.py:21
  10.6 6.0 %copy-start.2 = (bf16[256,1536]{1,0:T(8,128)(2,1)S(1)}, bf16[256,1536]{1,0:T(8,128)(2,1)}, u32[]{:S(2)}) copy-start(bf16[256,1536]{1,0:T(8,128)(2,1)} %param.6) | copy-start | bytes 2359300
  10.7 11.0 %collective-permute-start = (bf16[2,1536]{1,0:T(2,128)(2,1)S(1)}, bf16[2,1536]{1,0:T(2,128)(2,1)S(1)}, u32[]{:S(2)}, u32[]{:S(2)}) collective-permute-start(bf16[2,1536]{1,0:T(2,128)(2,1)S(1)} %get-tuple-element.23), channel_id=1, source_target_pairs={{0,4},{4,8},{8,12},{12,16},{16,20},{20,24},{24,28},{28,32},{32,36}... | collective-permute-start | bytes 18440 | tf_op jit(solution)/shard_map/ppermute | solution.py:20
  21.7 7.8 %slice-start = ((s8[5898240]{0:T(1024)(128)(4,1)}), s8[4194304]{0:T(1024)(128)(4,1)S(1)}, s32[]{:S(2)}) async-start(s8[5898240]{0:T(1024)(128)(4,1)} %bitcast.45), calls=%async_computation.4 | async-start | bytes 8388608
  24.3 5.2 %slice-start.1 = ((s8[5898240]{0:T(1024)(128)(4,1)}), s8[1703936]{0:T(1024)(128)(4,1)S(1)}, s32[]{:S(2)}) async-start(s8[5898240]{0:T(1024)(128)(4,1)} %bitcast.45), calls=%async_computation.5 | async-start | bytes 3407872
  27.1 4.9 %collective-permute-start.2 = (bf16[2,768]{1,0:T(2,128)(2,1)S(1)}, bf16[2,768]{1,0:T(2,128)(2,1)S(1)}, u32[]{:S(2)}, u32[]{:S(2)}) collective-permute-start(bf16[2,768]{1,0:T(2,128)(2,1)S(1)} %get-tuple-element.29), channel_id=1, source_target_pairs={{0,4},{4,8},{8,12},{12,16},{16,20},{20,24},{24,28},{28,32},{32,36}... | collective-permute-start | bytes 9224 | tf_op jit(solution)/shard_map/ppermute | solution.py:20
  30.0 4.9 %collective-permute-start.3 = (bf16[2,768]{1,0:T(2,128)(2,1)S(1)}, bf16[2,768]{1,0:T(2,128)(2,1)S(1)}, u32[]{:S(2)}, u32[]{:S(2)}) collective-permute-start(bf16[2,768]{1,0:T(2,128)(2,1)S(1)} %get-tuple-element.30), channel_id=1, source_target_pairs={{4,0},{8,4},{12,8},{16,12},{20,16},{24,20},{28,24},{32,28},{36,32}... | collective-permute-start | bytes 9224 | tf_op jit(solution)/shard_map/ppermute | solution.py:21
  35.9 3.6 %copy-start.1 = (bf16[768,1536]{1,0:T(8,128)(2,1)S(1)}, bf16[768,1536]{1,0:T(8,128)(2,1)}, u32[]{:S(2)}) copy-start(bf16[768,1536]{1,0:T(8,128)(2,1)} %param.9) | copy-start | bytes 7077892
  36.5 5.5 %copy-start = (bf16[256,768]{1,0:T(8,128)(2,1)}, bf16[256,768]{1,0:T(8,128)(2,1)S(1)}, u32[]{:S(2)}) copy-start(bf16[256,768]{1,0:T(8,128)(2,1)S(1)} %fusion.30.hid_ref) | copy-start | bytes 1179652
  37.2 93.9 %all-gather.11.cloned.1.call-start = ((), (), s32[]{:S(2)}) async-start(), calls=%async_computation.3 | async-start | bytes 1671168 | tf_op jit(solution)/shard_map/all_gather | solution.py:231
  38.0 138.6 %all-gather.9.cloned.1.call-start = ((), (), s32[]{:S(2)}) async-start(), calls=%async_computation.2 | async-start | bytes 1671168 | tf_op jit(solution)/shard_map/all_gather | solution.py:231
  38.7 183.2 %all-gather.7.cloned.1.call-start = ((), (), s32[]{:S(2)}) async-start(), calls=%async_computation.1 | async-start | bytes 1671168 | tf_op jit(solution)/shard_map/all_gather | solution.py:231
  39.3 2.6 %copy-start.5 = (f32[4]{0:T(128)S(1)}, f32[4]{0:T(128)}, u32[]{:S(2)}) copy-start(f32[4]{0:T(128)} %param.11) | copy-start | bytes 52
  39.3 2.6 %collective-permute-start.4 = (bf16[256,768]{1,0:T(8,128)(2,1)S(1)}, bf16[256,768]{1,0:T(8,128)(2,1)S(1)}, u32[]{:S(2)}, u32[]{:S(2)}) collective-permute-start(bf16[256,768]{1,0:T(8,128)(2,1)S(1)} %fusion.30.hid_ref), channel_id=1, source_target_pairs={{0,4},{4,0},{1,5},{5,1},{2,6},{6,2},{3,7},{7,3},{8,12},{12,8},{9,1... | collective-permute-start | bytes 1179656 | tf_op jit(solution)/shard_map/ppermute | solution.py:225
  238.1 4.0 %collective-permute-start.5 = (f32[256,512]{1,0:T(8,128)S(1)}, f32[256,512]{1,0:T(8,128)S(1)}, u32[]{:S(2)}, u32[]{:S(2)}) collective-permute-start(f32[256,512]{1,0:T(8,128)S(1)} %slice.126), channel_id=1, source_target_pairs={{0,4},{4,0},{1,5},{5,1},{2,6},{6,2},{3,7},{7,3},{8,12},{12,8},{9,1... | collective-permute-start | bytes 1572872 | tf_op jit(solution)/shard_map/ppermute | solution.py:234
  240.7 1.4 collective-permute-start.6
  242.2 0.7 copy-start.4
  242.8 0.8 copy-start.3
Sparse Core Ops, SparseCore 0:
  37.4 48.2 all-gather.4
  87.8 43.3 all-gather.10
  133.3 43.3 all-gather.8
  178.6 43.3 all-gather.6

commit v4 on v2

v4 whole, which is shorter than its diff:
```python
import functools
import math

import jax
import jax.numpy as jnp
import numpy as np
from jax import lax
from jax.experimental import pallas as pl
from jax.experimental.pallas import tpu as pltpu
from jax.sharding import Mesh
from jax.sharding import PartitionSpec as P

SEQ_AXES = ("zx", "core")


def padded_2(block, width):
    count = lax.axis_size(SEQ_AXES)
    forward = [(i, i + 1) for i in range(count - 1)]
    backward = [(target, source) for source, target in forward]
    low = lax.ppermute(lax.slice_in_dim(block, block.shape[0] - width, None, axis=0), SEQ_AXES, forward)
    high = lax.ppermute(lax.slice_in_dim(block, 0, width, axis=0), SEQ_AXES, backward)
    return jnp.concatenate([low, block, high], axis=0)


def convolve(padded, weight, row_count):
    conv_sum = jnp.dot(padded[0:row_count], weight[0], preferred_element_type=jnp.float32)
    for offset in range(1, weight.shape[0]):
        conv_sum = conv_sum + jnp.dot(
            padded[offset : offset + row_count], weight[offset], preferred_element_type=jnp.float32
        )
    return conv_sum


def head_rms(tensor):
    return tensor * lax.rsqrt(jnp.mean(tensor * tensor, axis=-1, keepdims=True) + 1e-06)


def head_norm(block, heads, head_size):
    parts = []
    for h in range(heads):
        part = block[:, h * head_size : (h + 1) * head_size]
        mean_sq = jnp.mean(part * part, axis=1, keepdims=True)
        parts.append(part * lax.rsqrt(mean_sq + 1e-06))
    return parts


def attend_kernel(heads, head_size, nk, hq_ref, hkv_ref, wqt_ref, wk_ref, wvt_ref, scale_ref,
                  o_ref, st_ref, qt_sc, m_sc, l_sc, acc_sc):
    j = pl.program_id(0)
    contract_last = (((1,), (1,)), ((), ()))

    @pl.when(j == 0)
    def _():
        proj_t = lax.dot_general(
            wqt_ref[...], hq_ref[...], contract_last, preferred_element_type=jnp.float32
        )
        for h in range(heads):
            rows = slice(h * head_size, (h + 1) * head_size)
            part = proj_t[rows, :]
            mean_sq = jnp.mean(part * part, axis=0, keepdims=True)
            normed = part * lax.rsqrt(mean_sq + 1e-06)
            qt_sc[rows, :] = (normed * scale_ref[rows, :]).astype(jnp.bfloat16)
        m_sc[...] = jnp.full(m_sc.shape, -jnp.inf, jnp.float32)
        l_sc[...] = jnp.zeros(l_sc.shape, jnp.float32)
        acc_sc[...] = jnp.zeros(acc_sc.shape, jnp.float32)

    hkv = hkv_ref[...]
    k_all = jnp.dot(hkv, wk_ref[...], preferred_element_type=jnp.float32)
    v_t = lax.dot_general(wvt_ref[...], hkv, contract_last, preferred_element_type=jnp.float32)
    for h in range(heads):
        rows = slice(h * head_size, (h + 1) * head_size)
        k_h = k_all[:, rows]
        k_h = (k_h * lax.rsqrt(jnp.mean(k_h * k_h, axis=1, keepdims=True) + 1e-06)).astype(
            jnp.bfloat16
        )
        s_t = jnp.dot(k_h, qt_sc[rows, :], preferred_element_type=jnp.float32)
        m_prev = m_sc[h]
        m_next = jnp.maximum(m_prev, jnp.max(s_t, axis=0, keepdims=True))
        alpha = jnp.exp(m_prev - m_next)
        p_t = jnp.exp(s_t - m_next)
        l_sc[h] = alpha * l_sc[h] + jnp.sum(p_t, axis=0, keepdims=True)
        acc_sc[rows, :] = alpha * acc_sc[rows, :] + jnp.dot(
            v_t[rows, :].astype(jnp.bfloat16), p_t.astype(jnp.bfloat16),
            preferred_element_type=jnp.float32,
        )
        m_sc[h] = m_next

    @pl.when(j == nk - 1)
    def _():
        o_ref[...] = acc_sc[...]
        for h in range(heads):
            st_ref[h : h + 1, :] = m_sc[h]
            st_ref[heads + h : heads + h + 1, :] = l_sc[h]


def attend_partial(hidden_q, hidden_kv, wqt, wk, wvt, scale_col, heads, head_size, tk=512):
    q_rows, channels = hidden_q.shape
    k_rows = hidden_kv.shape[0]
    width = heads * head_size
    nk = k_rows // tk
    whole = lambda j: (0, 0)
    return pl.pallas_call(
        functools.partial(attend_kernel, heads, head_size, nk),
        grid=(nk,),
        in_specs=[
            pl.BlockSpec((q_rows, channels), whole),
            pl.BlockSpec((tk, channels), lambda j: (j, 0)),
            pl.BlockSpec((width, channels), whole),
            pl.BlockSpec((channels, width), whole),
            pl.BlockSpec((width, channels), whole),
            pl.BlockSpec((width, 1), whole),
        ],
        out_specs=[
            pl.BlockSpec((width, q_rows), whole),
            pl.BlockSpec((2 * heads, q_rows), whole),
        ],
        out_shape=[
            jax.ShapeDtypeStruct((width, q_rows), jnp.float32),
            jax.ShapeDtypeStruct((2 * heads, q_rows), jnp.float32),
        ],
        scratch_shapes=[
            pltpu.VMEM((width, q_rows), jnp.bfloat16),
            pltpu.VMEM((heads, 1, q_rows), jnp.float32),
            pltpu.VMEM((heads, 1, q_rows), jnp.float32),
            pltpu.VMEM((width, q_rows), jnp.float32),
        ],
        compiler_params=pltpu.CompilerParams(dimension_semantics=("arbitrary",)),
        cost_estimate=pl.CostEstimate(
            flops=4 * q_rows * k_rows * width + 2 * k_rows * channels * 2 * width,
            transcendentals=q_rows * k_rows * heads,
            bytes_accessed=k_rows * channels * 2 + q_rows * width * 8,
        ),
    )(hidden_q, hidden_kv, wqt, wk, wvt, scale_col)


def finish_kernel(heads, head_size, o_ref, st_ref, og_ref, sg_ref, hid_ref, wo_ref, out_ref):
    st_own = st_ref[...]
    st_got = sg_ref[...]
    mixed = []
    for h in range(heads):
        rows = slice(h * head_size, (h + 1) * head_size)
        m_own = st_own[h : h + 1, :]
        m_got = st_got[h : h + 1, :]
        m_all = jnp.maximum(m_own, m_got)
        w_own = jnp.exp(m_own - m_all)
        w_got = jnp.exp(m_got - m_all)
        denom = st_own[heads + h : heads + h + 1, :] * w_own + st_got[heads + h : heads + h + 1, :] * w_got
        mixed.append((o_ref[rows, :] * w_own + og_ref[rows, :] * w_got) / denom)
    attended = jnp.concatenate(mixed, axis=0).T.astype(jnp.bfloat16)
    out = hid_ref[...].astype(jnp.float32) + jnp.dot(
        attended, wo_ref[...], preferred_element_type=jnp.float32
    )
    out_ref[...] = out.astype(out_ref.dtype)


def finish(o_part, st_part, o_got, st_got, hidden, out_weight, heads, head_size):
    rows, width_out = hidden.shape
    width = heads * head_size
    whole = lambda i: (0, 0)
    return pl.pallas_call(
        functools.partial(finish_kernel, heads, head_size),
        grid=(1,),
        in_specs=[
            pl.BlockSpec((width, rows), whole),
            pl.BlockSpec((2 * heads, rows), whole),
            pl.BlockSpec((width, rows), whole),
            pl.BlockSpec((2 * heads, rows), whole),
            pl.BlockSpec((rows, width_out), whole),
            pl.BlockSpec((width, width_out), whole),
        ],
        out_specs=pl.BlockSpec((rows, width_out), whole),
        out_shape=jax.ShapeDtypeStruct((rows, width_out), jnp.bfloat16),
    )(o_part, st_part, o_got, st_got, hidden, out_weight)


def body(sequence_input, conv_first, conv_second, qkv_weight, out_weight, logit_scale):
    row_count = sequence_input.shape[0]
    padded_input = padded_2(sequence_input, 2)
    first_out = jax.nn.gelu(convolve(padded_input, conv_first, row_count)).astype(jnp.bfloat16)
    padded_first = padded_2(first_out, 2)
    second = convolve(padded_first, conv_second, row_count)
    hidden = (first_out.astype(jnp.float32) + second).astype(jnp.bfloat16)
    head_count = logit_scale.shape[0]
    width_all = qkv_weight.shape[1] // 3
    head_size = width_all // head_count
    scale_col = jnp.repeat(logit_scale / math.sqrt(head_size), head_size)[:, None]
    wqt = qkv_weight[:, :width_all].T
    wk = qkv_weight[:, width_all : 2 * width_all]
    wvt = qkv_weight[:, 2 * width_all :].T

    swap = [(0, 1), (1, 0)]
    hidden_all = lax.all_gather(hidden, "zx", axis=0, tiled=True)
    hidden_other = lax.ppermute(hidden, "core", swap)
    hidden_q = jnp.concatenate([hidden, hidden_other], axis=0)
    o_part, st_part = attend_partial(hidden_q, hidden_all, wqt, wk, wvt, scale_col, head_count, head_size)
    o_got, st_got = lax.ppermute((o_part[:, row_count:], st_part[:, row_count:]), "core", swap)
    return finish(o_part, st_part, o_got, st_got, hidden, out_weight, head_count, head_size)


def solution(mesh):
    devices = np.asarray(mesh.devices)
    seq_size = mesh.shape["seq"]
    batch_size = mesh.shape["batch"]
    order = [mesh.axis_names.index("seq"), mesh.axis_names.index("batch")]
    devices = devices.transpose(order).reshape(seq_size // 2, 2, batch_size)
    split_mesh = Mesh(devices, ("zx", "core", "batch"))
    rows = P(("batch", "zx", "core"), None)
    in_specs = (rows, P(), P(), P(), P(), P())
    return jax.shard_map(body, mesh=split_mesh, in_specs=in_specs, out_specs=rows, check_vma=False)
```

time: 172 us -> 149 us (0.87)
  Pallas kernels: 52.3 us -> 31.1 us
  waiting for transfers between devices: 67.5 us -> 64 us
  local copies, waits for them, and re-layouts: 7.72 us -> 10.1 us
    pallas_call x1, Pallas kernels: 49 us -> 28.3 us  [attend_partial(): pl.pallas_call(functools.partial(attend_kernel, heads, head_size, nk), gr...]
    all_gather x1, waiting for transfers between devices: 63.4 us -> 60.1 us  [body(): hidden_all = lax.all_gather(hidden, 'zx', axis=0, tiled=True)]
    unnamed x17, local copies, waits for them, and re-layouts: 1.94 us -> 3.81 us
    slice x4 -> x3, local copies, waits for them, and re-layouts: 4.35 us -> 4.53 us  [the longest x1 2.76 us: body(): wvt = qkv_weight[:, 2 * width_all:].T]
  transfers between devices with their start and end apart: 8 -> 8, of which waited for: 4 -> 4; matrix products, arithmetic and copies ran while one was open for 7% -> 11% of each run, Pallas kernels for 0% -> 0%
where the time goes in v4:
time: 149 us
  waiting for transfers between devices  64 us (43%)
  Pallas kernels  31.1 us (21%)
  matrix products  16.2 us (11%)
  between operations  13.6 us (9%)
  starting transfers between devices  12.8 us (9%)
  local copies, waits for them, and re-layouts  10.1 us (7%)
    all_gather x1, waiting for transfers between devices, body(): hidden_all = lax.all_gather(hidden, 'zx', axis=0, tiled=True)  60.1 us
    pallas_call x1, Pallas kernels, attend_partial(): pl.pallas_call(functools.partial(attend_kernel, heads, head_size, nk), gr...  28.3 us
    dot_general x8, matrix products, convolve(): jnp.dot(padded[offset:offset + row_count], weight[offset], preferred_elem...  12.9 us
    ppermute x2, starting transfers between devices, padded_2(): lax.ppermute(lax.slice_in_dim(block, block.shape[0] - width, None, axis=0...  7.92 us
    ppermute x2, starting transfers between devices, padded_2(): lax.ppermute(lax.slice_in_dim(block, 0, width, axis=0), SEQ_AXES, backward)  3.97 us
    unnamed x17, local copies, waits for them, and re-layouts  3.81 us
    dot_general x2, matrix products, convolve(): jnp.dot(padded[0:row_count], weight[0], preferred_element_type=jnp.float32)  3.25 us
  transfers between devices with their start and end apart: 8, of which 4 were waited for; matrix products, arithmetic and copies ran while one was open for 11% of the time, Pallas kernels for 0%

profile of v4, /device:TPU:1, one launch (start us, length us, event | category | flops | bytes accessed | tf_op | source)
XLA Modules:
  0.0 148.8 jit_solution(1233456415242981013)
XLA Ops:
  6.5 0.0 all-gather.2.cloned.1.call-start
  6.5 0.8 fusion.78
  7.3 4.5 %collective-permute-start = (bf16[2,1536]{1,0:T(2,128)(2,1)S(1)}, bf16[2,1536]{1,0:T(2,128)(2,1)S(1)}, u32[]{:S(2)}, u32[]{:S(2)}) collective-permute-start(bf16[2,1536]{1,0:T(2,128)(2,1)S(1)} %get-tuple-element.12), channel_id=1, source_target_pairs={{0,4},{4,8},{8,12},{12,16},{16,20},{20,24},{24,28},{28,32},{32,36}... | collective-permute-start | bytes 18440 | tf_op jit(solution)/shard_map/ppermute | solution.py:20
  11.8 0.0 copy-start.1
  11.8 2.1 %collective-permute-start.1 = (bf16[2,1536]{1,0:T(2,128)(2,1)S(1)}, bf16[2,1536]{1,0:T(2,128)(2,1)S(1)}, u32[]{:S(2)}, u32[]{:S(2)}) collective-permute-start(bf16[2,1536]{1,0:T(2,128)(2,1)S(1)} %get-tuple-element.13), channel_id=1, source_target_pairs={{4,0},{8,4},{12,8},{16,12},{20,16},{24,20},{28,24},{32,28},{36,32}... | collective-permute-start | bytes 18440 | tf_op jit(solution)/shard_map/ppermute | solution.py:21
  13.9 2.7 %fusion.4 = f32[256,768]{1,0:T(8,128)S(1)} fusion(bf16[256,1536]{1,0:T(8,128)(2,1)} %param.6, bf16[5,1536,768]{2,1,0:T(8,128)(2,1)} %param.7), kind=kOutput, calls=%fused_computation.4 | convolution fusion | flops 603979776 | bytes 3932160 | tf_op jit(solution)/shard_map/dot_general | solution.py:28
  16.6 0.0 copy-done.1
  16.6 0.1 constant_dynamic-update-slice_fusion.1
  16.7 0.2 collective-permute-done.1
  16.9 2.5 %fusion = f32[256,768]{1,0:T(8,128)S(1)} fusion(bf16[5,1536,768]{2,1,0:T(8,128)(2,1)} %param.7, bf16[258,1536]{1,0:T(8,128)(2,1)S(1)} %constant_dynamic-update-slice_fusion), kind=kOutput, calls=%fused_computation | convolution fusion | flops 603979776 | bytes 3932160 | tf_op jit(solution)/shard_map/dot_general | solution.py:28
  19.4 2.5 %fusion.2 = f32[256,768]{1,0:T(8,128)S(1)} fusion(bf16[5,1536,768]{2,1,0:T(8,128)(2,1)} %param.7, bf16[258,1536]{1,0:T(8,128)(2,1)S(1)} %constant_dynamic-update-slice_fusion), kind=kOutput, calls=%fused_computation.2 | convolution fusion | flops 603979776 | bytes 3932160 | tf_op jit(solution)/shard_map/dot_general | solution.py:28
  21.9 0.0 collective-permute-done
  21.9 0.0 slice-start
  21.9 2.6 %fusion.6 = f32[256,768]{1,0:T(8,128)S(1)} fusion(bf16[5,1536,768]{2,1,0:T(8,128)(2,1)} %param.7, bf16[256,1536]{1,0:T(8,128)(2,1)S(1)} %copy-done.1, bf16[2,1536]{1,0:T(2,128)(2,1)S(1)} %collective-permute-done), kind=kOutput, calls=%fused_computation.6 | convolution fusion | flops 605552640 | bytes 3938304 | tf_op jit(solution)/shard_map/dot_general | solution.py:28
  24.5 0.0 slice-start.1
  24.5 2.8 %fusion.57 = bf16[256,768]{1,0:T(8,128)(2,1)S(1)} fusion(f32[256,768]{1,0:T(8,128)S(1)} %fusion, f32[256,768]{1,0:T(8,128)S(1)} %fusion.2, f32[256,768]{1,0:T(8,128)S(1)} %fusion.4, f32[256,768]{1,0:T(8,128)S(1)} %fusion.6, bf16[5,1536,768]{2,1,0:T(8,128)(2,1)} %param.7, bf16[2,1536]{1,0:T(2,128)(2,1)S(1)} %collective-permute-done, ...), kind=kOutput, calls=%fused_computation.49 | convolution fusion | flops 608108544 | bytes 6690816 | tf_op jit(solution)/shard_map/dot_general | solution.py:26
  27.3 3.4 %collective-permute-start.2 = (bf16[2,768]{1,0:T(2,128)(2,1)S(1)}, bf16[2,768]{1,0:T(2,128)(2,1)S(1)}, u32[]{:S(2)}, u32[]{:S(2)}) collective-permute-start(bf16[2,768]{1,0:T(2,128)(2,1)S(1)} %get-tuple-element.14), channel_id=1, source_target_pairs={{0,4},{4,8},{8,12},{12,16},{16,20},{20,24},{24,28},{28,32},{32,36}... | collective-permute-start | bytes 9224 | tf_op jit(solution)/shard_map/ppermute | solution.py:20
  30.7 1.9 %collective-permute-start.3 = (bf16[2,768]{1,0:T(2,128)(2,1)S(1)}, bf16[2,768]{1,0:T(2,128)(2,1)S(1)}, u32[]{:S(2)}, u32[]{:S(2)}) collective-permute-start(bf16[2,768]{1,0:T(2,128)(2,1)S(1)} %get-tuple-element.15), channel_id=1, source_target_pairs={{4,0},{8,4},{12,8},{16,12},{20,16},{24,20},{28,24},{32,28},{36,32}... | collective-permute-start | bytes 9224 | tf_op jit(solution)/shard_map/ppermute | solution.py:21
  32.7 0.0 slice-done
  32.7 0.5 fusion.34
  33.2 2.5 %collective-permute-done.3 = bf16[2,768]{1,0:T(2,128)(2,1)S(1)} collective-permute-done((bf16[2,768]{1,0:T(2,128)(2,1)S(1)}, bf16[2,768]{1,0:T(2,128)(2,1)S(1)}, u32[]{:S(2)}, u32[]{:S(2)}) %collective-permute-start.3) | collective-permute-done | bytes 3104 | tf_op jit(solution)/shard_map/ppermute | solution.py:21
  35.6 0.5 fusion.31
  36.1 0.0 collective-permute-done.2
  36.2 0.5 fusion.36
  36.6 0.5 fusion.23
  37.1 0.0 copy-start.4
  37.2 1.3 fusion.30.hid_ref
  38.4 0.0 all-gather.2.cloned.1.call-update
  38.5 0.1 collective-permute-start.4
  38.5 0.0 copy-done.4
  38.6 0.1 broadcast_in_dim.3
  38.6 0.9 copy.11.scale_ref
  39.5 2.8 %fusion.77 = (bf16[768,512]{1,0:T(8,128)(2,1)S(1)}, bf16[768,512]{1,0:T(8,128)(2,1)S(1)}, bf16[768,512]{1,0:T(8,128)(2,1)}) fusion(bf16[768,1536]{1,0:T(8,128)(2,1)} %param.9), kind=kLoop, calls=%fused_computation.74 | loop fusion | bytes 4718592 | tf_op jit(solution)/shard_map/slice | solution.py:189
  42.3 1.2 copy.13
  43.4 1.1 copy.12
  44.6 0.0 collective-permute-done.4
  44.6 1.0 pad_maximum_fusion.2.hq_ref
  45.6 60.1 %all-gather.2.cloned.1.call-done.hkv_ref = bf16[4096,768]{1,0:T(8,128)(2,1)} async-done(((bf16[256,768]{1,0:T(8,128)(2,1)}), bf16[4096,768]{1,0:T(8,128)(2,1)}) %all-gather.2.cloned.1.call-update) | async-done | bytes 6291472 | tf_op jit(solution)/shard_map/all_gather | solution.py:192
  105.7 28.3 %shard_map.64 = (f32[512,512]{1,0:T(8,128)}, f32[8,512]{1,0:T(8,128)}) custom-call(bf16[512,768]{1,0:T(8,128)(2,1)} %pad_maximum_fusion.2.hq_ref, bf16[4096,768]{1,0:T(8,128)(2,1)} %all-gather.2.cloned.1.call-done.hkv_ref, bf16[512,768]{1,0:T(8,128)(2,1)} %bitcast.50, bf16[768,512]{1,0:T(8,128)(2,1)} %get-tuple-element.11.wk_ref, bf16[512,768]{1,0:T(8,128)(2,1)} %bitcast.49, ...), custom_call_target="tpu_custom_call" | custom-call | flops 10737418240 | bytes 8388608 | tf_op jit(solution)/shard_map/pallas_call | solution.py:102
  134.0 1.1 slice.114
  135.1 0.8 collective-permute-start.5
  135.8 0.7 slice.115
  136.5 0.0 collective-permute-start.6
  136.5 1.2 collective-permute-done.6.sg_ref
  137.7 0.0 collective-permute-done.5.og_ref
  137.7 0.6 copy-done.3
  138.3 0.8 copy-done.2
  139.1 2.8 %shard_map.65 = bf16[256,768]{1,0:T(8,128)(2,1)} custom-call(f32[512,512]{1,0:T(8,128)} %get-tuple-element.7.o_ref, f32[8,512]{1,0:T(8,128)} %get-tuple-element.8.st_ref, f32[512,256]{1,0:T(8,128)} %copy-done.2, f32[8,256]{1,0:T(8,128)} %copy-done.3, bf16[256,768]{1,0:T(8,128)(2,1)} %fusion.30.hid_ref, bf16[512,768]{1,0:T(8,128)(2,1)} %wo_ref.1), custom_call_target="tpu_custom_call" | custom-call | tf_op jit(solution)/shard_map/pallas_call | solution.py:160
  (9 shorter events, 0.0 us)
Async XLA Ops:
  6.5 99.2 %all-gather.2.cloned.1.call-start = ((), (), s32[]{:S(2)}) async-start(), calls=%async_computation | async-start | bytes 6684672 | tf_op jit(solution)/shard_map/all_gather | solution.py:192
  7.3 14.6 %collective-permute-start = (bf16[2,1536]{1,0:T(2,128)(2,1)S(1)}, bf16[2,1536]{1,0:T(2,128)(2,1)S(1)}, u32[]{:S(2)}, u32[]{:S(2)}) collective-permute-start(bf16[2,1536]{1,0:T(2,128)(2,1)S(1)} %get-tuple-element.12), channel_id=1, source_target_pairs={{0,4},{4,8},{8,12},{12,16},{16,20},{20,24},{24,28},{28,32},{32,36}... | collective-permute-start | bytes 18440 | tf_op jit(solution)/shard_map/ppermute | solution.py:20
  11.8 4.8 %copy-start.1 = (bf16[256,1536]{1,0:T(8,128)(2,1)S(1)}, bf16[256,1536]{1,0:T(8,128)(2,1)}, u32[]{:S(2)}) copy-start(bf16[256,1536]{1,0:T(8,128)(2,1)} %param.6) | copy-start | bytes 2359300
  11.8 5.1 %collective-permute-start.1 = (bf16[2,1536]{1,0:T(2,128)(2,1)S(1)}, bf16[2,1536]{1,0:T(2,128)(2,1)S(1)}, u32[]{:S(2)}, u32[]{:S(2)}) collective-permute-start(bf16[2,1536]{1,0:T(2,128)(2,1)S(1)} %get-tuple-element.13), channel_id=1, source_target_pairs={{4,0},{8,4},{12,8},{16,12},{20,16},{24,20},{28,24},{32,28},{36,32}... | collective-permute-start | bytes 18440 | tf_op jit(solution)/shard_map/ppermute | solution.py:21
  21.9 10.8 %slice-start = ((s8[5898240]{0:T(1024)(128)(4,1)}), s8[4194304]{0:T(1024)(128)(4,1)S(1)}, s32[]{:S(2)}) async-start(s8[5898240]{0:T(1024)(128)(4,1)} %bitcast.47), calls=%async_computation.1 | async-start | bytes 8388608
  24.5 8.2 %slice-start.1 = ((s8[5898240]{0:T(1024)(128)(4,1)}), s8[1703936]{0:T(1024)(128)(4,1)S(1)}, s32[]{:S(2)}) async-start(s8[5898240]{0:T(1024)(128)(4,1)} %bitcast.47), calls=%async_computation.2 | async-start | bytes 3407872
  27.3 8.8 %collective-permute-start.2 = (bf16[2,768]{1,0:T(2,128)(2,1)S(1)}, bf16[2,768]{1,0:T(2,128)(2,1)S(1)}, u32[]{:S(2)}, u32[]{:S(2)}) collective-permute-start(bf16[2,768]{1,0:T(2,128)(2,1)S(1)} %get-tuple-element.14), channel_id=1, source_target_pairs={{0,4},{4,8},{8,12},{12,16},{16,20},{20,24},{24,28},{28,32},{32,36}... | collective-permute-start | bytes 9224 | tf_op jit(solution)/shard_map/ppermute | solution.py:20
  30.7 4.9 %collective-permute-start.3 = (bf16[2,768]{1,0:T(2,128)(2,1)S(1)}, bf16[2,768]{1,0:T(2,128)(2,1)S(1)}, u32[]{:S(2)}, u32[]{:S(2)}) collective-permute-start(bf16[2,768]{1,0:T(2,128)(2,1)S(1)} %get-tuple-element.15), channel_id=1, source_target_pairs={{4,0},{8,4},{12,8},{16,12},{20,16},{24,20},{28,24},{32,28},{36,32}... | collective-permute-start | bytes 9224 | tf_op jit(solution)/shard_map/ppermute | solution.py:21
  37.1 1.4 copy-start.4
  38.5 6.1 %collective-permute-start.4 = (bf16[256,768]{1,0:T(8,128)(2,1)}, bf16[256,768]{1,0:T(8,128)(2,1)S(1)}, u32[]{:S(2)}, u32[]{:S(2)}) collective-permute-start(bf16[256,768]{1,0:T(8,128)(2,1)} %fusion.30.hid_ref), channel_id=1, source_target_pairs={{0,4},{4,0},{1,5},{5,1},{2,6},{6,2},{3,7},{7,3},{8,12},{12,8},{9,1... | collective-permute-start | bytes 1179656 | tf_op jit(solution)/shard_map/ppermute | solution.py:193
  42.3 2.3 %copy-start = (bf16[256,768]{1,0:T(8,128)(2,1)S(1)}, bf16[256,768]{1,0:T(8,128)(2,1)}, u32[]{:S(2)}) copy-start(bf16[256,768]{1,0:T(8,128)(2,1)} %fusion.30.hid_ref) | copy-start | bytes 1179652
  135.1 2.6 %collective-permute-start.5 = (f32[512,256]{1,0:T(8,128)S(1)}, f32[512,256]{1,0:T(8,128)S(1)}, u32[]{:S(2)}, u32[]{:S(2)}) collective-permute-start(f32[512,256]{1,0:T(8,128)S(1)} %slice.114), channel_id=1, source_target_pairs={{0,4},{4,0},{1,5},{5,1},{2,6},{6,2},{3,7},{7,3},{8,12},{12,8},{9,1... | collective-permute-start | bytes 1572872 | tf_op jit(solution)/shard_map/ppermute | solution.py:196
  136.5 1.2 collective-permute-start.6
  137.7 0.6 copy-start.3
  138.3 0.8 copy-start.2
Sparse Core Ops, SparseCore 0:
  38.6 67.0 all-gather.1

commit v5 on v4

--- a/solution.py
+++ b/solution.py
@@ -10,7 +10,7 @@
 from jax.sharding import Mesh
 from jax.sharding import PartitionSpec as P
 
-SEQ_AXES = ("zx", "core")
+SEQ_AXES = ("z", "x", "core")
 
 
 def padded_2(block, width):
@@ -189,7 +189,7 @@
     wvt = qkv_weight[:, 2 * width_all :].T
 
     swap = [(0, 1), (1, 0)]
-    hidden_all = lax.all_gather(hidden, "zx", axis=0, tiled=True)
+    hidden_all = lax.all_gather(lax.all_gather(hidden, "x", axis=0, tiled=True), "z", axis=0, tiled=True)
     hidden_other = lax.ppermute(hidden, "core", swap)
     hidden_q = jnp.concatenate([hidden, hidden_other], axis=0)
     o_part, st_part = attend_partial(hidden_q, hidden_all, wqt, wk, wvt, scale_col, head_count, head_size)
@@ -202,8 +202,9 @@
     seq_size = mesh.shape["seq"]
     batch_size = mesh.shape["batch"]
     order = [mesh.axis_names.index("seq"), mesh.axis_names.index("batch")]
-    devices = devices.transpose(order).reshape(seq_size // 2, 2, batch_size)
-    split_mesh = Mesh(devices, ("zx", "core", "batch"))
-    rows = P(("batch", "zx", "core"), None)
+    side = math.isqrt(seq_size // 2)
+    devices = devices.transpose(order).reshape(seq_size // 2 // side, side, 2, batch_size)
+    split_mesh = Mesh(devices, ("z", "x", "core", "batch"))
+    rows = P(("batch", "z", "x", "core"), None)
     in_specs = (rows, P(), P(), P(), P(), P())
     return jax.shard_map(body, mesh=split_mesh, in_specs=in_specs, out_specs=rows, check_vma=False)

time: 149 us -> 182 us (1.22)
  waiting for transfers between devices: 64 us -> 96.1 us
    all_gather x1 -> x2, waiting for transfers between devices: 60.1 us -> 92.1 us  [the longest x1 59.9 us: body(): lax.all_gather(lax.all_gather(hidden, 'x', axis=0, tiled=True), 'z', axis...]
  transfers between devices with their start and end apart: 8 -> 9, of which waited for: 4 -> 5; matrix products, arithmetic and copies ran while one was open for 11% -> 9% of each run, Pallas kernels for 0% -> 0%
where the time goes in v5:
time: 182 us
  waiting for transfers between devices  96.1 us (53%)
  Pallas kernels  31.1 us (17%)
  matrix products  16.2 us (9%)
  between operations  13.6 us (7%)
  starting transfers between devices  13.5 us (7%)
  local copies, waits for them, and re-layouts  10.1 us (6%)
    all_gather x1, waiting for transfers between devices, body(): lax.all_gather(lax.all_gather(hidden, 'x', axis=0, tiled=True), 'z', axis...  59.9 us
    all_gather x1, waiting for transfers between devices, body(): lax.all_gather(hidden, 'x', axis=0, tiled=True)  32.3 us
    pallas_call x1, Pallas kernels, attend_partial(): pl.pallas_call(functools.partial(attend_kernel, heads, head_size, nk), gr...  28.3 us
    dot_general x8, matrix products, convolve(): jnp.dot(padded[offset:offset + row_count], weight[offset], preferred_elem...  12.9 us
    ppermute x2, starting transfers between devices, padded_2(): lax.ppermute(lax.slice_in_dim(block, block.shape[0] - width, None, axis=0...  7.92 us
    ppermute x2, starting transfers between devices, padded_2(): lax.ppermute(lax.slice_in_dim(block, 0, width, axis=0), SEQ_AXES, backward)  3.97 us
    unnamed x17, local copies, waits for them, and re-layouts  3.79 us
  transfers between devices with their start and end apart: 9, of which 5 were waited for; matrix products, arithmetic and copies ran while one was open for 9% of the time, Pallas kernels for 0%

profile of v5, /device:TPU:1, one launch (start us, length us, event | category | flops | bytes accessed | tf_op | source)
XLA Modules:
  0.0 181.5 jit_solution(9187348325609610283)
XLA Ops:
  6.5 0.8 fusion.78
  7.3 4.5 %collective-permute-start = (bf16[2,1536]{1,0:T(2,128)(2,1)S(1)}, bf16[2,1536]{1,0:T(2,128)(2,1)S(1)}, u32[]{:S(2)}, u32[]{:S(2)}) collective-permute-start(bf16[2,1536]{1,0:T(2,128)(2,1)S(1)} %get-tuple-element.12), channel_id=1, source_target_pairs={{0,4},{4,8},{8,12},{12,16},{16,20},{20,24},{24,28},{28,32},{32,36}... | collective-permute-start | bytes 18440 | tf_op jit(solution)/shard_map/ppermute | solution.py:20
  11.8 0.0 copy-start.1
  11.8 2.1 %collective-permute-start.1 = (bf16[2,1536]{1,0:T(2,128)(2,1)S(1)}, bf16[2,1536]{1,0:T(2,128)(2,1)S(1)}, u32[]{:S(2)}, u32[]{:S(2)}) collective-permute-start(bf16[2,1536]{1,0:T(2,128)(2,1)S(1)} %get-tuple-element.13), channel_id=1, source_target_pairs={{4,0},{8,4},{12,8},{16,12},{20,16},{24,20},{28,24},{32,28},{36,32}... | collective-permute-start | bytes 18440 | tf_op jit(solution)/shard_map/ppermute | solution.py:21
  13.9 2.7 %fusion.4 = f32[256,768]{1,0:T(8,128)S(1)} fusion(bf16[256,1536]{1,0:T(8,128)(2,1)} %param.6, bf16[5,1536,768]{2,1,0:T(8,128)(2,1)} %param.7), kind=kOutput, calls=%fused_computation.4 | convolution fusion | flops 603979776 | bytes 3932160 | tf_op jit(solution)/shard_map/dot_general | solution.py:28
  16.6 0.1 constant_dynamic-update-slice_fusion.1
  16.7 0.2 collective-permute-done.1
  16.9 2.5 %fusion = f32[256,768]{1,0:T(8,128)S(1)} fusion(bf16[5,1536,768]{2,1,0:T(8,128)(2,1)} %param.7, bf16[258,1536]{1,0:T(8,128)(2,1)S(1)} %constant_dynamic-update-slice_fusion), kind=kOutput, calls=%fused_computation | convolution fusion | flops 603979776 | bytes 3932160 | tf_op jit(solution)/shard_map/dot_general | solution.py:28
  19.4 2.5 %fusion.2 = f32[256,768]{1,0:T(8,128)S(1)} fusion(bf16[5,1536,768]{2,1,0:T(8,128)(2,1)} %param.7, bf16[258,1536]{1,0:T(8,128)(2,1)S(1)} %constant_dynamic-update-slice_fusion), kind=kOutput, calls=%fused_computation.2 | convolution fusion | flops 603979776 | bytes 3932160 | tf_op jit(solution)/shard_map/dot_general | solution.py:28
  21.9 0.0 collective-permute-done
  21.9 0.0 slice-start
  21.9 2.6 %fusion.6 = f32[256,768]{1,0:T(8,128)S(1)} fusion(bf16[5,1536,768]{2,1,0:T(8,128)(2,1)} %param.7, bf16[256,1536]{1,0:T(8,128)(2,1)S(1)} %copy-done.1, bf16[2,1536]{1,0:T(2,128)(2,1)S(1)} %collective-permute-done), kind=kOutput, calls=%fused_computation.6 | convolution fusion | flops 605552640 | bytes 3938304 | tf_op jit(solution)/shard_map/dot_general | solution.py:28
  24.5 0.0 slice-start.1
  24.5 2.8 %fusion.57 = bf16[256,768]{1,0:T(8,128)(2,1)S(1)} fusion(f32[256,768]{1,0:T(8,128)S(1)} %fusion, f32[256,768]{1,0:T(8,128)S(1)} %fusion.2, f32[256,768]{1,0:T(8,128)S(1)} %fusion.4, f32[256,768]{1,0:T(8,128)S(1)} %fusion.6, bf16[5,1536,768]{2,1,0:T(8,128)(2,1)} %param.7, bf16[2,1536]{1,0:T(2,128)(2,1)S(1)} %collective-permute-done, ...), kind=kOutput, calls=%fused_computation.49 | convolution fusion | flops 608108544 | bytes 6690816 | tf_op jit(solution)/shard_map/dot_general | solution.py:26
  27.3 3.4 %collective-permute-start.2 = (bf16[2,768]{1,0:T(2,128)(2,1)S(1)}, bf16[2,768]{1,0:T(2,128)(2,1)S(1)}, u32[]{:S(2)}, u32[]{:S(2)}) collective-permute-start(bf16[2,768]{1,0:T(2,128)(2,1)S(1)} %get-tuple-element.14), channel_id=1, source_target_pairs={{0,4},{4,8},{8,12},{12,16},{16,20},{20,24},{24,28},{28,32},{32,36}... | collective-permute-start | bytes 9224 | tf_op jit(solution)/shard_map/ppermute | solution.py:20
  30.7 1.9 %collective-permute-start.3 = (bf16[2,768]{1,0:T(2,128)(2,1)S(1)}, bf16[2,768]{1,0:T(2,128)(2,1)S(1)}, u32[]{:S(2)}, u32[]{:S(2)}) collective-permute-start(bf16[2,768]{1,0:T(2,128)(2,1)S(1)} %get-tuple-element.15), channel_id=1, source_target_pairs={{4,0},{8,4},{12,8},{16,12},{20,16},{24,20},{28,24},{32,28},{36,32}... | collective-permute-start | bytes 9224 | tf_op jit(solution)/shard_map/ppermute | solution.py:21
  32.7 0.5 fusion.34
  33.2 2.5 %collective-permute-done.3 = bf16[2,768]{1,0:T(2,128)(2,1)S(1)} collective-permute-done((bf16[2,768]{1,0:T(2,128)(2,1)S(1)}, bf16[2,768]{1,0:T(2,128)(2,1)S(1)}, u32[]{:S(2)}, u32[]{:S(2)}) %collective-permute-start.3) | collective-permute-done | bytes 3104 | tf_op jit(solution)/shard_map/ppermute | solution.py:21
  35.6 0.5 fusion.31
  36.1 0.0 collective-permute-done.2
  36.2 0.5 fusion.36
  36.6 0.5 fusion.23
  37.1 0.0 copy-start.4
  37.2 1.3 fusion.30.hid_ref
  38.4 0.0 all-gather.3.cloned.1.call-update
  38.4 0.0 all-gather.5.cloned.1.call-start
  38.5 32.3 %all-gather.3.cloned.1.call-done = bf16[1024,768]{1,0:T(8,128)(2,1)} async-done(((bf16[256,768]{1,0:T(8,128)(2,1)}), bf16[1024,768]{1,0:T(8,128)(2,1)}) %all-gather.3.cloned.1.call-update) | async-done | bytes 1572880 | tf_op jit(solution)/shard_map/all_gather | solution.py:192
  70.8 0.0 all-gather.5.cloned.1.call-update
  70.8 0.8 collective-permute-start.4
  71.6 0.1 broadcast_in_dim.3
  71.6 0.9 copy.11.scale_ref
  72.5 2.8 %fusion.77 = (bf16[768,512]{1,0:T(8,128)(2,1)S(1)}, bf16[768,512]{1,0:T(8,128)(2,1)S(1)}, bf16[768,512]{1,0:T(8,128)(2,1)}) fusion(bf16[768,1536]{1,0:T(8,128)(2,1)} %param.9), kind=kLoop, calls=%fused_computation.74 | loop fusion | bytes 4718592 | tf_op jit(solution)/shard_map/slice | solution.py:189
  75.3 1.2 copy.13
  76.4 1.2 copy.12
  77.6 0.0 collective-permute-done.4
  77.6 0.0 copy-done
  77.6 1.0 pad_maximum_fusion.2.hq_ref
  78.6 59.9 %all-gather.5.cloned.1.call-done.hkv_ref = bf16[4096,768]{1,0:T(8,128)(2,1)} async-done(((bf16[1024,768]{1,0:T(8,128)(2,1)}), bf16[4096,768]{1,0:T(8,128)(2,1)}) %all-gather.5.cloned.1.call-update) | async-done | bytes 6291472 | tf_op jit(solution)/shard_map/all_gather | solution.py:192
  138.4 28.3 %shard_map.64 = (f32[512,512]{1,0:T(8,128)}, f32[8,512]{1,0:T(8,128)}) custom-call(bf16[512,768]{1,0:T(8,128)(2,1)} %pad_maximum_fusion.2.hq_ref, bf16[4096,768]{1,0:T(8,128)(2,1)} %all-gather.5.cloned.1.call-done.hkv_ref, bf16[512,768]{1,0:T(8,128)(2,1)} %bitcast.50, bf16[768,512]{1,0:T(8,128)(2,1)} %get-tuple-element.11.wk_ref, bf16[512,768]{1,0:T(8,128)(2,1)} %bitcast.49, ...), custom_call_target="tpu_custom_call" | custom-call | flops 10737418240 | bytes 8388608 | tf_op jit(solution)/shard_map/pallas_call | solution.py:102
  166.7 1.1 slice.114
  167.8 0.8 collective-permute-start.5
  168.6 0.7 slice.115
  169.3 0.0 collective-permute-start.6
  169.3 1.2 collective-permute-done.6.sg_ref
  170.5 0.0 collective-permute-done.5.og_ref
  170.5 0.6 copy-done.3
  171.1 0.8 copy-done.2
  171.9 2.8 %shard_map.65 = bf16[256,768]{1,0:T(8,128)(2,1)} custom-call(f32[512,512]{1,0:T(8,128)} %get-tuple-element.7.o_ref, f32[8,512]{1,0:T(8,128)} %get-tuple-element.8.st_ref, f32[512,256]{1,0:T(8,128)} %copy-done.2, f32[8,256]{1,0:T(8,128)} %copy-done.3, bf16[256,768]{1,0:T(8,128)(2,1)} %fusion.30.hid_ref, bf16[512,768]{1,0:T(8,128)(2,1)} %wo_ref.1), custom_call_target="tpu_custom_call" | custom-call | tf_op jit(solution)/shard_map/pallas_call | solution.py:160
  (12 shorter events, 0.0 us)
Async XLA Ops:
  6.5 64.2 %all-gather.3.cloned.1.call-start = ((), (), s32[]{:S(2)}) async-start(), calls=%async_computation | async-start | bytes 1966080 | tf_op jit(solution)/shard_map/all_gather | solution.py:192
  7.3 14.6 %collective-permute-start = (bf16[2,1536]{1,0:T(2,128)(2,1)S(1)}, bf16[2,1536]{1,0:T(2,128)(2,1)S(1)}, u32[]{:S(2)}, u32[]{:S(2)}) collective-permute-start(bf16[2,1536]{1,0:T(2,128)(2,1)S(1)} %get-tuple-element.12), channel_id=1, source_target_pairs={{0,4},{4,8},{8,12},{12,16},{16,20},{20,24},{24,28},{28,32},{32,36}... | collective-permute-start | bytes 18440 | tf_op jit(solution)/shard_map/ppermute | solution.py:20
  11.8 4.8 %copy-start.1 = (bf16[256,1536]{1,0:T(8,128)(2,1)S(1)}, bf16[256,1536]{1,0:T(8,128)(2,1)}, u32[]{:S(2)}) copy-start(bf16[256,1536]{1,0:T(8,128)(2,1)} %param.6) | copy-start | bytes 2359300
  11.8 5.1 %collective-permute-start.1 = (bf16[2,1536]{1,0:T(2,128)(2,1)S(1)}, bf16[2,1536]{1,0:T(2,128)(2,1)S(1)}, u32[]{:S(2)}, u32[]{:S(2)}) collective-permute-start(bf16[2,1536]{1,0:T(2,128)(2,1)S(1)} %get-tuple-element.13), channel_id=1, source_target_pairs={{4,0},{8,4},{12,8},{16,12},{20,16},{24,20},{28,24},{32,28},{36,32}... | collective-permute-start | bytes 18440 | tf_op jit(solution)/shard_map/ppermute | solution.py:21
  21.9 10.8 %slice-start = ((s8[5898240]{0:T(1024)(128)(4,1)}), s8[4194304]{0:T(1024)(128)(4,1)S(1)}, s32[]{:S(2)}) async-start(s8[5898240]{0:T(1024)(128)(4,1)} %bitcast.47), calls=%async_computation.2 | async-start | bytes 8388608
  24.5 8.2 %slice-start.1 = ((s8[5898240]{0:T(1024)(128)(4,1)}), s8[1703936]{0:T(1024)(128)(4,1)S(1)}, s32[]{:S(2)}) async-start(s8[5898240]{0:T(1024)(128)(4,1)} %bitcast.47), calls=%async_computation.3 | async-start | bytes 3407872
  27.3 8.8 %collective-permute-start.2 = (bf16[2,768]{1,0:T(2,128)(2,1)S(1)}, bf16[2,768]{1,0:T(2,128)(2,1)S(1)}, u32[]{:S(2)}, u32[]{:S(2)}) collective-permute-start(bf16[2,768]{1,0:T(2,128)(2,1)S(1)} %get-tuple-element.14), channel_id=1, source_target_pairs={{0,4},{4,8},{8,12},{12,16},{16,20},{20,24},{24,28},{28,32},{32,36}... | collective-permute-start | bytes 9224 | tf_op jit(solution)/shard_map/ppermute | solution.py:20
  30.7 4.9 %collective-permute-start.3 = (bf16[2,768]{1,0:T(2,128)(2,1)S(1)}, bf16[2,768]{1,0:T(2,128)(2,1)S(1)}, u32[]{:S(2)}, u32[]{:S(2)}) collective-permute-start(bf16[2,768]{1,0:T(2,128)(2,1)S(1)} %get-tuple-element.15), channel_id=1, source_target_pairs={{4,0},{8,4},{12,8},{16,12},{20,16},{24,20},{28,24},{32,28},{36,32}... | collective-permute-start | bytes 9224 | tf_op jit(solution)/shard_map/ppermute | solution.py:21
  37.1 34.4 %copy-start.4 = (f32[4]{0:T(128)S(1)}, f32[4]{0:T(128)}, u32[]{:S(2)}) copy-start(f32[4]{0:T(128)} %param.11) | copy-start | bytes 52
  38.4 100.0 %all-gather.5.cloned.1.call-start = ((), (), s32[]{:S(2)}) async-start(), calls=%async_computation.1 | async-start | bytes 7864320 | tf_op jit(solution)/shard_map/all_gather | solution.py:192
  70.8 6.8 %collective-permute-start.4 = (bf16[256,768]{1,0:T(8,128)(2,1)}, bf16[256,768]{1,0:T(8,128)(2,1)S(1)}, u32[]{:S(2)}, u32[]{:S(2)}) collective-permute-start(bf16[256,768]{1,0:T(8,128)(2,1)} %fusion.30.hid_ref), channel_id=1, source_target_pairs={{0,4},{4,0},{1,5},{5,1},{2,6},{6,2},{3,7},{7,3},{8,12},{12,8},{9,1... | collective-permute-start | bytes 1179656 | tf_op jit(solution)/shard_map/ppermute | solution.py:193
  75.3 2.3 %copy-start = (bf16[256,768]{1,0:T(8,128)(2,1)S(1)}, bf16[256,768]{1,0:T(8,128)(2,1)}, u32[]{:S(2)}) copy-start(bf16[256,768]{1,0:T(8,128)(2,1)} %fusion.30.hid_ref) | copy-start | bytes 1179652
  167.8 2.7 %collective-permute-start.5 = (f32[512,256]{1,0:T(8,128)S(1)}, f32[512,256]{1,0:T(8,128)S(1)}, u32[]{:S(2)}, u32[]{:S(2)}) collective-permute-start(f32[512,256]{1,0:T(8,128)S(1)} %slice.114), channel_id=1, source_target_pairs={{0,4},{4,0},{1,5},{5,1},{2,6},{6,2},{3,7},{7,3},{8,12},{12,8},{9,1... | collective-permute-start | bytes 1572872 | tf_op jit(solution)/shard_map/ppermute | solution.py:196
  169.3 1.2 collective-permute-start.6
  170.5 0.6 copy-start.3
  171.1 0.8 copy-start.2
Sparse Core Ops, SparseCore 0:
  38.6 32.1 all-gather.2
  72.4 65.9 all-gather.4

commit v6 on v4

--- a/solution.py
+++ b/solution.py
@@ -173,6 +173,60 @@
     )(o_part, st_part, o_got, st_got, hidden, out_weight)
 
 
+def gather_kernel(axis, n, x_ref, out_ref, send_sem, recv_sem, local_sem):
+    me = lax.axis_index(axis)
+    rows = x_ref.shape[0]
+    mesh_ids = pl.DeviceIdType.MESH
+    barrier = pltpu.get_barrier_semaphore()
+    for i in range(1, n):
+        pl.semaphore_signal(barrier, inc=1, device_id={axis: lax.rem(me + i, n)}, device_id_type=mesh_ids)
+    pl.semaphore_wait(barrier, n - 1)
+    own_slot = out_ref.at[pl.ds(pl.multiple_of(me * rows, rows), rows)]
+    local = pltpu.make_async_copy(x_ref, own_slot, local_sem)
+    local.start()
+    sends = []
+    for i in range(1, n):
+        copy = pltpu.make_async_remote_copy(
+            src_ref=x_ref,
+            dst_ref=own_slot,
+            send_sem=send_sem.at[i],
+            recv_sem=recv_sem.at[i],
+            device_id={axis: lax.rem(me + i, n)},
+            device_id_type=mesh_ids,
+        )
+        copy.start()
+        sends.append(copy)
+    local.wait()
+    for i in range(1, n):
+        sends[i - 1].wait_send()
+        source = lax.rem(me + n - i, n)
+        pltpu.make_async_remote_copy(
+            src_ref=x_ref,
+            dst_ref=out_ref.at[pl.ds(pl.multiple_of(source * rows, rows), rows)],
+            send_sem=send_sem.at[i],
+            recv_sem=recv_sem.at[i],
+            device_id={axis: source},
+            device_id_type=mesh_ids,
+        ).wait_recv()
+
+
+def gather_rows(block, axis):
+    n = lax.axis_size(axis)
+    rows, width = block.shape
+    return pl.pallas_call(
+        functools.partial(gather_kernel, axis, n),
+        in_specs=[pl.BlockSpec(memory_space=pl.ANY)],
+        out_specs=pl.BlockSpec(memory_space=pl.ANY),
+        out_shape=jax.ShapeDtypeStruct((n * rows, width), block.dtype),
+        scratch_shapes=[
+            pltpu.SemaphoreType.DMA((n,)),
+            pltpu.SemaphoreType.DMA((n,)),
+            pltpu.SemaphoreType.DMA,
+        ],
+        compiler_params=pltpu.CompilerParams(collective_id=0, has_side_effects=True),
+    )(block)
+
+
 def body(sequence_input, conv_first, conv_second, qkv_weight, out_weight, logit_scale):
     row_count = sequence_input.shape[0]
     padded_input = padded_2(sequence_input, 2)
@@ -189,7 +243,7 @@
     wvt = qkv_weight[:, 2 * width_all :].T
 
     swap = [(0, 1), (1, 0)]
-    hidden_all = lax.all_gather(hidden, "zx", axis=0, tiled=True)
+    hidden_all = gather_rows(hidden, "zx")
     hidden_other = lax.ppermute(hidden, "core", swap)
     hidden_q = jnp.concatenate([hidden, hidden_other], axis=0)
     o_part, st_part = attend_partial(hidden_q, hidden_all, wqt, wk, wvt, scale_col, head_count, head_size)

time: 149 us -> 197 us (1.32)
  the two profiles are of different devices: /device:TPU:1 before, /device:TPU:49 now
where the time goes in v6:
time: 197 us
  Pallas kernels  149 us (76%)
  starting transfers between devices  16.4 us (8%)
  matrix products  15.5 us (8%)
  local copies, waits for them, and re-layouts  10 us (5%)
  waiting for transfers between devices  3.18 us (2%)
  other arithmetic  1.97 us (1%)
    pallas_call x1, Pallas kernels, gather_rows(): pl.pallas_call(functools.partial(gather_kernel, axis, n), in_specs=[pl.Bl...  118 us
    pallas_call x1, Pallas kernels, attend_partial(): pl.pallas_call(functools.partial(attend_kernel, heads, head_size, nk), gr...  28.3 us
    dot_general x8, matrix products, convolve(): jnp.dot(padded[offset:offset + row_count], weight[offset], preferred_elem...  12.2 us
    ppermute x2, starting transfers between devices, padded_2(): lax.ppermute(lax.slice_in_dim(block, block.shape[0] - width, None, axis=0...  7.09 us
    ppermute x2, starting transfers between devices, padded_2(): lax.ppermute(lax.slice_in_dim(block, 0, width, axis=0), SEQ_AXES, backward)  4.98 us
  transfers between devices with their start and end apart: 7, of which 3 were waited for; matrix products, arithmetic and copies ran while one was open for 8% of the time, Pallas kernels for 60%

profile of v6, /device:TPU:49, one launch (start us, length us, event | category | flops | bytes accessed | tf_op | source)
XLA Modules:
  0.0 196.7 jit_solution(7174410997596654072)
XLA Ops:
  0.0 0.8 fusion.78
  0.8 3.7 %collective-permute-start = (bf16[2,1536]{1,0:T(2,128)(2,1)S(1)}, bf16[2,1536]{1,0:T(2,128)(2,1)S(1)}, u32[]{:S(2)}, u32[]{:S(2)}) collective-permute-start(bf16[2,1536]{1,0:T(2,128)(2,1)S(1)} %get-tuple-element.12), channel_id=1, source_target_pairs={{0,4},{4,8},{8,12},{12,16},{16,20},{20,24},{24,28},{28,32},{32,36}... | collective-permute-start | bytes 18440 | tf_op jit(solution)/shard_map/ppermute | solution.py:20
  4.5 0.0 copy-start.1
  4.5 2.1 %collective-permute-start.1 = (bf16[2,1536]{1,0:T(2,128)(2,1)S(1)}, bf16[2,1536]{1,0:T(2,128)(2,1)S(1)}, u32[]{:S(2)}, u32[]{:S(2)}) collective-permute-start(bf16[2,1536]{1,0:T(2,128)(2,1)S(1)} %get-tuple-element.13), channel_id=1, source_target_pairs={{4,0},{8,4},{12,8},{16,12},{20,16},{24,20},{28,24},{32,28},{36,32}... | collective-permute-start | bytes 18440 | tf_op jit(solution)/shard_map/ppermute | solution.py:21
  6.5 2.7 %fusion.4 = f32[256,768]{1,0:T(8,128)S(1)} fusion(bf16[256,1536]{1,0:T(8,128)(2,1)} %param.6, bf16[5,1536,768]{2,1,0:T(8,128)(2,1)} %param.7), kind=kOutput, calls=%fused_computation.4 | convolution fusion | flops 603979776 | bytes 3932160 | tf_op jit(solution)/shard_map/dot_general | solution.py:28
  9.2 0.0 copy-done.1
  9.2 0.1 constant_dynamic-update-slice_fusion.1
  9.3 0.2 collective-permute-done.1
  9.6 2.5 %fusion = f32[256,768]{1,0:T(8,128)S(1)} fusion(bf16[5,1536,768]{2,1,0:T(8,128)(2,1)} %param.7, bf16[258,1536]{1,0:T(8,128)(2,1)S(1)} %constant_dynamic-update-slice_fusion), kind=kOutput, calls=%fused_computation | convolution fusion | flops 603979776 | bytes 3932160 | tf_op jit(solution)/shard_map/dot_general | solution.py:28
  12.0 2.5 %fusion.2 = f32[256,768]{1,0:T(8,128)S(1)} fusion(bf16[5,1536,768]{2,1,0:T(8,128)(2,1)} %param.7, bf16[258,1536]{1,0:T(8,128)(2,1)S(1)} %constant_dynamic-update-slice_fusion), kind=kOutput, calls=%fused_computation.2 | convolution fusion | flops 603979776 | bytes 3932160 | tf_op jit(solution)/shard_map/dot_general | solution.py:28
  14.5 0.0 collective-permute-done
  14.5 0.0 slice-start
  14.5 2.6 %fusion.6 = f32[256,768]{1,0:T(8,128)S(1)} fusion(bf16[5,1536,768]{2,1,0:T(8,128)(2,1)} %param.7, bf16[256,1536]{1,0:T(8,128)(2,1)S(1)} %copy-done.1, bf16[2,1536]{1,0:T(2,128)(2,1)S(1)} %collective-permute-done), kind=kOutput, calls=%fused_computation.6 | convolution fusion | flops 605552640 | bytes 3938304 | tf_op jit(solution)/shard_map/dot_general | solution.py:28
  17.1 0.0 slice-start.1
  17.2 2.8 %fusion.57 = bf16[256,768]{1,0:T(8,128)(2,1)S(1)} fusion(f32[256,768]{1,0:T(8,128)S(1)} %fusion, f32[256,768]{1,0:T(8,128)S(1)} %fusion.2, f32[256,768]{1,0:T(8,128)S(1)} %fusion.4, f32[256,768]{1,0:T(8,128)S(1)} %fusion.6, bf16[5,1536,768]{2,1,0:T(8,128)(2,1)} %param.7, bf16[2,1536]{1,0:T(2,128)(2,1)S(1)} %collective-permute-done, ...), kind=kOutput, calls=%fused_computation.49 | convolution fusion | flops 608108544 | bytes 6690816 | tf_op jit(solution)/shard_map/dot_general | solution.py:26
  19.9 3.4 %collective-permute-start.2 = (bf16[2,768]{1,0:T(2,128)(2,1)S(1)}, bf16[2,768]{1,0:T(2,128)(2,1)S(1)}, u32[]{:S(2)}, u32[]{:S(2)}) collective-permute-start(bf16[2,768]{1,0:T(2,128)(2,1)S(1)} %get-tuple-element.14), channel_id=1, source_target_pairs={{0,4},{4,8},{8,12},{12,16},{16,20},{20,24},{24,28},{28,32},{32,36}... | collective-permute-start | bytes 9224 | tf_op jit(solution)/shard_map/ppermute | solution.py:20
  23.4 2.9 %collective-permute-start.3 = (bf16[2,768]{1,0:T(2,128)(2,1)S(1)}, bf16[2,768]{1,0:T(2,128)(2,1)S(1)}, u32[]{:S(2)}, u32[]{:S(2)}) collective-permute-start(bf16[2,768]{1,0:T(2,128)(2,1)S(1)} %get-tuple-element.15), channel_id=1, source_target_pairs={{4,0},{8,4},{12,8},{16,12},{20,16},{24,20},{28,24},{32,28},{36,32}... | collective-permute-start | bytes 9224 | tf_op jit(solution)/shard_map/ppermute | solution.py:21
  26.3 0.0 slice-done
  26.3 0.0 slice-done.1
  26.3 0.5 fusion.34
  26.8 1.8 collective-permute-done.3
  28.6 0.5 fusion.31
  29.1 0.0 collective-permute-done.2
  29.1 0.5 fusion.36
  29.6 0.5 fusion.23
  30.1 0.0 copy-start.4
  30.1 0.5 fusion.30.x_ref.hid_ref
  30.6 0.0 copy-start
  30.6 2.9 %collective-permute-start.4 = (bf16[256,768]{1,0:T(8,128)(2,1)S(1)}, bf16[256,768]{1,0:T(8,128)(2,1)S(1)}, u32[]{:S(2)}, u32[]{:S(2)}) collective-permute-start(bf16[256,768]{1,0:T(8,128)(2,1)S(1)} %fusion.30.x_ref.hid_ref), channel_id=1, source_target_pairs={{0,4},{4,0},{1,5},{5,1},{2,6},{6,2},{3,7},{7,3},{8,12},{12,8},{9,1... | collective-permute-start | bytes 1179656 | tf_op jit(solution)/shard_map/ppermute | solution.py:247
  33.6 0.0 copy-done.4
  33.6 0.1 broadcast_in_dim.3
  33.7 0.9 copy.11.scale_ref
  34.5 2.7 %fusion.77 = (bf16[768,512]{1,0:T(8,128)(2,1)S(1)}, bf16[768,512]{1,0:T(8,128)(2,1)S(1)}, bf16[768,512]{1,0:T(8,128)(2,1)}) fusion(bf16[768,1536]{1,0:T(8,128)(2,1)} %param.9), kind=kLoop, calls=%fused_computation.74 | loop fusion | bytes 4718592 | tf_op jit(solution)/shard_map/slice | solution.py:243
  37.3 1.2 copy.13
  38.4 1.2 copy.12
  39.6 118.3 %shard_map.64.hkv_ref = bf16[4096,768]{1,0:T(8,128)(2,1)} custom-call(bf16[256,768]{1,0:T(8,128)(2,1)} %copy-done), custom_call_target="tpu_custom_call" | custom-call | tf_op jit(solution)/shard_map/pallas_call | solution.py:216
  157.9 0.0 collective-permute-done.4
  157.9 2.0 %pad_maximum_fusion.2.hq_ref = bf16[512,768]{1,0:T(8,128)(2,1)} fusion(bf16[256,768]{1,0:T(8,128)(2,1)S(1)} %collective-permute-done.4, bf16[256,768]{1,0:T(8,128)(2,1)} %copy-done), kind=kLoop, calls=%fused_computation.54 | loop fusion | flops 1572864 | bytes 1572864 | tf_op jit(solution)/shard_map/concatenate | solution.py:248
  159.9 28.3 %shard_map.65 = (f32[512,512]{1,0:T(8,128)}, f32[8,512]{1,0:T(8,128)}) custom-call(bf16[512,768]{1,0:T(8,128)(2,1)} %pad_maximum_fusion.2.hq_ref, bf16[4096,768]{1,0:T(8,128)(2,1)} %shard_map.64.hkv_ref, bf16[512,768]{1,0:T(8,128)(2,1)} %bitcast.50, bf16[768,512]{1,0:T(8,128)(2,1)} %get-tuple-element.11.wk_ref, bf16[512,768]{1,0:T(8,128)(2,1)} %bitcast.49, ...), custom_call_target="tpu_custom_call" | custom-call | flops 10737418240 | bytes 8388608 | tf_op jit(solution)/shard_map/pallas_call | solution.py:102
  188.2 1.1 slice.114
  189.2 1.4 collective-permute-start.5
  190.7 0.7 slice.115
  191.4 0.0 collective-permute-start.6
  191.4 1.2 collective-permute-done.6.sg_ref
  192.5 0.0 collective-permute-done.5.og_ref
  192.5 0.6 copy-done.3
  193.1 0.8 copy-done.2
  193.9 2.8 %shard_map.66 = bf16[256,768]{1,0:T(8,128)(2,1)} custom-call(f32[512,512]{1,0:T(8,128)} %get-tuple-element.7.o_ref, f32[8,512]{1,0:T(8,128)} %get-tuple-element.8.st_ref, f32[512,256]{1,0:T(8,128)} %copy-done.2, f32[8,256]{1,0:T(8,128)} %copy-done.3, bf16[256,768]{1,0:T(8,128)(2,1)} %copy-done, bf16[512,768]{1,0:T(8,128)(2,1)} %wo_ref.1), custom_call_target="tpu_custom_call" | custom-call | tf_op jit(solution)/shard_map/pallas_call | solution.py:160
  (7 shorter events, 0.0 us)
Async XLA Ops:
  0.8 13.7 %collective-permute-start = (bf16[2,1536]{1,0:T(2,128)(2,1)S(1)}, bf16[2,1536]{1,0:T(2,128)(2,1)S(1)}, u32[]{:S(2)}, u32[]{:S(2)}) collective-permute-start(bf16[2,1536]{1,0:T(2,128)(2,1)S(1)} %get-tuple-element.12), channel_id=1, source_target_pairs={{0,4},{4,8},{8,12},{12,16},{16,20},{20,24},{24,28},{28,32},{32,36}... | collective-permute-start | bytes 18440 | tf_op jit(solution)/shard_map/ppermute | solution.py:20
  4.5 4.8 %copy-start.1 = (bf16[256,1536]{1,0:T(8,128)(2,1)S(1)}, bf16[256,1536]{1,0:T(8,128)(2,1)}, u32[]{:S(2)}) copy-start(bf16[256,1536]{1,0:T(8,128)(2,1)} %param.6) | copy-start | bytes 2359300
  4.5 5.1 %collective-permute-start.1 = (bf16[2,1536]{1,0:T(2,128)(2,1)S(1)}, bf16[2,1536]{1,0:T(2,128)(2,1)S(1)}, u32[]{:S(2)}, u32[]{:S(2)}) collective-permute-start(bf16[2,1536]{1,0:T(2,128)(2,1)S(1)} %get-tuple-element.13), channel_id=1, source_target_pairs={{4,0},{8,4},{12,8},{16,12},{20,16},{24,20},{28,24},{32,28},{36,32}... | collective-permute-start | bytes 18440 | tf_op jit(solution)/shard_map/ppermute | solution.py:21
  14.5 11.8 %slice-start = ((s8[5898240]{0:T(1024)(128)(4,1)}), s8[4194304]{0:T(1024)(128)(4,1)S(1)}, s32[]{:S(2)}) async-start(s8[5898240]{0:T(1024)(128)(4,1)} %bitcast.47), calls=%async_computation | async-start | bytes 8388608
  17.1 9.2 %slice-start.1 = ((s8[5898240]{0:T(1024)(128)(4,1)}), s8[1703936]{0:T(1024)(128)(4,1)S(1)}, s32[]{:S(2)}) async-start(s8[5898240]{0:T(1024)(128)(4,1)} %bitcast.47), calls=%async_computation.1 | async-start | bytes 3407872
  19.9 9.1 %collective-permute-start.2 = (bf16[2,768]{1,0:T(2,128)(2,1)S(1)}, bf16[2,768]{1,0:T(2,128)(2,1)S(1)}, u32[]{:S(2)}, u32[]{:S(2)}) collective-permute-start(bf16[2,768]{1,0:T(2,128)(2,1)S(1)} %get-tuple-element.14), channel_id=1, source_target_pairs={{0,4},{4,8},{8,12},{12,16},{16,20},{20,24},{24,28},{28,32},{32,36}... | collective-permute-start | bytes 9224 | tf_op jit(solution)/shard_map/ppermute | solution.py:20
  23.4 5.2 %collective-permute-start.3 = (bf16[2,768]{1,0:T(2,128)(2,1)S(1)}, bf16[2,768]{1,0:T(2,128)(2,1)S(1)}, u32[]{:S(2)}, u32[]{:S(2)}) collective-permute-start(bf16[2,768]{1,0:T(2,128)(2,1)S(1)} %get-tuple-element.15), channel_id=1, source_target_pairs={{4,0},{8,4},{12,8},{16,12},{20,16},{24,20},{28,24},{32,28},{36,32}... | collective-permute-start | bytes 9224 | tf_op jit(solution)/shard_map/ppermute | solution.py:21
  30.1 3.5 %copy-start.4 = (f32[4]{0:T(128)S(1)}, f32[4]{0:T(128)}, u32[]{:S(2)}) copy-start(f32[4]{0:T(128)} %param.11) | copy-start | bytes 52
  30.6 9.0 %copy-start = (bf16[256,768]{1,0:T(8,128)(2,1)}, bf16[256,768]{1,0:T(8,128)(2,1)S(1)}, u32[]{:S(2)}) copy-start(bf16[256,768]{1,0:T(8,128)(2,1)S(1)} %fusion.30.x_ref.hid_ref) | copy-start | bytes 1179652
  30.6 127.3 %collective-permute-start.4 = (bf16[256,768]{1,0:T(8,128)(2,1)S(1)}, bf16[256,768]{1,0:T(8,128)(2,1)S(1)}, u32[]{:S(2)}, u32[]{:S(2)}) collective-permute-start(bf16[256,768]{1,0:T(8,128)(2,1)S(1)} %fusion.30.x_ref.hid_ref), channel_id=1, source_target_pairs={{0,4},{4,0},{1,5},{5,1},{2,6},{6,2},{3,7},{7,3},{8,12},{12,8},{9,1... | collective-permute-start | bytes 1179656 | tf_op jit(solution)/shard_map/ppermute | solution.py:247
  189.2 3.3 %collective-permute-start.5 = (f32[512,256]{1,0:T(8,128)S(1)}, f32[512,256]{1,0:T(8,128)S(1)}, u32[]{:S(2)}, u32[]{:S(2)}) collective-permute-start(f32[512,256]{1,0:T(8,128)S(1)} %slice.114), channel_id=1, source_target_pairs={{0,4},{4,0},{1,5},{5,1},{2,6},{6,2},{3,7},{7,3},{8,12},{12,8},{9,1... | collective-permute-start | bytes 1572872 | tf_op jit(solution)/shard_map/ppermute | solution.py:250
  191.4 1.2 collective-permute-start.6
  192.5 0.6 copy-start.3
  193.1 0.8 copy-start.2

commit v7 on v4

--- a/solution.py
+++ b/solution.py
@@ -173,6 +173,105 @@
     )(o_part, st_part, o_got, st_got, hidden, out_weight)
 
 
+def ring_gather_kernel(side, x_ref, out_ref, send_sem, recv_sem, local_sem):
+    me = lax.axis_index("zx")
+    z, x = me // side, me % side
+    half = x_ref.shape[1]
+    q = half // 2
+    mesh_ids = pl.DeviceIdType.MESH
+
+    def slot(stream, a, b):
+        a = lax.rem(a + side, side)
+        b = lax.rem(b + side, side)
+        return b * side + a if stream == 0 else a * side + b
+
+    own = [(x, z), (z, x)]
+    barrier = pltpu.get_barrier_semaphore()
+    for target in (slot(0, x + 1, z), slot(0, x - 1, z), slot(1, z + 1, x), slot(1, z - 1, x)):
+        pl.semaphore_signal(barrier, inc=1, device_id={"zx": target}, device_id_type=mesh_ids)
+    pl.semaphore_wait(barrier, 4)
+    local = pltpu.make_async_copy(x_ref, out_ref.at[me], local_sem)
+    local.start()
+
+    sends = []
+    index = {}
+
+    def send(key, src, view, target):
+        idx = len(index)
+        index[key] = idx
+        copy = pltpu.make_async_remote_copy(
+            src_ref=src, dst_ref=view, send_sem=send_sem.at[idx], recv_sem=recv_sem.at[idx],
+            device_id={"zx": target}, device_id_type=mesh_ids,
+        )
+        copy.start()
+        sends.append(copy)
+
+    def recv(key, view, source):
+        idx = index[key]
+        pltpu.make_async_remote_copy(
+            src_ref=view, dst_ref=view, send_sem=send_sem.at[idx], recv_sem=recv_sem.at[idx],
+            device_id={"zx": source}, device_id_type=mesh_ids,
+        ).wait_recv()
+
+    def part(stream, a, b, lo=None):
+        view = out_ref.at[slot(stream, a, b), stream]
+        return view if lo is None else view.at[pl.ds(lo, q)]
+
+    for st in range(2):
+        a0, b0 = own[st]
+        send((st, 1, 1), x_ref.at[st], part(st, a0, b0), slot(st, a0 + 1, b0))
+        send((st, 1, -1), x_ref.at[st], part(st, a0, b0), slot(st, a0 - 1, b0))
+    for st in range(2):
+        a0, b0 = own[st]
+        recv((st, 1, 1), part(st, a0 - 1, b0), slot(st, a0 - 1, b0))
+        recv((st, 1, -1), part(st, a0 + 1, b0), slot(st, a0 + 1, b0))
+        send((st, 2, 1), part(st, a0 - 1, b0, 0), part(st, a0 - 1, b0, 0), slot(st, a0 + 1, b0))
+        send((st, 2, -1), part(st, a0 + 1, b0, q), part(st, a0 + 1, b0, q), slot(st, a0 - 1, b0))
+    for st in range(2):
+        a0, b0 = own[st]
+        recv((st, 2, 1), part(st, a0 - 2, b0, 0), slot(st, a0 - 1, b0))
+        recv((st, 2, -1), part(st, a0 + 2, b0, q), slot(st, a0 + 1, b0))
+        for k in range(side):
+            src = x_ref.at[st] if k == 0 else part(st, a0 + k, b0)
+            send((st, 3, 1, k), src, part(st, a0 + k, b0), slot(st, a0, b0 + 1))
+            send((st, 3, -1, k), src, part(st, a0 + k, b0), slot(st, a0, b0 - 1))
+    for st in range(2):
+        a0, b0 = own[st]
+        for k in range(side):
+            recv((st, 3, 1, k), part(st, a0 + k, b0 - 1), slot(st, a0, b0 - 1))
+            recv((st, 3, -1, k), part(st, a0 + k, b0 + 1), slot(st, a0, b0 + 1))
+            send((st, 4, 1, k), part(st, a0 + k, b0 - 1, 0), part(st, a0 + k, b0 - 1, 0), slot(st, a0, b0 + 1))
+            send((st, 4, -1, k), part(st, a0 + k, b0 + 1, q), part(st, a0 + k, b0 + 1, q), slot(st, a0, b0 - 1))
+    for st in range(2):
+        a0, b0 = own[st]
+        for k in range(side):
+            recv((st, 4, 1, k), part(st, a0 + k, b0 - 2, 0), slot(st, a0, b0 - 1))
+            recv((st, 4, -1, k), part(st, a0 + k, b0 + 2, q), slot(st, a0, b0 + 1))
+    local.wait()
+    for copy in sends:
+        copy.wait_send()
+
+
+def gather_rows(block, axis):
+    n = lax.axis_size(axis)
+    side = math.isqrt(n)
+    rows, width = block.shape
+    copies = 2 * (2 + 2 + 4 * side)
+    out = pl.pallas_call(
+        functools.partial(ring_gather_kernel, side),
+        in_specs=[pl.BlockSpec(memory_space=pl.ANY)],
+        out_specs=pl.BlockSpec(memory_space=pl.ANY),
+        out_shape=jax.ShapeDtypeStruct((n, 2, rows // 2, width), block.dtype),
+        scratch_shapes=[
+            pltpu.SemaphoreType.DMA((copies,)),
+            pltpu.SemaphoreType.DMA((copies,)),
+            pltpu.SemaphoreType.DMA,
+        ],
+        compiler_params=pltpu.CompilerParams(collective_id=0, has_side_effects=True),
+    )(block.reshape(2, rows // 2, width))
+    return out.reshape(n * rows, width)
+
+
 def body(sequence_input, conv_first, conv_second, qkv_weight, out_weight, logit_scale):
     row_count = sequence_input.shape[0]
     padded_input = padded_2(sequence_input, 2)
@@ -189,7 +288,7 @@
     wvt = qkv_weight[:, 2 * width_all :].T
 
     swap = [(0, 1), (1, 0)]
-    hidden_all = lax.all_gather(hidden, "zx", axis=0, tiled=True)
+    hidden_all = gather_rows(hidden, "zx")
     hidden_other = lax.ppermute(hidden, "core", swap)
     hidden_q = jnp.concatenate([hidden, hidden_other], axis=0)
     o_part, st_part = attend_partial(hidden_q, hidden_all, wqt, wk, wvt, scale_col, head_count, head_size)

time: 149 us -> 124 us (0.83)
  waiting for transfers between devices: 64 us -> 3.89 us
  Pallas kernels: 31.1 us -> 75.4 us
  between operations: 13.6 us -> 0.26 us
  starting transfers between devices: 12.8 us -> 16.6 us
    all_gather x1 -> x0, waiting for transfers between devices: 60.1 us -> none  [body(): hidden_all = lax.all_gather(hidden, 'zx', axis=0, tiled=True)]
    pallas_call x0 -> x1, Pallas kernels: none -> 44.3 us  [gather_rows(): pl.pallas_call(functools.partial(ring_gather_kernel, side), in_specs=[pl....]
    ppermute x2, starting transfers between devices: 0.77 us -> 4.65 us  [body(): lax.ppermute((o_part[:, row_count:], st_part[:, row_count:]), 'core', swap)]
  transfers between devices with their start and end apart: 8 -> 7, of which waited for: 4 -> 3; matrix products, arithmetic and copies ran while one was open for 11% -> 12% of each run, Pallas kernels for 0% -> 36%
where the time goes in v7:
time: 124 us
  Pallas kernels  75.4 us (61%)
  starting transfers between devices  16.6 us (13%)
  matrix products  15.5 us (12%)
  local copies, waits for them, and re-layouts  10 us (8%)
  waiting for transfers between devices  3.89 us (3%)
  other arithmetic  1.97 us (2%)
    pallas_call x1, Pallas kernels, gather_rows(): pl.pallas_call(functools.partial(ring_gather_kernel, side), in_specs=[pl....  44.3 us
    pallas_call x1, Pallas kernels, attend_partial(): pl.pallas_call(functools.partial(attend_kernel, heads, head_size, nk), gr...  28.3 us
    dot_general x8, matrix products, convolve(): jnp.dot(padded[offset:offset + row_count], weight[offset], preferred_elem...  12.2 us
    ppermute x2, starting transfers between devices, padded_2(): lax.ppermute(lax.slice_in_dim(block, block.shape[0] - width, None, axis=0...  7.92 us
    ppermute x2, starting transfers between devices, body(): lax.ppermute((o_part[:, row_count:], st_part[:, row_count:]), 'core', swap)  4.65 us
    ppermute x2, starting transfers between devices, padded_2(): lax.ppermute(lax.slice_in_dim(block, 0, width, axis=0), SEQ_AXES, backward)  3.97 us
    unnamed x17, local copies, waits for them, and re-layouts  3.81 us
    dot_general x2, matrix products, convolve(): jnp.dot(padded[0:row_count], weight[0], preferred_element_type=jnp.float32)  3.26 us
  transfers between devices with their start and end apart: 7, of which 3 were waited for; matrix products, arithmetic and copies ran while one was open for 12% of the time, Pallas kernels for 36%

profile of v7, /device:TPU:1, one launch (start us, length us, event | category | flops | bytes accessed | tf_op | source)
XLA Modules:
  0.0 123.6 jit_solution(6242480791429724823)
XLA Ops:
  0.0 0.8 fusion.78
  0.8 4.5 %collective-permute-start = (bf16[2,1536]{1,0:T(2,128)(2,1)S(1)}, bf16[2,1536]{1,0:T(2,128)(2,1)S(1)}, u32[]{:S(2)}, u32[]{:S(2)}) collective-permute-start(bf16[2,1536]{1,0:T(2,128)(2,1)S(1)} %get-tuple-element.12), channel_id=1, source_target_pairs={{0,4},{4,8},{8,12},{12,16},{16,20},{20,24},{24,28},{28,32},{32,36}... | collective-permute-start | bytes 18440 | tf_op jit(solution)/shard_map/ppermute | solution.py:20
  5.3 0.0 copy-start.1
  5.3 2.1 %collective-permute-start.1 = (bf16[2,1536]{1,0:T(2,128)(2,1)S(1)}, bf16[2,1536]{1,0:T(2,128)(2,1)S(1)}, u32[]{:S(2)}, u32[]{:S(2)}) collective-permute-start(bf16[2,1536]{1,0:T(2,128)(2,1)S(1)} %get-tuple-element.13), channel_id=1, source_target_pairs={{4,0},{8,4},{12,8},{16,12},{20,16},{24,20},{28,24},{32,28},{36,32}... | collective-permute-start | bytes 18440 | tf_op jit(solution)/shard_map/ppermute | solution.py:21
  7.4 2.7 %fusion.4 = f32[256,768]{1,0:T(8,128)S(1)} fusion(bf16[256,1536]{1,0:T(8,128)(2,1)} %param.6, bf16[5,1536,768]{2,1,0:T(8,128)(2,1)} %param.7), kind=kOutput, calls=%fused_computation.4 | convolution fusion | flops 603979776 | bytes 3932160 | tf_op jit(solution)/shard_map/dot_general | solution.py:28
  10.1 0.0 copy-done.1
  10.1 0.1 constant_dynamic-update-slice_fusion.1
  10.1 0.2 collective-permute-done.1
  10.4 2.5 %fusion = f32[256,768]{1,0:T(8,128)S(1)} fusion(bf16[5,1536,768]{2,1,0:T(8,128)(2,1)} %param.7, bf16[258,1536]{1,0:T(8,128)(2,1)S(1)} %constant_dynamic-update-slice_fusion), kind=kOutput, calls=%fused_computation | convolution fusion | flops 603979776 | bytes 3932160 | tf_op jit(solution)/shard_map/dot_general | solution.py:28
  12.9 2.5 %fusion.2 = f32[256,768]{1,0:T(8,128)S(1)} fusion(bf16[5,1536,768]{2,1,0:T(8,128)(2,1)} %param.7, bf16[258,1536]{1,0:T(8,128)(2,1)S(1)} %constant_dynamic-update-slice_fusion), kind=kOutput, calls=%fused_computation.2 | convolution fusion | flops 603979776 | bytes 3932160 | tf_op jit(solution)/shard_map/dot_general | solution.py:28
  15.3 0.0 collective-permute-done
  15.3 0.0 slice-start
  15.3 2.6 %fusion.6 = f32[256,768]{1,0:T(8,128)S(1)} fusion(bf16[5,1536,768]{2,1,0:T(8,128)(2,1)} %param.7, bf16[256,1536]{1,0:T(8,128)(2,1)S(1)} %copy-done.1, bf16[2,1536]{1,0:T(2,128)(2,1)S(1)} %collective-permute-done), kind=kOutput, calls=%fused_computation.6 | convolution fusion | flops 605552640 | bytes 3938304 | tf_op jit(solution)/shard_map/dot_general | solution.py:28
  18.0 0.0 slice-start.1
  18.0 2.8 %fusion.57 = bf16[256,768]{1,0:T(8,128)(2,1)S(1)} fusion(f32[256,768]{1,0:T(8,128)S(1)} %fusion, f32[256,768]{1,0:T(8,128)S(1)} %fusion.2, f32[256,768]{1,0:T(8,128)S(1)} %fusion.4, f32[256,768]{1,0:T(8,128)S(1)} %fusion.6, bf16[5,1536,768]{2,1,0:T(8,128)(2,1)} %param.7, bf16[2,1536]{1,0:T(2,128)(2,1)S(1)} %collective-permute-done, ...), kind=kOutput, calls=%fused_computation.49 | convolution fusion | flops 608108544 | bytes 6690816 | tf_op jit(solution)/shard_map/dot_general | solution.py:26
  20.8 3.4 %collective-permute-start.2 = (bf16[2,768]{1,0:T(2,128)(2,1)S(1)}, bf16[2,768]{1,0:T(2,128)(2,1)S(1)}, u32[]{:S(2)}, u32[]{:S(2)}) collective-permute-start(bf16[2,768]{1,0:T(2,128)(2,1)S(1)} %get-tuple-element.14), channel_id=1, source_target_pairs={{0,4},{4,8},{8,12},{12,16},{16,20},{20,24},{24,28},{28,32},{32,36}... | collective-permute-start | bytes 9224 | tf_op jit(solution)/shard_map/ppermute | solution.py:20
  24.2 1.9 %collective-permute-start.3 = (bf16[2,768]{1,0:T(2,128)(2,1)S(1)}, bf16[2,768]{1,0:T(2,128)(2,1)S(1)}, u32[]{:S(2)}, u32[]{:S(2)}) collective-permute-start(bf16[2,768]{1,0:T(2,128)(2,1)S(1)} %get-tuple-element.15), channel_id=1, source_target_pairs={{4,0},{8,4},{12,8},{16,12},{20,16},{24,20},{28,24},{32,28},{36,32}... | collective-permute-start | bytes 9224 | tf_op jit(solution)/shard_map/ppermute | solution.py:21
  26.1 0.0 slice-done
  26.1 0.0 slice-done.1
  26.1 0.5 fusion.34
  26.6 2.5 %collective-permute-done.3 = bf16[2,768]{1,0:T(2,128)(2,1)S(1)} collective-permute-done((bf16[2,768]{1,0:T(2,128)(2,1)S(1)}, bf16[2,768]{1,0:T(2,128)(2,1)S(1)}, u32[]{:S(2)}, u32[]{:S(2)}) %collective-permute-start.3) | collective-permute-done | bytes 3104 | tf_op jit(solution)/shard_map/ppermute | solution.py:21
  29.1 0.5 fusion.31
  29.6 0.0 collective-permute-done.2
  29.6 0.5 fusion.36
  30.1 0.5 fusion.23
  30.6 0.0 copy-start.4
  30.6 0.5 fusion.30.hid_ref
  31.2 0.1 collective-permute-start.4
  31.3 0.0 copy-done.4
  31.3 0.1 broadcast_in_dim.3
  31.3 0.9 copy.11.scale_ref
  32.2 2.7 %fusion.77 = (bf16[768,512]{1,0:T(8,128)(2,1)S(1)}, bf16[768,512]{1,0:T(8,128)(2,1)S(1)}, bf16[768,512]{1,0:T(8,128)(2,1)}) fusion(bf16[768,1536]{1,0:T(8,128)(2,1)} %param.9), kind=kLoop, calls=%fused_computation.74 | loop fusion | bytes 4718592 | tf_op jit(solution)/shard_map/slice | solution.py:288
  35.0 1.2 copy.13
  36.1 1.2 copy.12
  37.3 0.0 copy-done
  37.3 44.3 %shard_map.64 = bf16[16,2,128,768]{3,2,1,0:T(8,128)(2,1)} custom-call(bf16[2,128,768]{2,1,0:T(8,128)(2,1)} %bitcast.50), custom_call_target="tpu_custom_call" | custom-call | tf_op jit(solution)/shard_map/pallas_call | solution.py:260
  81.6 0.0 collective-permute-done.4
  81.6 2.0 %pad_maximum_fusion.2.hq_ref = bf16[512,768]{1,0:T(8,128)(2,1)} fusion(bf16[256,768]{1,0:T(8,128)(2,1)S(1)} %collective-permute-done.4, bf16[256,768]{1,0:T(8,128)(2,1)} %copy-done), kind=kLoop, calls=%fused_computation.54 | loop fusion | flops 1572864 | bytes 1572864 | tf_op jit(solution)/shard_map/concatenate | solution.py:293
  83.6 28.3 %shard_map.65 = (f32[512,512]{1,0:T(8,128)}, f32[8,512]{1,0:T(8,128)}) custom-call(bf16[512,768]{1,0:T(8,128)(2,1)} %pad_maximum_fusion.2.hq_ref, bf16[4096,768]{1,0:T(8,128)(2,1)} %bitcast.49, bf16[512,768]{1,0:T(8,128)(2,1)} %bitcast.54, bf16[768,512]{1,0:T(8,128)(2,1)} %get-tuple-element.11.wk_ref, bf16[512,768]{1,0:T(8,128)(2,1)} %bitcast.53, ...), custom_call_target="tpu_custom_call" | custom-call | flops 10737418240 | bytes 8388608 | tf_op jit(solution)/shard_map/pallas_call | solution.py:102
  111.8 1.1 slice.114
  112.9 4.6 %collective-permute-start.5 = (f32[512,256]{1,0:T(8,128)S(1)}, f32[512,256]{1,0:T(8,128)S(1)}, u32[]{:S(2)}, u32[]{:S(2)}) collective-permute-start(f32[512,256]{1,0:T(8,128)S(1)} %slice.114), channel_id=1, source_target_pairs={{0,4},{4,0},{1,5},{5,1},{2,6},{6,2},{3,7},{7,3},{8,12},{12,8},{9,1... | collective-permute-start | bytes 1572872 | tf_op jit(solution)/shard_map/ppermute | solution.py:295
  117.5 0.7 slice.115
  118.2 0.0 collective-permute-start.6
  118.3 1.2 collective-permute-done.6.sg_ref
  119.4 0.0 collective-permute-done.5.og_ref
  119.4 0.6 copy-done.3
  120.0 0.8 copy-done.2
  120.8 2.8 %shard_map.66 = bf16[256,768]{1,0:T(8,128)(2,1)} custom-call(f32[512,512]{1,0:T(8,128)} %get-tuple-element.7.o_ref, f32[8,512]{1,0:T(8,128)} %get-tuple-element.8.st_ref, f32[512,256]{1,0:T(8,128)} %copy-done.2, f32[8,256]{1,0:T(8,128)} %copy-done.3, bf16[256,768]{1,0:T(8,128)(2,1)} %copy-done, bf16[512,768]{1,0:T(8,128)(2,1)} %wo_ref.1), custom_call_target="tpu_custom_call" | custom-call | tf_op jit(solution)/shard_map/pallas_call | solution.py:160
  (7 shorter events, 0.0 us)
Async XLA Ops:
  0.8 14.6 %collective-permute-start = (bf16[2,1536]{1,0:T(2,128)(2,1)S(1)}, bf16[2,1536]{1,0:T(2,128)(2,1)S(1)}, u32[]{:S(2)}, u32[]{:S(2)}) collective-permute-start(bf16[2,1536]{1,0:T(2,128)(2,1)S(1)} %get-tuple-element.12), channel_id=1, source_target_pairs={{0,4},{4,8},{8,12},{12,16},{16,20},{20,24},{24,28},{28,32},{32,36}... | collective-permute-start | bytes 18440 | tf_op jit(solution)/shard_map/ppermute | solution.py:20
  5.3 4.8 %copy-start.1 = (bf16[256,1536]{1,0:T(8,128)(2,1)S(1)}, bf16[256,1536]{1,0:T(8,128)(2,1)}, u32[]{:S(2)}) copy-start(bf16[256,1536]{1,0:T(8,128)(2,1)} %param.6) | copy-start | bytes 2359300
  5.3 5.1 %collective-permute-start.1 = (bf16[2,1536]{1,0:T(2,128)(2,1)S(1)}, bf16[2,1536]{1,0:T(2,128)(2,1)S(1)}, u32[]{:S(2)}, u32[]{:S(2)}) collective-permute-start(bf16[2,1536]{1,0:T(2,128)(2,1)S(1)} %get-tuple-element.13), channel_id=1, source_target_pairs={{4,0},{8,4},{12,8},{16,12},{20,16},{24,20},{28,24},{32,28},{36,32}... | collective-permute-start | bytes 18440 | tf_op jit(solution)/shard_map/ppermute | solution.py:21
  15.3 10.8 %slice-start = ((s8[5898240]{0:T(1024)(128)(4,1)}), s8[4194304]{0:T(1024)(128)(4,1)S(1)}, s32[]{:S(2)}) async-start(s8[5898240]{0:T(1024)(128)(4,1)} %bitcast.51), calls=%async_computation | async-start | bytes 8388608
  18.0 8.2 %slice-start.1 = ((s8[5898240]{0:T(1024)(128)(4,1)}), s8[1703936]{0:T(1024)(128)(4,1)S(1)}, s32[]{:S(2)}) async-start(s8[5898240]{0:T(1024)(128)(4,1)} %bitcast.51), calls=%async_computation.1 | async-start | bytes 3407872
  20.8 8.8 %collective-permute-start.2 = (bf16[2,768]{1,0:T(2,128)(2,1)S(1)}, bf16[2,768]{1,0:T(2,128)(2,1)S(1)}, u32[]{:S(2)}, u32[]{:S(2)}) collective-permute-start(bf16[2,768]{1,0:T(2,128)(2,1)S(1)} %get-tuple-element.14), channel_id=1, source_target_pairs={{0,4},{4,8},{8,12},{12,16},{16,20},{20,24},{24,28},{28,32},{32,36}... | collective-permute-start | bytes 9224 | tf_op jit(solution)/shard_map/ppermute | solution.py:20
  24.2 4.9 %collective-permute-start.3 = (bf16[2,768]{1,0:T(2,128)(2,1)S(1)}, bf16[2,768]{1,0:T(2,128)(2,1)S(1)}, u32[]{:S(2)}, u32[]{:S(2)}) collective-permute-start(bf16[2,768]{1,0:T(2,128)(2,1)S(1)} %get-tuple-element.15), channel_id=1, source_target_pairs={{4,0},{8,4},{12,8},{16,12},{20,16},{24,20},{28,24},{32,28},{36,32}... | collective-permute-start | bytes 9224 | tf_op jit(solution)/shard_map/ppermute | solution.py:21
  30.6 0.7 copy-start.4
  31.2 6.1 %copy-start = (bf16[256,768]{1,0:T(8,128)(2,1)}, bf16[256,768]{1,0:T(8,128)(2,1)S(1)}, u32[]{:S(2)}) copy-start(bf16[256,768]{1,0:T(8,128)(2,1)S(1)} %fusion.30.hid_ref) | copy-start | bytes 1179652
  31.2 50.4 %collective-permute-start.4 = (bf16[256,768]{1,0:T(8,128)(2,1)S(1)}, bf16[256,768]{1,0:T(8,128)(2,1)S(1)}, u32[]{:S(2)}, u32[]{:S(2)}) collective-permute-start(bf16[256,768]{1,0:T(8,128)(2,1)S(1)} %fusion.30.hid_ref), channel_id=1, source_target_pairs={{0,4},{4,0},{1,5},{5,1},{2,6},{6,2},{3,7},{7,3},{8,12},{12,8},{9,1... | collective-permute-start | bytes 1179656 | tf_op jit(solution)/shard_map/ppermute | solution.py:292
  112.9 6.5 %collective-permute-start.5 = (f32[512,256]{1,0:T(8,128)S(1)}, f32[512,256]{1,0:T(8,128)S(1)}, u32[]{:S(2)}, u32[]{:S(2)}) collective-permute-start(f32[512,256]{1,0:T(8,128)S(1)} %slice.114), channel_id=1, source_target_pairs={{0,4},{4,0},{1,5},{5,1},{2,6},{6,2},{3,7},{7,3},{8,12},{12,8},{9,1... | collective-permute-start | bytes 1572872 | tf_op jit(solution)/shard_map/ppermute | solution.py:295
  118.2 1.2 collective-permute-start.6
  119.4 0.6 copy-start.3
  120.0 0.8 copy-start.2

commit v8 on v7

--- a/solution.py
+++ b/solution.py
@@ -272,10 +272,51 @@
     return out.reshape(n * rows, width)
 
 
+def conv_gelu_kernel(taps, rows, x_ref, w_ref, o_ref, acc_sc):
+    j = pl.program_id(0)
+    product = jnp.dot(x_ref[...], w_ref[...], preferred_element_type=jnp.float32)
+    for t in range(taps):
+
+        @pl.when(j == t)
+        def _():
+            if t == 0:
+                acc_sc[...] = product[t : t + rows]
+            else:
+                acc_sc[...] = acc_sc[...] + product[t : t + rows]
+
+    @pl.when(j == taps - 1)
+    def _():
+        o_ref[...] = jax.nn.gelu(acc_sc[...]).astype(o_ref.dtype)
+
+
+def conv_gelu(padded, weight, rows):
+    taps, channels, width = weight.shape
+    extra = (-padded.shape[0]) % 8
+    padded = jnp.pad(padded, ((0, extra), (0, 0)))
+    whole = lambda j: (0, 0)
+    return pl.pallas_call(
+        functools.partial(conv_gelu_kernel, taps, rows),
+        grid=(taps,),
+        in_specs=[
+            pl.BlockSpec(padded.shape, whole),
+            pl.BlockSpec((None, channels, width), lambda j: (j, 0, 0)),
+        ],
+        out_specs=pl.BlockSpec((rows, width), whole),
+        out_shape=jax.ShapeDtypeStruct((rows, width), jnp.bfloat16),
+        scratch_shapes=[pltpu.VMEM((rows, width), jnp.float32)],
+        compiler_params=pltpu.CompilerParams(dimension_semantics=("arbitrary",)),
+        cost_estimate=pl.CostEstimate(
+            flops=2 * taps * padded.shape[0] * channels * width,
+            transcendentals=rows * width,
+            bytes_accessed=taps * channels * width * 2 + padded.size * 2 + rows * width * 2,
+        ),
+    )(padded, weight)
+
+
 def body(sequence_input, conv_first, conv_second, qkv_weight, out_weight, logit_scale):
     row_count = sequence_input.shape[0]
     padded_input = padded_2(sequence_input, 2)
-    first_out = jax.nn.gelu(convolve(padded_input, conv_first, row_count)).astype(jnp.bfloat16)
+    first_out = conv_gelu(padded_input, conv_first, row_count)
     padded_first = padded_2(first_out, 2)
     second = convolve(padded_first, conv_second, row_count)
     hidden = (first_out.astype(jnp.float32) + second).astype(jnp.bfloat16)

time: 124 us -> 130 us (1.048)
  Pallas kernels: 75.4 us -> 84.7 us
  matrix products: 15.5 us -> 8.92 us
  other arithmetic: 1.97 us -> 4.18 us
    pallas_call x0 -> x1, Pallas kernels: none -> 9.18 us  [conv_gelu(): pl.pallas_call(functools.partial(conv_gelu_kernel, taps, rows), grid=(tap...]
    dot_general x8 -> x4, matrix products: 12.2 us -> 7.16 us  [convolve(): jnp.dot(padded[offset:offset + row_count], weight[offset], preferred_elem...]
    concatenate x0 -> x1, other arithmetic: none -> 2.24 us  [padded_2(): return jnp.concatenate([low, block, high], axis=0)]
    dot_general x2 -> x1, matrix products: 3.26 us -> 1.76 us  [convolve(): jnp.dot(padded[0:row_count], weight[0], preferred_element_type=jnp.float32)]
    ppermute x2, starting transfers between devices: 7.92 us -> 6.46 us  [padded_2(): lax.ppermute(lax.slice_in_dim(block, block.shape[0] - width, None, axis=0...]
    unnamed x17 -> x12, local copies, waits for them, and re-layouts: 3.81 us -> 3.72 us
  transfers between devices with their start and end apart: 7 -> 7, of which waited for: 3 -> 3; matrix products, arithmetic and copies ran while one was open for 12% -> 8% of each run, Pallas kernels for 36% -> 34%
where the time goes in v8:
time: 130 us; the launch traced here: 129 us
  Pallas kernels  84.7 us (65%)
  starting transfers between devices  15.4 us (12%)
  local copies, waits for them, and re-layouts  10.7 us (8%)
  matrix products  8.92 us (7%)
  waiting for transfers between devices  4.83 us (4%)
  other arithmetic  4.18 us (3%)
    pallas_call x1, Pallas kernels, gather_rows(): pl.pallas_call(functools.partial(ring_gather_kernel, side), in_specs=[pl....  44.4 us
    pallas_call x1, Pallas kernels, attend_partial(): pl.pallas_call(functools.partial(attend_kernel, heads, head_size, nk), gr...  28.3 us
    pallas_call x1, Pallas kernels, conv_gelu(): pl.pallas_call(functools.partial(conv_gelu_kernel, taps, rows), grid=(tap...  9.18 us
    dot_general x4, matrix products, convolve(): jnp.dot(padded[offset:offset + row_count], weight[offset], preferred_elem...  7.16 us
    ppermute x2, starting transfers between devices, padded_2(): lax.ppermute(lax.slice_in_dim(block, block.shape[0] - width, None, axis=0...  6.46 us
    ppermute x2, starting transfers between devices, body(): lax.ppermute((o_part[:, row_count:], st_part[:, row_count:]), 'core', swap)  4.55 us
    ppermute x2, starting transfers between devices, padded_2(): lax.ppermute(lax.slice_in_dim(block, 0, width, axis=0), SEQ_AXES, backward)  4.3 us
    unnamed x12, local copies, waits for them, and re-layouts  3.72 us
  transfers between devices with their start and end apart: 7, of which 3 were waited for; matrix products, arithmetic and copies ran while one was open for 8% of the time, Pallas kernels for 34%

profile of v8, /device:TPU:1, one launch (start us, length us, event | category | flops | bytes accessed | tf_op | source)
XLA Modules:
  0.0 128.9 jit_solution(2370330064959363696)
XLA Ops:
  0.0 0.8 fusion.35
  0.8 4.5 %collective-permute-start = (bf16[2,1536]{1,0:T(2,128)(2,1)S(1)}, bf16[2,1536]{1,0:T(2,128)(2,1)S(1)}, u32[]{:S(2)}, u32[]{:S(2)}) collective-permute-start(bf16[2,1536]{1,0:T(2,128)(2,1)S(1)} %get-tuple-element.12), channel_id=1, source_target_pairs={{0,4},{4,8},{8,12},{12,16},{16,20},{20,24},{24,28},{28,32},{32,36}... | collective-permute-start | bytes 18440 | tf_op jit(solution)/shard_map/ppermute | solution.py:20
  5.3 1.9 %collective-permute-start.1 = (bf16[2,1536]{1,0:T(2,128)(2,1)S(1)}, bf16[2,1536]{1,0:T(2,128)(2,1)S(1)}, u32[]{:S(2)}, u32[]{:S(2)}) collective-permute-start(bf16[2,1536]{1,0:T(2,128)(2,1)S(1)} %get-tuple-element.13), channel_id=1, source_target_pairs={{4,0},{8,4},{12,8},{16,12},{20,16},{24,20},{28,24},{32,28},{36,32}... | collective-permute-start | bytes 18440 | tf_op jit(solution)/shard_map/ppermute | solution.py:21
  7.2 0.0 collective-permute-done
  7.2 3.0 %collective-permute-done.1 = bf16[2,1536]{1,0:T(2,128)(2,1)S(1)} collective-permute-done((bf16[2,1536]{1,0:T(2,128)(2,1)S(1)}, bf16[2,1536]{1,0:T(2,128)(2,1)S(1)}, u32[]{:S(2)}, u32[]{:S(2)}) %collective-permute-start.1) | collective-permute-done | bytes 6176 | tf_op jit(solution)/shard_map/ppermute | solution.py:21
  10.2 2.2 %fusion.19.x_ref = bf16[264,1536]{1,0:T(8,128)(2,1)} fusion(bf16[2,1536]{1,0:T(2,128)(2,1)S(1)} %collective-permute-done.1, bf16[256,1536]{1,0:T(8,128)(2,1)} %param.6, bf16[2,1536]{1,0:T(2,128)(2,1)S(1)} %collective-permute-done), kind=kLoop, calls=%fused_computation.22 | loop fusion | flops 4055040 | bytes 1609728 | tf_op jit(solution)/shard_map/concatenate | solution.py:22
  12.5 9.2 %shard_map.64 = bf16[256,768]{1,0:T(8,128)(2,1)} custom-call(bf16[264,1536]{1,0:T(8,128)(2,1)} %fusion.19.x_ref, bf16[5,1536,768]{2,1,0:T(8,128)(2,1)} %w_ref.1), custom_call_target="tpu_custom_call" | custom-call | flops 3114270720 | bytes 13000704 | tf_op jit(solution)/shard_map/pallas_call | solution.py:297
  21.7 0.0 copy-start
  21.7 0.8 fusion.36
  22.5 1.9 %collective-permute-start.2 = (bf16[2,768]{1,0:T(2,128)(2,1)S(1)}, bf16[2,768]{1,0:T(2,128)(2,1)S(1)}, u32[]{:S(2)}, u32[]{:S(2)}) collective-permute-start(bf16[2,768]{1,0:T(2,128)(2,1)S(1)} %get-tuple-element.14), channel_id=1, source_target_pairs={{0,4},{4,8},{8,12},{12,16},{16,20},{20,24},{24,28},{28,32},{32,36}... | collective-permute-start | bytes 9224 | tf_op jit(solution)/shard_map/ppermute | solution.py:20
  24.4 2.4 %collective-permute-start.3 = (bf16[2,768]{1,0:T(2,128)(2,1)S(1)}, bf16[2,768]{1,0:T(2,128)(2,1)S(1)}, u32[]{:S(2)}, u32[]{:S(2)}) collective-permute-start(bf16[2,768]{1,0:T(2,128)(2,1)S(1)} %get-tuple-element.15), channel_id=1, source_target_pairs={{4,0},{8,4},{12,8},{16,12},{20,16},{24,20},{28,24},{32,28},{36,32}... | collective-permute-start | bytes 9224 | tf_op jit(solution)/shard_map/ppermute | solution.py:21
  26.8 1.9 %fusion.8 = f32[256,768]{1,0:T(8,128)S(1)} fusion(bf16[256,768]{1,0:T(8,128)(2,1)} %shard_map.64, bf16[5,768,768]{2,1,0:T(8,128)(2,1)} %param.8), kind=kOutput, calls=%fused_computation.11 | convolution fusion | flops 301989888 | bytes 2359296 | tf_op jit(solution)/shard_map/dot_general | solution.py:28
  28.7 0.6 collective-permute-done.3
  29.3 0.0 copy-done
  29.3 1.8 %fusion.5 = f32[256,768]{1,0:T(8,128)S(1)} fusion(bf16[5,768,768]{2,1,0:T(8,128)(2,1)} %param.8, bf16[2,768]{1,0:T(2,128)(2,1)S(1)} %collective-permute-done.3, bf16[256,768]{1,0:T(8,128)(2,1)S(1)} %copy-done), kind=kOutput, calls=%fused_computation.8 | convolution fusion | flops 302776320 | bytes 2362368 | tf_op jit(solution)/shard_map/dot_general | solution.py:28
  31.1 0.0 collective-permute-done.2
  31.1 1.8 %fusion.10 = f32[256,768]{1,0:T(8,128)S(1)} fusion(bf16[5,768,768]{2,1,0:T(8,128)(2,1)} %param.8, bf16[256,768]{1,0:T(8,128)(2,1)S(1)} %copy-done, bf16[2,768]{1,0:T(2,128)(2,1)S(1)} %collective-permute-done.2), kind=kOutput, calls=%fused_computation.13 | convolution fusion | flops 302776320 | bytes 2362368 | tf_op jit(solution)/shard_map/dot_general | solution.py:28
  32.9 1.8 %fusion.4 = f32[256,768]{1,0:T(8,128)S(1)} fusion(f32[256,768]{1,0:T(8,128)S(1)} %fusion.8, f32[256,768]{1,0:T(8,128)S(1)} %fusion.10, bf16[5,768,768]{2,1,0:T(8,128)(2,1)} %param.8, bf16[2,768]{1,0:T(2,128)(2,1)S(1)} %collective-permute-done.2, bf16[256,768]{1,0:T(8,128)(2,1)S(1)} %copy-done), kind=kOutput, calls=%fused_computation.7 | convolution fusion | flops 303169536 | bytes 3935232 | tf_op jit(solution)/shard_map/dot_general | solution.py:26
  34.6 0.0 copy-start.4
  34.6 1.8 %add_convert_fusion.hid_ref = bf16[256,768]{1,0:T(8,128)(2,1)S(1)} fusion(bf16[256,768]{1,0:T(8,128)(2,1)S(1)} %copy-done, f32[256,768]{1,0:T(8,128)S(1)} %fusion.5, f32[256,768]{1,0:T(8,128)S(1)} %fusion.4, bf16[5,768,768]{2,1,0:T(8,128)(2,1)} %param.8, bf16[2,768]{1,0:T(2,128)(2,1)S(1)} %collective-permute-done.3), kind=kOutput, calls=%fused_computation.24 | convolution fusion | flops 303759360 | bytes 3935232 | tf_op jit(solution)/shard_map/dot_general | solution.py:28
  36.4 0.0 copy-start.1
  36.4 0.1 collective-permute-start.4
  36.5 0.0 copy-done.4
  36.6 0.1 broadcast_in_dim.3
  36.6 0.9 copy.11.scale_ref
  37.5 2.8 %fusion.34 = (bf16[768,512]{1,0:T(8,128)(2,1)S(1)}, bf16[768,512]{1,0:T(8,128)(2,1)S(1)}, bf16[768,512]{1,0:T(8,128)(2,1)}) fusion(bf16[768,1536]{1,0:T(8,128)(2,1)} %param.9), kind=kLoop, calls=%fused_computation.40 | loop fusion | bytes 4718592 | tf_op jit(solution)/shard_map/slice | solution.py:329
  40.2 1.2 copy.13
  41.4 1.2 copy.12
  42.6 0.0 copy-done.1
  42.6 44.4 %shard_map.65 = bf16[16,2,128,768]{3,2,1,0:T(8,128)(2,1)} custom-call(bf16[2,128,768]{2,1,0:T(8,128)(2,1)} %bitcast.24), custom_call_target="tpu_custom_call" | custom-call | tf_op jit(solution)/shard_map/pallas_call | solution.py:260
  87.0 0.0 collective-permute-done.4
  87.0 1.9 %pad_maximum_fusion.hq_ref = bf16[512,768]{1,0:T(8,128)(2,1)} fusion(bf16[256,768]{1,0:T(8,128)(2,1)S(1)} %collective-permute-done.4, bf16[256,768]{1,0:T(8,128)(2,1)} %copy-done.1), kind=kLoop, calls=%fused_computation.23 | loop fusion | flops 1572864 | bytes 1572864 | tf_op jit(solution)/shard_map/concatenate | solution.py:334
  88.9 28.3 %shard_map.66 = (f32[512,512]{1,0:T(8,128)}, f32[8,512]{1,0:T(8,128)}) custom-call(bf16[512,768]{1,0:T(8,128)(2,1)} %pad_maximum_fusion.hq_ref, bf16[4096,768]{1,0:T(8,128)(2,1)} %bitcast.23, bf16[512,768]{1,0:T(8,128)(2,1)} %bitcast.26, bf16[768,512]{1,0:T(8,128)(2,1)} %get-tuple-element.11.wk_ref, bf16[512,768]{1,0:T(8,128)(2,1)} %bitcast.25, ...), custom_call_target="tpu_custom_call" | custom-call | flops 10737418240 | bytes 8388608 | tf_op jit(solution)/shard_map/pallas_call | solution.py:102
  117.2 1.1 slice.74
  118.3 4.5 %collective-permute-start.5 = (f32[512,256]{1,0:T(8,128)S(1)}, f32[512,256]{1,0:T(8,128)S(1)}, u32[]{:S(2)}, u32[]{:S(2)}) collective-permute-start(f32[512,256]{1,0:T(8,128)S(1)} %slice.74), channel_id=1, source_target_pairs={{0,4},{4,0},{1,5},{5,1},{2,6},{6,2},{3,7},{7,3},{8,12},{12,8},{9,1... | collective-permute-start | bytes 1572872 | tf_op jit(solution)/shard_map/ppermute | solution.py:336
  122.8 0.7 slice.75
  123.5 0.0 collective-permute-start.6
  123.6 1.2 collective-permute-done.6.sg_ref
  124.7 0.0 copy-start.3
  124.7 0.0 collective-permute-done.5.og_ref
  124.7 0.6 copy-done.3
  125.3 0.0 copy-start.2
  125.3 0.8 copy-done.2
  126.1 2.8 %shard_map.67 = bf16[256,768]{1,0:T(8,128)(2,1)} custom-call(f32[512,512]{1,0:T(8,128)} %get-tuple-element.7.o_ref, f32[8,512]{1,0:T(8,128)} %get-tuple-element.8.st_ref, f32[512,256]{1,0:T(8,128)} %copy-done.2, f32[8,256]{1,0:T(8,128)} %copy-done.3, bf16[256,768]{1,0:T(8,128)(2,1)} %copy-done.1, bf16[512,768]{1,0:T(8,128)(2,1)} %wo_ref.1), custom_call_target="tpu_custom_call" | custom-call | tf_op jit(solution)/shard_map/pallas_call | solution.py:160
  (1 shorter events, 0.0 us)
Async XLA Ops:
  0.8 6.4 %collective-permute-start = (bf16[2,1536]{1,0:T(2,128)(2,1)S(1)}, bf16[2,1536]{1,0:T(2,128)(2,1)S(1)}, u32[]{:S(2)}, u32[]{:S(2)}) collective-permute-start(bf16[2,1536]{1,0:T(2,128)(2,1)S(1)} %get-tuple-element.12), channel_id=1, source_target_pairs={{0,4},{4,8},{8,12},{12,16},{16,20},{20,24},{24,28},{28,32},{32,36}... | collective-permute-start | bytes 18440 | tf_op jit(solution)/shard_map/ppermute | solution.py:20
  5.3 4.9 %collective-permute-start.1 = (bf16[2,1536]{1,0:T(2,128)(2,1)S(1)}, bf16[2,1536]{1,0:T(2,128)(2,1)S(1)}, u32[]{:S(2)}, u32[]{:S(2)}) collective-permute-start(bf16[2,1536]{1,0:T(2,128)(2,1)S(1)} %get-tuple-element.13), channel_id=1, source_target_pairs={{4,0},{8,4},{12,8},{16,12},{20,16},{24,20},{28,24},{32,28},{36,32}... | collective-permute-start | bytes 18440 | tf_op jit(solution)/shard_map/ppermute | solution.py:21
  21.7 7.7 %copy-start = (bf16[256,768]{1,0:T(8,128)(2,1)S(1)}, bf16[256,768]{1,0:T(8,128)(2,1)}, u32[]{:S(2)}) copy-start(bf16[256,768]{1,0:T(8,128)(2,1)} %shard_map.64) | copy-start | bytes 1179652
  22.5 8.6 %collective-permute-start.2 = (bf16[2,768]{1,0:T(2,128)(2,1)S(1)}, bf16[2,768]{1,0:T(2,128)(2,1)S(1)}, u32[]{:S(2)}, u32[]{:S(2)}) collective-permute-start(bf16[2,768]{1,0:T(2,128)(2,1)S(1)} %get-tuple-element.14), channel_id=1, source_target_pairs={{0,4},{4,8},{8,12},{12,16},{16,20},{20,24},{24,28},{28,32},{32,36}... | collective-permute-start | bytes 9224 | tf_op jit(solution)/shard_map/ppermute | solution.py:20
  24.4 4.9 %collective-permute-start.3 = (bf16[2,768]{1,0:T(2,128)(2,1)S(1)}, bf16[2,768]{1,0:T(2,128)(2,1)S(1)}, u32[]{:S(2)}, u32[]{:S(2)}) collective-permute-start(bf16[2,768]{1,0:T(2,128)(2,1)S(1)} %get-tuple-element.15), channel_id=1, source_target_pairs={{4,0},{8,4},{12,8},{16,12},{20,16},{24,20},{28,24},{32,28},{36,32}... | collective-permute-start | bytes 9224 | tf_op jit(solution)/shard_map/ppermute | solution.py:21
  34.6 1.9 %copy-start.4 = (f32[4]{0:T(128)S(1)}, f32[4]{0:T(128)}, u32[]{:S(2)}) copy-start(f32[4]{0:T(128)} %param.11) | copy-start | bytes 52
  36.4 6.1 %copy-start.1 = (bf16[256,768]{1,0:T(8,128)(2,1)}, bf16[256,768]{1,0:T(8,128)(2,1)S(1)}, u32[]{:S(2)}) copy-start(bf16[256,768]{1,0:T(8,128)(2,1)S(1)} %add_convert_fusion.hid_ref) | copy-start | bytes 1179652
  36.4 50.5 %collective-permute-start.4 = (bf16[256,768]{1,0:T(8,128)(2,1)S(1)}, bf16[256,768]{1,0:T(8,128)(2,1)S(1)}, u32[]{:S(2)}, u32[]{:S(2)}) collective-permute-start(bf16[256,768]{1,0:T(8,128)(2,1)S(1)} %add_convert_fusion.hid_ref), channel_id=1, source_target_pairs={{0,4},{4,0},{1,5},{5,1},{2,6},{6,2},{3,7},{7,3},{8,12},{12,8},{9,1... | collective-permute-start | bytes 1179656 | tf_op jit(solution)/shard_map/ppermute | solution.py:333
  118.3 6.4 %collective-permute-start.5 = (f32[512,256]{1,0:T(8,128)S(1)}, f32[512,256]{1,0:T(8,128)S(1)}, u32[]{:S(2)}, u32[]{:S(2)}) collective-permute-start(f32[512,256]{1,0:T(8,128)S(1)} %slice.74), channel_id=1, source_target_pairs={{0,4},{4,0},{1,5},{5,1},{2,6},{6,2},{3,7},{7,3},{8,12},{12,8},{9,1... | collective-permute-start | bytes 1572872 | tf_op jit(solution)/shard_map/ppermute | solution.py:336
  123.5 1.2 collective-permute-start.6
  124.7 0.6 copy-start.3
  125.3 0.8 copy-start.2

commit v9 on v7

--- a/solution.py
+++ b/solution.py
@@ -44,22 +44,16 @@
     return parts
 
 
-def attend_kernel(heads, head_size, nk, hq_ref, hkv_ref, wqt_ref, wk_ref, wvt_ref, scale_ref,
+def attend_kernel(heads, head_size, nk, qa_ref, qb_ref, hkv_ref, wk_ref, wvt_ref,
                   o_ref, st_ref, qt_sc, m_sc, l_sc, acc_sc):
     j = pl.program_id(0)
     contract_last = (((1,), (1,)), ((), ()))
 
     @pl.when(j == 0)
     def _():
-        proj_t = lax.dot_general(
-            wqt_ref[...], hq_ref[...], contract_last, preferred_element_type=jnp.float32
-        )
-        for h in range(heads):
-            rows = slice(h * head_size, (h + 1) * head_size)
-            part = proj_t[rows, :]
-            mean_sq = jnp.mean(part * part, axis=0, keepdims=True)
-            normed = part * lax.rsqrt(mean_sq + 1e-06)
-            qt_sc[rows, :] = (normed * scale_ref[rows, :]).astype(jnp.bfloat16)
+        own = qa_ref.shape[1]
+        qt_sc[:, :own] = qa_ref[...]
+        qt_sc[:, own:] = qb_ref[...]
         m_sc[...] = jnp.full(m_sc.shape, -jnp.inf, jnp.float32)
         l_sc[...] = jnp.zeros(l_sc.shape, jnp.float32)
         acc_sc[...] = jnp.zeros(acc_sc.shape, jnp.float32)
@@ -93,22 +87,21 @@
             st_ref[heads + h : heads + h + 1, :] = l_sc[h]
 
 
-def attend_partial(hidden_q, hidden_kv, wqt, wk, wvt, scale_col, heads, head_size, tk=512):
-    q_rows, channels = hidden_q.shape
-    k_rows = hidden_kv.shape[0]
-    width = heads * head_size
+def attend_partial(qt_own, qt_other, hidden_kv, qkv_weight, wvt, heads, head_size, tk=512):
+    width, own = qt_own.shape
+    q_rows = 2 * own
+    k_rows, channels = hidden_kv.shape
     nk = k_rows // tk
     whole = lambda j: (0, 0)
     return pl.pallas_call(
         functools.partial(attend_kernel, heads, head_size, nk),
         grid=(nk,),
         in_specs=[
-            pl.BlockSpec((q_rows, channels), whole),
+            pl.BlockSpec((width, own), whole),
+            pl.BlockSpec((width, own), whole),
             pl.BlockSpec((tk, channels), lambda j: (j, 0)),
+            pl.BlockSpec((channels, width), lambda j: (0, 1)),
             pl.BlockSpec((width, channels), whole),
-            pl.BlockSpec((channels, width), whole),
-            pl.BlockSpec((width, channels), whole),
-            pl.BlockSpec((width, 1), whole),
         ],
         out_specs=[
             pl.BlockSpec((width, q_rows), whole),
@@ -130,7 +123,7 @@
             transcendentals=q_rows * k_rows * heads,
             bytes_accessed=k_rows * channels * 2 + q_rows * width * 8,
         ),
-    )(hidden_q, hidden_kv, wqt, wk, wvt, scale_col)
+    )(qt_own, qt_other, hidden_kv, qkv_weight, wvt)
 
 
 def finish_kernel(heads, head_size, o_ref, st_ref, og_ref, sg_ref, hid_ref, wo_ref, out_ref):
@@ -173,7 +166,8 @@
     )(o_part, st_part, o_got, st_got, hidden, out_weight)
 
 
-def ring_gather_kernel(side, x_ref, out_ref, send_sem, recv_sem, local_sem):
+def ring_gather_kernel(side, heads, head_size, x_ref, h_ref, wq_ref, wv_ref, scale_ref,
+                       out_ref, qt_ref, wvt_ref, send_sem, recv_sem, local_sem):
     me = lax.axis_index("zx")
     z, x = me // side, me % side
     half = x_ref.shape[1]
@@ -221,6 +215,16 @@
         a0, b0 = own[st]
         send((st, 1, 1), x_ref.at[st], part(st, a0, b0), slot(st, a0 + 1, b0))
         send((st, 1, -1), x_ref.at[st], part(st, a0, b0), slot(st, a0 - 1, b0))
+    proj = jnp.dot(h_ref[...], wq_ref[...], preferred_element_type=jnp.float32)
+    scale = scale_ref[...]
+    normed = []
+    for h in range(heads):
+        cols = slice(h * head_size, (h + 1) * head_size)
+        part_q = proj[:, cols]
+        mean_sq = jnp.mean(part_q * part_q, axis=1, keepdims=True)
+        normed.append(part_q * lax.rsqrt(mean_sq + 1e-06) * scale[:, cols])
+    qt_ref[...] = jnp.concatenate(normed, axis=1).T.astype(qt_ref.dtype)
+    wvt_ref[...] = wv_ref[...].astype(jnp.float32).T.astype(wvt_ref.dtype)
     for st in range(2):
         a0, b0 = own[st]
         recv((st, 1, 1), part(st, a0 - 1, b0), slot(st, a0 - 1, b0))
@@ -252,24 +256,42 @@
         copy.wait_send()
 
 
-def gather_rows(block, axis):
+def gather_rows(block, qkv_weight, scale_row, heads, head_size, axis):
     n = lax.axis_size(axis)
     side = math.isqrt(n)
     rows, width = block.shape
+    channels, width_qkv = qkv_weight.shape
+    width_all = width_qkv // 3
     copies = 2 * (2 + 2 + 4 * side)
-    out = pl.pallas_call(
-        functools.partial(ring_gather_kernel, side),
-        in_specs=[pl.BlockSpec(memory_space=pl.ANY)],
-        out_specs=pl.BlockSpec(memory_space=pl.ANY),
-        out_shape=jax.ShapeDtypeStruct((n, 2, rows // 2, width), block.dtype),
+    whole = lambda i: (0, 0)
+    out, qt, wvt = pl.pallas_call(
+        functools.partial(ring_gather_kernel, side, heads, head_size),
+        grid=(1,),
+        in_specs=[
+            pl.BlockSpec(memory_space=pl.ANY),
+            pl.BlockSpec((rows, width), whole),
+            pl.BlockSpec((channels, width_all), lambda i: (0, 0)),
+            pl.BlockSpec((channels, width_all), lambda i: (0, 2)),
+            pl.BlockSpec((1, width_all), whole),
+        ],
+        out_specs=[
+            pl.BlockSpec(memory_space=pl.ANY),
+            pl.BlockSpec((width_all, rows), whole),
+            pl.BlockSpec((width_all, channels), whole),
+        ],
+        out_shape=[
+            jax.ShapeDtypeStruct((n, 2, rows // 2, width), block.dtype),
+            jax.ShapeDtypeStruct((width_all, rows), jnp.bfloat16),
+            jax.ShapeDtypeStruct((width_all, channels), jnp.bfloat16),
+        ],
         scratch_shapes=[
             pltpu.SemaphoreType.DMA((copies,)),
             pltpu.SemaphoreType.DMA((copies,)),
             pltpu.SemaphoreType.DMA,
         ],
         compiler_params=pltpu.CompilerParams(collective_id=0, has_side_effects=True),
-    )(block.reshape(2, rows // 2, width))
-    return out.reshape(n * rows, width)
+    )(block.reshape(2, rows // 2, width), block, qkv_weight, qkv_weight, scale_row)
+    return out.reshape(n * rows, width), qt, wvt
 
 
 def body(sequence_input, conv_first, conv_second, qkv_weight, out_weight, logit_scale):
@@ -282,16 +304,12 @@
     head_count = logit_scale.shape[0]
     width_all = qkv_weight.shape[1] // 3
     head_size = width_all // head_count
-    scale_col = jnp.repeat(logit_scale / math.sqrt(head_size), head_size)[:, None]
-    wqt = qkv_weight[:, :width_all].T
-    wk = qkv_weight[:, width_all : 2 * width_all]
-    wvt = qkv_weight[:, 2 * width_all :].T
+    scale_row = jnp.repeat(logit_scale / math.sqrt(head_size), head_size)[None, :]
 
     swap = [(0, 1), (1, 0)]
-    hidden_all = gather_rows(hidden, "zx")
-    hidden_other = lax.ppermute(hidden, "core", swap)
-    hidden_q = jnp.concatenate([hidden, hidden_other], axis=0)
-    o_part, st_part = attend_partial(hidden_q, hidden_all, wqt, wk, wvt, scale_col, head_count, head_size)
+    hidden_all, qt_own, wvt = gather_rows(hidden, qkv_weight, scale_row, head_count, head_size, "zx")
+    qt_other = lax.ppermute(qt_own, "core", swap)
+    o_part, st_part = attend_partial(qt_own, qt_other, hidden_all, qkv_weight, wvt, head_count, head_size)
     o_got, st_got = lax.ppermute((o_part[:, row_count:], st_part[:, row_count:]), "core", swap)
     return finish(o_part, st_part, o_got, st_got, hidden, out_weight, head_count, head_size)
 

time: 124 us -> 120 us (0.968)
  Pallas kernels: 75.4 us -> 80.2 us
  matrix products: 15.5 us -> 11.3 us
  local copies, waits for them, and re-layouts: 10 us -> 6.98 us
    pallas_call x1, Pallas kernels: 44.3 us -> 50.1 us  [gather_rows(): pl.pallas_call(functools.partial(ring_gather_kernel, side, heads, head_si...]
    ppermute x2, starting transfers between devices: 4.65 us -> 0.59 us  [body(): lax.ppermute((o_part[:, row_count:], st_part[:, row_count:]), 'core', swap)]
    slice x1 -> x0, local copies, waits for them, and re-layouts: 2.74 us -> none  [body(): wvt = qkv_weight[:, 2 * width_all:].T]
    ppermute x1, starting transfers between devices: 0.09 us -> 2.8 us  [body(): qt_other = lax.ppermute(qt_own, 'core', swap)]
    dot_general x8, matrix products: 12.2 us -> 9.74 us  [convolve(): jnp.dot(padded[offset:offset + row_count], weight[offset], preferred_elem...]
    concatenate x1 -> x0, other arithmetic: 1.97 us -> none  [body(): hidden_q = jnp.concatenate([hidden, hidden_other], axis=0)]
    dot_general x2, matrix products: 3.26 us -> 1.52 us  [convolve(): jnp.dot(padded[0:row_count], weight[0], preferred_element_type=jnp.float32)]
    ppermute x1, waiting for transfers between devices: 0.01 us -> 1.37 us  [body(): qt_other = lax.ppermute(qt_own, 'core', swap)]
  transfers between devices with their start and end apart: 7 -> 7, of which waited for: 3 -> 3; matrix products, arithmetic and copies ran while one was open for 12% -> 8% of each run, Pallas kernels for 36% -> 0%
where the time goes in v9:
time: 120 us
  Pallas kernels  80.2 us (67%)
  starting transfers between devices  15.4 us (13%)
  matrix products  11.3 us (9%)
  local copies, waits for them, and re-layouts  6.98 us (6%)
  waiting for transfers between devices  4.89 us (4%)
    pallas_call x1, Pallas kernels, gather_rows(): pl.pallas_call(functools.partial(ring_gather_kernel, side, heads, head_si...  50.1 us
    pallas_call x1, Pallas kernels, attend_partial(): pl.pallas_call(functools.partial(attend_kernel, heads, head_size, nk), gr...  27.3 us
    dot_general x8, matrix products, convolve(): jnp.dot(padded[offset:offset + row_count], weight[offset], preferred_elem...  9.74 us
    ppermute x2, starting transfers between devices, padded_2(): lax.ppermute(lax.slice_in_dim(block, block.shape[0] - width, None, axis=0...  8.15 us
    ppermute x2, starting transfers between devices, padded_2(): lax.ppermute(lax.slice_in_dim(block, 0, width, axis=0), SEQ_AXES, backward)  3.84 us
    unnamed x15, local copies, waits for them, and re-layouts  3.77 us
    pallas_call x1, Pallas kernels, finish(): pl.pallas_call(functools.partial(finish_kernel, heads, head_size), grid=(...  2.82 us
    ppermute x1, starting transfers between devices, body(): qt_other = lax.ppermute(qt_own, 'core', swap)  2.8 us
  transfers between devices with their start and end apart: 7, of which 3 were waited for; matrix products, arithmetic and copies ran while one was open for 8% of the time, Pallas kernels for 0%

profile of v9, /device:TPU:1, one launch (start us, length us, event | category | flops | bytes accessed | tf_op | source)
XLA Modules:
  0.0 119.9 jit_solution(11868211834056360531)
XLA Ops:
  0.0 0.8 fusion.77
  0.8 4.5 %collective-permute-start = (bf16[2,1536]{1,0:T(2,128)(2,1)S(1)}, bf16[2,1536]{1,0:T(2,128)(2,1)S(1)}, u32[]{:S(2)}, u32[]{:S(2)}) collective-permute-start(bf16[2,1536]{1,0:T(2,128)(2,1)S(1)} %get-tuple-element.15), channel_id=1, source_target_pairs={{0,4},{4,8},{8,12},{12,16},{16,20},{20,24},{24,28},{28,32},{32,36}... | collective-permute-start | bytes 18440 | tf_op jit(solution)/shard_map/ppermute | solution.py:20
  5.3 1.9 %collective-permute-start.1 = (bf16[2,1536]{1,0:T(2,128)(2,1)S(1)}, bf16[2,1536]{1,0:T(2,128)(2,1)S(1)}, u32[]{:S(2)}, u32[]{:S(2)}) collective-permute-start(bf16[2,1536]{1,0:T(2,128)(2,1)S(1)} %get-tuple-element.16), channel_id=1, source_target_pairs={{4,0},{8,4},{12,8},{16,12},{20,16},{24,20},{28,24},{32,28},{36,32}... | collective-permute-start | bytes 18440 | tf_op jit(solution)/shard_map/ppermute | solution.py:21
  7.2 0.0 copy-start.3
  7.2 1.3 %constant_dynamic-update-slice_fusion.1 = bf16[258,1536]{1,0:T(8,128)(2,1)S(1)} fusion(bf16[256,1536]{1,0:T(8,128)(2,1)} %param.6), kind=kLoop, calls=%fused_computation.65 | loop fusion | bytes 1572864
  8.6 2.9 %fusion.4 = f32[256,768]{1,0:T(8,128)S(1)} fusion(bf16[256,1536]{1,0:T(8,128)(2,1)} %param.6, bf16[5,1536,768]{2,1,0:T(8,128)(2,1)} %param.7), kind=kOutput, calls=%fused_computation.4 | convolution fusion | flops 603979776 | bytes 3932160 | tf_op jit(solution)/shard_map/dot_general | solution.py:28
  11.5 0.9 broadcast_multiply_fusion
  12.4 0.0 collective-permute-done.1
  12.4 2.5 %fusion = f32[256,768]{1,0:T(8,128)S(1)} fusion(bf16[5,1536,768]{2,1,0:T(8,128)(2,1)} %param.7, bf16[258,1536]{1,0:T(8,128)(2,1)S(1)} %constant_dynamic-update-slice_fusion), kind=kOutput, calls=%fused_computation | convolution fusion | flops 603979776 | bytes 3932160 | tf_op jit(solution)/shard_map/dot_general | solution.py:28
  14.9 0.0 copy-done.3
  14.9 0.0 copy-start
  14.9 0.8 fusion.2
  15.7 0.0 collective-permute-done
  15.7 0.3 copy-done
  16.0 0.0 slice-start
  16.0 0.8 fusion.6
  16.9 0.0 slice-start.1
  16.9 1.0 fusion.57
  17.9 3.6 %collective-permute-start.2 = (bf16[2,768]{1,0:T(2,128)(2,1)S(1)}, bf16[2,768]{1,0:T(2,128)(2,1)S(1)}, u32[]{:S(2)}, u32[]{:S(2)}) collective-permute-start(bf16[2,768]{1,0:T(2,128)(2,1)S(1)} %get-tuple-element.17), channel_id=1, source_target_pairs={{0,4},{4,8},{8,12},{12,16},{16,20},{20,24},{24,28},{28,32},{32,36}... | collective-permute-start | bytes 9224 | tf_op jit(solution)/shard_map/ppermute | solution.py:20
  21.6 1.9 %collective-permute-start.3 = (bf16[2,768]{1,0:T(2,128)(2,1)S(1)}, bf16[2,768]{1,0:T(2,128)(2,1)S(1)}, u32[]{:S(2)}, u32[]{:S(2)}) collective-permute-start(bf16[2,768]{1,0:T(2,128)(2,1)S(1)} %get-tuple-element.18), channel_id=1, source_target_pairs={{4,0},{8,4},{12,8},{16,12},{20,16},{24,20},{28,24},{32,28},{36,32}... | collective-permute-start | bytes 9224 | tf_op jit(solution)/shard_map/ppermute | solution.py:21
  23.5 0.0 slice-done
  23.5 0.0 slice-done.1
  23.5 0.5 fusion.34
  24.0 2.5 %collective-permute-done.3 = bf16[2,768]{1,0:T(2,128)(2,1)S(1)} collective-permute-done((bf16[2,768]{1,0:T(2,128)(2,1)S(1)}, bf16[2,768]{1,0:T(2,128)(2,1)S(1)}, u32[]{:S(2)}, u32[]{:S(2)}) %collective-permute-start.3) | collective-permute-done | bytes 3104 | tf_op jit(solution)/shard_map/ppermute | solution.py:21
  26.5 0.5 fusion.31
  27.0 0.0 collective-permute-done.2
  27.0 0.5 fusion.36
  27.5 0.5 fusion.23
  28.0 1.3 %fusion.30.h_ref.hid_ref = bf16[256,768]{1,0:T(8,128)(2,1)} fusion(f32[256,768]{1,0:T(8,128)S(1)} %fusion.31, f32[256,768]{1,0:T(8,128)S(1)} %fusion.23, bf16[5,768,768]{2,1,0:T(8,128)(2,1)S(1)} %bitcast.49, bf16[256,768]{1,0:T(8,128)(2,1)S(1)} %fusion.57, bf16[2,768]{1,0:T(2,128)(2,1)S(1)} %collective-permute-done.3), kind=kOutput, calls=%fused_computation.24 | convolution fusion | flops 303759360 | bytes 3935232 | tf_op jit(solution)/shard_map/dot_general | solution.py:28
  29.3 0.6 broadcast_in_dim.3
  30.0 50.1 %shard_map.64 = (bf16[16,2,128,768]{3,2,1,0:T(8,128)(2,1)}, bf16[512,256]{1,0:T(8,128)(2,1)}, bf16[512,768]{1,0:T(8,128)(2,1)}) custom-call(bf16[2,128,768]{2,1,0:T(8,128)(2,1)} %bitcast.47, bf16[256,768]{1,0:T(8,128)(2,1)} %fusion.30.h_ref.hid_ref, bf16[768,1536]{1,0:T(8,128)(2,1)} %wk_ref.1, bf16[768,1536]{1,0:T(8,128)(2,1)} %wk_ref.1, f32[1,512]{1,0:T(1,128)} %bitcast.50), custom_call_target="tpu_custom_call" | custom-call | tf_op jit(solution)/shard_map/pallas_call | solution.py:267
  80.1 2.8 %collective-permute-start.4 = (bf16[512,256]{1,0:T(8,128)(2,1)}, bf16[512,256]{1,0:T(8,128)(2,1)S(1)}, u32[]{:S(2)}, u32[]{:S(2)}) collective-permute-start(bf16[512,256]{1,0:T(8,128)(2,1)} %get-tuple-element.10.qa_ref), channel_id=1, source_target_pairs={{0,4},{4,0},{1,5},{5,1},{2,6},{6,2},{3,7},{7,3},{8,12},{12,8},{9,1... | collective-permute-start | bytes 786440 | tf_op jit(solution)/shard_map/ppermute | solution.py:311
  82.9 1.4 %collective-permute-done.4.qb_ref = bf16[512,256]{1,0:T(8,128)(2,1)S(1)} collective-permute-done((bf16[512,256]{1,0:T(8,128)(2,1)}, bf16[512,256]{1,0:T(8,128)(2,1)S(1)}, u32[]{:S(2)}, u32[]{:S(2)}) %collective-permute-start.4) | collective-permute-done | bytes 262176 | tf_op jit(solution)/shard_map/ppermute | solution.py:311
  84.3 0.0 copy-start.4
  84.3 0.7 copy-done.4
  85.0 27.3 %shard_map.65 = (f32[512,512]{1,0:T(8,128)}, f32[8,512]{1,0:T(8,128)}) custom-call(bf16[512,256]{1,0:T(8,128)(2,1)} %get-tuple-element.10.qa_ref, bf16[512,256]{1,0:T(8,128)(2,1)} %copy-done.4, bf16[4096,768]{1,0:T(8,128)(2,1)} %bitcast.51, bf16[768,1536]{1,0:T(8,128)(2,1)} %wk_ref.1, bf16[512,768]{1,0:T(8,128)(2,1)} %get-tuple-element.12.wvt_ref), custom_call_target="tpu_custom_call" | custom-call | flops 10737418240 | bytes 8388608 | tf_op jit(solution)/shard_map/pallas_call | solution.py:96
  112.2 1.1 slice.102
  113.3 0.5 collective-permute-start.5
  113.8 0.7 slice.103
  114.5 0.1 collective-permute-start.6
  114.6 1.0 collective-permute-done.6.sg_ref
  115.6 0.0 copy-start.2
  115.6 0.0 collective-permute-done.5.og_ref
  115.6 0.6 copy-done.2
  116.2 0.0 copy-start.1
  116.2 0.8 copy-done.1
  117.0 2.8 %shard_map.66 = bf16[256,768]{1,0:T(8,128)(2,1)} custom-call(f32[512,512]{1,0:T(8,128)} %get-tuple-element.13.o_ref, f32[8,512]{1,0:T(8,128)} %get-tuple-element.14.st_ref, f32[512,256]{1,0:T(8,128)} %copy-done.1, f32[8,256]{1,0:T(8,128)} %copy-done.2, bf16[256,768]{1,0:T(8,128)(2,1)} %fusion.30.h_ref.hid_ref, bf16[512,768]{1,0:T(8,128)(2,1)} %wo_ref.1), custom_call_target="tpu_custom_call" | custom-call | tf_op jit(solution)/shard_map/pallas_call | solution.py:153
  (3 shorter events, 0.0 us)
Async XLA Ops:
  0.8 14.9 %collective-permute-start = (bf16[2,1536]{1,0:T(2,128)(2,1)S(1)}, bf16[2,1536]{1,0:T(2,128)(2,1)S(1)}, u32[]{:S(2)}, u32[]{:S(2)}) collective-permute-start(bf16[2,1536]{1,0:T(2,128)(2,1)S(1)} %get-tuple-element.15), channel_id=1, source_target_pairs={{0,4},{4,8},{8,12},{12,16},{16,20},{20,24},{24,28},{28,32},{32,36}... | collective-permute-start | bytes 18440 | tf_op jit(solution)/shard_map/ppermute | solution.py:20
  5.3 7.1 %collective-permute-start.1 = (bf16[2,1536]{1,0:T(2,128)(2,1)S(1)}, bf16[2,1536]{1,0:T(2,128)(2,1)S(1)}, u32[]{:S(2)}, u32[]{:S(2)}) collective-permute-start(bf16[2,1536]{1,0:T(2,128)(2,1)S(1)} %get-tuple-element.16), channel_id=1, source_target_pairs={{4,0},{8,4},{12,8},{16,12},{20,16},{24,20},{28,24},{32,28},{36,32}... | collective-permute-start | bytes 18440 | tf_op jit(solution)/shard_map/ppermute | solution.py:21
  7.2 7.7 %copy-start.3 = (bf16[5,1536,768]{2,1,0:T(8,128)(2,1)S(1)}, bf16[5,1536,768]{2,1,0:T(8,128)(2,1)}, u32[]{:S(2)}) copy-start(bf16[5,1536,768]{2,1,0:T(8,128)(2,1)} %param.7) | copy-start | bytes 35389444
  14.9 1.1 copy-start
  16.0 7.4 %slice-start = ((s8[5898240]{0:T(1024)(128)(4,1)}), s8[4194304]{0:T(1024)(128)(4,1)S(1)}, s32[]{:S(2)}) async-start(s8[5898240]{0:T(1024)(128)(4,1)} %bitcast.48), calls=%async_computation | async-start | bytes 8388608
  16.9 6.6 %slice-start.1 = ((s8[5898240]{0:T(1024)(128)(4,1)}), s8[1703936]{0:T(1024)(128)(4,1)S(1)}, s32[]{:S(2)}) async-start(s8[5898240]{0:T(1024)(128)(4,1)} %bitcast.48), calls=%async_computation.1 | async-start | bytes 3407872
  17.9 9.1 %collective-permute-start.2 = (bf16[2,768]{1,0:T(2,128)(2,1)S(1)}, bf16[2,768]{1,0:T(2,128)(2,1)S(1)}, u32[]{:S(2)}, u32[]{:S(2)}) collective-permute-start(bf16[2,768]{1,0:T(2,128)(2,1)S(1)} %get-tuple-element.17), channel_id=1, source_target_pairs={{0,4},{4,8},{8,12},{12,16},{16,20},{20,24},{24,28},{28,32},{32,36}... | collective-permute-start | bytes 9224 | tf_op jit(solution)/shard_map/ppermute | solution.py:20
  21.6 4.9 %collective-permute-start.3 = (bf16[2,768]{1,0:T(2,128)(2,1)S(1)}, bf16[2,768]{1,0:T(2,128)(2,1)S(1)}, u32[]{:S(2)}, u32[]{:S(2)}) collective-permute-start(bf16[2,768]{1,0:T(2,128)(2,1)S(1)} %get-tuple-element.18), channel_id=1, source_target_pairs={{4,0},{8,4},{12,8},{16,12},{20,16},{24,20},{28,24},{32,28},{36,32}... | collective-permute-start | bytes 9224 | tf_op jit(solution)/shard_map/ppermute | solution.py:21
  80.1 4.2 %collective-permute-start.4 = (bf16[512,256]{1,0:T(8,128)(2,1)}, bf16[512,256]{1,0:T(8,128)(2,1)S(1)}, u32[]{:S(2)}, u32[]{:S(2)}) collective-permute-start(bf16[512,256]{1,0:T(8,128)(2,1)} %get-tuple-element.10.qa_ref), channel_id=1, source_target_pairs={{0,4},{4,0},{1,5},{5,1},{2,6},{6,2},{3,7},{7,3},{8,12},{12,8},{9,1... | collective-permute-start | bytes 786440 | tf_op jit(solution)/shard_map/ppermute | solution.py:311
  84.3 0.7 copy-start.4
  113.3 2.3 %collective-permute-start.5 = (f32[512,256]{1,0:T(8,128)S(1)}, f32[512,256]{1,0:T(8,128)S(1)}, u32[]{:S(2)}, u32[]{:S(2)}) collective-permute-start(f32[512,256]{1,0:T(8,128)S(1)} %slice.102), channel_id=1, source_target_pairs={{0,4},{4,0},{1,5},{5,1},{2,6},{6,2},{3,7},{7,3},{8,12},{12,8},{9,1... | collective-permute-start | bytes 1572872 | tf_op jit(solution)/shard_map/ppermute | solution.py:313
  114.5 1.2 collective-permute-start.6
  115.6 0.6 copy-start.2
  116.2 0.8 copy-start.1

commit v10 on v9

--- a/solution.py
+++ b/solution.py
@@ -45,7 +45,7 @@
 
 
 def attend_kernel(heads, head_size, nk, qa_ref, qb_ref, hkv_ref, wk_ref, wvt_ref,
-                  o_ref, st_ref, qt_sc, m_sc, l_sc, acc_sc):
+                  o_ref, st_ref, ob_ref, sb_ref, qt_sc, m_sc, l_sc, acc_sc):
     j = pl.program_id(0)
     contract_last = (((1,), (1,)), ((), ()))
 
@@ -81,10 +81,14 @@
 
     @pl.when(j == nk - 1)
     def _():
-        o_ref[...] = acc_sc[...]
+        own = o_ref.shape[1]
+        o_ref[...] = acc_sc[:, :own]
+        ob_ref[...] = acc_sc[:, own:]
         for h in range(heads):
-            st_ref[h : h + 1, :] = m_sc[h]
-            st_ref[heads + h : heads + h + 1, :] = l_sc[h]
+            st_ref[h : h + 1, :] = m_sc[h][:, :own]
+            st_ref[heads + h : heads + h + 1, :] = l_sc[h][:, :own]
+            sb_ref[h : h + 1, :] = m_sc[h][:, own:]
+            sb_ref[heads + h : heads + h + 1, :] = l_sc[h][:, own:]
 
 
 def attend_partial(qt_own, qt_other, hidden_kv, qkv_weight, wvt, heads, head_size, tk=512):
@@ -104,13 +108,13 @@
             pl.BlockSpec((width, channels), whole),
         ],
         out_specs=[
-            pl.BlockSpec((width, q_rows), whole),
-            pl.BlockSpec((2 * heads, q_rows), whole),
-        ],
+            pl.BlockSpec((width, own), whole),
+            pl.BlockSpec((2 * heads, own), whole),
+        ] * 2,
         out_shape=[
-            jax.ShapeDtypeStruct((width, q_rows), jnp.float32),
-            jax.ShapeDtypeStruct((2 * heads, q_rows), jnp.float32),
-        ],
+            jax.ShapeDtypeStruct((width, own), jnp.float32),
+            jax.ShapeDtypeStruct((2 * heads, own), jnp.float32),
+        ] * 2,
         scratch_shapes=[
             pltpu.VMEM((width, q_rows), jnp.bfloat16),
             pltpu.VMEM((heads, 1, q_rows), jnp.float32),
@@ -215,6 +219,27 @@
         a0, b0 = own[st]
         send((st, 1, 1), x_ref.at[st], part(st, a0, b0), slot(st, a0 + 1, b0))
         send((st, 1, -1), x_ref.at[st], part(st, a0, b0), slot(st, a0 - 1, b0))
+    for st in range(2):
+        a0, b0 = own[st]
+        recv((st, 1, 1), part(st, a0 - 1, b0), slot(st, a0 - 1, b0))
+        recv((st, 1, -1), part(st, a0 + 1, b0), slot(st, a0 + 1, b0))
+        send((st, 2, 1), part(st, a0 - 1, b0, 0), part(st, a0 - 1, b0, 0), slot(st, a0 + 1, b0))
+        send((st, 2, -1), part(st, a0 + 1, b0, q), part(st, a0 + 1, b0, q), slot(st, a0 - 1, b0))
+    for st in range(2):
+        a0, b0 = own[st]
+        recv((st, 2, 1), part(st, a0 - 2, b0, 0), slot(st, a0 - 1, b0))
+        recv((st, 2, -1), part(st, a0 + 2, b0, q), slot(st, a0 + 1, b0))
+        for k in range(side):
+            src = x_ref.at[st] if k == 0 else part(st, a0 + k, b0)
+            send((st, 3, 1, k), src, part(st, a0 + k, b0), slot(st, a0, b0 + 1))
+            send((st, 3, -1, k), src, part(st, a0 + k, b0), slot(st, a0, b0 - 1))
+    for st in range(2):
+        a0, b0 = own[st]
+        for k in range(side):
+            recv((st, 3, 1, k), part(st, a0 + k, b0 - 1), slot(st, a0, b0 - 1))
+            recv((st, 3, -1, k), part(st, a0 + k, b0 + 1), slot(st, a0, b0 + 1))
+            send((st, 4, 1, k), part(st, a0 + k, b0 - 1, 0), part(st, a0 + k, b0 - 1, 0), slot(st, a0, b0 + 1))
+            send((st, 4, -1, k), part(st, a0 + k, b0 + 1, q), part(st, a0 + k, b0 + 1, q), slot(st, a0, b0 - 1))
     proj = jnp.dot(h_ref[...], wq_ref[...], preferred_element_type=jnp.float32)
     scale = scale_ref[...]
     normed = []
@@ -225,27 +250,6 @@
         normed.append(part_q * lax.rsqrt(mean_sq + 1e-06) * scale[:, cols])
     qt_ref[...] = jnp.concatenate(normed, axis=1).T.astype(qt_ref.dtype)
     wvt_ref[...] = wv_ref[...].astype(jnp.float32).T.astype(wvt_ref.dtype)
-    for st in range(2):
-        a0, b0 = own[st]
-        recv((st, 1, 1), part(st, a0 - 1, b0), slot(st, a0 - 1, b0))
-        recv((st, 1, -1), part(st, a0 + 1, b0), slot(st, a0 + 1, b0))
-        send((st, 2, 1), part(st, a0 - 1, b0, 0), part(st, a0 - 1, b0, 0), slot(st, a0 + 1, b0))
-        send((st, 2, -1), part(st, a0 + 1, b0, q), part(st, a0 + 1, b0, q), slot(st, a0 - 1, b0))
-    for st in range(2):
-        a0, b0 = own[st]
-        recv((st, 2, 1), part(st, a0 - 2, b0, 0), slot(st, a0 - 1, b0))
-        recv((st, 2, -1), part(st, a0 + 2, b0, q), slot(st, a0 + 1, b0))
-        for k in range(side):
-            src = x_ref.at[st] if k == 0 else part(st, a0 + k, b0)
-            send((st, 3, 1, k), src, part(st, a0 + k, b0), slot(st, a0, b0 + 1))
-            send((st, 3, -1, k), src, part(st, a0 + k, b0), slot(st, a0, b0 - 1))
-    for st in range(2):
-        a0, b0 = own[st]
-        for k in range(side):
-            recv((st, 3, 1, k), part(st, a0 + k, b0 - 1), slot(st, a0, b0 - 1))
-            recv((st, 3, -1, k), part(st, a0 + k, b0 + 1), slot(st, a0, b0 + 1))
-            send((st, 4, 1, k), part(st, a0 + k, b0 - 1, 0), part(st, a0 + k, b0 - 1, 0), slot(st, a0, b0 + 1))
-            send((st, 4, -1, k), part(st, a0 + k, b0 + 1, q), part(st, a0 + k, b0 + 1, q), slot(st, a0, b0 - 1))
     for st in range(2):
         a0, b0 = own[st]
         for k in range(side):
@@ -309,8 +313,10 @@
     swap = [(0, 1), (1, 0)]
     hidden_all, qt_own, wvt = gather_rows(hidden, qkv_weight, scale_row, head_count, head_size, "zx")
     qt_other = lax.ppermute(qt_own, "core", swap)
-    o_part, st_part = attend_partial(qt_own, qt_other, hidden_all, qkv_weight, wvt, head_count, head_size)
-    o_got, st_got = lax.ppermute((o_part[:, row_count:], st_part[:, row_count:]), "core", swap)
+    o_part, st_part, o_send, st_send = attend_partial(
+        qt_own, qt_other, hidden_all, qkv_weight, wvt, head_count, head_size
+    )
+    o_got, st_got = lax.ppermute((o_send, st_send), "core", swap)
     return finish(o_part, st_part, o_got, st_got, hidden, out_weight, head_count, head_size)
 
 

time: 120 us -> 118 us (0.983)
  local copies, waits for them, and re-layouts: 6.98 us -> 4.62 us
    slice x2 -> x0, local copies, waits for them, and re-layouts: 1.77 us -> none  [the longest x1 1.08 us: body(): o_part[:, row_count:]]
where the time goes in v10:
time: 118 us
  Pallas kernels  80.2 us (68%)
  starting transfers between devices  15.3 us (13%)
  matrix products  11.3 us (10%)
  waiting for transfers between devices  5.49 us (5%)
  local copies, waits for them, and re-layouts  4.62 us (4%)
    pallas_call x1, Pallas kernels, gather_rows(): pl.pallas_call(functools.partial(ring_gather_kernel, side, heads, head_si...  50.1 us
    pallas_call x1, Pallas kernels, attend_partial(): pl.pallas_call(functools.partial(attend_kernel, heads, head_size, nk), gr...  27.3 us
    dot_general x8, matrix products, convolve(): jnp.dot(padded[offset:offset + row_count], weight[offset], preferred_elem...  9.74 us
    ppermute x2, starting transfers between devices, padded_2(): lax.ppermute(lax.slice_in_dim(block, block.shape[0] - width, None, axis=0...  8.15 us
    ppermute x2, starting transfers between devices, padded_2(): lax.ppermute(lax.slice_in_dim(block, 0, width, axis=0), SEQ_AXES, backward)  3.84 us
    unnamed x15, local copies, waits for them, and re-layouts  3.18 us
    pallas_call x1, Pallas kernels, finish(): pl.pallas_call(functools.partial(finish_kernel, heads, head_size), grid=(...  2.81 us
    ppermute x1, starting transfers between devices, body(): qt_other = lax.ppermute(qt_own, 'core', swap)  2.8 us
  transfers between devices with their start and end apart: 7, of which 3 were waited for; matrix products, arithmetic and copies ran while one was open for 8% of the time, Pallas kernels for 0%

profile of v10, /device:TPU:1, one launch (start us, length us, event | category | flops | bytes accessed | tf_op | source)
XLA Modules:
  0.0 118.0 jit_solution(15269288056429708848)
XLA Ops:
  0.0 0.8 fusion.77
  0.8 4.5 %collective-permute-start = (bf16[2,1536]{1,0:T(2,128)(2,1)S(1)}, bf16[2,1536]{1,0:T(2,128)(2,1)S(1)}, u32[]{:S(2)}, u32[]{:S(2)}) collective-permute-start(bf16[2,1536]{1,0:T(2,128)(2,1)S(1)} %get-tuple-element.19), channel_id=1, source_target_pairs={{0,4},{4,8},{8,12},{12,16},{16,20},{20,24},{24,28},{28,32},{32,36}... | collective-permute-start | bytes 18440 | tf_op jit(solution)/shard_map/ppermute | solution.py:20
  5.3 1.9 %collective-permute-start.1 = (bf16[2,1536]{1,0:T(2,128)(2,1)S(1)}, bf16[2,1536]{1,0:T(2,128)(2,1)S(1)}, u32[]{:S(2)}, u32[]{:S(2)}) collective-permute-start(bf16[2,1536]{1,0:T(2,128)(2,1)S(1)} %get-tuple-element.20), channel_id=1, source_target_pairs={{4,0},{8,4},{12,8},{16,12},{20,16},{24,20},{28,24},{32,28},{36,32}... | collective-permute-start | bytes 18440 | tf_op jit(solution)/shard_map/ppermute | solution.py:21
  7.2 0.0 copy-start.3
  7.2 1.3 %constant_dynamic-update-slice_fusion.1 = bf16[258,1536]{1,0:T(8,128)(2,1)S(1)} fusion(bf16[256,1536]{1,0:T(8,128)(2,1)} %param.6), kind=kLoop, calls=%fused_computation.65 | loop fusion | bytes 1572864
  8.6 2.9 %fusion.4 = f32[256,768]{1,0:T(8,128)S(1)} fusion(bf16[256,1536]{1,0:T(8,128)(2,1)} %param.6, bf16[5,1536,768]{2,1,0:T(8,128)(2,1)} %param.7), kind=kOutput, calls=%fused_computation.4 | convolution fusion | flops 603979776 | bytes 3932160 | tf_op jit(solution)/shard_map/dot_general | solution.py:28
  11.5 0.9 broadcast_multiply_fusion
  12.4 0.0 collective-permute-done.1
  12.4 2.5 %fusion = f32[256,768]{1,0:T(8,128)S(1)} fusion(bf16[5,1536,768]{2,1,0:T(8,128)(2,1)} %param.7, bf16[258,1536]{1,0:T(8,128)(2,1)S(1)} %constant_dynamic-update-slice_fusion), kind=kOutput, calls=%fused_computation | convolution fusion | flops 603979776 | bytes 3932160 | tf_op jit(solution)/shard_map/dot_general | solution.py:28
  14.9 0.0 copy-done.3
  14.9 0.0 copy-start
  14.9 0.8 fusion.2
  15.7 0.0 collective-permute-done
  15.7 0.3 copy-done
  16.0 0.0 slice-start
  16.0 0.8 fusion.6
  16.9 0.0 slice-start.1
  16.9 1.0 fusion.57
  17.9 3.6 %collective-permute-start.2 = (bf16[2,768]{1,0:T(2,128)(2,1)S(1)}, bf16[2,768]{1,0:T(2,128)(2,1)S(1)}, u32[]{:S(2)}, u32[]{:S(2)}) collective-permute-start(bf16[2,768]{1,0:T(2,128)(2,1)S(1)} %get-tuple-element.21), channel_id=1, source_target_pairs={{0,4},{4,8},{8,12},{12,16},{16,20},{20,24},{24,28},{28,32},{32,36}... | collective-permute-start | bytes 9224 | tf_op jit(solution)/shard_map/ppermute | solution.py:20
  21.6 1.9 %collective-permute-start.3 = (bf16[2,768]{1,0:T(2,128)(2,1)S(1)}, bf16[2,768]{1,0:T(2,128)(2,1)S(1)}, u32[]{:S(2)}, u32[]{:S(2)}) collective-permute-start(bf16[2,768]{1,0:T(2,128)(2,1)S(1)} %get-tuple-element.22), channel_id=1, source_target_pairs={{4,0},{8,4},{12,8},{16,12},{20,16},{24,20},{28,24},{32,28},{36,32}... | collective-permute-start | bytes 9224 | tf_op jit(solution)/shard_map/ppermute | solution.py:21
  23.5 0.0 slice-done
  23.5 0.0 slice-done.1
  23.5 0.5 fusion.34
  24.0 2.5 %collective-permute-done.3 = bf16[2,768]{1,0:T(2,128)(2,1)S(1)} collective-permute-done((bf16[2,768]{1,0:T(2,128)(2,1)S(1)}, bf16[2,768]{1,0:T(2,128)(2,1)S(1)}, u32[]{:S(2)}, u32[]{:S(2)}) %collective-permute-start.3) | collective-permute-done | bytes 3104 | tf_op jit(solution)/shard_map/ppermute | solution.py:21
  26.5 0.5 fusion.31
  27.0 0.0 collective-permute-done.2
  27.0 0.5 fusion.36
  27.5 0.5 fusion.23
  28.0 1.3 %fusion.30.h_ref.hid_ref = bf16[256,768]{1,0:T(8,128)(2,1)} fusion(f32[256,768]{1,0:T(8,128)S(1)} %fusion.31, f32[256,768]{1,0:T(8,128)S(1)} %fusion.23, bf16[5,768,768]{2,1,0:T(8,128)(2,1)S(1)} %bitcast.49, bf16[256,768]{1,0:T(8,128)(2,1)S(1)} %fusion.57, bf16[2,768]{1,0:T(2,128)(2,1)S(1)} %collective-permute-done.3), kind=kOutput, calls=%fused_computation.24 | convolution fusion | flops 303759360 | bytes 3935232 | tf_op jit(solution)/shard_map/dot_general | solution.py:28
  29.3 0.6 broadcast_in_dim.3
  30.0 50.1 %shard_map.64 = (bf16[16,2,128,768]{3,2,1,0:T(8,128)(2,1)}, bf16[512,256]{1,0:T(8,128)(2,1)}, bf16[512,768]{1,0:T(8,128)(2,1)}) custom-call(bf16[2,128,768]{2,1,0:T(8,128)(2,1)} %bitcast.47, bf16[256,768]{1,0:T(8,128)(2,1)} %fusion.30.h_ref.hid_ref, bf16[768,1536]{1,0:T(8,128)(2,1)} %wk_ref.1, bf16[768,1536]{1,0:T(8,128)(2,1)} %wk_ref.1, f32[1,512]{1,0:T(1,128)} %bitcast.50), custom_call_target="tpu_custom_call" | custom-call | tf_op jit(solution)/shard_map/pallas_call | solution.py:271
  80.1 2.8 %collective-permute-start.4 = (bf16[512,256]{1,0:T(8,128)(2,1)}, bf16[512,256]{1,0:T(8,128)(2,1)S(1)}, u32[]{:S(2)}, u32[]{:S(2)}) collective-permute-start(bf16[512,256]{1,0:T(8,128)(2,1)} %get-tuple-element.12.qa_ref), channel_id=1, source_target_pairs={{0,4},{4,0},{1,5},{5,1},{2,6},{6,2},{3,7},{7,3},{8,12},{12,8},{9,1... | collective-permute-start | bytes 786440 | tf_op jit(solution)/shard_map/ppermute | solution.py:315
  82.9 1.4 %collective-permute-done.4.qb_ref = bf16[512,256]{1,0:T(8,128)(2,1)S(1)} collective-permute-done((bf16[512,256]{1,0:T(8,128)(2,1)}, bf16[512,256]{1,0:T(8,128)(2,1)S(1)}, u32[]{:S(2)}, u32[]{:S(2)}) %collective-permute-start.4) | collective-permute-done | bytes 262176 | tf_op jit(solution)/shard_map/ppermute | solution.py:315
  84.3 0.0 copy-start.4
  84.3 0.7 copy-done.4
  85.0 27.3 %shard_map.65 = (f32[512,256]{1,0:T(8,128)}, f32[8,256]{1,0:T(8,128)}, f32[512,256]{1,0:T(8,128)}, f32[8,256]{1,0:T(8,128)}) custom-call(bf16[512,256]{1,0:T(8,128)(2,1)} %get-tuple-element.12.qa_ref, bf16[512,256]{1,0:T(8,128)(2,1)} %copy-done.4, bf16[4096,768]{1,0:T(8,128)(2,1)} %bitcast.51, bf16[768,1536]{1,0:T(8,128)(2,1)} %wk_ref.1, ...), custom_call_target="tpu_custom_call" | custom-call | flops 10737418240 | bytes 8388608 | tf_op jit(solution)/shard_map/pallas_call | solution.py:100
  112.3 0.4 collective-permute-start.5
  112.7 0.1 collective-permute-start.6
  112.8 1.6 %collective-permute-done.6.sg_ref = f32[8,256]{1,0:T(8,128)S(1)} collective-permute-done((f32[8,256]{1,0:T(8,128)}, f32[8,256]{1,0:T(8,128)S(1)}, u32[]{:S(2)}, u32[]{:S(2)}) %collective-permute-start.6) | collective-permute-done | bytes 8224 | tf_op jit(solution)/shard_map/ppermute | solution.py:319
  114.4 0.0 copy-start.2
  114.4 0.0 collective-permute-done.5.og_ref
  114.4 0.0 copy-start.1
  114.4 0.6 copy-done.2
  115.0 0.2 copy-done.1
  115.2 2.8 %shard_map.66 = bf16[256,768]{1,0:T(8,128)(2,1)} custom-call(f32[512,256]{1,0:T(8,128)} %get-tuple-element.15.o_ref, f32[8,256]{1,0:T(8,128)} %get-tuple-element.16.st_ref, f32[512,256]{1,0:T(8,128)} %copy-done.1, f32[8,256]{1,0:T(8,128)} %copy-done.2, bf16[256,768]{1,0:T(8,128)(2,1)} %fusion.30.h_ref.hid_ref, bf16[512,768]{1,0:T(8,128)(2,1)} %wo_ref.1), custom_call_target="tpu_custom_call" | custom-call | tf_op jit(solution)/shard_map/pallas_call | solution.py:157
  (3 shorter events, 0.0 us)
Async XLA Ops:
  0.8 14.9 %collective-permute-start = (bf16[2,1536]{1,0:T(2,128)(2,1)S(1)}, bf16[2,1536]{1,0:T(2,128)(2,1)S(1)}, u32[]{:S(2)}, u32[]{:S(2)}) collective-permute-start(bf16[2,1536]{1,0:T(2,128)(2,1)S(1)} %get-tuple-element.19), channel_id=1, source_target_pairs={{0,4},{4,8},{8,12},{12,16},{16,20},{20,24},{24,28},{28,32},{32,36}... | collective-permute-start | bytes 18440 | tf_op jit(solution)/shard_map/ppermute | solution.py:20
  5.3 7.1 %collective-permute-start.1 = (bf16[2,1536]{1,0:T(2,128)(2,1)S(1)}, bf16[2,1536]{1,0:T(2,128)(2,1)S(1)}, u32[]{:S(2)}, u32[]{:S(2)}) collective-permute-start(bf16[2,1536]{1,0:T(2,128)(2,1)S(1)} %get-tuple-element.20), channel_id=1, source_target_pairs={{4,0},{8,4},{12,8},{16,12},{20,16},{24,20},{28,24},{32,28},{36,32}... | collective-permute-start | bytes 18440 | tf_op jit(solution)/shard_map/ppermute | solution.py:21
  7.2 7.7 %copy-start.3 = (bf16[5,1536,768]{2,1,0:T(8,128)(2,1)S(1)}, bf16[5,1536,768]{2,1,0:T(8,128)(2,1)}, u32[]{:S(2)}) copy-start(bf16[5,1536,768]{2,1,0:T(8,128)(2,1)} %param.7) | copy-start | bytes 35389444
  14.9 1.1 copy-start
  16.0 7.4 %slice-start = ((s8[5898240]{0:T(1024)(128)(4,1)}), s8[4194304]{0:T(1024)(128)(4,1)S(1)}, s32[]{:S(2)}) async-start(s8[5898240]{0:T(1024)(128)(4,1)} %bitcast.48), calls=%async_computation | async-start | bytes 8388608
  16.9 6.6 %slice-start.1 = ((s8[5898240]{0:T(1024)(128)(4,1)}), s8[1703936]{0:T(1024)(128)(4,1)S(1)}, s32[]{:S(2)}) async-start(s8[5898240]{0:T(1024)(128)(4,1)} %bitcast.48), calls=%async_computation.1 | async-start | bytes 3407872
  17.9 9.1 %collective-permute-start.2 = (bf16[2,768]{1,0:T(2,128)(2,1)S(1)}, bf16[2,768]{1,0:T(2,128)(2,1)S(1)}, u32[]{:S(2)}, u32[]{:S(2)}) collective-permute-start(bf16[2,768]{1,0:T(2,128)(2,1)S(1)} %get-tuple-element.21), channel_id=1, source_target_pairs={{0,4},{4,8},{8,12},{12,16},{16,20},{20,24},{24,28},{28,32},{32,36}... | collective-permute-start | bytes 9224 | tf_op jit(solution)/shard_map/ppermute | solution.py:20
  21.6 4.9 %collective-permute-start.3 = (bf16[2,768]{1,0:T(2,128)(2,1)S(1)}, bf16[2,768]{1,0:T(2,128)(2,1)S(1)}, u32[]{:S(2)}, u32[]{:S(2)}) collective-permute-start(bf16[2,768]{1,0:T(2,128)(2,1)S(1)} %get-tuple-element.22), channel_id=1, source_target_pairs={{4,0},{8,4},{12,8},{16,12},{20,16},{24,20},{28,24},{32,28},{36,32}... | collective-permute-start | bytes 9224 | tf_op jit(solution)/shard_map/ppermute | solution.py:21
  80.1 4.2 %collective-permute-start.4 = (bf16[512,256]{1,0:T(8,128)(2,1)}, bf16[512,256]{1,0:T(8,128)(2,1)S(1)}, u32[]{:S(2)}, u32[]{:S(2)}) collective-permute-start(bf16[512,256]{1,0:T(8,128)(2,1)} %get-tuple-element.12.qa_ref), channel_id=1, source_target_pairs={{0,4},{4,0},{1,5},{5,1},{2,6},{6,2},{3,7},{7,3},{8,12},{12,8},{9,1... | collective-permute-start | bytes 786440 | tf_op jit(solution)/shard_map/ppermute | solution.py:315
  84.3 0.7 copy-start.4
  112.3 2.1 %collective-permute-start.5 = (f32[512,256]{1,0:T(8,128)}, f32[512,256]{1,0:T(8,128)S(1)}, u32[]{:S(2)}, u32[]{:S(2)}) collective-permute-start(f32[512,256]{1,0:T(8,128)} %get-tuple-element.17), channel_id=1, source_target_pairs={{0,4},{4,0},{1,5},{5,1},{2,6},{6,2},{3,7},{7,3},{8,12},{12,8},{9,1... | collective-permute-start | bytes 1572872 | tf_op jit(solution)/shard_map/ppermute | solution.py:319
  112.7 1.8 %collective-permute-start.6 = (f32[8,256]{1,0:T(8,128)}, f32[8,256]{1,0:T(8,128)S(1)}, u32[]{:S(2)}, u32[]{:S(2)}) collective-permute-start(f32[8,256]{1,0:T(8,128)} %get-tuple-element.18), channel_id=1, source_target_pairs={{0,4},{4,0},{1,5},{5,1},{2,6},{6,2},{3,7},{7,3},{8,12},{12,8},{9,1... | collective-permute-start | bytes 24584 | tf_op jit(solution)/shard_map/ppermute | solution.py:319
  114.4 0.6 copy-start.2
  114.4 0.8 copy-start.1

commit v11 on v10

--- a/solution.py
+++ b/solution.py
@@ -91,7 +91,7 @@
             sb_ref[heads + h : heads + h + 1, :] = l_sc[h][:, own:]
 
 
-def attend_partial(qt_own, qt_other, hidden_kv, qkv_weight, wvt, heads, head_size, tk=512):
+def attend_partial(qt_own, qt_other, hidden_kv, qkv_weight, wvt, heads, head_size, tk=1024):
     width, own = qt_own.shape
     q_rows = 2 * own
     k_rows, channels = hidden_kv.shape

time: 118 us -> 116 us (0.983)
  Pallas kernels: 80.2 us -> 77.8 us
    pallas_call x1, Pallas kernels: 27.3 us -> 24.9 us  [attend_partial(): pl.pallas_call(functools.partial(attend_kernel, heads, head_size, nk), gr...]
where the time goes in v11:
time: 116 us
  Pallas kernels  77.8 us (67%)
  starting transfers between devices  15.5 us (13%)
  matrix products  11.3 us (10%)
  waiting for transfers between devices  5.49 us (5%)
  local copies, waits for them, and re-layouts  4.62 us (4%)
    pallas_call x1, Pallas kernels, gather_rows(): pl.pallas_call(functools.partial(ring_gather_kernel, side, heads, head_si...  50.1 us
    pallas_call x1, Pallas kernels, attend_partial(): pl.pallas_call(functools.partial(attend_kernel, heads, head_size, nk), gr...  24.9 us
    dot_general x8, matrix products, convolve(): jnp.dot(padded[offset:offset + row_count], weight[offset], preferred_elem...  9.75 us
    ppermute x2, starting transfers between devices, padded_2(): lax.ppermute(lax.slice_in_dim(block, block.shape[0] - width, None, axis=0...  8.15 us
    ppermute x2, starting transfers between devices, padded_2(): lax.ppermute(lax.slice_in_dim(block, 0, width, axis=0), SEQ_AXES, backward)  3.84 us
    unnamed x15, local copies, waits for them, and re-layouts  3.18 us
    ppermute x1, starting transfers between devices, body(): qt_other = lax.ppermute(qt_own, 'core', swap)  2.98 us
    pallas_call x1, Pallas kernels, finish(): pl.pallas_call(functools.partial(finish_kernel, heads, head_size), grid=(...  2.81 us
  transfers between devices with their start and end apart: 7, of which 3 were waited for; matrix products, arithmetic and copies ran while one was open for 8% of the time, Pallas kernels for 0%

profile of v11, /device:TPU:1, one launch (start us, length us, event | category | flops | bytes accessed | tf_op | source)
XLA Modules:
  0.0 115.8 jit_solution(9350138993795227960)
XLA Ops:
  0.0 0.8 fusion.77
  0.8 4.5 %collective-permute-start = (bf16[2,1536]{1,0:T(2,128)(2,1)S(1)}, bf16[2,1536]{1,0:T(2,128)(2,1)S(1)}, u32[]{:S(2)}, u32[]{:S(2)}) collective-permute-start(bf16[2,1536]{1,0:T(2,128)(2,1)S(1)} %get-tuple-element.19), channel_id=1, source_target_pairs={{0,4},{4,8},{8,12},{12,16},{16,20},{20,24},{24,28},{28,32},{32,36}... | collective-permute-start | bytes 18440 | tf_op jit(solution)/shard_map/ppermute | solution.py:20
  5.3 1.9 %collective-permute-start.1 = (bf16[2,1536]{1,0:T(2,128)(2,1)S(1)}, bf16[2,1536]{1,0:T(2,128)(2,1)S(1)}, u32[]{:S(2)}, u32[]{:S(2)}) collective-permute-start(bf16[2,1536]{1,0:T(2,128)(2,1)S(1)} %get-tuple-element.20), channel_id=1, source_target_pairs={{4,0},{8,4},{12,8},{16,12},{20,16},{24,20},{28,24},{32,28},{36,32}... | collective-permute-start | bytes 18440 | tf_op jit(solution)/shard_map/ppermute | solution.py:21
  7.2 0.0 copy-start.3
  7.2 1.3 %constant_dynamic-update-slice_fusion.1 = bf16[258,1536]{1,0:T(8,128)(2,1)S(1)} fusion(bf16[256,1536]{1,0:T(8,128)(2,1)} %param.6), kind=kLoop, calls=%fused_computation.65 | loop fusion | bytes 1572864
  8.6 2.9 %fusion.4 = f32[256,768]{1,0:T(8,128)S(1)} fusion(bf16[256,1536]{1,0:T(8,128)(2,1)} %param.6, bf16[5,1536,768]{2,1,0:T(8,128)(2,1)} %param.7), kind=kOutput, calls=%fused_computation.4 | convolution fusion | flops 603979776 | bytes 3932160 | tf_op jit(solution)/shard_map/dot_general | solution.py:28
  11.5 0.9 broadcast_multiply_fusion
  12.4 0.0 collective-permute-done.1
  12.4 2.5 %fusion = f32[256,768]{1,0:T(8,128)S(1)} fusion(bf16[5,1536,768]{2,1,0:T(8,128)(2,1)} %param.7, bf16[258,1536]{1,0:T(8,128)(2,1)S(1)} %constant_dynamic-update-slice_fusion), kind=kOutput, calls=%fused_computation | convolution fusion | flops 603979776 | bytes 3932160 | tf_op jit(solution)/shard_map/dot_general | solution.py:28
  14.9 0.0 copy-done.3
  14.9 0.0 copy-start
  14.9 0.8 fusion.2
  15.7 0.0 collective-permute-done
  15.7 0.3 copy-done
  16.0 0.0 slice-start
  16.0 0.8 fusion.6
  16.9 0.0 slice-start.1
  16.9 1.0 fusion.57
  17.9 3.6 %collective-permute-start.2 = (bf16[2,768]{1,0:T(2,128)(2,1)S(1)}, bf16[2,768]{1,0:T(2,128)(2,1)S(1)}, u32[]{:S(2)}, u32[]{:S(2)}) collective-permute-start(bf16[2,768]{1,0:T(2,128)(2,1)S(1)} %get-tuple-element.21), channel_id=1, source_target_pairs={{0,4},{4,8},{8,12},{12,16},{16,20},{20,24},{24,28},{28,32},{32,36}... | collective-permute-start | bytes 9224 | tf_op jit(solution)/shard_map/ppermute | solution.py:20
  21.6 1.9 %collective-permute-start.3 = (bf16[2,768]{1,0:T(2,128)(2,1)S(1)}, bf16[2,768]{1,0:T(2,128)(2,1)S(1)}, u32[]{:S(2)}, u32[]{:S(2)}) collective-permute-start(bf16[2,768]{1,0:T(2,128)(2,1)S(1)} %get-tuple-element.22), channel_id=1, source_target_pairs={{4,0},{8,4},{12,8},{16,12},{20,16},{24,20},{28,24},{32,28},{36,32}... | collective-permute-start | bytes 9224 | tf_op jit(solution)/shard_map/ppermute | solution.py:21
  23.5 0.0 slice-done
  23.5 0.0 slice-done.1
  23.5 0.5 fusion.34
  24.0 2.5 %collective-permute-done.3 = bf16[2,768]{1,0:T(2,128)(2,1)S(1)} collective-permute-done((bf16[2,768]{1,0:T(2,128)(2,1)S(1)}, bf16[2,768]{1,0:T(2,128)(2,1)S(1)}, u32[]{:S(2)}, u32[]{:S(2)}) %collective-permute-start.3) | collective-permute-done | bytes 3104 | tf_op jit(solution)/shard_map/ppermute | solution.py:21
  26.5 0.5 fusion.31
  27.0 0.0 collective-permute-done.2
  27.0 0.5 fusion.36
  27.5 0.5 fusion.23
  28.0 1.3 %fusion.30.h_ref.hid_ref = bf16[256,768]{1,0:T(8,128)(2,1)} fusion(f32[256,768]{1,0:T(8,128)S(1)} %fusion.31, f32[256,768]{1,0:T(8,128)S(1)} %fusion.23, bf16[5,768,768]{2,1,0:T(8,128)(2,1)S(1)} %bitcast.49, bf16[256,768]{1,0:T(8,128)(2,1)S(1)} %fusion.57, bf16[2,768]{1,0:T(2,128)(2,1)S(1)} %collective-permute-done.3), kind=kOutput, calls=%fused_computation.24 | convolution fusion | flops 303759360 | bytes 3935232 | tf_op jit(solution)/shard_map/dot_general | solution.py:28
  29.3 0.6 broadcast_in_dim.3
  30.0 50.1 %shard_map.64 = (bf16[16,2,128,768]{3,2,1,0:T(8,128)(2,1)}, bf16[512,256]{1,0:T(8,128)(2,1)}, bf16[512,768]{1,0:T(8,128)(2,1)}) custom-call(bf16[2,128,768]{2,1,0:T(8,128)(2,1)} %bitcast.47, bf16[256,768]{1,0:T(8,128)(2,1)} %fusion.30.h_ref.hid_ref, bf16[768,1536]{1,0:T(8,128)(2,1)} %wk_ref.1, bf16[768,1536]{1,0:T(8,128)(2,1)} %wk_ref.1, f32[1,512]{1,0:T(1,128)} %bitcast.50), custom_call_target="tpu_custom_call" | custom-call | tf_op jit(solution)/shard_map/pallas_call | solution.py:271
  80.1 3.0 %collective-permute-start.4 = (bf16[512,256]{1,0:T(8,128)(2,1)}, bf16[512,256]{1,0:T(8,128)(2,1)S(1)}, u32[]{:S(2)}, u32[]{:S(2)}) collective-permute-start(bf16[512,256]{1,0:T(8,128)(2,1)} %get-tuple-element.12.qa_ref), channel_id=1, source_target_pairs={{0,4},{4,0},{1,5},{5,1},{2,6},{6,2},{3,7},{7,3},{8,12},{12,8},{9,1... | collective-permute-start | bytes 786440 | tf_op jit(solution)/shard_map/ppermute | solution.py:315
  83.1 1.4 %collective-permute-done.4.qb_ref = bf16[512,256]{1,0:T(8,128)(2,1)S(1)} collective-permute-done((bf16[512,256]{1,0:T(8,128)(2,1)}, bf16[512,256]{1,0:T(8,128)(2,1)S(1)}, u32[]{:S(2)}, u32[]{:S(2)}) %collective-permute-start.4) | collective-permute-done | bytes 262176 | tf_op jit(solution)/shard_map/ppermute | solution.py:315
  84.4 0.0 copy-start.4
  84.4 0.7 copy-done.4
  85.1 24.9 %shard_map.65 = (f32[512,256]{1,0:T(8,128)}, f32[8,256]{1,0:T(8,128)}, f32[512,256]{1,0:T(8,128)}, f32[8,256]{1,0:T(8,128)}) custom-call(bf16[512,256]{1,0:T(8,128)(2,1)} %get-tuple-element.12.qa_ref, bf16[512,256]{1,0:T(8,128)(2,1)} %copy-done.4, bf16[4096,768]{1,0:T(8,128)(2,1)} %bitcast.51, bf16[768,1536]{1,0:T(8,128)(2,1)} %wk_ref.1, ...), custom_call_target="tpu_custom_call" | custom-call | flops 10737418240 | bytes 8388608 | tf_op jit(solution)/shard_map/pallas_call | solution.py:100
  110.0 0.4 collective-permute-start.5
  110.4 0.1 collective-permute-start.6
  110.5 1.6 %collective-permute-done.6.sg_ref = f32[8,256]{1,0:T(8,128)S(1)} collective-permute-done((f32[8,256]{1,0:T(8,128)}, f32[8,256]{1,0:T(8,128)S(1)}, u32[]{:S(2)}, u32[]{:S(2)}) %collective-permute-start.6) | collective-permute-done | bytes 8224 | tf_op jit(solution)/shard_map/ppermute | solution.py:319
  112.2 0.0 copy-start.2
  112.2 0.0 collective-permute-done.5.og_ref
  112.2 0.0 copy-start.1
  112.2 0.6 copy-done.2
  112.8 0.2 copy-done.1
  113.0 2.8 %shard_map.66 = bf16[256,768]{1,0:T(8,128)(2,1)} custom-call(f32[512,256]{1,0:T(8,128)} %get-tuple-element.15.o_ref, f32[8,256]{1,0:T(8,128)} %get-tuple-element.16.st_ref, f32[512,256]{1,0:T(8,128)} %copy-done.1, f32[8,256]{1,0:T(8,128)} %copy-done.2, bf16[256,768]{1,0:T(8,128)(2,1)} %fusion.30.h_ref.hid_ref, bf16[512,768]{1,0:T(8,128)(2,1)} %wo_ref.1), custom_call_target="tpu_custom_call" | custom-call | tf_op jit(solution)/shard_map/pallas_call | solution.py:157
  (3 shorter events, 0.0 us)
Async XLA Ops:
  0.8 14.9 %collective-permute-start = (bf16[2,1536]{1,0:T(2,128)(2,1)S(1)}, bf16[2,1536]{1,0:T(2,128)(2,1)S(1)}, u32[]{:S(2)}, u32[]{:S(2)}) collective-permute-start(bf16[2,1536]{1,0:T(2,128)(2,1)S(1)} %get-tuple-element.19), channel_id=1, source_target_pairs={{0,4},{4,8},{8,12},{12,16},{16,20},{20,24},{24,28},{28,32},{32,36}... | collective-permute-start | bytes 18440 | tf_op jit(solution)/shard_map/ppermute | solution.py:20
  5.3 7.1 %collective-permute-start.1 = (bf16[2,1536]{1,0:T(2,128)(2,1)S(1)}, bf16[2,1536]{1,0:T(2,128)(2,1)S(1)}, u32[]{:S(2)}, u32[]{:S(2)}) collective-permute-start(bf16[2,1536]{1,0:T(2,128)(2,1)S(1)} %get-tuple-element.20), channel_id=1, source_target_pairs={{4,0},{8,4},{12,8},{16,12},{20,16},{24,20},{28,24},{32,28},{36,32}... | collective-permute-start | bytes 18440 | tf_op jit(solution)/shard_map/ppermute | solution.py:21
  7.2 7.7 %copy-start.3 = (bf16[5,1536,768]{2,1,0:T(8,128)(2,1)S(1)}, bf16[5,1536,768]{2,1,0:T(8,128)(2,1)}, u32[]{:S(2)}) copy-start(bf16[5,1536,768]{2,1,0:T(8,128)(2,1)} %param.7) | copy-start | bytes 35389444
  14.9 1.1 copy-start
  16.0 7.4 %slice-start = ((s8[5898240]{0:T(1024)(128)(4,1)}), s8[4194304]{0:T(1024)(128)(4,1)S(1)}, s32[]{:S(2)}) async-start(s8[5898240]{0:T(1024)(128)(4,1)} %bitcast.48), calls=%async_computation | async-start | bytes 8388608
  16.9 6.6 %slice-start.1 = ((s8[5898240]{0:T(1024)(128)(4,1)}), s8[1703936]{0:T(1024)(128)(4,1)S(1)}, s32[]{:S(2)}) async-start(s8[5898240]{0:T(1024)(128)(4,1)} %bitcast.48), calls=%async_computation.1 | async-start | bytes 3407872
  17.9 9.1 %collective-permute-start.2 = (bf16[2,768]{1,0:T(2,128)(2,1)S(1)}, bf16[2,768]{1,0:T(2,128)(2,1)S(1)}, u32[]{:S(2)}, u32[]{:S(2)}) collective-permute-start(bf16[2,768]{1,0:T(2,128)(2,1)S(1)} %get-tuple-element.21), channel_id=1, source_target_pairs={{0,4},{4,8},{8,12},{12,16},{16,20},{20,24},{24,28},{28,32},{32,36}... | collective-permute-start | bytes 9224 | tf_op jit(solution)/shard_map/ppermute | solution.py:20
  21.6 4.9 %collective-permute-start.3 = (bf16[2,768]{1,0:T(2,128)(2,1)S(1)}, bf16[2,768]{1,0:T(2,128)(2,1)S(1)}, u32[]{:S(2)}, u32[]{:S(2)}) collective-permute-start(bf16[2,768]{1,0:T(2,128)(2,1)S(1)} %get-tuple-element.22), channel_id=1, source_target_pairs={{4,0},{8,4},{12,8},{16,12},{20,16},{24,20},{28,24},{32,28},{36,32}... | collective-permute-start | bytes 9224 | tf_op jit(solution)/shard_map/ppermute | solution.py:21
  80.1 4.4 %collective-permute-start.4 = (bf16[512,256]{1,0:T(8,128)(2,1)}, bf16[512,256]{1,0:T(8,128)(2,1)S(1)}, u32[]{:S(2)}, u32[]{:S(2)}) collective-permute-start(bf16[512,256]{1,0:T(8,128)(2,1)} %get-tuple-element.12.qa_ref), channel_id=1, source_target_pairs={{0,4},{4,0},{1,5},{5,1},{2,6},{6,2},{3,7},{7,3},{8,12},{12,8},{9,1... | collective-permute-start | bytes 786440 | tf_op jit(solution)/shard_map/ppermute | solution.py:315
  84.4 0.7 copy-start.4
  110.0 2.1 %collective-permute-start.5 = (f32[512,256]{1,0:T(8,128)}, f32[512,256]{1,0:T(8,128)S(1)}, u32[]{:S(2)}, u32[]{:S(2)}) collective-permute-start(f32[512,256]{1,0:T(8,128)} %get-tuple-element.17), channel_id=1, source_target_pairs={{0,4},{4,0},{1,5},{5,1},{2,6},{6,2},{3,7},{7,3},{8,12},{12,8},{9,1... | collective-permute-start | bytes 1572872 | tf_op jit(solution)/shard_map/ppermute | solution.py:319
  110.4 1.8 %collective-permute-start.6 = (f32[8,256]{1,0:T(8,128)}, f32[8,256]{1,0:T(8,128)S(1)}, u32[]{:S(2)}, u32[]{:S(2)}) collective-permute-start(f32[8,256]{1,0:T(8,128)} %get-tuple-element.18), channel_id=1, source_target_pairs={{0,4},{4,0},{1,5},{5,1},{2,6},{6,2},{3,7},{7,3},{8,12},{12,8},{9,1... | collective-permute-start | bytes 24584 | tf_op jit(solution)/shard_map/ppermute | solution.py:319
  112.2 0.6 copy-start.2
  112.2 0.8 copy-start.1

commit v12 on v11

--- a/solution.py
+++ b/solution.py
@@ -13,13 +13,15 @@
 SEQ_AXES = ("zx", "core")
 
 
-def padded_2(block, width):
+def padded_2(block, width, align=1):
     count = lax.axis_size(SEQ_AXES)
     forward = [(i, i + 1) for i in range(count - 1)]
     backward = [(target, source) for source, target in forward]
     low = lax.ppermute(lax.slice_in_dim(block, block.shape[0] - width, None, axis=0), SEQ_AXES, forward)
     high = lax.ppermute(lax.slice_in_dim(block, 0, width, axis=0), SEQ_AXES, backward)
-    return jnp.concatenate([low, block, high], axis=0)
+    extra = (-(block.shape[0] + 2 * width)) % align
+    fill = jnp.zeros((extra, block.shape[1]), block.dtype)
+    return jnp.concatenate([low, block, high, fill], axis=0)
 
 
 def convolve(padded, weight, row_count):
@@ -298,10 +300,51 @@
     return out.reshape(n * rows, width), qt, wvt
 
 
+def conv_gelu_kernel(taps, rows, x_ref, w_ref, o_ref, acc_sc):
+    j = pl.program_id(0)
+    product = jnp.dot(x_ref[...], w_ref[...], preferred_element_type=jnp.float32)
+    for t in range(taps):
+
+        @pl.when(j == t)
+        def _():
+            if t == 0:
+                acc_sc[...] = product[t : t + rows]
+            else:
+                acc_sc[...] = acc_sc[...] + product[t : t + rows]
+
+    @pl.when(j == taps - 1)
+    def _():
+        o_ref[...] = jax.nn.gelu(acc_sc[...]).astype(o_ref.dtype)
+
+
+def conv_gelu(padded, weight, rows):
+    taps, channels, width = weight.shape
+    whole = lambda j: (0, 0)
+    return pl.pallas_call(
+        functools.partial(conv_gelu_kernel, taps, rows),
+        grid=(taps,),
+        in_specs=[
+            pl.BlockSpec(padded.shape, whole),
+            pl.BlockSpec((None, channels, width), lambda j: (j, 0, 0)),
+        ],
+        out_specs=pl.BlockSpec((rows, width), whole),
+        out_shape=jax.ShapeDtypeStruct((rows, width), jnp.bfloat16),
+        scratch_shapes=[pltpu.VMEM((rows, width), jnp.float32)],
+        compiler_params=pltpu.CompilerParams(
+            dimension_semantics=("arbitrary",), vmem_limit_bytes=24 * 1024 * 1024
+        ),
+        cost_estimate=pl.CostEstimate(
+            flops=2 * taps * padded.shape[0] * channels * width,
+            transcendentals=rows * width,
+            bytes_accessed=taps * channels * width * 2 + padded.size * 2 + rows * width * 2,
+        ),
+    )(padded, weight)
+
+
 def body(sequence_input, conv_first, conv_second, qkv_weight, out_weight, logit_scale):
     row_count = sequence_input.shape[0]
-    padded_input = padded_2(sequence_input, 2)
-    first_out = jax.nn.gelu(convolve(padded_input, conv_first, row_count)).astype(jnp.bfloat16)
+    padded_input = padded_2(sequence_input, 2, align=8)
+    first_out = conv_gelu(padded_input, conv_first, row_count)
     padded_first = padded_2(first_out, 2)
     second = convolve(padded_first, conv_second, row_count)
     hidden = (first_out.astype(jnp.float32) + second).astype(jnp.bfloat16)

time: 116 us -> 117 us (level)
  matrix products: 11.3 us -> 3.28 us
  Pallas kernels: 77.8 us -> 82.8 us
  local copies, waits for them, and re-layouts: 4.62 us -> 7.35 us
  waiting for transfers between devices: 5.49 us -> 7.32 us
  starting transfers between devices: 15.5 us -> 14.1 us
    dot_general x8 -> x4, matrix products: 9.75 us -> 2.78 us  [convolve(): jnp.dot(padded[offset:offset + row_count], weight[offset], preferred_elem...]
    pallas_call x0 -> x1, Pallas kernels: none -> 5.05 us  [conv_gelu(): pl.pallas_call(functools.partial(conv_gelu_kernel, taps, rows), grid=(tap...]
    unnamed x15 -> x10, local copies, waits for them, and re-layouts: 3.18 us -> 5.84 us
    ppermute x2, waiting for transfers between devices: 2.48 us -> 4.31 us  [padded_2(): lax.ppermute(lax.slice_in_dim(block, 0, width, axis=0), SEQ_AXES, backward)]
    ppermute x2, starting transfers between devices: 8.15 us -> 6.46 us  [padded_2(): lax.ppermute(lax.slice_in_dim(block, block.shape[0] - width, None, axis=0...]
    concatenate x0 -> x1, other arithmetic: none -> 1.4 us  [padded_2(): return jnp.concatenate([low, block, high, fill], axis=0)]
  transfers between devices with their start and end apart: 7 -> 7, of which waited for: 3 -> 4; matrix products, arithmetic and copies ran while one was open for 8% -> 1% of each run, Pallas kernels for 0% -> 0%
where the time goes in v12:
time: 117 us
  Pallas kernels  82.8 us (71%)
  starting transfers between devices  14.1 us (12%)
  local copies, waits for them, and re-layouts  7.35 us (6%)
  waiting for transfers between devices  7.32 us (6%)
  matrix products  3.28 us (3%)
  other arithmetic  2.06 us (2%)
    pallas_call x1, Pallas kernels, gather_rows(): pl.pallas_call(functools.partial(ring_gather_kernel, side, heads, head_si...  50.1 us
    pallas_call x1, Pallas kernels, attend_partial(): pl.pallas_call(functools.partial(attend_kernel, heads, head_size, nk), gr...  24.9 us
    ppermute x2, starting transfers between devices, padded_2(): lax.ppermute(lax.slice_in_dim(block, block.shape[0] - width, None, axis=0...  6.46 us
    unnamed x10, local copies, waits for them, and re-layouts  5.84 us
    pallas_call x1, Pallas kernels, conv_gelu(): pl.pallas_call(functools.partial(conv_gelu_kernel, taps, rows), grid=(tap...  5.05 us
    ppermute x2, waiting for transfers between devices, padded_2(): lax.ppermute(lax.slice_in_dim(block, 0, width, axis=0), SEQ_AXES, backward)  4.31 us
    ppermute x2, starting transfers between devices, padded_2(): lax.ppermute(lax.slice_in_dim(block, 0, width, axis=0), SEQ_AXES, backward)  4.3 us
    pallas_call x1, Pallas kernels, finish(): pl.pallas_call(functools.partial(finish_kernel, heads, head_size), grid=(...  2.81 us
  transfers between devices with their start and end apart: 7, of which 4 were waited for; matrix products, arithmetic and copies ran while one was open for 1% of the time, Pallas kernels for 0%

profile of v12, /device:TPU:1, one launch (start us, length us, event | category | flops | bytes accessed | tf_op | source)
XLA Modules:
  0.0 117.0 jit_solution(6457639449517257891)
XLA Ops:
  0.0 0.8 fusion.29
  0.8 4.5 %collective-permute-start = (bf16[2,1536]{1,0:T(2,128)(2,1)S(1)}, bf16[2,1536]{1,0:T(2,128)(2,1)S(1)}, u32[]{:S(2)}, u32[]{:S(2)}) collective-permute-start(bf16[2,1536]{1,0:T(2,128)(2,1)S(1)} %get-tuple-element.19), channel_id=1, source_target_pairs={{0,4},{4,8},{8,12},{12,16},{16,20},{20,24},{24,28},{28,32},{32,36}... | collective-permute-start | bytes 18440 | tf_op jit(solution)/shard_map/ppermute | solution.py:20
  5.3 1.9 %collective-permute-start.1 = (bf16[2,1536]{1,0:T(2,128)(2,1)S(1)}, bf16[2,1536]{1,0:T(2,128)(2,1)S(1)}, u32[]{:S(2)}, u32[]{:S(2)}) collective-permute-start(bf16[2,1536]{1,0:T(2,128)(2,1)S(1)} %get-tuple-element.20), channel_id=1, source_target_pairs={{4,0},{8,4},{12,8},{16,12},{20,16},{24,20},{28,24},{32,28},{36,32}... | collective-permute-start | bytes 18440 | tf_op jit(solution)/shard_map/ppermute | solution.py:21
  7.2 0.7 broadcast_multiply_fusion
  7.9 0.1 pad.7.clone
  8.0 0.0 collective-permute-done
  8.0 2.3 %collective-permute-done.1 = bf16[2,1536]{1,0:T(2,128)(2,1)S(1)} collective-permute-done((bf16[2,1536]{1,0:T(2,128)(2,1)S(1)}, bf16[2,1536]{1,0:T(2,128)(2,1)S(1)}, u32[]{:S(2)}, u32[]{:S(2)}) %collective-permute-start.1) | collective-permute-done | bytes 6176 | tf_op jit(solution)/shard_map/ppermute | solution.py:21
  10.2 1.4 %maximum_maximum_fusion.x_ref = bf16[264,1536]{1,0:T(8,128)(2,1)S(1)} fusion(bf16[2,1536]{1,0:T(2,128)(2,1)S(1)} %collective-permute-done.1, bf16[256,1536]{1,0:T(8,128)(2,1)} %param.6, bf16[2,1536]{1,0:T(2,128)(2,1)S(1)} %collective-permute-done, bf16[264]{0:T(512)(128)(2,1)S(1)} %pad.7.clone), kind=kLoop, calls=%fused_computation.17 | loop fusion | flops 3244032 | bytes 1610256 | tf_op jit(solution)/shard_map/concatenate | solution.py:24
  11.6 0.0 copy-start
  11.7 4.3 %copy-done = bf16[5,1536,768]{2,1,0:T(8,128)(2,1)S(1)} copy-done((bf16[5,1536,768]{2,1,0:T(8,128)(2,1)S(1)}, bf16[5,1536,768]{2,1,0:T(8,128)(2,1)}, u32[]{:S(2)}) %copy-start) | copy-done | bytes 11796504
  16.0 0.0 copy-start.1
  16.0 5.0 %shard_map.64 = bf16[256,768]{1,0:T(8,128)(2,1)S(1)} custom-call(bf16[264,1536]{1,0:T(8,128)(2,1)S(1)} %maximum_maximum_fusion.x_ref, bf16[5,1536,768]{2,1,0:T(8,128)(2,1)S(1)} %copy-done), custom_call_target="tpu_custom_call" | custom-call | flops 3114270720 | bytes 13000704 | tf_op jit(solution)/shard_map/pallas_call | solution.py:323
  21.1 1.9 %collective-permute-start.2 = (bf16[2,768]{1,0:T(2,128)(2,1)S(1)}, bf16[2,768]{1,0:T(2,128)(2,1)S(1)}, u32[]{:S(2)}, u32[]{:S(2)}) collective-permute-start(bf16[2,768]{1,0:T(2,128)(2,1)S(1)} %get-tuple-element.21), channel_id=1, source_target_pairs={{0,4},{4,8},{8,12},{12,16},{16,20},{20,24},{24,28},{28,32},{32,36}... | collective-permute-start | bytes 9224 | tf_op jit(solution)/shard_map/ppermute | solution.py:20
  23.0 2.4 %collective-permute-start.3 = (bf16[2,768]{1,0:T(2,128)(2,1)S(1)}, bf16[2,768]{1,0:T(2,128)(2,1)S(1)}, u32[]{:S(2)}, u32[]{:S(2)}) collective-permute-start(bf16[2,768]{1,0:T(2,128)(2,1)S(1)} %get-tuple-element.22), channel_id=1, source_target_pairs={{4,0},{8,4},{12,8},{16,12},{20,16},{24,20},{28,24},{32,28},{36,32}... | collective-permute-start | bytes 9224 | tf_op jit(solution)/shard_map/ppermute | solution.py:21
  25.4 0.0 copy-done.1
  25.4 0.5 fusion.5
  25.9 2.0 %collective-permute-done.3 = bf16[2,768]{1,0:T(2,128)(2,1)S(1)} collective-permute-done((bf16[2,768]{1,0:T(2,128)(2,1)S(1)}, bf16[2,768]{1,0:T(2,128)(2,1)S(1)}, u32[]{:S(2)}, u32[]{:S(2)}) %collective-permute-start.3) | collective-permute-done | bytes 3104 | tf_op jit(solution)/shard_map/ppermute | solution.py:21
  27.9 0.5 fusion.2
  28.4 0.0 collective-permute-done.2
  28.4 0.5 fusion.7
  28.9 0.5 fusion.1
  29.5 1.3 %add_convert_fusion.h_ref.hid_ref = bf16[256,768]{1,0:T(8,128)(2,1)} fusion(bf16[256,768]{1,0:T(8,128)(2,1)S(1)} %shard_map.64, f32[256,768]{1,0:T(8,128)S(1)} %fusion.2, f32[256,768]{1,0:T(8,128)S(1)} %fusion.1, bf16[5,768,768]{2,1,0:T(8,128)(2,1)S(1)} %copy-done.1, bf16[2,768]{1,0:T(2,128)(2,1)S(1)} %collective-permute-done.3), kind=kOutput, calls=%fused_computation.18 | convolution fusion | flops 303759360 | bytes 3935232 | tf_op jit(solution)/shard_map/dot_general | solution.py:30
  30.8 0.6 broadcast_in_dim.7
  31.4 50.1 %shard_map.65 = (bf16[16,2,128,768]{3,2,1,0:T(8,128)(2,1)}, bf16[512,256]{1,0:T(8,128)(2,1)}, bf16[512,768]{1,0:T(8,128)(2,1)}) custom-call(bf16[2,128,768]{2,1,0:T(8,128)(2,1)} %bitcast.21, bf16[256,768]{1,0:T(8,128)(2,1)} %add_convert_fusion.h_ref.hid_ref, bf16[768,1536]{1,0:T(8,128)(2,1)} %wk_ref.1, bf16[768,1536]{1,0:T(8,128)(2,1)} %wk_ref.1, ...), custom_call_target="tpu_custom_call" | custom-call | tf_op jit(solution)/shard_map/pallas_call | solution.py:273
  81.5 2.8 %collective-permute-start.4 = (bf16[512,256]{1,0:T(8,128)(2,1)}, bf16[512,256]{1,0:T(8,128)(2,1)S(1)}, u32[]{:S(2)}, u32[]{:S(2)}) collective-permute-start(bf16[512,256]{1,0:T(8,128)(2,1)} %get-tuple-element.12.qa_ref), channel_id=1, source_target_pairs={{0,4},{4,0},{1,5},{5,1},{2,6},{6,2},{3,7},{7,3},{8,12},{12,8},{9,1... | collective-permute-start | bytes 786440 | tf_op jit(solution)/shard_map/ppermute | solution.py:358
  84.3 1.4 %collective-permute-done.4.qb_ref = bf16[512,256]{1,0:T(8,128)(2,1)S(1)} collective-permute-done((bf16[512,256]{1,0:T(8,128)(2,1)}, bf16[512,256]{1,0:T(8,128)(2,1)S(1)}, u32[]{:S(2)}, u32[]{:S(2)}) %collective-permute-start.4) | collective-permute-done | bytes 262176 | tf_op jit(solution)/shard_map/ppermute | solution.py:358
  85.7 0.0 copy-start.4
  85.7 0.7 copy-done.4
  86.4 24.9 %shard_map.66 = (f32[512,256]{1,0:T(8,128)}, f32[8,256]{1,0:T(8,128)}, f32[512,256]{1,0:T(8,128)}, f32[8,256]{1,0:T(8,128)}) custom-call(bf16[512,256]{1,0:T(8,128)(2,1)} %get-tuple-element.12.qa_ref, bf16[512,256]{1,0:T(8,128)(2,1)} %copy-done.4, bf16[4096,768]{1,0:T(8,128)(2,1)} %bitcast.23, bf16[768,1536]{1,0:T(8,128)(2,1)} %wk_ref.1, ...), custom_call_target="tpu_custom_call" | custom-call | flops 10737418240 | bytes 8388608 | tf_op jit(solution)/shard_map/pallas_call | solution.py:102
  111.3 0.4 collective-permute-start.5
  111.6 0.1 collective-permute-start.6
  111.8 1.6 %collective-permute-done.6.sg_ref = f32[8,256]{1,0:T(8,128)S(1)} collective-permute-done((f32[8,256]{1,0:T(8,128)}, f32[8,256]{1,0:T(8,128)S(1)}, u32[]{:S(2)}, u32[]{:S(2)}) %collective-permute-start.6) | collective-permute-done | bytes 8224 | tf_op jit(solution)/shard_map/ppermute | solution.py:362
  113.4 0.0 copy-start.3
  113.4 0.0 collective-permute-done.5.og_ref
  113.4 0.0 copy-start.2
  113.4 0.6 copy-done.3
  114.0 0.2 copy-done.2
  114.2 2.8 %shard_map.67 = bf16[256,768]{1,0:T(8,128)(2,1)} custom-call(f32[512,256]{1,0:T(8,128)} %get-tuple-element.15.o_ref, f32[8,256]{1,0:T(8,128)} %get-tuple-element.16.st_ref, f32[512,256]{1,0:T(8,128)} %copy-done.2, f32[8,256]{1,0:T(8,128)} %copy-done.3, bf16[256,768]{1,0:T(8,128)(2,1)} %add_convert_fusion.h_ref.hid_ref, bf16[512,768]{1,0:T(8,128)(2,1)} %wo_ref.1), custom_call_target="tpu_custom_call" | custom-call | tf_op jit(solution)/shard_map/pallas_call | solution.py:159
  (2 shorter events, 0.0 us)
Async XLA Ops:
  0.8 7.2 %collective-permute-start = (bf16[2,1536]{1,0:T(2,128)(2,1)S(1)}, bf16[2,1536]{1,0:T(2,128)(2,1)S(1)}, u32[]{:S(2)}, u32[]{:S(2)}) collective-permute-start(bf16[2,1536]{1,0:T(2,128)(2,1)S(1)} %get-tuple-element.19), channel_id=1, source_target_pairs={{0,4},{4,8},{8,12},{12,16},{16,20},{20,24},{24,28},{28,32},{32,36}... | collective-permute-start | bytes 18440 | tf_op jit(solution)/shard_map/ppermute | solution.py:20
  5.3 4.9 %collective-permute-start.1 = (bf16[2,1536]{1,0:T(2,128)(2,1)S(1)}, bf16[2,1536]{1,0:T(2,128)(2,1)S(1)}, u32[]{:S(2)}, u32[]{:S(2)}) collective-permute-start(bf16[2,1536]{1,0:T(2,128)(2,1)S(1)} %get-tuple-element.20), channel_id=1, source_target_pairs={{4,0},{8,4},{12,8},{16,12},{20,16},{24,20},{28,24},{32,28},{36,32}... | collective-permute-start | bytes 18440 | tf_op jit(solution)/shard_map/ppermute | solution.py:21
  11.6 4.4 %copy-start = (bf16[5,1536,768]{2,1,0:T(8,128)(2,1)S(1)}, bf16[5,1536,768]{2,1,0:T(8,128)(2,1)}, u32[]{:S(2)}) copy-start(bf16[5,1536,768]{2,1,0:T(8,128)(2,1)} %w_ref.1) | copy-start | bytes 35389444
  16.0 9.4 %copy-start.1 = (bf16[5,768,768]{2,1,0:T(8,128)(2,1)S(1)}, bf16[5,768,768]{2,1,0:T(8,128)(2,1)}, u32[]{:S(2)}) copy-start(bf16[5,768,768]{2,1,0:T(8,128)(2,1)} %param.8) | copy-start | bytes 17694724
  21.1 7.4 %collective-permute-start.2 = (bf16[2,768]{1,0:T(2,128)(2,1)S(1)}, bf16[2,768]{1,0:T(2,128)(2,1)S(1)}, u32[]{:S(2)}, u32[]{:S(2)}) collective-permute-start(bf16[2,768]{1,0:T(2,128)(2,1)S(1)} %get-tuple-element.21), channel_id=1, source_target_pairs={{0,4},{4,8},{8,12},{12,16},{16,20},{20,24},{24,28},{28,32},{32,36}... | collective-permute-start | bytes 9224 | tf_op jit(solution)/shard_map/ppermute | solution.py:20
  23.0 4.9 %collective-permute-start.3 = (bf16[2,768]{1,0:T(2,128)(2,1)S(1)}, bf16[2,768]{1,0:T(2,128)(2,1)S(1)}, u32[]{:S(2)}, u32[]{:S(2)}) collective-permute-start(bf16[2,768]{1,0:T(2,128)(2,1)S(1)} %get-tuple-element.22), channel_id=1, source_target_pairs={{4,0},{8,4},{12,8},{16,12},{20,16},{24,20},{28,24},{32,28},{36,32}... | collective-permute-start | bytes 9224 | tf_op jit(solution)/shard_map/ppermute | solution.py:21
  81.5 4.2 %collective-permute-start.4 = (bf16[512,256]{1,0:T(8,128)(2,1)}, bf16[512,256]{1,0:T(8,128)(2,1)S(1)}, u32[]{:S(2)}, u32[]{:S(2)}) collective-permute-start(bf16[512,256]{1,0:T(8,128)(2,1)} %get-tuple-element.12.qa_ref), channel_id=1, source_target_pairs={{0,4},{4,0},{1,5},{5,1},{2,6},{6,2},{3,7},{7,3},{8,12},{12,8},{9,1... | collective-permute-start | bytes 786440 | tf_op jit(solution)/shard_map/ppermute | solution.py:358
  85.7 0.7 copy-start.4
  111.3 2.1 %collective-permute-start.5 = (f32[512,256]{1,0:T(8,128)}, f32[512,256]{1,0:T(8,128)S(1)}, u32[]{:S(2)}, u32[]{:S(2)}) collective-permute-start(f32[512,256]{1,0:T(8,128)} %get-tuple-element.17), channel_id=1, source_target_pairs={{0,4},{4,0},{1,5},{5,1},{2,6},{6,2},{3,7},{7,3},{8,12},{12,8},{9,1... | collective-permute-start | bytes 1572872 | tf_op jit(solution)/shard_map/ppermute | solution.py:362
  111.6 1.8 %collective-permute-start.6 = (f32[8,256]{1,0:T(8,128)}, f32[8,256]{1,0:T(8,128)S(1)}, u32[]{:S(2)}, u32[]{:S(2)}) collective-permute-start(f32[8,256]{1,0:T(8,128)} %get-tuple-element.18), channel_id=1, source_target_pairs={{0,4},{4,0},{1,5},{5,1},{2,6},{6,2},{3,7},{7,3},{8,12},{12,8},{9,1... | collective-permute-start | bytes 24584 | tf_op jit(solution)/shard_map/ppermute | solution.py:362
  113.4 0.6 copy-start.3
  113.4 0.8 copy-start.2

commit v13 on v12

--- a/solution.py
+++ b/solution.py
@@ -300,7 +300,7 @@
     return out.reshape(n * rows, width), qt, wvt
 
 
-def conv_gelu_kernel(taps, rows, x_ref, w_ref, o_ref, acc_sc):
+def conv_gelu_kernel(taps, rows, halo, x_ref, w_ref, o_ref, acc_sc):
     j = pl.program_id(0)
     product = jnp.dot(x_ref[...], w_ref[...], preferred_element_type=jnp.float32)
     for t in range(taps):
@@ -314,14 +314,23 @@
 
     @pl.when(j == taps - 1)
     def _():
-        o_ref[...] = jax.nn.gelu(acc_sc[...]).astype(o_ref.dtype)
-
-
-def conv_gelu(padded, weight, rows):
+        place = lax.axis_index(SEQ_AXES)
+        last = lax.axis_size(SEQ_AXES) - 1
+        row = lax.broadcasted_iota(jnp.int32, acc_sc.shape, 0)
+        outside = jnp.logical_or(
+            jnp.logical_and(place == 0, row < halo),
+            jnp.logical_and(place == last, row >= rows - halo),
+        )
+        value = jax.nn.gelu(acc_sc[...])
+        o_ref[...] = jnp.where(outside, 0.0, value).astype(o_ref.dtype)
+
+
+def conv_gelu(padded, weight, halo):
     taps, channels, width = weight.shape
+    rows = padded.shape[0] - taps + 1
     whole = lambda j: (0, 0)
     return pl.pallas_call(
-        functools.partial(conv_gelu_kernel, taps, rows),
+        functools.partial(conv_gelu_kernel, taps, rows, halo),
         grid=(taps,),
         in_specs=[
             pl.BlockSpec(padded.shape, whole),
@@ -343,9 +352,9 @@
 
 def body(sequence_input, conv_first, conv_second, qkv_weight, out_weight, logit_scale):
     row_count = sequence_input.shape[0]
-    padded_input = padded_2(sequence_input, 2, align=8)
-    first_out = conv_gelu(padded_input, conv_first, row_count)
-    padded_first = padded_2(first_out, 2)
+    padded_input = padded_2(sequence_input, 4)
+    padded_first = conv_gelu(padded_input, conv_first, 2)
+    first_out = padded_first[2 : 2 + row_count]
     second = convolve(padded_first, conv_second, row_count)
     hidden = (first_out.astype(jnp.float32) + second).astype(jnp.bfloat16)
     head_count = logit_scale.shape[0]

time: 117 us -> 109 us (0.932)
  starting transfers between devices: 14.1 us -> 9.87 us
  Pallas kernels: 82.8 us -> 80.5 us
  waiting for transfers between devices: 7.32 us -> 5.44 us
    pallas_call x1, Pallas kernels: 50.1 us -> 47.7 us  [gather_rows(): pl.pallas_call(functools.partial(ring_gather_kernel, side, heads, head_si...]
    ppermute x2 -> x1, starting transfers between devices: 4.3 us -> 1.92 us  [padded_2(): lax.ppermute(lax.slice_in_dim(block, 0, width, axis=0), SEQ_AXES, backward)]
    ppermute x2 -> x1, starting transfers between devices: 6.46 us -> 4.51 us  [padded_2(): lax.ppermute(lax.slice_in_dim(block, block.shape[0] - width, None, axis=0...]
    ppermute x2 -> x1, waiting for transfers between devices: 4.31 us -> 2.42 us  [padded_2(): lax.ppermute(lax.slice_in_dim(block, 0, width, axis=0), SEQ_AXES, backward)]
  transfers between devices with their start and end apart: 7 -> 5, of which waited for: 4 -> 3; matrix products, arithmetic and copies ran while one was open for 1% -> 1% of each run, Pallas kernels for 0% -> 0%
where the time goes in v13:
time: 109 us; the launch traced here: 108 us
  Pallas kernels  80.5 us (74%)
  starting transfers between devices  9.87 us (9%)
  local copies, waits for them, and re-layouts  7.27 us (7%)
  waiting for transfers between devices  5.44 us (5%)
  matrix products  3.24 us (3%)
  other arithmetic  1.99 us (2%)
    pallas_call x1, Pallas kernels, gather_rows(): pl.pallas_call(functools.partial(ring_gather_kernel, side, heads, head_si...  47.7 us
    pallas_call x1, Pallas kernels, attend_partial(): pl.pallas_call(functools.partial(attend_kernel, heads, head_size, nk), gr...  24.9 us
    unnamed x10, local copies, waits for them, and re-layouts  5.86 us
    pallas_call x1, Pallas kernels, conv_gelu(): pl.pallas_call(functools.partial(conv_gelu_kernel, taps, rows, halo), gri...  5.06 us
    ppermute x1, starting transfers between devices, padded_2(): lax.ppermute(lax.slice_in_dim(block, block.shape[0] - width, None, axis=0...  4.51 us
    ppermute x1, starting transfers between devices, body(): qt_other = lax.ppermute(qt_own, 'core', swap)  2.93 us
    pallas_call x1, Pallas kernels, finish(): pl.pallas_call(functools.partial(finish_kernel, heads, head_size), grid=(...  2.82 us
    dot_general x4, matrix products, convolve(): jnp.dot(padded[offset:offset + row_count], weight[offset], preferred_elem...  2.75 us
  transfers between devices with their start and end apart: 5, of which 3 were waited for; matrix products, arithmetic and copies ran while one was open for 1% of the time, Pallas kernels for 0%

profile of v13, /device:TPU:1, one launch (start us, length us, event | category | flops | bytes accessed | tf_op | source)
XLA Modules:
  0.0 108.4 jit_solution(2032316390480594772)
XLA Ops:
  0.0 0.8 fusion.20
  0.8 4.5 %collective-permute-start = (bf16[4,1536]{1,0:T(4,128)(2,1)S(1)}, bf16[4,1536]{1,0:T(4,128)(2,1)S(1)}, u32[]{:S(2)}, u32[]{:S(2)}) collective-permute-start(bf16[4,1536]{1,0:T(4,128)(2,1)S(1)} %get-tuple-element.19), channel_id=1, source_target_pairs={{0,4},{4,8},{8,12},{12,16},{16,20},{20,24},{24,28},{28,32},{32,36}... | collective-permute-start | bytes 36872 | tf_op jit(solution)/shard_map/ppermute | solution.py:20
  5.3 1.9 %collective-permute-start.1 = (bf16[4,1536]{1,0:T(4,128)(2,1)S(1)}, bf16[4,1536]{1,0:T(4,128)(2,1)S(1)}, u32[]{:S(2)}, u32[]{:S(2)}) collective-permute-start(bf16[4,1536]{1,0:T(4,128)(2,1)S(1)} %get-tuple-element.20), channel_id=1, source_target_pairs={{4,0},{8,4},{12,8},{16,12},{20,16},{24,20},{28,24},{32,28},{36,32}... | collective-permute-start | bytes 36872 | tf_op jit(solution)/shard_map/ppermute | solution.py:21
  7.2 0.7 broadcast_multiply_fusion
  7.9 0.0 collective-permute-done
  7.9 2.4 %collective-permute-done.1 = bf16[4,1536]{1,0:T(4,128)(2,1)S(1)} collective-permute-done((bf16[4,1536]{1,0:T(4,128)(2,1)S(1)}, bf16[4,1536]{1,0:T(4,128)(2,1)S(1)}, u32[]{:S(2)}, u32[]{:S(2)}) %collective-permute-start.1) | collective-permute-done | bytes 12320 | tf_op jit(solution)/shard_map/ppermute | solution.py:21
  10.3 1.3 %pad_maximum_fusion.x_ref = bf16[264,1536]{1,0:T(8,128)(2,1)S(1)} fusion(bf16[4,1536]{1,0:T(4,128)(2,1)S(1)} %collective-permute-done.1, bf16[256,1536]{1,0:T(8,128)(2,1)} %param.6, bf16[4,1536]{1,0:T(4,128)(2,1)S(1)} %collective-permute-done), kind=kLoop, calls=%fused_computation.15 | loop fusion | flops 2433024 | bytes 1622016 | tf_op jit(solution)/shard_map/concatenate | solution.py:24
  11.6 0.0 copy-start
  11.7 4.3 %copy-done = bf16[5,1536,768]{2,1,0:T(8,128)(2,1)S(1)} copy-done((bf16[5,1536,768]{2,1,0:T(8,128)(2,1)S(1)}, bf16[5,1536,768]{2,1,0:T(8,128)(2,1)}, u32[]{:S(2)}) %copy-start) | copy-done | bytes 11796504
  16.0 0.0 copy-start.1
  16.0 5.1 %shard_map.64 = bf16[260,768]{1,0:T(8,128)(2,1)S(1)} custom-call(bf16[264,1536]{1,0:T(8,128)(2,1)S(1)} %pad_maximum_fusion.x_ref, bf16[5,1536,768]{2,1,0:T(8,128)(2,1)S(1)} %copy-done), custom_call_target="tpu_custom_call" | custom-call | flops 3114270720 | bytes 13006848 | tf_op jit(solution)/shard_map/pallas_call | solution.py:332
  21.1 0.0 copy-done.1
  21.1 0.5 fusion.3
  21.6 0.5 convolution_add_fusion.3
  22.1 0.5 convolution_add_fusion.2
  22.6 0.5 convolution_add_fusion.1
  23.0 1.3 %add_convert_fusion.h_ref.hid_ref = bf16[256,768]{1,0:T(8,128)(2,1)} fusion(f32[256,768]{1,0:T(8,128)S(1)} %convolution_add_fusion.1, bf16[5,768,768]{2,1,0:T(8,128)(2,1)S(1)} %copy-done.1, bf16[260,768]{1,0:T(8,128)(2,1)S(1)} %shard_map.64), kind=kOutput, calls=%fused_computation.16 | convolution fusion | flops 302776320 | bytes 3145728 | tf_op jit(solution)/shard_map/dot_general | solution.py:30
  24.3 0.6 broadcast_in_dim.3
  25.0 47.7 %shard_map.65 = (bf16[16,2,128,768]{3,2,1,0:T(8,128)(2,1)}, bf16[512,256]{1,0:T(8,128)(2,1)}, bf16[512,768]{1,0:T(8,128)(2,1)}) custom-call(bf16[2,128,768]{2,1,0:T(8,128)(2,1)} %bitcast.20, bf16[256,768]{1,0:T(8,128)(2,1)} %add_convert_fusion.h_ref.hid_ref, bf16[768,1536]{1,0:T(8,128)(2,1)} %wk_ref.1, bf16[768,1536]{1,0:T(8,128)(2,1)} %wk_ref.1, ...), custom_call_target="tpu_custom_call" | custom-call | tf_op jit(solution)/shard_map/pallas_call | solution.py:273
  72.7 2.9 %collective-permute-start.2 = (bf16[512,256]{1,0:T(8,128)(2,1)}, bf16[512,256]{1,0:T(8,128)(2,1)S(1)}, u32[]{:S(2)}, u32[]{:S(2)}) collective-permute-start(bf16[512,256]{1,0:T(8,128)(2,1)} %get-tuple-element.12.qa_ref), channel_id=1, source_target_pairs={{0,4},{4,0},{1,5},{5,1},{2,6},{6,2},{3,7},{7,3},{8,12},{12,8},{9,1... | collective-permute-start | bytes 786440 | tf_op jit(solution)/shard_map/ppermute | solution.py:367
  75.7 1.4 %collective-permute-done.2.qb_ref = bf16[512,256]{1,0:T(8,128)(2,1)S(1)} collective-permute-done((bf16[512,256]{1,0:T(8,128)(2,1)}, bf16[512,256]{1,0:T(8,128)(2,1)S(1)}, u32[]{:S(2)}, u32[]{:S(2)}) %collective-permute-start.2) | collective-permute-done | bytes 262176 | tf_op jit(solution)/shard_map/ppermute | solution.py:367
  77.0 0.0 copy-start.4
  77.0 0.7 copy-done.4
  77.7 24.9 %shard_map.66 = (f32[512,256]{1,0:T(8,128)}, f32[8,256]{1,0:T(8,128)}, f32[512,256]{1,0:T(8,128)}, f32[8,256]{1,0:T(8,128)}) custom-call(bf16[512,256]{1,0:T(8,128)(2,1)} %get-tuple-element.12.qa_ref, bf16[512,256]{1,0:T(8,128)(2,1)} %copy-done.4, bf16[4096,768]{1,0:T(8,128)(2,1)} %bitcast.22, bf16[768,1536]{1,0:T(8,128)(2,1)} %wk_ref.1, ...), custom_call_target="tpu_custom_call" | custom-call | flops 10737418240 | bytes 8388608 | tf_op jit(solution)/shard_map/pallas_call | solution.py:102
  102.6 0.4 collective-permute-start.3
  103.0 0.1 collective-permute-start.4
  103.1 1.6 %collective-permute-done.4.sg_ref = f32[8,256]{1,0:T(8,128)S(1)} collective-permute-done((f32[8,256]{1,0:T(8,128)}, f32[8,256]{1,0:T(8,128)S(1)}, u32[]{:S(2)}, u32[]{:S(2)}) %collective-permute-start.4) | collective-permute-done | bytes 8224 | tf_op jit(solution)/shard_map/ppermute | solution.py:371
  104.7 0.0 copy-start.3
  104.7 0.0 collective-permute-done.3.og_ref
  104.7 0.0 copy-start.2
  104.7 0.6 copy-done.3
  105.3 0.2 copy-done.2
  105.5 2.8 %shard_map.67 = bf16[256,768]{1,0:T(8,128)(2,1)} custom-call(f32[512,256]{1,0:T(8,128)} %get-tuple-element.15.o_ref, f32[8,256]{1,0:T(8,128)} %get-tuple-element.16.st_ref, f32[512,256]{1,0:T(8,128)} %copy-done.2, f32[8,256]{1,0:T(8,128)} %copy-done.3, bf16[256,768]{1,0:T(8,128)(2,1)} %add_convert_fusion.h_ref.hid_ref, bf16[512,768]{1,0:T(8,128)(2,1)} %wo_ref.1), custom_call_target="tpu_custom_call" | custom-call | tf_op jit(solution)/shard_map/pallas_call | solution.py:159
Async XLA Ops:
  0.8 7.1 %collective-permute-start = (bf16[4,1536]{1,0:T(4,128)(2,1)S(1)}, bf16[4,1536]{1,0:T(4,128)(2,1)S(1)}, u32[]{:S(2)}, u32[]{:S(2)}) collective-permute-start(bf16[4,1536]{1,0:T(4,128)(2,1)S(1)} %get-tuple-element.19), channel_id=1, source_target_pairs={{0,4},{4,8},{8,12},{12,16},{16,20},{20,24},{24,28},{28,32},{32,36}... | collective-permute-start | bytes 36872 | tf_op jit(solution)/shard_map/ppermute | solution.py:20
  5.3 5.0 %collective-permute-start.1 = (bf16[4,1536]{1,0:T(4,128)(2,1)S(1)}, bf16[4,1536]{1,0:T(4,128)(2,1)S(1)}, u32[]{:S(2)}, u32[]{:S(2)}) collective-permute-start(bf16[4,1536]{1,0:T(4,128)(2,1)S(1)} %get-tuple-element.20), channel_id=1, source_target_pairs={{4,0},{8,4},{12,8},{16,12},{20,16},{24,20},{28,24},{32,28},{36,32}... | collective-permute-start | bytes 36872 | tf_op jit(solution)/shard_map/ppermute | solution.py:21
  11.6 4.4 %copy-start = (bf16[5,1536,768]{2,1,0:T(8,128)(2,1)S(1)}, bf16[5,1536,768]{2,1,0:T(8,128)(2,1)}, u32[]{:S(2)}) copy-start(bf16[5,1536,768]{2,1,0:T(8,128)(2,1)} %w_ref.1) | copy-start | bytes 35389444
  16.0 5.1 %copy-start.1 = (bf16[5,768,768]{2,1,0:T(8,128)(2,1)S(1)}, bf16[5,768,768]{2,1,0:T(8,128)(2,1)}, u32[]{:S(2)}) copy-start(bf16[5,768,768]{2,1,0:T(8,128)(2,1)} %param.8) | copy-start | bytes 17694724
  72.7 4.3 %collective-permute-start.2 = (bf16[512,256]{1,0:T(8,128)(2,1)}, bf16[512,256]{1,0:T(8,128)(2,1)S(1)}, u32[]{:S(2)}, u32[]{:S(2)}) collective-permute-start(bf16[512,256]{1,0:T(8,128)(2,1)} %get-tuple-element.12.qa_ref), channel_id=1, source_target_pairs={{0,4},{4,0},{1,5},{5,1},{2,6},{6,2},{3,7},{7,3},{8,12},{12,8},{9,1... | collective-permute-start | bytes 786440 | tf_op jit(solution)/shard_map/ppermute | solution.py:367
  77.0 0.7 copy-start.4
  102.6 2.2 %collective-permute-start.3 = (f32[512,256]{1,0:T(8,128)}, f32[512,256]{1,0:T(8,128)S(1)}, u32[]{:S(2)}, u32[]{:S(2)}) collective-permute-start(f32[512,256]{1,0:T(8,128)} %get-tuple-element.17), channel_id=1, source_target_pairs={{0,4},{4,0},{1,5},{5,1},{2,6},{6,2},{3,7},{7,3},{8,12},{12,8},{9,1... | collective-permute-start | bytes 1572872 | tf_op jit(solution)/shard_map/ppermute | solution.py:371
  103.0 1.8 %collective-permute-start.4 = (f32[8,256]{1,0:T(8,128)}, f32[8,256]{1,0:T(8,128)S(1)}, u32[]{:S(2)}, u32[]{:S(2)}) collective-permute-start(f32[8,256]{1,0:T(8,128)} %get-tuple-element.18), channel_id=1, source_target_pairs={{0,4},{4,0},{1,5},{5,1},{2,6},{6,2},{3,7},{7,3},{8,12},{12,8},{9,1... | collective-permute-start | bytes 24584 | tf_op jit(solution)/shard_map/ppermute | solution.py:371
  104.7 0.6 copy-start.3
  104.7 0.8 copy-start.2

commit v14 on v13

--- a/solution.py
+++ b/solution.py
@@ -217,24 +217,31 @@
         view = out_ref.at[slot(stream, a, b), stream]
         return view if lo is None else view.at[pl.ds(lo, q)]
 
+    def send_row(st, k):
+        a0, b0 = own[st]
+        src = x_ref.at[st] if k == 0 else part(st, a0 + k, b0)
+        send((st, 3, 1, k), src, part(st, a0 + k, b0), slot(st, a0, b0 + 1))
+        send((st, 3, -1, k), src, part(st, a0 + k, b0), slot(st, a0, b0 - 1))
+
     for st in range(2):
         a0, b0 = own[st]
         send((st, 1, 1), x_ref.at[st], part(st, a0, b0), slot(st, a0 + 1, b0))
         send((st, 1, -1), x_ref.at[st], part(st, a0, b0), slot(st, a0 - 1, b0))
+        send_row(st, 0)
     for st in range(2):
         a0, b0 = own[st]
         recv((st, 1, 1), part(st, a0 - 1, b0), slot(st, a0 - 1, b0))
         recv((st, 1, -1), part(st, a0 + 1, b0), slot(st, a0 + 1, b0))
         send((st, 2, 1), part(st, a0 - 1, b0, 0), part(st, a0 - 1, b0, 0), slot(st, a0 + 1, b0))
         send((st, 2, -1), part(st, a0 + 1, b0, q), part(st, a0 + 1, b0, q), slot(st, a0 - 1, b0))
+        send_row(st, 1)
+        send_row(st, side - 1)
     for st in range(2):
         a0, b0 = own[st]
         recv((st, 2, 1), part(st, a0 - 2, b0, 0), slot(st, a0 - 1, b0))
         recv((st, 2, -1), part(st, a0 + 2, b0, q), slot(st, a0 + 1, b0))
-        for k in range(side):
-            src = x_ref.at[st] if k == 0 else part(st, a0 + k, b0)
-            send((st, 3, 1, k), src, part(st, a0 + k, b0), slot(st, a0, b0 + 1))
-            send((st, 3, -1, k), src, part(st, a0 + k, b0), slot(st, a0, b0 - 1))
+        for k in range(2, side - 1):
+            send_row(st, k)
     for st in range(2):
         a0, b0 = own[st]
         for k in range(side):

time: 109 us -> 104 us (0.954)
  starting transfers between devices: 9.87 us -> 7.31 us
  Pallas kernels: 80.5 us -> 78.5 us
    ppermute x1, starting transfers between devices: 2.93 us -> 0.37 us  [body(): qt_other = lax.ppermute(qt_own, 'core', swap)]
    pallas_call x1, Pallas kernels: 47.7 us -> 45.8 us  [gather_rows(): pl.pallas_call(functools.partial(ring_gather_kernel, side, heads, head_si...]
where the time goes in v14:
time: 104 us
  Pallas kernels  78.5 us (75%)
  starting transfers between devices  7.31 us (7%)
  local copies, waits for them, and re-layouts  7.27 us (7%)
  waiting for transfers between devices  5.51 us (5%)
  matrix products  3.24 us (3%)
  other arithmetic  1.99 us (2%)
    pallas_call x1, Pallas kernels, gather_rows(): pl.pallas_call(functools.partial(ring_gather_kernel, side, heads, head_si...  45.8 us
    pallas_call x1, Pallas kernels, attend_partial(): pl.pallas_call(functools.partial(attend_kernel, heads, head_size, nk), gr...  24.9 us
    unnamed x10, local copies, waits for them, and re-layouts  5.86 us
    pallas_call x1, Pallas kernels, conv_gelu(): pl.pallas_call(functools.partial(conv_gelu_kernel, taps, rows, halo), gri...  5.06 us
    ppermute x1, starting transfers between devices, padded_2(): lax.ppermute(lax.slice_in_dim(block, block.shape[0] - width, None, axis=0...  4.51 us
    pallas_call x1, Pallas kernels, finish(): pl.pallas_call(functools.partial(finish_kernel, heads, head_size), grid=(...  2.81 us
    dot_general x4, matrix products, convolve(): jnp.dot(padded[offset:offset + row_count], weight[offset], preferred_elem...  2.75 us
    ppermute x1, waiting for transfers between devices, padded_2(): lax.ppermute(lax.slice_in_dim(block, 0, width, axis=0), SEQ_AXES, backward)  2.42 us
  transfers between devices with their start and end apart: 5, of which 3 were waited for; matrix products, arithmetic and copies ran while one was open for 1% of the time, Pallas kernels for 0%

profile of v14, /device:TPU:1, one launch (start us, length us, event | category | flops | bytes accessed | tf_op | source)
XLA Modules:
  0.0 103.9 jit_solution(16865879749427109909)
XLA Ops:
  0.0 0.8 fusion.20
  0.8 4.5 %collective-permute-start = (bf16[4,1536]{1,0:T(4,128)(2,1)S(1)}, bf16[4,1536]{1,0:T(4,128)(2,1)S(1)}, u32[]{:S(2)}, u32[]{:S(2)}) collective-permute-start(bf16[4,1536]{1,0:T(4,128)(2,1)S(1)} %get-tuple-element.19), channel_id=1, source_target_pairs={{0,4},{4,8},{8,12},{12,16},{16,20},{20,24},{24,28},{28,32},{32,36}... | collective-permute-start | bytes 36872 | tf_op jit(solution)/shard_map/ppermute | solution.py:20
  5.3 1.9 %collective-permute-start.1 = (bf16[4,1536]{1,0:T(4,128)(2,1)S(1)}, bf16[4,1536]{1,0:T(4,128)(2,1)S(1)}, u32[]{:S(2)}, u32[]{:S(2)}) collective-permute-start(bf16[4,1536]{1,0:T(4,128)(2,1)S(1)} %get-tuple-element.20), channel_id=1, source_target_pairs={{4,0},{8,4},{12,8},{16,12},{20,16},{24,20},{28,24},{32,28},{36,32}... | collective-permute-start | bytes 36872 | tf_op jit(solution)/shard_map/ppermute | solution.py:21
  7.2 0.7 broadcast_multiply_fusion
  7.9 0.0 collective-permute-done
  7.9 2.4 %collective-permute-done.1 = bf16[4,1536]{1,0:T(4,128)(2,1)S(1)} collective-permute-done((bf16[4,1536]{1,0:T(4,128)(2,1)S(1)}, bf16[4,1536]{1,0:T(4,128)(2,1)S(1)}, u32[]{:S(2)}, u32[]{:S(2)}) %collective-permute-start.1) | collective-permute-done | bytes 12320 | tf_op jit(solution)/shard_map/ppermute | solution.py:21
  10.3 1.3 %pad_maximum_fusion.x_ref = bf16[264,1536]{1,0:T(8,128)(2,1)S(1)} fusion(bf16[4,1536]{1,0:T(4,128)(2,1)S(1)} %collective-permute-done.1, bf16[256,1536]{1,0:T(8,128)(2,1)} %param.6, bf16[4,1536]{1,0:T(4,128)(2,1)S(1)} %collective-permute-done), kind=kLoop, calls=%fused_computation.15 | loop fusion | flops 2433024 | bytes 1622016 | tf_op jit(solution)/shard_map/concatenate | solution.py:24
  11.6 0.0 copy-start
  11.7 4.3 %copy-done = bf16[5,1536,768]{2,1,0:T(8,128)(2,1)S(1)} copy-done((bf16[5,1536,768]{2,1,0:T(8,128)(2,1)S(1)}, bf16[5,1536,768]{2,1,0:T(8,128)(2,1)}, u32[]{:S(2)}) %copy-start) | copy-done | bytes 11796504
  16.0 0.0 copy-start.1
  16.0 5.1 %shard_map.64 = bf16[260,768]{1,0:T(8,128)(2,1)S(1)} custom-call(bf16[264,1536]{1,0:T(8,128)(2,1)S(1)} %pad_maximum_fusion.x_ref, bf16[5,1536,768]{2,1,0:T(8,128)(2,1)S(1)} %copy-done), custom_call_target="tpu_custom_call" | custom-call | flops 3114270720 | bytes 13006848 | tf_op jit(solution)/shard_map/pallas_call | solution.py:339
  21.1 0.0 copy-done.1
  21.1 0.5 fusion.3
  21.6 0.5 convolution_add_fusion.3
  22.1 0.5 convolution_add_fusion.2
  22.6 0.5 convolution_add_fusion.1
  23.0 1.3 %add_convert_fusion.h_ref.hid_ref = bf16[256,768]{1,0:T(8,128)(2,1)} fusion(f32[256,768]{1,0:T(8,128)S(1)} %convolution_add_fusion.1, bf16[5,768,768]{2,1,0:T(8,128)(2,1)S(1)} %copy-done.1, bf16[260,768]{1,0:T(8,128)(2,1)S(1)} %shard_map.64), kind=kOutput, calls=%fused_computation.16 | convolution fusion | flops 302776320 | bytes 3145728 | tf_op jit(solution)/shard_map/dot_general | solution.py:30
  24.3 0.6 broadcast_in_dim.3
  25.0 45.8 %shard_map.65 = (bf16[16,2,128,768]{3,2,1,0:T(8,128)(2,1)}, bf16[512,256]{1,0:T(8,128)(2,1)}, bf16[512,768]{1,0:T(8,128)(2,1)}) custom-call(bf16[2,128,768]{2,1,0:T(8,128)(2,1)} %bitcast.20, bf16[256,768]{1,0:T(8,128)(2,1)} %add_convert_fusion.h_ref.hid_ref, bf16[768,1536]{1,0:T(8,128)(2,1)} %wk_ref.1, bf16[768,1536]{1,0:T(8,128)(2,1)} %wk_ref.1, ...), custom_call_target="tpu_custom_call" | custom-call | tf_op jit(solution)/shard_map/pallas_call | solution.py:280
  70.8 0.4 collective-permute-start.2
  71.1 1.5 %collective-permute-done.2.qb_ref = bf16[512,256]{1,0:T(8,128)(2,1)S(1)} collective-permute-done((bf16[512,256]{1,0:T(8,128)(2,1)}, bf16[512,256]{1,0:T(8,128)(2,1)S(1)}, u32[]{:S(2)}, u32[]{:S(2)}) %collective-permute-start.2) | collective-permute-done | bytes 262176 | tf_op jit(solution)/shard_map/ppermute | solution.py:374
  72.6 0.0 copy-start.4
  72.6 0.7 copy-done.4
  73.3 24.9 %shard_map.66 = (f32[512,256]{1,0:T(8,128)}, f32[8,256]{1,0:T(8,128)}, f32[512,256]{1,0:T(8,128)}, f32[8,256]{1,0:T(8,128)}) custom-call(bf16[512,256]{1,0:T(8,128)(2,1)} %get-tuple-element.12.qa_ref, bf16[512,256]{1,0:T(8,128)(2,1)} %copy-done.4, bf16[4096,768]{1,0:T(8,128)(2,1)} %bitcast.22, bf16[768,1536]{1,0:T(8,128)(2,1)} %wk_ref.1, ...), custom_call_target="tpu_custom_call" | custom-call | flops 10737418240 | bytes 8388608 | tf_op jit(solution)/shard_map/pallas_call | solution.py:102
  98.2 0.3 collective-permute-start.3
  98.4 0.2 collective-permute-start.4
  98.7 1.6 %collective-permute-done.4.sg_ref = f32[8,256]{1,0:T(8,128)S(1)} collective-permute-done((f32[8,256]{1,0:T(8,128)}, f32[8,256]{1,0:T(8,128)S(1)}, u32[]{:S(2)}, u32[]{:S(2)}) %collective-permute-start.4) | collective-permute-done | bytes 8224 | tf_op jit(solution)/shard_map/ppermute | solution.py:378
  100.3 0.0 copy-start.3
  100.3 0.0 collective-permute-done.3.og_ref
  100.3 0.0 copy-start.2
  100.3 0.6 copy-done.3
  100.9 0.2 copy-done.2
  101.1 2.8 %shard_map.67 = bf16[256,768]{1,0:T(8,128)(2,1)} custom-call(f32[512,256]{1,0:T(8,128)} %get-tuple-element.15.o_ref, f32[8,256]{1,0:T(8,128)} %get-tuple-element.16.st_ref, f32[512,256]{1,0:T(8,128)} %copy-done.2, f32[8,256]{1,0:T(8,128)} %copy-done.3, bf16[256,768]{1,0:T(8,128)(2,1)} %add_convert_fusion.h_ref.hid_ref, bf16[512,768]{1,0:T(8,128)(2,1)} %wo_ref.1), custom_call_target="tpu_custom_call" | custom-call | tf_op jit(solution)/shard_map/pallas_call | solution.py:159
Async XLA Ops:
  0.8 7.1 %collective-permute-start = (bf16[4,1536]{1,0:T(4,128)(2,1)S(1)}, bf16[4,1536]{1,0:T(4,128)(2,1)S(1)}, u32[]{:S(2)}, u32[]{:S(2)}) collective-permute-start(bf16[4,1536]{1,0:T(4,128)(2,1)S(1)} %get-tuple-element.19), channel_id=1, source_target_pairs={{0,4},{4,8},{8,12},{12,16},{16,20},{20,24},{24,28},{28,32},{32,36}... | collective-permute-start | bytes 36872 | tf_op jit(solution)/shard_map/ppermute | solution.py:20
  5.3 5.0 %collective-permute-start.1 = (bf16[4,1536]{1,0:T(4,128)(2,1)S(1)}, bf16[4,1536]{1,0:T(4,128)(2,1)S(1)}, u32[]{:S(2)}, u32[]{:S(2)}) collective-permute-start(bf16[4,1536]{1,0:T(4,128)(2,1)S(1)} %get-tuple-element.20), channel_id=1, source_target_pairs={{4,0},{8,4},{12,8},{16,12},{20,16},{24,20},{28,24},{32,28},{36,32}... | collective-permute-start | bytes 36872 | tf_op jit(solution)/shard_map/ppermute | solution.py:21
  11.6 4.4 %copy-start = (bf16[5,1536,768]{2,1,0:T(8,128)(2,1)S(1)}, bf16[5,1536,768]{2,1,0:T(8,128)(2,1)}, u32[]{:S(2)}) copy-start(bf16[5,1536,768]{2,1,0:T(8,128)(2,1)} %w_ref.1) | copy-start | bytes 35389444
  16.0 5.1 %copy-start.1 = (bf16[5,768,768]{2,1,0:T(8,128)(2,1)S(1)}, bf16[5,768,768]{2,1,0:T(8,128)(2,1)}, u32[]{:S(2)}) copy-start(bf16[5,768,768]{2,1,0:T(8,128)(2,1)} %param.8) | copy-start | bytes 17694724
  70.8 1.8 %collective-permute-start.2 = (bf16[512,256]{1,0:T(8,128)(2,1)}, bf16[512,256]{1,0:T(8,128)(2,1)S(1)}, u32[]{:S(2)}, u32[]{:S(2)}) collective-permute-start(bf16[512,256]{1,0:T(8,128)(2,1)} %get-tuple-element.12.qa_ref), channel_id=1, source_target_pairs={{0,4},{4,0},{1,5},{5,1},{2,6},{6,2},{3,7},{7,3},{8,12},{12,8},{9,1... | collective-permute-start | bytes 786440 | tf_op jit(solution)/shard_map/ppermute | solution.py:374
  72.6 0.7 copy-start.4
  98.2 2.1 %collective-permute-start.3 = (f32[512,256]{1,0:T(8,128)}, f32[512,256]{1,0:T(8,128)S(1)}, u32[]{:S(2)}, u32[]{:S(2)}) collective-permute-start(f32[512,256]{1,0:T(8,128)} %get-tuple-element.17), channel_id=1, source_target_pairs={{0,4},{4,0},{1,5},{5,1},{2,6},{6,2},{3,7},{7,3},{8,12},{12,8},{9,1... | collective-permute-start | bytes 1572872 | tf_op jit(solution)/shard_map/ppermute | solution.py:378
  98.4 1.8 %collective-permute-start.4 = (f32[8,256]{1,0:T(8,128)}, f32[8,256]{1,0:T(8,128)S(1)}, u32[]{:S(2)}, u32[]{:S(2)}) collective-permute-start(f32[8,256]{1,0:T(8,128)} %get-tuple-element.18), channel_id=1, source_target_pairs={{0,4},{4,0},{1,5},{5,1},{2,6},{6,2},{3,7},{7,3},{8,12},{12,8},{9,1... | collective-permute-start | bytes 24584 | tf_op jit(solution)/shard_map/ppermute | solution.py:378
  100.3 0.6 copy-start.3
  100.3 0.8 copy-start.2

commit v15 on v14

--- a/solution.py
+++ b/solution.py
@@ -236,19 +236,6 @@
         send((st, 2, -1), part(st, a0 + 1, b0, q), part(st, a0 + 1, b0, q), slot(st, a0 - 1, b0))
         send_row(st, 1)
         send_row(st, side - 1)
-    for st in range(2):
-        a0, b0 = own[st]
-        recv((st, 2, 1), part(st, a0 - 2, b0, 0), slot(st, a0 - 1, b0))
-        recv((st, 2, -1), part(st, a0 + 2, b0, q), slot(st, a0 + 1, b0))
-        for k in range(2, side - 1):
-            send_row(st, k)
-    for st in range(2):
-        a0, b0 = own[st]
-        for k in range(side):
-            recv((st, 3, 1, k), part(st, a0 + k, b0 - 1), slot(st, a0, b0 - 1))
-            recv((st, 3, -1, k), part(st, a0 + k, b0 + 1), slot(st, a0, b0 + 1))
-            send((st, 4, 1, k), part(st, a0 + k, b0 - 1, 0), part(st, a0 + k, b0 - 1, 0), slot(st, a0, b0 + 1))
-            send((st, 4, -1, k), part(st, a0 + k, b0 + 1, q), part(st, a0 + k, b0 + 1, q), slot(st, a0, b0 - 1))
     proj = jnp.dot(h_ref[...], wq_ref[...], preferred_element_type=jnp.float32)
     scale = scale_ref[...]
     normed = []
@@ -259,6 +246,19 @@
         normed.append(part_q * lax.rsqrt(mean_sq + 1e-06) * scale[:, cols])
     qt_ref[...] = jnp.concatenate(normed, axis=1).T.astype(qt_ref.dtype)
     wvt_ref[...] = wv_ref[...].astype(jnp.float32).T.astype(wvt_ref.dtype)
+    for st in range(2):
+        a0, b0 = own[st]
+        recv((st, 2, 1), part(st, a0 - 2, b0, 0), slot(st, a0 - 1, b0))
+        recv((st, 2, -1), part(st, a0 + 2, b0, q), slot(st, a0 + 1, b0))
+        for k in range(2, side - 1):
+            send_row(st, k)
+    for st in range(2):
+        a0, b0 = own[st]
+        for k in range(side):
+            recv((st, 3, 1, k), part(st, a0 + k, b0 - 1), slot(st, a0, b0 - 1))
+            recv((st, 3, -1, k), part(st, a0 + k, b0 + 1), slot(st, a0, b0 + 1))
+            send((st, 4, 1, k), part(st, a0 + k, b0 - 1, 0), part(st, a0 + k, b0 - 1, 0), slot(st, a0, b0 + 1))
+            send((st, 4, -1, k), part(st, a0 + k, b0 + 1, q), part(st, a0 + k, b0 + 1, q), slot(st, a0, b0 - 1))
     for st in range(2):
         a0, b0 = own[st]
         for k in range(side):

time: 104 us -> 104 us (level)
  no operation moved by 1% of the time
where the time goes in v15:
time: 104 us
  Pallas kernels  78.5 us (75%)
  starting transfers between devices  7.31 us (7%)
  local copies, waits for them, and re-layouts  7.27 us (7%)
  waiting for transfers between devices  5.51 us (5%)
  matrix products  3.24 us (3%)
  other arithmetic  1.99 us (2%)
    pallas_call x1, Pallas kernels, gather_rows(): pl.pallas_call(functools.partial(ring_gather_kernel, side, heads, head_si...  45.8 us
    pallas_call x1, Pallas kernels, attend_partial(): pl.pallas_call(functools.partial(attend_kernel, heads, head_size, nk), gr...  24.9 us
    unnamed x10, local copies, waits for them, and re-layouts  5.86 us
    pallas_call x1, Pallas kernels, conv_gelu(): pl.pallas_call(functools.partial(conv_gelu_kernel, taps, rows, halo), gri...  5.06 us
    ppermute x1, starting transfers between devices, padded_2(): lax.ppermute(lax.slice_in_dim(block, block.shape[0] - width, None, axis=0...  4.51 us
    pallas_call x1, Pallas kernels, finish(): pl.pallas_call(functools.partial(finish_kernel, heads, head_size), grid=(...  2.81 us
    dot_general x4, matrix products, convolve(): jnp.dot(padded[offset:offset + row_count], weight[offset], preferred_elem...  2.75 us
    ppermute x1, waiting for transfers between devices, padded_2(): lax.ppermute(lax.slice_in_dim(block, 0, width, axis=0), SEQ_AXES, backward)  2.42 us
  transfers between devices with their start and end apart: 5, of which 3 were waited for; matrix products, arithmetic and copies ran while one was open for 1% of the time, Pallas kernels for 0%

profile of v15, /device:TPU:1, one launch (start us, length us, event | category | flops | bytes accessed | tf_op | source)
XLA Modules:
  0.0 103.9 jit_solution(16717761775425420946)
XLA Ops:
  0.0 0.8 fusion.20
  0.8 4.5 %collective-permute-start = (bf16[4,1536]{1,0:T(4,128)(2,1)S(1)}, bf16[4,1536]{1,0:T(4,128)(2,1)S(1)}, u32[]{:S(2)}, u32[]{:S(2)}) collective-permute-start(bf16[4,1536]{1,0:T(4,128)(2,1)S(1)} %get-tuple-element.19), channel_id=1, source_target_pairs={{0,4},{4,8},{8,12},{12,16},{16,20},{20,24},{24,28},{28,32},{32,36}... | collective-permute-start | bytes 36872 | tf_op jit(solution)/shard_map/ppermute | solution.py:20
  5.3 1.9 %collective-permute-start.1 = (bf16[4,1536]{1,0:T(4,128)(2,1)S(1)}, bf16[4,1536]{1,0:T(4,128)(2,1)S(1)}, u32[]{:S(2)}, u32[]{:S(2)}) collective-permute-start(bf16[4,1536]{1,0:T(4,128)(2,1)S(1)} %get-tuple-element.20), channel_id=1, source_target_pairs={{4,0},{8,4},{12,8},{16,12},{20,16},{24,20},{28,24},{32,28},{36,32}... | collective-permute-start | bytes 36872 | tf_op jit(solution)/shard_map/ppermute | solution.py:21
  7.2 0.7 broadcast_multiply_fusion
  7.9 0.0 collective-permute-done
  7.9 2.4 %collective-permute-done.1 = bf16[4,1536]{1,0:T(4,128)(2,1)S(1)} collective-permute-done((bf16[4,1536]{1,0:T(4,128)(2,1)S(1)}, bf16[4,1536]{1,0:T(4,128)(2,1)S(1)}, u32[]{:S(2)}, u32[]{:S(2)}) %collective-permute-start.1) | collective-permute-done | bytes 12320 | tf_op jit(solution)/shard_map/ppermute | solution.py:21
  10.3 1.3 %pad_maximum_fusion.x_ref = bf16[264,1536]{1,0:T(8,128)(2,1)S(1)} fusion(bf16[4,1536]{1,0:T(4,128)(2,1)S(1)} %collective-permute-done.1, bf16[256,1536]{1,0:T(8,128)(2,1)} %param.6, bf16[4,1536]{1,0:T(4,128)(2,1)S(1)} %collective-permute-done), kind=kLoop, calls=%fused_computation.15 | loop fusion | flops 2433024 | bytes 1622016 | tf_op jit(solution)/shard_map/concatenate | solution.py:24
  11.6 0.0 copy-start
  11.7 4.3 %copy-done = bf16[5,1536,768]{2,1,0:T(8,128)(2,1)S(1)} copy-done((bf16[5,1536,768]{2,1,0:T(8,128)(2,1)S(1)}, bf16[5,1536,768]{2,1,0:T(8,128)(2,1)}, u32[]{:S(2)}) %copy-start) | copy-done | bytes 11796504
  16.0 0.0 copy-start.1
  16.0 5.1 %shard_map.64 = bf16[260,768]{1,0:T(8,128)(2,1)S(1)} custom-call(bf16[264,1536]{1,0:T(8,128)(2,1)S(1)} %pad_maximum_fusion.x_ref, bf16[5,1536,768]{2,1,0:T(8,128)(2,1)S(1)} %copy-done), custom_call_target="tpu_custom_call" | custom-call | flops 3114270720 | bytes 13006848 | tf_op jit(solution)/shard_map/pallas_call | solution.py:339
  21.1 0.0 copy-done.1
  21.1 0.5 fusion.3
  21.6 0.5 convolution_add_fusion.3
  22.1 0.5 convolution_add_fusion.2
  22.6 0.5 convolution_add_fusion.1
  23.0 1.3 %add_convert_fusion.h_ref.hid_ref = bf16[256,768]{1,0:T(8,128)(2,1)} fusion(f32[256,768]{1,0:T(8,128)S(1)} %convolution_add_fusion.1, bf16[5,768,768]{2,1,0:T(8,128)(2,1)S(1)} %copy-done.1, bf16[260,768]{1,0:T(8,128)(2,1)S(1)} %shard_map.64), kind=kOutput, calls=%fused_computation.16 | convolution fusion | flops 302776320 | bytes 3145728 | tf_op jit(solution)/shard_map/dot_general | solution.py:30
  24.3 0.6 broadcast_in_dim.3
  25.0 45.8 %shard_map.65 = (bf16[16,2,128,768]{3,2,1,0:T(8,128)(2,1)}, bf16[512,256]{1,0:T(8,128)(2,1)}, bf16[512,768]{1,0:T(8,128)(2,1)}) custom-call(bf16[2,128,768]{2,1,0:T(8,128)(2,1)} %bitcast.20, bf16[256,768]{1,0:T(8,128)(2,1)} %add_convert_fusion.h_ref.hid_ref, bf16[768,1536]{1,0:T(8,128)(2,1)} %wk_ref.1, bf16[768,1536]{1,0:T(8,128)(2,1)} %wk_ref.1, ...), custom_call_target="tpu_custom_call" | custom-call | tf_op jit(solution)/shard_map/pallas_call | solution.py:280
  70.8 0.4 collective-permute-start.2
  71.1 1.5 %collective-permute-done.2.qb_ref = bf16[512,256]{1,0:T(8,128)(2,1)S(1)} collective-permute-done((bf16[512,256]{1,0:T(8,128)(2,1)}, bf16[512,256]{1,0:T(8,128)(2,1)S(1)}, u32[]{:S(2)}, u32[]{:S(2)}) %collective-permute-start.2) | collective-permute-done | bytes 262176 | tf_op jit(solution)/shard_map/ppermute | solution.py:374
  72.6 0.0 copy-start.4
  72.6 0.7 copy-done.4
  73.3 24.9 %shard_map.66 = (f32[512,256]{1,0:T(8,128)}, f32[8,256]{1,0:T(8,128)}, f32[512,256]{1,0:T(8,128)}, f32[8,256]{1,0:T(8,128)}) custom-call(bf16[512,256]{1,0:T(8,128)(2,1)} %get-tuple-element.12.qa_ref, bf16[512,256]{1,0:T(8,128)(2,1)} %copy-done.4, bf16[4096,768]{1,0:T(8,128)(2,1)} %bitcast.22, bf16[768,1536]{1,0:T(8,128)(2,1)} %wk_ref.1, ...), custom_call_target="tpu_custom_call" | custom-call | flops 10737418240 | bytes 8388608 | tf_op jit(solution)/shard_map/pallas_call | solution.py:102
  98.2 0.3 collective-permute-start.3
  98.4 0.2 collective-permute-start.4
  98.7 1.6 %collective-permute-done.4.sg_ref = f32[8,256]{1,0:T(8,128)S(1)} collective-permute-done((f32[8,256]{1,0:T(8,128)}, f32[8,256]{1,0:T(8,128)S(1)}, u32[]{:S(2)}, u32[]{:S(2)}) %collective-permute-start.4) | collective-permute-done | bytes 8224 | tf_op jit(solution)/shard_map/ppermute | solution.py:378
  100.3 0.0 copy-start.3
  100.3 0.0 collective-permute-done.3.og_ref
  100.3 0.0 copy-start.2
  100.3 0.6 copy-done.3
  100.9 0.2 copy-done.2
  101.1 2.8 %shard_map.67 = bf16[256,768]{1,0:T(8,128)(2,1)} custom-call(f32[512,256]{1,0:T(8,128)} %get-tuple-element.15.o_ref, f32[8,256]{1,0:T(8,128)} %get-tuple-element.16.st_ref, f32[512,256]{1,0:T(8,128)} %copy-done.2, f32[8,256]{1,0:T(8,128)} %copy-done.3, bf16[256,768]{1,0:T(8,128)(2,1)} %add_convert_fusion.h_ref.hid_ref, bf16[512,768]{1,0:T(8,128)(2,1)} %wo_ref.1), custom_call_target="tpu_custom_call" | custom-call | tf_op jit(solution)/shard_map/pallas_call | solution.py:159
Async XLA Ops:
  0.8 7.1 %collective-permute-start = (bf16[4,1536]{1,0:T(4,128)(2,1)S(1)}, bf16[4,1536]{1,0:T(4,128)(2,1)S(1)}, u32[]{:S(2)}, u32[]{:S(2)}) collective-permute-start(bf16[4,1536]{1,0:T(4,128)(2,1)S(1)} %get-tuple-element.19), channel_id=1, source_target_pairs={{0,4},{4,8},{8,12},{12,16},{16,20},{20,24},{24,28},{28,32},{32,36}... | collective-permute-start | bytes 36872 | tf_op jit(solution)/shard_map/ppermute | solution.py:20
  5.3 5.0 %collective-permute-start.1 = (bf16[4,1536]{1,0:T(4,128)(2,1)S(1)}, bf16[4,1536]{1,0:T(4,128)(2,1)S(1)}, u32[]{:S(2)}, u32[]{:S(2)}) collective-permute-start(bf16[4,1536]{1,0:T(4,128)(2,1)S(1)} %get-tuple-element.20), channel_id=1, source_target_pairs={{4,0},{8,4},{12,8},{16,12},{20,16},{24,20},{28,24},{32,28},{36,32}... | collective-permute-start | bytes 36872 | tf_op jit(solution)/shard_map/ppermute | solution.py:21
  11.6 4.4 %copy-start = (bf16[5,1536,768]{2,1,0:T(8,128)(2,1)S(1)}, bf16[5,1536,768]{2,1,0:T(8,128)(2,1)}, u32[]{:S(2)}) copy-start(bf16[5,1536,768]{2,1,0:T(8,128)(2,1)} %w_ref.1) | copy-start | bytes 35389444
  16.0 5.1 %copy-start.1 = (bf16[5,768,768]{2,1,0:T(8,128)(2,1)S(1)}, bf16[5,768,768]{2,1,0:T(8,128)(2,1)}, u32[]{:S(2)}) copy-start(bf16[5,768,768]{2,1,0:T(8,128)(2,1)} %param.8) | copy-start | bytes 17694724
  70.8 1.8 %collective-permute-start.2 = (bf16[512,256]{1,0:T(8,128)(2,1)}, bf16[512,256]{1,0:T(8,128)(2,1)S(1)}, u32[]{:S(2)}, u32[]{:S(2)}) collective-permute-start(bf16[512,256]{1,0:T(8,128)(2,1)} %get-tuple-element.12.qa_ref), channel_id=1, source_target_pairs={{0,4},{4,0},{1,5},{5,1},{2,6},{6,2},{3,7},{7,3},{8,12},{12,8},{9,1... | collective-permute-start | bytes 786440 | tf_op jit(solution)/shard_map/ppermute | solution.py:374
  72.6 0.7 copy-start.4
  98.2 2.1 %collective-permute-start.3 = (f32[512,256]{1,0:T(8,128)}, f32[512,256]{1,0:T(8,128)S(1)}, u32[]{:S(2)}, u32[]{:S(2)}) collective-permute-start(f32[512,256]{1,0:T(8,128)} %get-tuple-element.17), channel_id=1, source_target_pairs={{0,4},{4,0},{1,5},{5,1},{2,6},{6,2},{3,7},{7,3},{8,12},{12,8},{9,1... | collective-permute-start | bytes 1572872 | tf_op jit(solution)/shard_map/ppermute | solution.py:378
  98.4 1.8 %collective-permute-start.4 = (f32[8,256]{1,0:T(8,128)}, f32[8,256]{1,0:T(8,128)S(1)}, u32[]{:S(2)}, u32[]{:S(2)}) collective-permute-start(f32[8,256]{1,0:T(8,128)} %get-tuple-element.18), channel_id=1, source_target_pairs={{0,4},{4,0},{1,5},{5,1},{2,6},{6,2},{3,7},{7,3},{8,12},{12,8},{9,1... | collective-permute-start | bytes 24584 | tf_op jit(solution)/shard_map/ppermute | solution.py:378
  100.3 0.6 copy-start.3
  100.3 0.8 copy-start.2

commit v16 on v14

--- a/solution.py
+++ b/solution.py
@@ -93,7 +93,7 @@
             sb_ref[heads + h : heads + h + 1, :] = l_sc[h][:, own:]
 
 
-def attend_partial(qt_own, qt_other, hidden_kv, qkv_weight, wvt, heads, head_size, tk=1024):
+def attend_partial(qt_own, qt_other, hidden_kv, qkv_weight, wvt, heads, head_size, tk=2048):
     width, own = qt_own.shape
     q_rows = 2 * own
     k_rows, channels = hidden_kv.shape

time: 104 us -> 102 us (0.981)
  Pallas kernels: 78.5 us -> 76.5 us
    pallas_call x1, Pallas kernels: 24.9 us -> 22.8 us  [attend_partial(): pl.pallas_call(functools.partial(attend_kernel, heads, head_size, nk), gr...]
where the time goes in v16:
time: 102 us
  Pallas kernels  76.5 us (75%)
  starting transfers between devices  7.51 us (7%)
  local copies, waits for them, and re-layouts  7.27 us (7%)
  waiting for transfers between devices  5.48 us (5%)
  matrix products  3.24 us (3%)
  other arithmetic  1.99 us (2%)
    pallas_call x1, Pallas kernels, gather_rows(): pl.pallas_call(functools.partial(ring_gather_kernel, side, heads, head_si...  45.8 us
    pallas_call x1, Pallas kernels, attend_partial(): pl.pallas_call(functools.partial(attend_kernel, heads, head_size, nk), gr...  22.8 us
    unnamed x10, local copies, waits for them, and re-layouts  5.86 us
    pallas_call x1, Pallas kernels, conv_gelu(): pl.pallas_call(functools.partial(conv_gelu_kernel, taps, rows, halo), gri...  5.06 us
    ppermute x1, starting transfers between devices, padded_2(): lax.ppermute(lax.slice_in_dim(block, block.shape[0] - width, None, axis=0...  4.51 us
    pallas_call x1, Pallas kernels, finish(): pl.pallas_call(functools.partial(finish_kernel, heads, head_size), grid=(...  2.81 us
    dot_general x4, matrix products, convolve(): jnp.dot(padded[offset:offset + row_count], weight[offset], preferred_elem...  2.75 us
    ppermute x1, waiting for transfers between devices, padded_2(): lax.ppermute(lax.slice_in_dim(block, 0, width, axis=0), SEQ_AXES, backward)  2.42 us
  transfers between devices with their start and end apart: 5, of which 3 were waited for; matrix products, arithmetic and copies ran while one was open for 1% of the time, Pallas kernels for 0%

profile of v16, /device:TPU:1, one launch (start us, length us, event | category | flops | bytes accessed | tf_op | source)
XLA Modules:
  0.0 102.1 jit_solution(10416359308510672693)
XLA Ops:
  0.0 0.8 fusion.20
  0.8 4.5 %collective-permute-start = (bf16[4,1536]{1,0:T(4,128)(2,1)S(1)}, bf16[4,1536]{1,0:T(4,128)(2,1)S(1)}, u32[]{:S(2)}, u32[]{:S(2)}) collective-permute-start(bf16[4,1536]{1,0:T(4,128)(2,1)S(1)} %get-tuple-element.19), channel_id=1, source_target_pairs={{0,4},{4,8},{8,12},{12,16},{16,20},{20,24},{24,28},{28,32},{32,36}... | collective-permute-start | bytes 36872 | tf_op jit(solution)/shard_map/ppermute | solution.py:20
  5.3 1.9 %collective-permute-start.1 = (bf16[4,1536]{1,0:T(4,128)(2,1)S(1)}, bf16[4,1536]{1,0:T(4,128)(2,1)S(1)}, u32[]{:S(2)}, u32[]{:S(2)}) collective-permute-start(bf16[4,1536]{1,0:T(4,128)(2,1)S(1)} %get-tuple-element.20), channel_id=1, source_target_pairs={{4,0},{8,4},{12,8},{16,12},{20,16},{24,20},{28,24},{32,28},{36,32}... | collective-permute-start | bytes 36872 | tf_op jit(solution)/shard_map/ppermute | solution.py:21
  7.2 0.7 broadcast_multiply_fusion
  7.9 0.0 collective-permute-done
  7.9 2.4 %collective-permute-done.1 = bf16[4,1536]{1,0:T(4,128)(2,1)S(1)} collective-permute-done((bf16[4,1536]{1,0:T(4,128)(2,1)S(1)}, bf16[4,1536]{1,0:T(4,128)(2,1)S(1)}, u32[]{:S(2)}, u32[]{:S(2)}) %collective-permute-start.1) | collective-permute-done | bytes 12320 | tf_op jit(solution)/shard_map/ppermute | solution.py:21
  10.3 1.3 %pad_maximum_fusion.x_ref = bf16[264,1536]{1,0:T(8,128)(2,1)S(1)} fusion(bf16[4,1536]{1,0:T(4,128)(2,1)S(1)} %collective-permute-done.1, bf16[256,1536]{1,0:T(8,128)(2,1)} %param.6, bf16[4,1536]{1,0:T(4,128)(2,1)S(1)} %collective-permute-done), kind=kLoop, calls=%fused_computation.15 | loop fusion | flops 2433024 | bytes 1622016 | tf_op jit(solution)/shard_map/concatenate | solution.py:24
  11.6 0.0 copy-start
  11.7 4.3 %copy-done = bf16[5,1536,768]{2,1,0:T(8,128)(2,1)S(1)} copy-done((bf16[5,1536,768]{2,1,0:T(8,128)(2,1)S(1)}, bf16[5,1536,768]{2,1,0:T(8,128)(2,1)}, u32[]{:S(2)}) %copy-start) | copy-done | bytes 11796504
  16.0 0.0 copy-start.1
  16.0 5.1 %shard_map.64 = bf16[260,768]{1,0:T(8,128)(2,1)S(1)} custom-call(bf16[264,1536]{1,0:T(8,128)(2,1)S(1)} %pad_maximum_fusion.x_ref, bf16[5,1536,768]{2,1,0:T(8,128)(2,1)S(1)} %copy-done), custom_call_target="tpu_custom_call" | custom-call | flops 3114270720 | bytes 13006848 | tf_op jit(solution)/shard_map/pallas_call | solution.py:339
  21.1 0.0 copy-done.1
  21.1 0.5 fusion.3
  21.6 0.5 convolution_add_fusion.3
  22.1 0.5 convolution_add_fusion.2
  22.6 0.5 convolution_add_fusion.1
  23.1 1.3 %add_convert_fusion.h_ref.hid_ref = bf16[256,768]{1,0:T(8,128)(2,1)} fusion(f32[256,768]{1,0:T(8,128)S(1)} %convolution_add_fusion.1, bf16[5,768,768]{2,1,0:T(8,128)(2,1)S(1)} %copy-done.1, bf16[260,768]{1,0:T(8,128)(2,1)S(1)} %shard_map.64), kind=kOutput, calls=%fused_computation.16 | convolution fusion | flops 302776320 | bytes 3145728 | tf_op jit(solution)/shard_map/dot_general | solution.py:30
  24.3 0.6 broadcast_in_dim.3
  25.0 45.8 %shard_map.65 = (bf16[16,2,128,768]{3,2,1,0:T(8,128)(2,1)}, bf16[512,256]{1,0:T(8,128)(2,1)}, bf16[512,768]{1,0:T(8,128)(2,1)}) custom-call(bf16[2,128,768]{2,1,0:T(8,128)(2,1)} %bitcast.20, bf16[256,768]{1,0:T(8,128)(2,1)} %add_convert_fusion.h_ref.hid_ref, bf16[768,1536]{1,0:T(8,128)(2,1)} %wk_ref.1, bf16[768,1536]{1,0:T(8,128)(2,1)} %wk_ref.1, ...), custom_call_target="tpu_custom_call" | custom-call | tf_op jit(solution)/shard_map/pallas_call | solution.py:280
  70.8 0.6 collective-permute-start.2
  71.3 1.4 %collective-permute-done.2.qb_ref = bf16[512,256]{1,0:T(8,128)(2,1)S(1)} collective-permute-done((bf16[512,256]{1,0:T(8,128)(2,1)}, bf16[512,256]{1,0:T(8,128)(2,1)S(1)}, u32[]{:S(2)}, u32[]{:S(2)}) %collective-permute-start.2) | collective-permute-done | bytes 262176 | tf_op jit(solution)/shard_map/ppermute | solution.py:374
  72.8 0.0 copy-start.4
  72.8 0.7 copy-done.4
  73.5 22.8 %shard_map.66 = (f32[512,256]{1,0:T(8,128)}, f32[8,256]{1,0:T(8,128)}, f32[512,256]{1,0:T(8,128)}, f32[8,256]{1,0:T(8,128)}) custom-call(bf16[512,256]{1,0:T(8,128)(2,1)} %get-tuple-element.12.qa_ref, bf16[512,256]{1,0:T(8,128)(2,1)} %copy-done.4, bf16[4096,768]{1,0:T(8,128)(2,1)} %bitcast.22, bf16[768,1536]{1,0:T(8,128)(2,1)} %wk_ref.1, ...), custom_call_target="tpu_custom_call" | custom-call | flops 10737418240 | bytes 8388608 | tf_op jit(solution)/shard_map/pallas_call | solution.py:102
  96.3 0.3 collective-permute-start.3
  96.6 0.2 collective-permute-start.4
  96.8 1.6 %collective-permute-done.4.sg_ref = f32[8,256]{1,0:T(8,128)S(1)} collective-permute-done((f32[8,256]{1,0:T(8,128)}, f32[8,256]{1,0:T(8,128)S(1)}, u32[]{:S(2)}, u32[]{:S(2)}) %collective-permute-start.4) | collective-permute-done | bytes 8224 | tf_op jit(solution)/shard_map/ppermute | solution.py:378
  98.4 0.0 copy-start.3
  98.4 0.0 collective-permute-done.3.og_ref
  98.4 0.0 copy-start.2
  98.4 0.6 copy-done.3
  99.0 0.2 copy-done.2
  99.3 2.8 %shard_map.67 = bf16[256,768]{1,0:T(8,128)(2,1)} custom-call(f32[512,256]{1,0:T(8,128)} %get-tuple-element.15.o_ref, f32[8,256]{1,0:T(8,128)} %get-tuple-element.16.st_ref, f32[512,256]{1,0:T(8,128)} %copy-done.2, f32[8,256]{1,0:T(8,128)} %copy-done.3, bf16[256,768]{1,0:T(8,128)(2,1)} %add_convert_fusion.h_ref.hid_ref, bf16[512,768]{1,0:T(8,128)(2,1)} %wo_ref.1), custom_call_target="tpu_custom_call" | custom-call | tf_op jit(solution)/shard_map/pallas_call | solution.py:159
Async XLA Ops:
  0.8 7.1 %collective-permute-start = (bf16[4,1536]{1,0:T(4,128)(2,1)S(1)}, bf16[4,1536]{1,0:T(4,128)(2,1)S(1)}, u32[]{:S(2)}, u32[]{:S(2)}) collective-permute-start(bf16[4,1536]{1,0:T(4,128)(2,1)S(1)} %get-tuple-element.19), channel_id=1, source_target_pairs={{0,4},{4,8},{8,12},{12,16},{16,20},{20,24},{24,28},{28,32},{32,36}... | collective-permute-start | bytes 36872 | tf_op jit(solution)/shard_map/ppermute | solution.py:20
  5.3 5.0 %collective-permute-start.1 = (bf16[4,1536]{1,0:T(4,128)(2,1)S(1)}, bf16[4,1536]{1,0:T(4,128)(2,1)S(1)}, u32[]{:S(2)}, u32[]{:S(2)}) collective-permute-start(bf16[4,1536]{1,0:T(4,128)(2,1)S(1)} %get-tuple-element.20), channel_id=1, source_target_pairs={{4,0},{8,4},{12,8},{16,12},{20,16},{24,20},{28,24},{32,28},{36,32}... | collective-permute-start | bytes 36872 | tf_op jit(solution)/shard_map/ppermute | solution.py:21
  11.6 4.4 %copy-start = (bf16[5,1536,768]{2,1,0:T(8,128)(2,1)S(1)}, bf16[5,1536,768]{2,1,0:T(8,128)(2,1)}, u32[]{:S(2)}) copy-start(bf16[5,1536,768]{2,1,0:T(8,128)(2,1)} %w_ref.1) | copy-start | bytes 35389444
  16.0 5.1 %copy-start.1 = (bf16[5,768,768]{2,1,0:T(8,128)(2,1)S(1)}, bf16[5,768,768]{2,1,0:T(8,128)(2,1)}, u32[]{:S(2)}) copy-start(bf16[5,768,768]{2,1,0:T(8,128)(2,1)} %param.8) | copy-start | bytes 17694724
  70.8 2.0 %collective-permute-start.2 = (bf16[512,256]{1,0:T(8,128)(2,1)}, bf16[512,256]{1,0:T(8,128)(2,1)S(1)}, u32[]{:S(2)}, u32[]{:S(2)}) collective-permute-start(bf16[512,256]{1,0:T(8,128)(2,1)} %get-tuple-element.12.qa_ref), channel_id=1, source_target_pairs={{0,4},{4,0},{1,5},{5,1},{2,6},{6,2},{3,7},{7,3},{8,12},{12,8},{9,1... | collective-permute-start | bytes 786440 | tf_op jit(solution)/shard_map/ppermute | solution.py:374
  72.8 0.7 copy-start.4
  96.3 2.1 %collective-permute-start.3 = (f32[512,256]{1,0:T(8,128)}, f32[512,256]{1,0:T(8,128)S(1)}, u32[]{:S(2)}, u32[]{:S(2)}) collective-permute-start(f32[512,256]{1,0:T(8,128)} %get-tuple-element.17), channel_id=1, source_target_pairs={{0,4},{4,0},{1,5},{5,1},{2,6},{6,2},{3,7},{7,3},{8,12},{12,8},{9,1... | collective-permute-start | bytes 1572872 | tf_op jit(solution)/shard_map/ppermute | solution.py:378
  96.6 1.8 %collective-permute-start.4 = (f32[8,256]{1,0:T(8,128)}, f32[8,256]{1,0:T(8,128)S(1)}, u32[]{:S(2)}, u32[]{:S(2)}) collective-permute-start(f32[8,256]{1,0:T(8,128)} %get-tuple-element.18), channel_id=1, source_target_pairs={{0,4},{4,0},{1,5},{5,1},{2,6},{6,2},{3,7},{7,3},{8,12},{12,8},{9,1... | collective-permute-start | bytes 24584 | tf_op jit(solution)/shard_map/ppermute | solution.py:378
  98.4 0.6 copy-start.3
  98.4 0.8 copy-start.2

commit v17 on v16

--- a/solution.py
+++ b/solution.py
@@ -242,9 +242,10 @@
         recv((st, 2, -1), part(st, a0 + 2, b0, q), slot(st, a0 + 1, b0))
         for k in range(2, side - 1):
             send_row(st, k)
-    for st in range(2):
-        a0, b0 = own[st]
-        for k in range(side):
+    arrival = [0, 1, side - 1] + list(range(2, side - 1))
+    for k in arrival:
+        for st in range(2):
+            a0, b0 = own[st]
             recv((st, 3, 1, k), part(st, a0 + k, b0 - 1), slot(st, a0, b0 - 1))
             recv((st, 3, -1, k), part(st, a0 + k, b0 + 1), slot(st, a0, b0 + 1))
             send((st, 4, 1, k), part(st, a0 + k, b0 - 1, 0), part(st, a0 + k, b0 - 1, 0), slot(st, a0, b0 + 1))

time: 102 us -> 102 us (level)
  no operation moved by 1% of the time
where the time goes in v17:
time: 102 us
  Pallas kernels  76.5 us (75%)
  starting transfers between devices  7.51 us (7%)
  local copies, waits for them, and re-layouts  7.27 us (7%)
  waiting for transfers between devices  5.48 us (5%)
  matrix products  3.24 us (3%)
  other arithmetic  1.99 us (2%)
    pallas_call x1, Pallas kernels, gather_rows(): pl.pallas_call(functools.partial(ring_gather_kernel, side, heads, head_si...  45.8 us
    pallas_call x1, Pallas kernels, attend_partial(): pl.pallas_call(functools.partial(attend_kernel, heads, head_size, nk), gr...  22.8 us
    unnamed x10, local copies, waits for them, and re-layouts  5.86 us
    pallas_call x1, Pallas kernels, conv_gelu(): pl.pallas_call(functools.partial(conv_gelu_kernel, taps, rows, halo), gri...  5.06 us
    ppermute x1, starting transfers between devices, padded_2(): lax.ppermute(lax.slice_in_dim(block, block.shape[0] - width, None, axis=0...  4.51 us
    pallas_call x1, Pallas kernels, finish(): pl.pallas_call(functools.partial(finish_kernel, heads, head_size), grid=(...  2.81 us
    dot_general x4, matrix products, convolve(): jnp.dot(padded[offset:offset + row_count], weight[offset], preferred_elem...  2.75 us
    ppermute x1, waiting for transfers between devices, padded_2(): lax.ppermute(lax.slice_in_dim(block, 0, width, axis=0), SEQ_AXES, backward)  2.42 us
  transfers between devices with their start and end apart: 5, of which 3 were waited for; matrix products, arithmetic and copies ran while one was open for 1% of the time, Pallas kernels for 0%

profile of v17, /device:TPU:1, one launch (start us, length us, event | category | flops | bytes accessed | tf_op | source)
XLA Modules:
  0.0 102.1 jit_solution(7877544961077991859)
XLA Ops:
  0.0 0.8 fusion.20
  0.8 4.5 %collective-permute-start = (bf16[4,1536]{1,0:T(4,128)(2,1)S(1)}, bf16[4,1536]{1,0:T(4,128)(2,1)S(1)}, u32[]{:S(2)}, u32[]{:S(2)}) collective-permute-start(bf16[4,1536]{1,0:T(4,128)(2,1)S(1)} %get-tuple-element.19), channel_id=1, source_target_pairs={{0,4},{4,8},{8,12},{12,16},{16,20},{20,24},{24,28},{28,32},{32,36}... | collective-permute-start | bytes 36872 | tf_op jit(solution)/shard_map/ppermute | solution.py:20
  5.3 1.9 %collective-permute-start.1 = (bf16[4,1536]{1,0:T(4,128)(2,1)S(1)}, bf16[4,1536]{1,0:T(4,128)(2,1)S(1)}, u32[]{:S(2)}, u32[]{:S(2)}) collective-permute-start(bf16[4,1536]{1,0:T(4,128)(2,1)S(1)} %get-tuple-element.20), channel_id=1, source_target_pairs={{4,0},{8,4},{12,8},{16,12},{20,16},{24,20},{28,24},{32,28},{36,32}... | collective-permute-start | bytes 36872 | tf_op jit(solution)/shard_map/ppermute | solution.py:21
  7.2 0.7 broadcast_multiply_fusion
  7.9 0.0 collective-permute-done
  7.9 2.4 %collective-permute-done.1 = bf16[4,1536]{1,0:T(4,128)(2,1)S(1)} collective-permute-done((bf16[4,1536]{1,0:T(4,128)(2,1)S(1)}, bf16[4,1536]{1,0:T(4,128)(2,1)S(1)}, u32[]{:S(2)}, u32[]{:S(2)}) %collective-permute-start.1) | collective-permute-done | bytes 12320 | tf_op jit(solution)/shard_map/ppermute | solution.py:21
  10.3 1.3 %pad_maximum_fusion.x_ref = bf16[264,1536]{1,0:T(8,128)(2,1)S(1)} fusion(bf16[4,1536]{1,0:T(4,128)(2,1)S(1)} %collective-permute-done.1, bf16[256,1536]{1,0:T(8,128)(2,1)} %param.6, bf16[4,1536]{1,0:T(4,128)(2,1)S(1)} %collective-permute-done), kind=kLoop, calls=%fused_computation.15 | loop fusion | flops 2433024 | bytes 1622016 | tf_op jit(solution)/shard_map/concatenate | solution.py:24
  11.6 0.0 copy-start
  11.7 4.3 %copy-done = bf16[5,1536,768]{2,1,0:T(8,128)(2,1)S(1)} copy-done((bf16[5,1536,768]{2,1,0:T(8,128)(2,1)S(1)}, bf16[5,1536,768]{2,1,0:T(8,128)(2,1)}, u32[]{:S(2)}) %copy-start) | copy-done | bytes 11796504
  16.0 0.0 copy-start.1
  16.0 5.1 %shard_map.64 = bf16[260,768]{1,0:T(8,128)(2,1)S(1)} custom-call(bf16[264,1536]{1,0:T(8,128)(2,1)S(1)} %pad_maximum_fusion.x_ref, bf16[5,1536,768]{2,1,0:T(8,128)(2,1)S(1)} %copy-done), custom_call_target="tpu_custom_call" | custom-call | flops 3114270720 | bytes 13006848 | tf_op jit(solution)/shard_map/pallas_call | solution.py:340
  21.1 0.0 copy-done.1
  21.1 0.5 fusion.3
  21.6 0.5 convolution_add_fusion.3
  22.1 0.5 convolution_add_fusion.2
  22.6 0.5 convolution_add_fusion.1
  23.1 1.3 %add_convert_fusion.h_ref.hid_ref = bf16[256,768]{1,0:T(8,128)(2,1)} fusion(f32[256,768]{1,0:T(8,128)S(1)} %convolution_add_fusion.1, bf16[5,768,768]{2,1,0:T(8,128)(2,1)S(1)} %copy-done.1, bf16[260,768]{1,0:T(8,128)(2,1)S(1)} %shard_map.64), kind=kOutput, calls=%fused_computation.16 | convolution fusion | flops 302776320 | bytes 3145728 | tf_op jit(solution)/shard_map/dot_general | solution.py:30
  24.3 0.6 broadcast_in_dim.3
  25.0 45.8 %shard_map.65 = (bf16[16,2,128,768]{3,2,1,0:T(8,128)(2,1)}, bf16[512,256]{1,0:T(8,128)(2,1)}, bf16[512,768]{1,0:T(8,128)(2,1)}) custom-call(bf16[2,128,768]{2,1,0:T(8,128)(2,1)} %bitcast.20, bf16[256,768]{1,0:T(8,128)(2,1)} %add_convert_fusion.h_ref.hid_ref, bf16[768,1536]{1,0:T(8,128)(2,1)} %wk_ref.1, bf16[768,1536]{1,0:T(8,128)(2,1)} %wk_ref.1, ...), custom_call_target="tpu_custom_call" | custom-call | tf_op jit(solution)/shard_map/pallas_call | solution.py:281
  70.8 0.6 collective-permute-start.2
  71.3 1.4 %collective-permute-done.2.qb_ref = bf16[512,256]{1,0:T(8,128)(2,1)S(1)} collective-permute-done((bf16[512,256]{1,0:T(8,128)(2,1)}, bf16[512,256]{1,0:T(8,128)(2,1)S(1)}, u32[]{:S(2)}, u32[]{:S(2)}) %collective-permute-start.2) | collective-permute-done | bytes 262176 | tf_op jit(solution)/shard_map/ppermute | solution.py:375
  72.8 0.0 copy-start.4
  72.8 0.7 copy-done.4
  73.5 22.8 %shard_map.66 = (f32[512,256]{1,0:T(8,128)}, f32[8,256]{1,0:T(8,128)}, f32[512,256]{1,0:T(8,128)}, f32[8,256]{1,0:T(8,128)}) custom-call(bf16[512,256]{1,0:T(8,128)(2,1)} %get-tuple-element.12.qa_ref, bf16[512,256]{1,0:T(8,128)(2,1)} %copy-done.4, bf16[4096,768]{1,0:T(8,128)(2,1)} %bitcast.22, bf16[768,1536]{1,0:T(8,128)(2,1)} %wk_ref.1, ...), custom_call_target="tpu_custom_call" | custom-call | flops 10737418240 | bytes 8388608 | tf_op jit(solution)/shard_map/pallas_call | solution.py:102
  96.3 0.3 collective-permute-start.3
  96.6 0.2 collective-permute-start.4
  96.8 1.6 %collective-permute-done.4.sg_ref = f32[8,256]{1,0:T(8,128)S(1)} collective-permute-done((f32[8,256]{1,0:T(8,128)}, f32[8,256]{1,0:T(8,128)S(1)}, u32[]{:S(2)}, u32[]{:S(2)}) %collective-permute-start.4) | collective-permute-done | bytes 8224 | tf_op jit(solution)/shard_map/ppermute | solution.py:379
  98.4 0.0 copy-start.3
  98.4 0.0 collective-permute-done.3.og_ref
  98.4 0.0 copy-start.2
  98.4 0.6 copy-done.3
  99.0 0.2 copy-done.2
  99.3 2.8 %shard_map.67 = bf16[256,768]{1,0:T(8,128)(2,1)} custom-call(f32[512,256]{1,0:T(8,128)} %get-tuple-element.15.o_ref, f32[8,256]{1,0:T(8,128)} %get-tuple-element.16.st_ref, f32[512,256]{1,0:T(8,128)} %copy-done.2, f32[8,256]{1,0:T(8,128)} %copy-done.3, bf16[256,768]{1,0:T(8,128)(2,1)} %add_convert_fusion.h_ref.hid_ref, bf16[512,768]{1,0:T(8,128)(2,1)} %wo_ref.1), custom_call_target="tpu_custom_call" | custom-call | tf_op jit(solution)/shard_map/pallas_call | solution.py:159
Async XLA Ops:
  0.8 7.1 %collective-permute-start = (bf16[4,1536]{1,0:T(4,128)(2,1)S(1)}, bf16[4,1536]{1,0:T(4,128)(2,1)S(1)}, u32[]{:S(2)}, u32[]{:S(2)}) collective-permute-start(bf16[4,1536]{1,0:T(4,128)(2,1)S(1)} %get-tuple-element.19), channel_id=1, source_target_pairs={{0,4},{4,8},{8,12},{12,16},{16,20},{20,24},{24,28},{28,32},{32,36}... | collective-permute-start | bytes 36872 | tf_op jit(solution)/shard_map/ppermute | solution.py:20
  5.3 5.0 %collective-permute-start.1 = (bf16[4,1536]{1,0:T(4,128)(2,1)S(1)}, bf16[4,1536]{1,0:T(4,128)(2,1)S(1)}, u32[]{:S(2)}, u32[]{:S(2)}) collective-permute-start(bf16[4,1536]{1,0:T(4,128)(2,1)S(1)} %get-tuple-element.20), channel_id=1, source_target_pairs={{4,0},{8,4},{12,8},{16,12},{20,16},{24,20},{28,24},{32,28},{36,32}... | collective-permute-start | bytes 36872 | tf_op jit(solution)/shard_map/ppermute | solution.py:21
  11.6 4.4 %copy-start = (bf16[5,1536,768]{2,1,0:T(8,128)(2,1)S(1)}, bf16[5,1536,768]{2,1,0:T(8,128)(2,1)}, u32[]{:S(2)}) copy-start(bf16[5,1536,768]{2,1,0:T(8,128)(2,1)} %w_ref.1) | copy-start | bytes 35389444
  16.0 5.1 %copy-start.1 = (bf16[5,768,768]{2,1,0:T(8,128)(2,1)S(1)}, bf16[5,768,768]{2,1,0:T(8,128)(2,1)}, u32[]{:S(2)}) copy-start(bf16[5,768,768]{2,1,0:T(8,128)(2,1)} %param.8) | copy-start | bytes 17694724
  70.8 2.0 %collective-permute-start.2 = (bf16[512,256]{1,0:T(8,128)(2,1)}, bf16[512,256]{1,0:T(8,128)(2,1)S(1)}, u32[]{:S(2)}, u32[]{:S(2)}) collective-permute-start(bf16[512,256]{1,0:T(8,128)(2,1)} %get-tuple-element.12.qa_ref), channel_id=1, source_target_pairs={{0,4},{4,0},{1,5},{5,1},{2,6},{6,2},{3,7},{7,3},{8,12},{12,8},{9,1... | collective-permute-start | bytes 786440 | tf_op jit(solution)/shard_map/ppermute | solution.py:375
  72.8 0.7 copy-start.4
  96.3 2.1 %collective-permute-start.3 = (f32[512,256]{1,0:T(8,128)}, f32[512,256]{1,0:T(8,128)S(1)}, u32[]{:S(2)}, u32[]{:S(2)}) collective-permute-start(f32[512,256]{1,0:T(8,128)} %get-tuple-element.17), channel_id=1, source_target_pairs={{0,4},{4,0},{1,5},{5,1},{2,6},{6,2},{3,7},{7,3},{8,12},{12,8},{9,1... | collective-permute-start | bytes 1572872 | tf_op jit(solution)/shard_map/ppermute | solution.py:379
  96.6 1.8 %collective-permute-start.4 = (f32[8,256]{1,0:T(8,128)}, f32[8,256]{1,0:T(8,128)S(1)}, u32[]{:S(2)}, u32[]{:S(2)}) collective-permute-start(f32[8,256]{1,0:T(8,128)} %get-tuple-element.18), channel_id=1, source_target_pairs={{0,4},{4,0},{1,5},{5,1},{2,6},{6,2},{3,7},{7,3},{8,12},{12,8},{9,1... | collective-permute-start | bytes 24584 | tf_op jit(solution)/shard_map/ppermute | solution.py:379
  98.4 0.6 copy-start.3
  98.4 0.8 copy-start.2

commit v18 on v16

--- a/solution.py
+++ b/solution.py
@@ -189,66 +189,6 @@
     barrier = pltpu.get_barrier_semaphore()
     for target in (slot(0, x + 1, z), slot(0, x - 1, z), slot(1, z + 1, x), slot(1, z - 1, x)):
         pl.semaphore_signal(barrier, inc=1, device_id={"zx": target}, device_id_type=mesh_ids)
-    pl.semaphore_wait(barrier, 4)
-    local = pltpu.make_async_copy(x_ref, out_ref.at[me], local_sem)
-    local.start()
-
-    sends = []
-    index = {}
-
-    def send(key, src, view, target):
-        idx = len(index)
-        index[key] = idx
-        copy = pltpu.make_async_remote_copy(
-            src_ref=src, dst_ref=view, send_sem=send_sem.at[idx], recv_sem=recv_sem.at[idx],
-            device_id={"zx": target}, device_id_type=mesh_ids,
-        )
-        copy.start()
-        sends.append(copy)
-
-    def recv(key, view, source):
-        idx = index[key]
-        pltpu.make_async_remote_copy(
-            src_ref=view, dst_ref=view, send_sem=send_sem.at[idx], recv_sem=recv_sem.at[idx],
-            device_id={"zx": source}, device_id_type=mesh_ids,
-        ).wait_recv()
-
-    def part(stream, a, b, lo=None):
-        view = out_ref.at[slot(stream, a, b), stream]
-        return view if lo is None else view.at[pl.ds(lo, q)]
-
-    def send_row(st, k):
-        a0, b0 = own[st]
-        src = x_ref.at[st] if k == 0 else part(st, a0 + k, b0)
-        send((st, 3, 1, k), src, part(st, a0 + k, b0), slot(st, a0, b0 + 1))
-        send((st, 3, -1, k), src, part(st, a0 + k, b0), slot(st, a0, b0 - 1))
-
-    for st in range(2):
-        a0, b0 = own[st]
-        send((st, 1, 1), x_ref.at[st], part(st, a0, b0), slot(st, a0 + 1, b0))
-        send((st, 1, -1), x_ref.at[st], part(st, a0, b0), slot(st, a0 - 1, b0))
-        send_row(st, 0)
-    for st in range(2):
-        a0, b0 = own[st]
-        recv((st, 1, 1), part(st, a0 - 1, b0), slot(st, a0 - 1, b0))
-        recv((st, 1, -1), part(st, a0 + 1, b0), slot(st, a0 + 1, b0))
-        send((st, 2, 1), part(st, a0 - 1, b0, 0), part(st, a0 - 1, b0, 0), slot(st, a0 + 1, b0))
-        send((st, 2, -1), part(st, a0 + 1, b0, q), part(st, a0 + 1, b0, q), slot(st, a0 - 1, b0))
-        send_row(st, 1)
-        send_row(st, side - 1)
-    for st in range(2):
-        a0, b0 = own[st]
-        recv((st, 2, 1), part(st, a0 - 2, b0, 0), slot(st, a0 - 1, b0))
-        recv((st, 2, -1), part(st, a0 + 2, b0, q), slot(st, a0 + 1, b0))
-        for k in range(2, side - 1):
-            send_row(st, k)
-    for st in range(2):
-        a0, b0 = own[st]
-        for k in range(side):
-            recv((st, 3, 1, k), part(st, a0 + k, b0 - 1), slot(st, a0, b0 - 1))
-            recv((st, 3, -1, k), part(st, a0 + k, b0 + 1), slot(st, a0, b0 + 1))
-            send((st, 4, 1, k), part(st, a0 + k, b0 - 1, 0), part(st, a0 + k, b0 - 1, 0), slot(st, a0, b0 + 1))
-            send((st, 4, -1, k), part(st, a0 + k, b0 + 1, q), part(st, a0 + k, b0 + 1, q), slot(st, a0, b0 - 1))
     proj = jnp.dot(h_ref[...], wq_ref[...], preferred_element_type=jnp.float32)
     scale = scale_ref[...]
     normed = []
@@ -259,6 +199,66 @@
         normed.append(part_q * lax.rsqrt(mean_sq + 1e-06) * scale[:, cols])
     qt_ref[...] = jnp.concatenate(normed, axis=1).T.astype(qt_ref.dtype)
     wvt_ref[...] = wv_ref[...].astype(jnp.float32).T.astype(wvt_ref.dtype)
+    pl.semaphore_wait(barrier, 4)
+    local = pltpu.make_async_copy(x_ref, out_ref.at[me], local_sem)
+    local.start()
+
+    sends = []
+    index = {}
+
+    def send(key, src, view, target):
+        idx = len(index)
+        index[key] = idx
+        copy = pltpu.make_async_remote_copy(
+            src_ref=src, dst_ref=view, send_sem=send_sem.at[idx], recv_sem=recv_sem.at[idx],
+            device_id={"zx": target}, device_id_type=mesh_ids,
+        )
+        copy.start()
+        sends.append(copy)
+
+    def recv(key, view, source):
+        idx = index[key]
+        pltpu.make_async_remote_copy(
+            src_ref=view, dst_ref=view, send_sem=send_sem.at[idx], recv_sem=recv_sem.at[idx],
+            device_id={"zx": source}, device_id_type=mesh_ids,
+        ).wait_recv()
+
+    def part(stream, a, b, lo=None):
+        view = out_ref.at[slot(stream, a, b), stream]
+        return view if lo is None else view.at[pl.ds(lo, q)]
+
+    def send_row(st, k):
+        a0, b0 = own[st]
+        src = x_ref.at[st] if k == 0 else part(st, a0 + k, b0)
+        send((st, 3, 1, k), src, part(st, a0 + k, b0), slot(st, a0, b0 + 1))
+        send((st, 3, -1, k), src, part(st, a0 + k, b0), slot(st, a0, b0 - 1))
+
+    for st in range(2):
+        a0, b0 = own[st]
+        send((st, 1, 1), x_ref.at[st], part(st, a0, b0), slot(st, a0 + 1, b0))
+        send((st, 1, -1), x_ref.at[st], part(st, a0, b0), slot(st, a0 - 1, b0))
+        send_row(st, 0)
+    for st in range(2):
+        a0, b0 = own[st]
+        recv((st, 1, 1), part(st, a0 - 1, b0), slot(st, a0 - 1, b0))
+        recv((st, 1, -1), part(st, a0 + 1, b0), slot(st, a0 + 1, b0))
+        send((st, 2, 1), part(st, a0 - 1, b0, 0), part(st, a0 - 1, b0, 0), slot(st, a0 + 1, b0))
+        send((st, 2, -1), part(st, a0 + 1, b0, q), part(st, a0 + 1, b0, q), slot(st, a0 - 1, b0))
+        send_row(st, 1)
+        send_row(st, side - 1)
+    for st in range(2):
+        a0, b0 = own[st]
+        recv((st, 2, 1), part(st, a0 - 2, b0, 0), slot(st, a0 - 1, b0))
+        recv((st, 2, -1), part(st, a0 + 2, b0, q), slot(st, a0 + 1, b0))
+        for k in range(2, side - 1):
+            send_row(st, k)
+    for st in range(2):
+        a0, b0 = own[st]
+        for k in range(side):
+            recv((st, 3, 1, k), part(st, a0 + k, b0 - 1), slot(st, a0, b0 - 1))
+            recv((st, 3, -1, k), part(st, a0 + k, b0 + 1), slot(st, a0, b0 + 1))
+            send((st, 4, 1, k), part(st, a0 + k, b0 - 1, 0), part(st, a0 + k, b0 - 1, 0), slot(st, a0, b0 + 1))
+            send((st, 4, -1, k), part(st, a0 + k, b0 + 1, q), part(st, a0 + k, b0 + 1, q), slot(st, a0, b0 - 1))
     for st in range(2):
         a0, b0 = own[st]
         for k in range(side):

time: 102 us -> 102 us (level)
  no operation moved by 1% of the time
where the time goes in v18:
time: 102 us
  Pallas kernels  76.5 us (75%)
  starting transfers between devices  7.51 us (7%)
  local copies, waits for them, and re-layouts  7.27 us (7%)
  waiting for transfers between devices  5.48 us (5%)
  matrix products  3.24 us (3%)
  other arithmetic  1.99 us (2%)
    pallas_call x1, Pallas kernels, gather_rows(): pl.pallas_call(functools.partial(ring_gather_kernel, side, heads, head_si...  45.8 us
    pallas_call x1, Pallas kernels, attend_partial(): pl.pallas_call(functools.partial(attend_kernel, heads, head_size, nk), gr...  22.8 us
    unnamed x10, local copies, waits for them, and re-layouts  5.86 us
    pallas_call x1, Pallas kernels, conv_gelu(): pl.pallas_call(functools.partial(conv_gelu_kernel, taps, rows, halo), gri...  5.06 us
    ppermute x1, starting transfers between devices, padded_2(): lax.ppermute(lax.slice_in_dim(block, block.shape[0] - width, None, axis=0...  4.51 us
    pallas_call x1, Pallas kernels, finish(): pl.pallas_call(functools.partial(finish_kernel, heads, head_size), grid=(...  2.81 us
    dot_general x4, matrix products, convolve(): jnp.dot(padded[offset:offset + row_count], weight[offset], preferred_elem...  2.75 us
    ppermute x1, waiting for transfers between devices, padded_2(): lax.ppermute(lax.slice_in_dim(block, 0, width, axis=0), SEQ_AXES, backward)  2.42 us
  transfers between devices with their start and end apart: 5, of which 3 were waited for; matrix products, arithmetic and copies ran while one was open for 1% of the time, Pallas kernels for 0%

profile of v18, /device:TPU:1, one launch (start us, length us, event | category | flops | bytes accessed | tf_op | source)
XLA Modules:
  0.0 102.1 jit_solution(771070960756830891)
XLA Ops:
  0.0 0.8 fusion.20
  0.8 4.5 %collective-permute-start = (bf16[4,1536]{1,0:T(4,128)(2,1)S(1)}, bf16[4,1536]{1,0:T(4,128)(2,1)S(1)}, u32[]{:S(2)}, u32[]{:S(2)}) collective-permute-start(bf16[4,1536]{1,0:T(4,128)(2,1)S(1)} %get-tuple-element.19), channel_id=1, source_target_pairs={{0,4},{4,8},{8,12},{12,16},{16,20},{20,24},{24,28},{28,32},{32,36}... | collective-permute-start | bytes 36872 | tf_op jit(solution)/shard_map/ppermute | solution.py:20
  5.3 1.9 %collective-permute-start.1 = (bf16[4,1536]{1,0:T(4,128)(2,1)S(1)}, bf16[4,1536]{1,0:T(4,128)(2,1)S(1)}, u32[]{:S(2)}, u32[]{:S(2)}) collective-permute-start(bf16[4,1536]{1,0:T(4,128)(2,1)S(1)} %get-tuple-element.20), channel_id=1, source_target_pairs={{4,0},{8,4},{12,8},{16,12},{20,16},{24,20},{28,24},{32,28},{36,32}... | collective-permute-start | bytes 36872 | tf_op jit(solution)/shard_map/ppermute | solution.py:21
  7.2 0.7 broadcast_multiply_fusion
  7.9 0.0 collective-permute-done
  7.9 2.4 %collective-permute-done.1 = bf16[4,1536]{1,0:T(4,128)(2,1)S(1)} collective-permute-done((bf16[4,1536]{1,0:T(4,128)(2,1)S(1)}, bf16[4,1536]{1,0:T(4,128)(2,1)S(1)}, u32[]{:S(2)}, u32[]{:S(2)}) %collective-permute-start.1) | collective-permute-done | bytes 12320 | tf_op jit(solution)/shard_map/ppermute | solution.py:21
  10.3 1.3 %pad_maximum_fusion.x_ref = bf16[264,1536]{1,0:T(8,128)(2,1)S(1)} fusion(bf16[4,1536]{1,0:T(4,128)(2,1)S(1)} %collective-permute-done.1, bf16[256,1536]{1,0:T(8,128)(2,1)} %param.6, bf16[4,1536]{1,0:T(4,128)(2,1)S(1)} %collective-permute-done), kind=kLoop, calls=%fused_computation.15 | loop fusion | flops 2433024 | bytes 1622016 | tf_op jit(solution)/shard_map/concatenate | solution.py:24
  11.6 0.0 copy-start
  11.7 4.3 %copy-done = bf16[5,1536,768]{2,1,0:T(8,128)(2,1)S(1)} copy-done((bf16[5,1536,768]{2,1,0:T(8,128)(2,1)S(1)}, bf16[5,1536,768]{2,1,0:T(8,128)(2,1)}, u32[]{:S(2)}) %copy-start) | copy-done | bytes 11796504
  16.0 0.0 copy-start.1
  16.0 5.1 %shard_map.64 = bf16[260,768]{1,0:T(8,128)(2,1)S(1)} custom-call(bf16[264,1536]{1,0:T(8,128)(2,1)S(1)} %pad_maximum_fusion.x_ref, bf16[5,1536,768]{2,1,0:T(8,128)(2,1)S(1)} %copy-done), custom_call_target="tpu_custom_call" | custom-call | flops 3114270720 | bytes 13006848 | tf_op jit(solution)/shard_map/pallas_call | solution.py:339
  21.1 0.0 copy-done.1
  21.1 0.5 fusion.3
  21.6 0.5 convolution_add_fusion.3
  22.1 0.5 convolution_add_fusion.2
  22.6 0.5 convolution_add_fusion.1
  23.1 1.3 %add_convert_fusion.h_ref.hid_ref = bf16[256,768]{1,0:T(8,128)(2,1)} fusion(f32[256,768]{1,0:T(8,128)S(1)} %convolution_add_fusion.1, bf16[5,768,768]{2,1,0:T(8,128)(2,1)S(1)} %copy-done.1, bf16[260,768]{1,0:T(8,128)(2,1)S(1)} %shard_map.64), kind=kOutput, calls=%fused_computation.16 | convolution fusion | flops 302776320 | bytes 3145728 | tf_op jit(solution)/shard_map/dot_general | solution.py:30
  24.3 0.6 broadcast_in_dim.3
  25.0 45.8 %shard_map.65 = (bf16[16,2,128,768]{3,2,1,0:T(8,128)(2,1)}, bf16[512,256]{1,0:T(8,128)(2,1)}, bf16[512,768]{1,0:T(8,128)(2,1)}) custom-call(bf16[2,128,768]{2,1,0:T(8,128)(2,1)} %bitcast.20, bf16[256,768]{1,0:T(8,128)(2,1)} %add_convert_fusion.h_ref.hid_ref, bf16[768,1536]{1,0:T(8,128)(2,1)} %wk_ref.1, bf16[768,1536]{1,0:T(8,128)(2,1)} %wk_ref.1, ...), custom_call_target="tpu_custom_call" | custom-call | tf_op jit(solution)/shard_map/pallas_call | solution.py:280
  70.8 0.6 collective-permute-start.2
  71.3 1.4 %collective-permute-done.2.qb_ref = bf16[512,256]{1,0:T(8,128)(2,1)S(1)} collective-permute-done((bf16[512,256]{1,0:T(8,128)(2,1)}, bf16[512,256]{1,0:T(8,128)(2,1)S(1)}, u32[]{:S(2)}, u32[]{:S(2)}) %collective-permute-start.2) | collective-permute-done | bytes 262176 | tf_op jit(solution)/shard_map/ppermute | solution.py:374
  72.8 0.0 copy-start.4
  72.8 0.7 copy-done.4
  73.5 22.8 %shard_map.66 = (f32[512,256]{1,0:T(8,128)}, f32[8,256]{1,0:T(8,128)}, f32[512,256]{1,0:T(8,128)}, f32[8,256]{1,0:T(8,128)}) custom-call(bf16[512,256]{1,0:T(8,128)(2,1)} %get-tuple-element.12.qa_ref, bf16[512,256]{1,0:T(8,128)(2,1)} %copy-done.4, bf16[4096,768]{1,0:T(8,128)(2,1)} %bitcast.22, bf16[768,1536]{1,0:T(8,128)(2,1)} %wk_ref.1, ...), custom_call_target="tpu_custom_call" | custom-call | flops 10737418240 | bytes 8388608 | tf_op jit(solution)/shard_map/pallas_call | solution.py:102
  96.3 0.3 collective-permute-start.3
  96.6 0.2 collective-permute-start.4
  96.8 1.6 %collective-permute-done.4.sg_ref = f32[8,256]{1,0:T(8,128)S(1)} collective-permute-done((f32[8,256]{1,0:T(8,128)}, f32[8,256]{1,0:T(8,128)S(1)}, u32[]{:S(2)}, u32[]{:S(2)}) %collective-permute-start.4) | collective-permute-done | bytes 8224 | tf_op jit(solution)/shard_map/ppermute | solution.py:378
  98.4 0.0 copy-start.3
  98.4 0.0 collective-permute-done.3.og_ref
  98.4 0.0 copy-start.2
  98.4 0.6 copy-done.3
  99.0 0.2 copy-done.2
  99.3 2.8 %shard_map.67 = bf16[256,768]{1,0:T(8,128)(2,1)} custom-call(f32[512,256]{1,0:T(8,128)} %get-tuple-element.15.o_ref, f32[8,256]{1,0:T(8,128)} %get-tuple-element.16.st_ref, f32[512,256]{1,0:T(8,128)} %copy-done.2, f32[8,256]{1,0:T(8,128)} %copy-done.3, bf16[256,768]{1,0:T(8,128)(2,1)} %add_convert_fusion.h_ref.hid_ref, bf16[512,768]{1,0:T(8,128)(2,1)} %wo_ref.1), custom_call_target="tpu_custom_call" | custom-call | tf_op jit(solution)/shard_map/pallas_call | solution.py:159
Async XLA Ops:
  0.8 7.1 %collective-permute-start = (bf16[4,1536]{1,0:T(4,128)(2,1)S(1)}, bf16[4,1536]{1,0:T(4,128)(2,1)S(1)}, u32[]{:S(2)}, u32[]{:S(2)}) collective-permute-start(bf16[4,1536]{1,0:T(4,128)(2,1)S(1)} %get-tuple-element.19), channel_id=1, source_target_pairs={{0,4},{4,8},{8,12},{12,16},{16,20},{20,24},{24,28},{28,32},{32,36}... | collective-permute-start | bytes 36872 | tf_op jit(solution)/shard_map/ppermute | solution.py:20
  5.3 5.0 %collective-permute-start.1 = (bf16[4,1536]{1,0:T(4,128)(2,1)S(1)}, bf16[4,1536]{1,0:T(4,128)(2,1)S(1)}, u32[]{:S(2)}, u32[]{:S(2)}) collective-permute-start(bf16[4,1536]{1,0:T(4,128)(2,1)S(1)} %get-tuple-element.20), channel_id=1, source_target_pairs={{4,0},{8,4},{12,8},{16,12},{20,16},{24,20},{28,24},{32,28},{36,32}... | collective-permute-start | bytes 36872 | tf_op jit(solution)/shard_map/ppermute | solution.py:21
  11.6 4.4 %copy-start = (bf16[5,1536,768]{2,1,0:T(8,128)(2,1)S(1)}, bf16[5,1536,768]{2,1,0:T(8,128)(2,1)}, u32[]{:S(2)}) copy-start(bf16[5,1536,768]{2,1,0:T(8,128)(2,1)} %w_ref.1) | copy-start | bytes 35389444
  16.0 5.1 %copy-start.1 = (bf16[5,768,768]{2,1,0:T(8,128)(2,1)S(1)}, bf16[5,768,768]{2,1,0:T(8,128)(2,1)}, u32[]{:S(2)}) copy-start(bf16[5,768,768]{2,1,0:T(8,128)(2,1)} %param.8) | copy-start | bytes 17694724
  70.8 2.0 %collective-permute-start.2 = (bf16[512,256]{1,0:T(8,128)(2,1)}, bf16[512,256]{1,0:T(8,128)(2,1)S(1)}, u32[]{:S(2)}, u32[]{:S(2)}) collective-permute-start(bf16[512,256]{1,0:T(8,128)(2,1)} %get-tuple-element.12.qa_ref), channel_id=1, source_target_pairs={{0,4},{4,0},{1,5},{5,1},{2,6},{6,2},{3,7},{7,3},{8,12},{12,8},{9,1... | collective-permute-start | bytes 786440 | tf_op jit(solution)/shard_map/ppermute | solution.py:374
  72.8 0.7 copy-start.4
  96.3 2.1 %collective-permute-start.3 = (f32[512,256]{1,0:T(8,128)}, f32[512,256]{1,0:T(8,128)S(1)}, u32[]{:S(2)}, u32[]{:S(2)}) collective-permute-start(f32[512,256]{1,0:T(8,128)} %get-tuple-element.17), channel_id=1, source_target_pairs={{0,4},{4,0},{1,5},{5,1},{2,6},{6,2},{3,7},{7,3},{8,12},{12,8},{9,1... | collective-permute-start | bytes 1572872 | tf_op jit(solution)/shard_map/ppermute | solution.py:378
  96.6 1.8 %collective-permute-start.4 = (f32[8,256]{1,0:T(8,128)}, f32[8,256]{1,0:T(8,128)S(1)}, u32[]{:S(2)}, u32[]{:S(2)}) collective-permute-start(f32[8,256]{1,0:T(8,128)} %get-tuple-element.18), channel_id=1, source_target_pairs={{0,4},{4,0},{1,5},{5,1},{2,6},{6,2},{3,7},{7,3},{8,12},{12,8},{9,1... | collective-permute-start | bytes 24584 | tf_op jit(solution)/shard_map/ppermute | solution.py:378
  98.4 0.6 copy-start.3
  98.4 0.8 copy-start.2

commit v19 on v16

--- a/solution.py
+++ b/solution.py
@@ -173,7 +173,7 @@
 
 
 def ring_gather_kernel(side, heads, head_size, x_ref, h_ref, wq_ref, wv_ref, scale_ref,
-                       out_ref, qt_ref, wvt_ref, send_sem, recv_sem, local_sem):
+                       out_ref, qt_ref, wvt_ref, qo_ref, send_sem, recv_sem, local_sem, pair_sem):
     me = lax.axis_index("zx")
     z, x = me // side, me % side
     half = x_ref.shape[1]
@@ -189,7 +189,9 @@
     barrier = pltpu.get_barrier_semaphore()
     for target in (slot(0, x + 1, z), slot(0, x - 1, z), slot(1, z + 1, x), slot(1, z - 1, x)):
         pl.semaphore_signal(barrier, inc=1, device_id={"zx": target}, device_id_type=mesh_ids)
-    pl.semaphore_wait(barrier, 4)
+    sibling = 1 - lax.axis_index("core")
+    pl.semaphore_signal(barrier, inc=1, device_id={"core": sibling}, device_id_type=mesh_ids)
+    pl.semaphore_wait(barrier, 5)
     local = pltpu.make_async_copy(x_ref, out_ref.at[me], local_sem)
     local.start()
 
@@ -259,11 +261,18 @@
         normed.append(part_q * lax.rsqrt(mean_sq + 1e-06) * scale[:, cols])
     qt_ref[...] = jnp.concatenate(normed, axis=1).T.astype(qt_ref.dtype)
     wvt_ref[...] = wv_ref[...].astype(jnp.float32).T.astype(wvt_ref.dtype)
+    pair = pltpu.make_async_remote_copy(
+        src_ref=qt_ref, dst_ref=qo_ref, send_sem=pair_sem.at[0], recv_sem=pair_sem.at[1],
+        device_id={"core": sibling}, device_id_type=mesh_ids,
+    )
+    pair.start()
     for st in range(2):
         a0, b0 = own[st]
         for k in range(side):
             recv((st, 4, 1, k), part(st, a0 + k, b0 - 2, 0), slot(st, a0, b0 - 1))
             recv((st, 4, -1, k), part(st, a0 + k, b0 + 2, q), slot(st, a0, b0 + 1))
+    pair.wait_send()
+    pair.wait_recv()
     local.wait()
     for copy in sends:
         copy.wait_send()
@@ -277,7 +286,7 @@
     width_all = width_qkv // 3
     copies = 2 * (2 + 2 + 4 * side)
     whole = lambda i: (0, 0)
-    out, qt, wvt = pl.pallas_call(
+    out, qt, wvt, qo = pl.pallas_call(
         functools.partial(ring_gather_kernel, side, heads, head_size),
         grid=(1,),
         in_specs=[
@@ -291,20 +300,23 @@
             pl.BlockSpec(memory_space=pl.ANY),
             pl.BlockSpec((width_all, rows), whole),
             pl.BlockSpec((width_all, channels), whole),
+            pl.BlockSpec(memory_space=pl.ANY),
         ],
         out_shape=[
             jax.ShapeDtypeStruct((n, 2, rows // 2, width), block.dtype),
             jax.ShapeDtypeStruct((width_all, rows), jnp.bfloat16),
             jax.ShapeDtypeStruct((width_all, channels), jnp.bfloat16),
+            jax.ShapeDtypeStruct((width_all, rows), jnp.bfloat16),
         ],
         scratch_shapes=[
             pltpu.SemaphoreType.DMA((copies,)),
             pltpu.SemaphoreType.DMA((copies,)),
             pltpu.SemaphoreType.DMA,
+            pltpu.SemaphoreType.DMA((2,)),
         ],
         compiler_params=pltpu.CompilerParams(collective_id=0, has_side_effects=True),
     )(block.reshape(2, rows // 2, width), block, qkv_weight, qkv_weight, scale_row)
-    return out.reshape(n * rows, width), qt, wvt
+    return out.reshape(n * rows, width), qt, wvt, qo
 
 
 def conv_gelu_kernel(taps, rows, halo, x_ref, w_ref, o_ref, acc_sc):
@@ -370,8 +382,7 @@
     scale_row = jnp.repeat(logit_scale / math.sqrt(head_size), head_size)[None, :]
 
     swap = [(0, 1), (1, 0)]
-    hidden_all, qt_own, wvt = gather_rows(hidden, qkv_weight, scale_row, head_count, head_size, "zx")
-    qt_other = lax.ppermute(qt_own, "core", swap)
+    hidden_all, qt_own, wvt, qt_other = gather_rows(hidden, qkv_weight, scale_row, head_count, head_size, "zx")
     o_part, st_part, o_send, st_send = attend_partial(
         qt_own, qt_other, hidden_all, qkv_weight, wvt, head_count, head_size
     )

time: 102 us -> 99.9 us (0.979)
  waiting for transfers between devices: 5.48 us -> 4.05 us
    ppermute x1 -> x0, waiting for transfers between devices: 1.43 us -> none  [body(): qt_other = lax.ppermute(qt_own, 'core', swap)]
    unnamed x10 -> x8, local copies, waits for them, and re-layouts: 5.86 us -> 5.15 us
  transfers between devices with their start and end apart: 5 -> 4, of which waited for: 3 -> 2; matrix products, arithmetic and copies ran while one was open for 1% -> 1% of each run, Pallas kernels for 0% -> 0%
where the time goes in v19:
time: 99.9 us; the launch traced here: 99.6 us
  Pallas kernels  76.7 us (77%)
  starting transfers between devices  6.94 us (7%)
  local copies, waits for them, and re-layouts  6.56 us (7%)
  waiting for transfers between devices  4.05 us (4%)
  matrix products  3.25 us (3%)
  other arithmetic  1.99 us (2%)
    pallas_call x1, Pallas kernels, gather_rows(): pl.pallas_call(functools.partial(ring_gather_kernel, side, heads, head_si...  45.8 us
    pallas_call x1, Pallas kernels, attend_partial(): pl.pallas_call(functools.partial(attend_kernel, heads, head_size, nk), gr...  23 us
    unnamed x8, local copies, waits for them, and re-layouts  5.15 us
    pallas_call x1, Pallas kernels, conv_gelu(): pl.pallas_call(functools.partial(conv_gelu_kernel, taps, rows, halo), gri...  5.06 us
    ppermute x1, starting transfers between devices, padded_2(): lax.ppermute(lax.slice_in_dim(block, block.shape[0] - width, None, axis=0...  4.51 us
    pallas_call x1, Pallas kernels, finish(): pl.pallas_call(functools.partial(finish_kernel, heads, head_size), grid=(...  2.82 us
    dot_general x4, matrix products, convolve(): jnp.dot(padded[offset:offset + row_count], weight[offset], preferred_elem...  2.76 us
    ppermute x1, waiting for transfers between devices, padded_2(): lax.ppermute(lax.slice_in_dim(block, 0, width, axis=0), SEQ_AXES, backward)  2.42 us
  transfers between devices with their start and end apart: 4, of which 2 were waited for; matrix products, arithmetic and copies ran while one was open for 1% of the time, Pallas kernels for 0%

profile of v19, /device:TPU:1, one launch (start us, length us, event | category | flops | bytes accessed | tf_op | source)
XLA Modules:
  0.0 99.6 jit_solution(10899865978888224186)
XLA Ops:
  0.0 0.8 fusion.20
  0.8 4.5 %collective-permute-start = (bf16[4,1536]{1,0:T(4,128)(2,1)S(1)}, bf16[4,1536]{1,0:T(4,128)(2,1)S(1)}, u32[]{:S(2)}, u32[]{:S(2)}) collective-permute-start(bf16[4,1536]{1,0:T(4,128)(2,1)S(1)} %get-tuple-element.21), channel_id=1, source_target_pairs={{0,4},{4,8},{8,12},{12,16},{16,20},{20,24},{24,28},{28,32},{32,36}... | collective-permute-start | bytes 36872 | tf_op jit(solution)/shard_map/ppermute | solution.py:20
  5.3 1.9 %collective-permute-start.1 = (bf16[4,1536]{1,0:T(4,128)(2,1)S(1)}, bf16[4,1536]{1,0:T(4,128)(2,1)S(1)}, u32[]{:S(2)}, u32[]{:S(2)}) collective-permute-start(bf16[4,1536]{1,0:T(4,128)(2,1)S(1)} %get-tuple-element.22), channel_id=1, source_target_pairs={{4,0},{8,4},{12,8},{16,12},{20,16},{24,20},{28,24},{32,28},{36,32}... | collective-permute-start | bytes 36872 | tf_op jit(solution)/shard_map/ppermute | solution.py:21
  7.2 0.7 broadcast_multiply_fusion
  7.9 0.0 collective-permute-done
  7.9 2.4 %collective-permute-done.1 = bf16[4,1536]{1,0:T(4,128)(2,1)S(1)} collective-permute-done((bf16[4,1536]{1,0:T(4,128)(2,1)S(1)}, bf16[4,1536]{1,0:T(4,128)(2,1)S(1)}, u32[]{:S(2)}, u32[]{:S(2)}) %collective-permute-start.1) | collective-permute-done | bytes 12320 | tf_op jit(solution)/shard_map/ppermute | solution.py:21
  10.3 1.3 %pad_maximum_fusion.x_ref = bf16[264,1536]{1,0:T(8,128)(2,1)S(1)} fusion(bf16[4,1536]{1,0:T(4,128)(2,1)S(1)} %collective-permute-done.1, bf16[256,1536]{1,0:T(8,128)(2,1)} %param.6, bf16[4,1536]{1,0:T(4,128)(2,1)S(1)} %collective-permute-done), kind=kLoop, calls=%fused_computation.15 | loop fusion | flops 2433024 | bytes 1622016 | tf_op jit(solution)/shard_map/concatenate | solution.py:24
  11.6 0.0 copy-start
  11.7 4.3 %copy-done = bf16[5,1536,768]{2,1,0:T(8,128)(2,1)S(1)} copy-done((bf16[5,1536,768]{2,1,0:T(8,128)(2,1)S(1)}, bf16[5,1536,768]{2,1,0:T(8,128)(2,1)}, u32[]{:S(2)}) %copy-start) | copy-done | bytes 11796504
  16.0 0.0 copy-start.1
  16.0 5.1 %shard_map.64 = bf16[260,768]{1,0:T(8,128)(2,1)S(1)} custom-call(bf16[264,1536]{1,0:T(8,128)(2,1)S(1)} %pad_maximum_fusion.x_ref, bf16[5,1536,768]{2,1,0:T(8,128)(2,1)S(1)} %copy-done), custom_call_target="tpu_custom_call" | custom-call | flops 3114270720 | bytes 13006848 | tf_op jit(solution)/shard_map/pallas_call | solution.py:351
  21.1 0.0 copy-done.1
  21.1 0.5 fusion.3
  21.6 0.5 convolution_add_fusion.3
  22.1 0.5 convolution_add_fusion.2
  22.6 0.5 convolution_add_fusion.1
  23.1 1.3 %add_convert_fusion.h_ref.hid_ref = bf16[256,768]{1,0:T(8,128)(2,1)} fusion(f32[256,768]{1,0:T(8,128)S(1)} %convolution_add_fusion.1, bf16[5,768,768]{2,1,0:T(8,128)(2,1)S(1)} %copy-done.1, bf16[260,768]{1,0:T(8,128)(2,1)S(1)} %shard_map.64), kind=kOutput, calls=%fused_computation.16 | convolution fusion | flops 302776320 | bytes 3145728 | tf_op jit(solution)/shard_map/dot_general | solution.py:30
  24.4 0.6 broadcast_in_dim.3
  25.0 45.8 %shard_map.65 = (bf16[16,2,128,768]{3,2,1,0:T(8,128)(2,1)}, bf16[512,256]{1,0:T(8,128)(2,1)}, bf16[512,768]{1,0:T(8,128)(2,1)}, bf16[512,256]{1,0:T(8,128)(2,1)}) custom-call(bf16[2,128,768]{2,1,0:T(8,128)(2,1)} %bitcast.20, bf16[256,768]{1,0:T(8,128)(2,1)} %add_convert_fusion.h_ref.hid_ref, bf16[768,1536]{1,0:T(8,128)(2,1)} %wk_ref.1, ...), custom_call_target="tpu_custom_call" | custom-call | tf_op jit(solution)/shard_map/pallas_call | solution.py:289
  70.8 23.0 %shard_map.66 = (f32[512,256]{1,0:T(8,128)}, f32[8,256]{1,0:T(8,128)}, f32[512,256]{1,0:T(8,128)}, f32[8,256]{1,0:T(8,128)}) custom-call(bf16[512,256]{1,0:T(8,128)(2,1)} %get-tuple-element.13.qa_ref, bf16[512,256]{1,0:T(8,128)(2,1)} %get-tuple-element.14.qb_ref, bf16[4096,768]{1,0:T(8,128)(2,1)} %bitcast.22, bf16[768,1536]{1,0:T(8,128)(2,1)} %wk_ref.1, ...), custom_call_target="tpu_custom_call" | custom-call | flops 10737418240 | bytes 8388608 | tf_op jit(solution)/shard_map/pallas_call | solution.py:102
  93.8 0.3 collective-permute-start.2
  94.1 0.2 collective-permute-start.3
  94.3 1.6 %collective-permute-done.3.sg_ref = f32[8,256]{1,0:T(8,128)S(1)} collective-permute-done((f32[8,256]{1,0:T(8,128)}, f32[8,256]{1,0:T(8,128)S(1)}, u32[]{:S(2)}, u32[]{:S(2)}) %collective-permute-start.3) | collective-permute-done | bytes 8224 | tf_op jit(solution)/shard_map/ppermute | solution.py:389
  96.0 0.0 copy-start.3
  96.0 0.0 collective-permute-done.2.og_ref
  96.0 0.0 copy-start.2
  96.0 0.6 copy-done.3
  96.6 0.2 copy-done.2
  96.8 2.8 %shard_map.67 = bf16[256,768]{1,0:T(8,128)(2,1)} custom-call(f32[512,256]{1,0:T(8,128)} %get-tuple-element.17.o_ref, f32[8,256]{1,0:T(8,128)} %get-tuple-element.18.st_ref, f32[512,256]{1,0:T(8,128)} %copy-done.2, f32[8,256]{1,0:T(8,128)} %copy-done.3, bf16[256,768]{1,0:T(8,128)(2,1)} %add_convert_fusion.h_ref.hid_ref, bf16[512,768]{1,0:T(8,128)(2,1)} %wo_ref.1), custom_call_target="tpu_custom_call" | custom-call | tf_op jit(solution)/shard_map/pallas_call | solution.py:159
Async XLA Ops:
  0.8 7.1 %collective-permute-start = (bf16[4,1536]{1,0:T(4,128)(2,1)S(1)}, bf16[4,1536]{1,0:T(4,128)(2,1)S(1)}, u32[]{:S(2)}, u32[]{:S(2)}) collective-permute-start(bf16[4,1536]{1,0:T(4,128)(2,1)S(1)} %get-tuple-element.21), channel_id=1, source_target_pairs={{0,4},{4,8},{8,12},{12,16},{16,20},{20,24},{24,28},{28,32},{32,36}... | collective-permute-start | bytes 36872 | tf_op jit(solution)/shard_map/ppermute | solution.py:20
  5.3 5.0 %collective-permute-start.1 = (bf16[4,1536]{1,0:T(4,128)(2,1)S(1)}, bf16[4,1536]{1,0:T(4,128)(2,1)S(1)}, u32[]{:S(2)}, u32[]{:S(2)}) collective-permute-start(bf16[4,1536]{1,0:T(4,128)(2,1)S(1)} %get-tuple-element.22), channel_id=1, source_target_pairs={{4,0},{8,4},{12,8},{16,12},{20,16},{24,20},{28,24},{32,28},{36,32}... | collective-permute-start | bytes 36872 | tf_op jit(solution)/shard_map/ppermute | solution.py:21
  11.6 4.4 %copy-start = (bf16[5,1536,768]{2,1,0:T(8,128)(2,1)S(1)}, bf16[5,1536,768]{2,1,0:T(8,128)(2,1)}, u32[]{:S(2)}) copy-start(bf16[5,1536,768]{2,1,0:T(8,128)(2,1)} %w_ref.1) | copy-start | bytes 35389444
  16.0 5.1 %copy-start.1 = (bf16[5,768,768]{2,1,0:T(8,128)(2,1)S(1)}, bf16[5,768,768]{2,1,0:T(8,128)(2,1)}, u32[]{:S(2)}) copy-start(bf16[5,768,768]{2,1,0:T(8,128)(2,1)} %param.8) | copy-start | bytes 17694724
  93.8 2.1 %collective-permute-start.2 = (f32[512,256]{1,0:T(8,128)}, f32[512,256]{1,0:T(8,128)S(1)}, u32[]{:S(2)}, u32[]{:S(2)}) collective-permute-start(f32[512,256]{1,0:T(8,128)} %get-tuple-element.19), channel_id=1, source_target_pairs={{0,4},{4,0},{1,5},{5,1},{2,6},{6,2},{3,7},{7,3},{8,12},{12,8},{9,1... | collective-permute-start | bytes 1572872 | tf_op jit(solution)/shard_map/ppermute | solution.py:389
  94.1 1.8 %collective-permute-start.3 = (f32[8,256]{1,0:T(8,128)}, f32[8,256]{1,0:T(8,128)S(1)}, u32[]{:S(2)}, u32[]{:S(2)}) collective-permute-start(f32[8,256]{1,0:T(8,128)} %get-tuple-element.20), channel_id=1, source_target_pairs={{0,4},{4,0},{1,5},{5,1},{2,6},{6,2},{3,7},{7,3},{8,12},{12,8},{9,1... | collective-permute-start | bytes 24584 | tf_op jit(solution)/shard_map/ppermute | solution.py:389
  96.0 0.6 copy-start.3
  96.0 0.8 copy-start.2

commit v20 on v19

--- a/solution.py
+++ b/solution.py
@@ -47,12 +47,18 @@
 
 
 def attend_kernel(heads, head_size, nk, qa_ref, qb_ref, hkv_ref, wk_ref, wvt_ref,
-                  o_ref, st_ref, ob_ref, sb_ref, qt_sc, m_sc, l_sc, acc_sc):
+                  o_ref, st_ref, og_ref, sg_ref, qt_sc, m_sc, l_sc, acc_sc, st_send, pair_sem):
     j = pl.program_id(0)
     contract_last = (((1,), (1,)), ((), ()))
 
+    mesh_ids = pl.DeviceIdType.MESH
+    sibling = 1 - lax.axis_index("core")
+
     @pl.when(j == 0)
     def _():
+        barrier = pltpu.get_barrier_semaphore()
+        pl.semaphore_signal(barrier, inc=1, device_id={"core": sibling}, device_id_type=mesh_ids)
+        pl.semaphore_wait(barrier, 1)
         own = qa_ref.shape[1]
         qt_sc[:, :own] = qa_ref[...]
         qt_sc[:, own:] = qb_ref[...]
@@ -84,13 +90,25 @@
     @pl.when(j == nk - 1)
     def _():
         own = o_ref.shape[1]
+        for h in range(heads):
+            st_send[h : h + 1, :] = m_sc[h][:, own:]
+            st_send[heads + h : heads + h + 1, :] = l_sc[h][:, own:]
+        copies = [
+            pltpu.make_async_remote_copy(
+                src_ref=src, dst_ref=dst, send_sem=pair_sem.at[0, i], recv_sem=pair_sem.at[1, i],
+                device_id={"core": sibling}, device_id_type=mesh_ids,
+            )
+            for i, (src, dst) in enumerate(((acc_sc.at[:, pl.ds(own, own)], og_ref), (st_send, sg_ref)))
+        ]
+        for copy in copies:
+            copy.start()
         o_ref[...] = acc_sc[:, :own]
-        ob_ref[...] = acc_sc[:, own:]
         for h in range(heads):
             st_ref[h : h + 1, :] = m_sc[h][:, :own]
             st_ref[heads + h : heads + h + 1, :] = l_sc[h][:, :own]
-            sb_ref[h : h + 1, :] = m_sc[h][:, own:]
-            sb_ref[heads + h : heads + h + 1, :] = l_sc[h][:, own:]
+        for copy in copies:
+            copy.wait_send()
+            copy.wait_recv()
 
 
 def attend_partial(qt_own, qt_other, hidden_kv, qkv_weight, wvt, heads, head_size, tk=2048):
@@ -112,7 +130,9 @@
         out_specs=[
             pl.BlockSpec((width, own), whole),
             pl.BlockSpec((2 * heads, own), whole),
-        ] * 2,
+            pl.BlockSpec(memory_space=pl.ANY),
+            pl.BlockSpec(memory_space=pl.ANY),
+        ],
         out_shape=[
             jax.ShapeDtypeStruct((width, own), jnp.float32),
             jax.ShapeDtypeStruct((2 * heads, own), jnp.float32),
@@ -122,8 +142,12 @@
             pltpu.VMEM((heads, 1, q_rows), jnp.float32),
             pltpu.VMEM((heads, 1, q_rows), jnp.float32),
             pltpu.VMEM((width, q_rows), jnp.float32),
-        ],
-        compiler_params=pltpu.CompilerParams(dimension_semantics=("arbitrary",)),
+            pltpu.VMEM((2 * heads, own), jnp.float32),
+            pltpu.SemaphoreType.DMA((2, 2)),
+        ],
+        compiler_params=pltpu.CompilerParams(
+            dimension_semantics=("arbitrary",), collective_id=1, has_side_effects=True
+        ),
         cost_estimate=pl.CostEstimate(
             flops=4 * q_rows * k_rows * width + 2 * k_rows * channels * 2 * width,
             transcendentals=q_rows * k_rows * heads,
@@ -383,10 +407,9 @@
 
     swap = [(0, 1), (1, 0)]
     hidden_all, qt_own, wvt, qt_other = gather_rows(hidden, qkv_weight, scale_row, head_count, head_size, "zx")
-    o_part, st_part, o_send, st_send = attend_partial(
+    o_part, st_part, o_got, st_got = attend_partial(
         qt_own, qt_other, hidden_all, qkv_weight, wvt, head_count, head_size
     )
-    o_got, st_got = lax.ppermute((o_send, st_send), "core", swap)
     return finish(o_part, st_part, o_got, st_got, hidden, out_weight, head_count, head_size)
 
 

time: 99.9 us -> 98.9 us (0.990)
  Pallas kernels: 76.7 us -> 78.6 us
  waiting for transfers between devices: 4.05 us -> 2.42 us
    pallas_call x1, Pallas kernels: 23 us -> 24.9 us  [attend_partial(): pl.pallas_call(functools.partial(attend_kernel, heads, head_size, nk), gr...]
    ppermute x2 -> x0, waiting for transfers between devices: 1.62 us -> none  [body(): o_got, st_got = lax.ppermute((o_send, st_send), 'core', swap)]
    unnamed x8 -> x4, local copies, waits for them, and re-layouts: 5.15 us -> 4.35 us
  transfers between devices with their start and end apart: 4 -> 2, of which waited for: 2 -> 1; matrix products, arithmetic and copies ran while one was open for 1% -> 1% of each run, Pallas kernels for 0% -> 0%
where the time goes in v20:
time: 98.9 us; the launch traced here: 98.5 us
  Pallas kernels  78.6 us (79%)
  starting transfers between devices  6.43 us (7%)
  local copies, waits for them, and re-layouts  5.76 us (6%)
  matrix products  3.25 us (3%)
  waiting for transfers between devices  2.42 us (2%)
  other arithmetic  1.99 us (2%)
    pallas_call x1, Pallas kernels, gather_rows(): pl.pallas_call(functools.partial(ring_gather_kernel, side, heads, head_si...  45.8 us
    pallas_call x1, Pallas kernels, attend_partial(): pl.pallas_call(functools.partial(attend_kernel, heads, head_size, nk), gr...  24.9 us
    pallas_call x1, Pallas kernels, conv_gelu(): pl.pallas_call(functools.partial(conv_gelu_kernel, taps, rows, halo), gri...  5.06 us
    ppermute x1, starting transfers between devices, padded_2(): lax.ppermute(lax.slice_in_dim(block, block.shape[0] - width, None, axis=0...  4.51 us
    unnamed x4, local copies, waits for them, and re-layouts  4.35 us
    pallas_call x1, Pallas kernels, finish(): pl.pallas_call(functools.partial(finish_kernel, heads, head_size), grid=(...  2.82 us
    dot_general x4, matrix products, convolve(): jnp.dot(padded[offset:offset + row_count], weight[offset], preferred_elem...  2.76 us
    ppermute x1, waiting for transfers between devices, padded_2(): lax.ppermute(lax.slice_in_dim(block, 0, width, axis=0), SEQ_AXES, backward)  2.42 us
  transfers between devices with their start and end apart: 2, of which 1 were waited for; matrix products, arithmetic and copies ran while one was open for 1% of the time, Pallas kernels for 0%

profile of v20, /device:TPU:1, one launch (start us, length us, event | category | flops | bytes accessed | tf_op | source)
XLA Modules:
  0.0 98.5 jit_solution(10961264481982204172)
XLA Ops:
  0.0 0.8 fusion.20
  0.8 4.5 %collective-permute-start = (bf16[4,1536]{1,0:T(4,128)(2,1)S(1)}, bf16[4,1536]{1,0:T(4,128)(2,1)S(1)}, u32[]{:S(2)}, u32[]{:S(2)}) collective-permute-start(bf16[4,1536]{1,0:T(4,128)(2,1)S(1)} %get-tuple-element.21), channel_id=1, source_target_pairs={{0,4},{4,8},{8,12},{12,16},{16,20},{20,24},{24,28},{28,32},{32,36}... | collective-permute-start | bytes 36872 | tf_op jit(solution)/shard_map/ppermute | solution.py:20
  5.3 1.9 %collective-permute-start.1 = (bf16[4,1536]{1,0:T(4,128)(2,1)S(1)}, bf16[4,1536]{1,0:T(4,128)(2,1)S(1)}, u32[]{:S(2)}, u32[]{:S(2)}) collective-permute-start(bf16[4,1536]{1,0:T(4,128)(2,1)S(1)} %get-tuple-element.22), channel_id=1, source_target_pairs={{4,0},{8,4},{12,8},{16,12},{20,16},{24,20},{28,24},{32,28},{36,32}... | collective-permute-start | bytes 36872 | tf_op jit(solution)/shard_map/ppermute | solution.py:21
  7.2 0.7 broadcast_multiply_fusion
  7.9 0.0 collective-permute-done
  7.9 2.4 %collective-permute-done.1 = bf16[4,1536]{1,0:T(4,128)(2,1)S(1)} collective-permute-done((bf16[4,1536]{1,0:T(4,128)(2,1)S(1)}, bf16[4,1536]{1,0:T(4,128)(2,1)S(1)}, u32[]{:S(2)}, u32[]{:S(2)}) %collective-permute-start.1) | collective-permute-done | bytes 12320 | tf_op jit(solution)/shard_map/ppermute | solution.py:21
  10.3 1.3 %pad_maximum_fusion.x_ref = bf16[264,1536]{1,0:T(8,128)(2,1)S(1)} fusion(bf16[4,1536]{1,0:T(4,128)(2,1)S(1)} %collective-permute-done.1, bf16[256,1536]{1,0:T(8,128)(2,1)} %param.6, bf16[4,1536]{1,0:T(4,128)(2,1)S(1)} %collective-permute-done), kind=kLoop, calls=%fused_computation.15 | loop fusion | flops 2433024 | bytes 1622016 | tf_op jit(solution)/shard_map/concatenate | solution.py:24
  11.6 0.0 copy-start
  11.7 4.3 %copy-done = bf16[5,1536,768]{2,1,0:T(8,128)(2,1)S(1)} copy-done((bf16[5,1536,768]{2,1,0:T(8,128)(2,1)S(1)}, bf16[5,1536,768]{2,1,0:T(8,128)(2,1)}, u32[]{:S(2)}) %copy-start) | copy-done | bytes 11796504
  16.0 0.0 copy-start.1
  16.0 5.1 %shard_map.64 = bf16[260,768]{1,0:T(8,128)(2,1)S(1)} custom-call(bf16[264,1536]{1,0:T(8,128)(2,1)S(1)} %pad_maximum_fusion.x_ref, bf16[5,1536,768]{2,1,0:T(8,128)(2,1)S(1)} %copy-done), custom_call_target="tpu_custom_call" | custom-call | flops 3114270720 | bytes 13006848 | tf_op jit(solution)/shard_map/pallas_call | solution.py:375
  21.1 0.0 copy-done.1
  21.1 0.5 fusion.3
  21.6 0.5 convolution_add_fusion.3
  22.1 0.5 convolution_add_fusion.2
  22.6 0.5 convolution_add_fusion.1
  23.1 1.3 %add_convert_fusion.h_ref.hid_ref = bf16[256,768]{1,0:T(8,128)(2,1)} fusion(f32[256,768]{1,0:T(8,128)S(1)} %convolution_add_fusion.1, bf16[5,768,768]{2,1,0:T(8,128)(2,1)S(1)} %copy-done.1, bf16[260,768]{1,0:T(8,128)(2,1)S(1)} %shard_map.64), kind=kOutput, calls=%fused_computation.16 | convolution fusion | flops 302776320 | bytes 3145728 | tf_op jit(solution)/shard_map/dot_general | solution.py:30
  24.4 0.6 broadcast_in_dim.3
  25.0 45.8 %shard_map.65 = (bf16[16,2,128,768]{3,2,1,0:T(8,128)(2,1)}, bf16[512,256]{1,0:T(8,128)(2,1)}, bf16[512,768]{1,0:T(8,128)(2,1)}, bf16[512,256]{1,0:T(8,128)(2,1)}) custom-call(bf16[2,128,768]{2,1,0:T(8,128)(2,1)} %bitcast.20, bf16[256,768]{1,0:T(8,128)(2,1)} %add_convert_fusion.h_ref.hid_ref, bf16[768,1536]{1,0:T(8,128)(2,1)} %wk_ref.1, ...), custom_call_target="tpu_custom_call" | custom-call | tf_op jit(solution)/shard_map/pallas_call | solution.py:313
  70.8 24.9 %shard_map.66 = (f32[512,256]{1,0:T(8,128)}, f32[8,256]{1,0:T(8,128)}, f32[512,256]{1,0:T(8,128)}, f32[8,256]{1,0:T(8,128)}) custom-call(bf16[512,256]{1,0:T(8,128)(2,1)} %get-tuple-element.13.qa_ref, bf16[512,256]{1,0:T(8,128)(2,1)} %get-tuple-element.14.qb_ref, bf16[4096,768]{1,0:T(8,128)(2,1)} %bitcast.22, bf16[768,1536]{1,0:T(8,128)(2,1)} %wk_ref.1, ...), custom_call_target="tpu_custom_call" | custom-call | flops 10737418240 | bytes 8388608 | tf_op jit(solution)/shard_map/pallas_call | solution.py:120
  95.7 2.8 %shard_map.67 = bf16[256,768]{1,0:T(8,128)(2,1)} custom-call(f32[512,256]{1,0:T(8,128)} %get-tuple-element.17.o_ref, f32[8,256]{1,0:T(8,128)} %get-tuple-element.18.st_ref, f32[512,256]{1,0:T(8,128)} %get-tuple-element.19.og_ref, f32[8,256]{1,0:T(8,128)} %get-tuple-element.20.sg_ref, bf16[256,768]{1,0:T(8,128)(2,1)} %add_convert_fusion.h_ref.hid_ref, ...), custom_call_target="tpu_custom_call" | custom-call | tf_op jit(solution)/shard_map/pallas_call | solution.py:183
Async XLA Ops:
  0.8 7.1 %collective-permute-start = (bf16[4,1536]{1,0:T(4,128)(2,1)S(1)}, bf16[4,1536]{1,0:T(4,128)(2,1)S(1)}, u32[]{:S(2)}, u32[]{:S(2)}) collective-permute-start(bf16[4,1536]{1,0:T(4,128)(2,1)S(1)} %get-tuple-element.21), channel_id=1, source_target_pairs={{0,4},{4,8},{8,12},{12,16},{16,20},{20,24},{24,28},{28,32},{32,36}... | collective-permute-start | bytes 36872 | tf_op jit(solution)/shard_map/ppermute | solution.py:20
  5.3 5.0 %collective-permute-start.1 = (bf16[4,1536]{1,0:T(4,128)(2,1)S(1)}, bf16[4,1536]{1,0:T(4,128)(2,1)S(1)}, u32[]{:S(2)}, u32[]{:S(2)}) collective-permute-start(bf16[4,1536]{1,0:T(4,128)(2,1)S(1)} %get-tuple-element.22), channel_id=1, source_target_pairs={{4,0},{8,4},{12,8},{16,12},{20,16},{24,20},{28,24},{32,28},{36,32}... | collective-permute-start | bytes 36872 | tf_op jit(solution)/shard_map/ppermute | solution.py:21
  11.6 4.4 %copy-start = (bf16[5,1536,768]{2,1,0:T(8,128)(2,1)S(1)}, bf16[5,1536,768]{2,1,0:T(8,128)(2,1)}, u32[]{:S(2)}) copy-start(bf16[5,1536,768]{2,1,0:T(8,128)(2,1)} %w_ref.1) | copy-start | bytes 35389444
  16.0 5.1 %copy-start.1 = (bf16[5,768,768]{2,1,0:T(8,128)(2,1)S(1)}, bf16[5,768,768]{2,1,0:T(8,128)(2,1)}, u32[]{:S(2)}) copy-start(bf16[5,768,768]{2,1,0:T(8,128)(2,1)} %param.8) | copy-start | bytes 17694724

commit v21 on v20

--- a/solution.py
+++ b/solution.py
@@ -46,8 +46,8 @@
     return parts
 
 
-def attend_kernel(heads, head_size, nk, qa_ref, qb_ref, hkv_ref, wk_ref, wvt_ref,
-                  o_ref, st_ref, og_ref, sg_ref, qt_sc, m_sc, l_sc, acc_sc, st_send, pair_sem):
+def attend_kernel(heads, head_size, nk, qa_ref, qb_ref, hkv_ref, wk_ref, wvt_ref, hid_ref, wo_ref,
+                  out_ref, qt_sc, m_sc, l_sc, acc_sc, st_send, og_sc, sg_sc, pair_sem):
     j = pl.program_id(0)
     contract_last = (((1,), (1,)), ((), ()))
 
@@ -89,7 +89,7 @@
 
     @pl.when(j == nk - 1)
     def _():
-        own = o_ref.shape[1]
+        own = qa_ref.shape[1]
         for h in range(heads):
             st_send[h : h + 1, :] = m_sc[h][:, own:]
             st_send[heads + h : heads + h + 1, :] = l_sc[h][:, own:]
@@ -98,20 +98,32 @@
                 src_ref=src, dst_ref=dst, send_sem=pair_sem.at[0, i], recv_sem=pair_sem.at[1, i],
                 device_id={"core": sibling}, device_id_type=mesh_ids,
             )
-            for i, (src, dst) in enumerate(((acc_sc.at[:, pl.ds(own, own)], og_ref), (st_send, sg_ref)))
+            for i, (src, dst) in enumerate(((acc_sc.at[:, pl.ds(own, own)], og_sc), (st_send, sg_sc)))
         ]
         for copy in copies:
             copy.start()
-        o_ref[...] = acc_sc[:, :own]
-        for h in range(heads):
-            st_ref[h : h + 1, :] = m_sc[h][:, :own]
-            st_ref[heads + h : heads + h + 1, :] = l_sc[h][:, :own]
         for copy in copies:
             copy.wait_send()
             copy.wait_recv()
-
-
-def attend_partial(qt_own, qt_other, hidden_kv, qkv_weight, wvt, heads, head_size, tk=2048):
+        st_got = sg_sc[...]
+        mixed = []
+        for h in range(heads):
+            rows = slice(h * head_size, (h + 1) * head_size)
+            m_own = m_sc[h][:, :own]
+            m_got = st_got[h : h + 1, :]
+            m_all = jnp.maximum(m_own, m_got)
+            w_own = jnp.exp(m_own - m_all)
+            w_got = jnp.exp(m_got - m_all)
+            denom = l_sc[h][:, :own] * w_own + st_got[heads + h : heads + h + 1, :] * w_got
+            mixed.append((acc_sc[rows, :own] * w_own + og_sc[rows, :] * w_got) / denom)
+        attended = jnp.concatenate(mixed, axis=0).T.astype(jnp.bfloat16)
+        out = hid_ref[...].astype(jnp.float32) + jnp.dot(
+            attended, wo_ref[...], preferred_element_type=jnp.float32
+        )
+        out_ref[...] = out.astype(out_ref.dtype)
+
+
+def attend_partial(qt_own, qt_other, hidden_kv, qkv_weight, wvt, hidden, out_weight, heads, head_size, tk=2048):
     width, own = qt_own.shape
     q_rows = 2 * own
     k_rows, channels = hidden_kv.shape
@@ -126,22 +138,18 @@
             pl.BlockSpec((tk, channels), lambda j: (j, 0)),
             pl.BlockSpec((channels, width), lambda j: (0, 1)),
             pl.BlockSpec((width, channels), whole),
-        ],
-        out_specs=[
-            pl.BlockSpec((width, own), whole),
-            pl.BlockSpec((2 * heads, own), whole),
-            pl.BlockSpec(memory_space=pl.ANY),
-            pl.BlockSpec(memory_space=pl.ANY),
-        ],
-        out_shape=[
-            jax.ShapeDtypeStruct((width, own), jnp.float32),
-            jax.ShapeDtypeStruct((2 * heads, own), jnp.float32),
-        ] * 2,
+            pl.BlockSpec(hidden.shape, whole),
+            pl.BlockSpec(out_weight.shape, whole),
+        ],
+        out_specs=pl.BlockSpec(hidden.shape, whole),
+        out_shape=jax.ShapeDtypeStruct(hidden.shape, jnp.bfloat16),
         scratch_shapes=[
             pltpu.VMEM((width, q_rows), jnp.bfloat16),
             pltpu.VMEM((heads, 1, q_rows), jnp.float32),
             pltpu.VMEM((heads, 1, q_rows), jnp.float32),
             pltpu.VMEM((width, q_rows), jnp.float32),
+            pltpu.VMEM((2 * heads, own), jnp.float32),
+            pltpu.VMEM((width, own), jnp.float32),
             pltpu.VMEM((2 * heads, own), jnp.float32),
             pltpu.SemaphoreType.DMA((2, 2)),
         ],
@@ -153,7 +161,7 @@
             transcendentals=q_rows * k_rows * heads,
             bytes_accessed=k_rows * channels * 2 + q_rows * width * 8,
         ),
-    )(qt_own, qt_other, hidden_kv, qkv_weight, wvt)
+    )(qt_own, qt_other, hidden_kv, qkv_weight, wvt, hidden, out_weight)
 
 
 def finish_kernel(heads, head_size, o_ref, st_ref, og_ref, sg_ref, hid_ref, wo_ref, out_ref):
@@ -405,12 +413,10 @@
     head_size = width_all // head_count
     scale_row = jnp.repeat(logit_scale / math.sqrt(head_size), head_size)[None, :]
 
-    swap = [(0, 1), (1, 0)]
     hidden_all, qt_own, wvt, qt_other = gather_rows(hidden, qkv_weight, scale_row, head_count, head_size, "zx")
-    o_part, st_part, o_got, st_got = attend_partial(
-        qt_own, qt_other, hidden_all, qkv_weight, wvt, head_count, head_size
+    return attend_partial(
+        qt_own, qt_other, hidden_all, qkv_weight, wvt, hidden, out_weight, head_count, head_size
     )
-    return finish(o_part, st_part, o_got, st_got, hidden, out_weight, head_count, head_size)
 
 
 def solution(mesh):

time: 98.9 us -> 98.4 us (level)
  Pallas kernels: 78.6 us -> 76.4 us
  local copies, waits for them, and re-layouts: 5.76 us -> 7.52 us
    pallas_call x1 -> x0, Pallas kernels: 2.82 us -> none  [finish(): pl.pallas_call(functools.partial(finish_kernel, heads, head_size), grid=(...]
    unnamed x4 -> x5, local copies, waits for them, and re-layouts: 4.35 us -> 6.12 us
where the time goes in v21:
time: 98.4 us; the launch traced here: 98.1 us
  Pallas kernels  76.4 us (78%)
  local copies, waits for them, and re-layouts  7.52 us (8%)
  starting transfers between devices  6.43 us (7%)
  matrix products  3.19 us (3%)
  waiting for transfers between devices  2.42 us (2%)
  other arithmetic  1.99 us (2%)
    pallas_call x1, Pallas kernels, gather_rows(): pl.pallas_call(functools.partial(ring_gather_kernel, side, heads, head_si...  45.8 us
    pallas_call x1, Pallas kernels, attend_partial(): pl.pallas_call(functools.partial(attend_kernel, heads, head_size, nk), gr...  25.6 us
    unnamed x5, local copies, waits for them, and re-layouts  6.12 us
    pallas_call x1, Pallas kernels, conv_gelu(): pl.pallas_call(functools.partial(conv_gelu_kernel, taps, rows, halo), gri...  5.06 us
    ppermute x1, starting transfers between devices, padded_2(): lax.ppermute(lax.slice_in_dim(block, block.shape[0] - width, None, axis=0...  4.51 us
    dot_general x4, matrix products, convolve(): jnp.dot(padded[offset:offset + row_count], weight[offset], preferred_elem...  2.71 us
    ppermute x1, waiting for transfers between devices, padded_2(): lax.ppermute(lax.slice_in_dim(block, 0, width, axis=0), SEQ_AXES, backward)  2.42 us
  transfers between devices with their start and end apart: 2, of which 1 were waited for; matrix products, arithmetic and copies ran while one was open for 1% of the time, Pallas kernels for 0%

profile of v21, /device:TPU:1, one launch (start us, length us, event | category | flops | bytes accessed | tf_op | source)
XLA Modules:
  0.0 98.1 jit_solution(16816999363395457558)
XLA Ops:
  0.0 0.8 fusion.20
  0.8 4.5 %collective-permute-start = (bf16[4,1536]{1,0:T(4,128)(2,1)S(1)}, bf16[4,1536]{1,0:T(4,128)(2,1)S(1)}, u32[]{:S(2)}, u32[]{:S(2)}) collective-permute-start(bf16[4,1536]{1,0:T(4,128)(2,1)S(1)} %get-tuple-element.13), channel_id=1, source_target_pairs={{0,4},{4,8},{8,12},{12,16},{16,20},{20,24},{24,28},{28,32},{32,36}... | collective-permute-start | bytes 36872 | tf_op jit(solution)/shard_map/ppermute | solution.py:20
  5.3 1.9 %collective-permute-start.1 = (bf16[4,1536]{1,0:T(4,128)(2,1)S(1)}, bf16[4,1536]{1,0:T(4,128)(2,1)S(1)}, u32[]{:S(2)}, u32[]{:S(2)}) collective-permute-start(bf16[4,1536]{1,0:T(4,128)(2,1)S(1)} %get-tuple-element.14), channel_id=1, source_target_pairs={{4,0},{8,4},{12,8},{16,12},{20,16},{24,20},{28,24},{32,28},{36,32}... | collective-permute-start | bytes 36872 | tf_op jit(solution)/shard_map/ppermute | solution.py:21
  7.2 0.7 broadcast_multiply_fusion
  7.9 0.0 collective-permute-done
  7.9 2.4 %collective-permute-done.1 = bf16[4,1536]{1,0:T(4,128)(2,1)S(1)} collective-permute-done((bf16[4,1536]{1,0:T(4,128)(2,1)S(1)}, bf16[4,1536]{1,0:T(4,128)(2,1)S(1)}, u32[]{:S(2)}, u32[]{:S(2)}) %collective-permute-start.1) | collective-permute-done | bytes 12320 | tf_op jit(solution)/shard_map/ppermute | solution.py:21
  10.3 1.3 %pad_maximum_fusion.x_ref = bf16[264,1536]{1,0:T(8,128)(2,1)S(1)} fusion(bf16[4,1536]{1,0:T(4,128)(2,1)S(1)} %collective-permute-done.1, bf16[256,1536]{1,0:T(8,128)(2,1)} %param.6, bf16[4,1536]{1,0:T(4,128)(2,1)S(1)} %collective-permute-done), kind=kLoop, calls=%fused_computation.15 | loop fusion | flops 2433024 | bytes 1622016 | tf_op jit(solution)/shard_map/concatenate | solution.py:24
  11.6 0.0 copy-start
  11.7 4.3 %copy-done = bf16[5,1536,768]{2,1,0:T(8,128)(2,1)S(1)} copy-done((bf16[5,1536,768]{2,1,0:T(8,128)(2,1)S(1)}, bf16[5,1536,768]{2,1,0:T(8,128)(2,1)}, u32[]{:S(2)}) %copy-start) | copy-done | bytes 11796504
  16.0 0.0 copy-start.1
  16.0 5.1 %shard_map.64 = bf16[260,768]{1,0:T(8,128)(2,1)S(1)} custom-call(bf16[264,1536]{1,0:T(8,128)(2,1)S(1)} %pad_maximum_fusion.x_ref, bf16[5,1536,768]{2,1,0:T(8,128)(2,1)S(1)} %copy-done), custom_call_target="tpu_custom_call" | custom-call | flops 3114270720 | bytes 13006848 | tf_op jit(solution)/shard_map/pallas_call | solution.py:383
  21.1 0.0 copy-done.1
  21.1 0.5 fusion.3
  21.6 0.5 convolution_add_fusion.3
  22.1 0.5 convolution_add_fusion.2
  22.5 0.5 convolution_add_fusion.1
  23.0 1.2 %add_convert_fusion.h_ref.hid_ref = bf16[256,768]{1,0:T(8,128)(2,1)} fusion(f32[256,768]{1,0:T(8,128)S(1)} %convolution_add_fusion.1, bf16[5,768,768]{2,1,0:T(8,128)(2,1)S(1)} %copy-done.1, bf16[260,768]{1,0:T(8,128)(2,1)S(1)} %shard_map.64), kind=kOutput, calls=%fused_computation.16 | convolution fusion | flops 302776320 | bytes 3145728 | tf_op jit(solution)/shard_map/dot_general | solution.py:30
  24.3 0.6 broadcast_in_dim.3
  24.9 45.8 %shard_map.65 = (bf16[16,2,128,768]{3,2,1,0:T(8,128)(2,1)}, bf16[512,256]{1,0:T(8,128)(2,1)}, bf16[512,768]{1,0:T(8,128)(2,1)}, bf16[512,256]{1,0:T(8,128)(2,1)}) custom-call(bf16[2,128,768]{2,1,0:T(8,128)(2,1)} %bitcast.20, bf16[256,768]{1,0:T(8,128)(2,1)} %add_convert_fusion.h_ref.hid_ref, bf16[768,1536]{1,0:T(8,128)(2,1)} %wk_ref.1, ...), custom_call_target="tpu_custom_call" | custom-call | tf_op jit(solution)/shard_map/pallas_call | solution.py:321
  70.7 25.6 %shard_map.66 = bf16[256,768]{1,0:T(8,128)(2,1)} custom-call(bf16[512,256]{1,0:T(8,128)(2,1)} %get-tuple-element.9.qa_ref, bf16[512,256]{1,0:T(8,128)(2,1)} %get-tuple-element.10.qb_ref, bf16[4096,768]{1,0:T(8,128)(2,1)} %bitcast.22, bf16[768,1536]{1,0:T(8,128)(2,1)} %wk_ref.1, bf16[512,768]{1,0:T(8,128)(2,1)} %get-tuple-element.12.wvt_ref, ...), custom_call_target="tpu_custom_call" | custom-call | flops 10737418240 | bytes 8388608 | tf_op jit(solution)/shard_map/pallas_call | solution.py:132
  96.3 1.8 %copy.8 = bf16[256,768]{1,0:T(8,128)(2,1)} copy(bf16[256,768]{1,0:T(8,128)(2,1)} %shard_map.66) | data formatting | bytes 786432
Async XLA Ops:
  0.8 7.1 %collective-permute-start = (bf16[4,1536]{1,0:T(4,128)(2,1)S(1)}, bf16[4,1536]{1,0:T(4,128)(2,1)S(1)}, u32[]{:S(2)}, u32[]{:S(2)}) collective-permute-start(bf16[4,1536]{1,0:T(4,128)(2,1)S(1)} %get-tuple-element.13), channel_id=1, source_target_pairs={{0,4},{4,8},{8,12},{12,16},{16,20},{20,24},{24,28},{28,32},{32,36}... | collective-permute-start | bytes 36872 | tf_op jit(solution)/shard_map/ppermute | solution.py:20
  5.3 5.0 %collective-permute-start.1 = (bf16[4,1536]{1,0:T(4,128)(2,1)S(1)}, bf16[4,1536]{1,0:T(4,128)(2,1)S(1)}, u32[]{:S(2)}, u32[]{:S(2)}) collective-permute-start(bf16[4,1536]{1,0:T(4,128)(2,1)S(1)} %get-tuple-element.14), channel_id=1, source_target_pairs={{4,0},{8,4},{12,8},{16,12},{20,16},{24,20},{28,24},{32,28},{36,32}... | collective-permute-start | bytes 36872 | tf_op jit(solution)/shard_map/ppermute | solution.py:21
  11.6 4.4 %copy-start = (bf16[5,1536,768]{2,1,0:T(8,128)(2,1)S(1)}, bf16[5,1536,768]{2,1,0:T(8,128)(2,1)}, u32[]{:S(2)}) copy-start(bf16[5,1536,768]{2,1,0:T(8,128)(2,1)} %w_ref.1) | copy-start | bytes 35389444
  16.0 5.1 %copy-start.1 = (bf16[5,768,768]{2,1,0:T(8,128)(2,1)S(1)}, bf16[5,768,768]{2,1,0:T(8,128)(2,1)}, u32[]{:S(2)}) copy-start(bf16[5,768,768]{2,1,0:T(8,128)(2,1)} %param.8) | copy-start | bytes 17694724

commit v22 on v21

--- a/solution.py
+++ b/solution.py
@@ -46,7 +46,7 @@
     return parts
 
 
-def attend_kernel(heads, head_size, nk, qa_ref, qb_ref, hkv_ref, wk_ref, wvt_ref, hid_ref, wo_ref,
+def attend_kernel(heads, head_size, nk, qa_ref, qb_ref, hkv_ref, wk_ref, wvt_ref,
                   out_ref, qt_sc, m_sc, l_sc, acc_sc, st_send, og_sc, sg_sc, pair_sem):
     j = pl.program_id(0)
     contract_last = (((1,), (1,)), ((), ()))
@@ -116,14 +116,10 @@
             w_got = jnp.exp(m_got - m_all)
             denom = l_sc[h][:, :own] * w_own + st_got[heads + h : heads + h + 1, :] * w_got
             mixed.append((acc_sc[rows, :own] * w_own + og_sc[rows, :] * w_got) / denom)
-        attended = jnp.concatenate(mixed, axis=0).T.astype(jnp.bfloat16)
-        out = hid_ref[...].astype(jnp.float32) + jnp.dot(
-            attended, wo_ref[...], preferred_element_type=jnp.float32
-        )
-        out_ref[...] = out.astype(out_ref.dtype)
-
-
-def attend_partial(qt_own, qt_other, hidden_kv, qkv_weight, wvt, hidden, out_weight, heads, head_size, tk=2048):
+        out_ref[...] = jnp.concatenate(mixed, axis=0).T.astype(out_ref.dtype)
+
+
+def attend_partial(qt_own, qt_other, hidden_kv, qkv_weight, wvt, heads, head_size, tk=2048):
     width, own = qt_own.shape
     q_rows = 2 * own
     k_rows, channels = hidden_kv.shape
@@ -138,11 +134,9 @@
             pl.BlockSpec((tk, channels), lambda j: (j, 0)),
             pl.BlockSpec((channels, width), lambda j: (0, 1)),
             pl.BlockSpec((width, channels), whole),
-            pl.BlockSpec(hidden.shape, whole),
-            pl.BlockSpec(out_weight.shape, whole),
-        ],
-        out_specs=pl.BlockSpec(hidden.shape, whole),
-        out_shape=jax.ShapeDtypeStruct(hidden.shape, jnp.bfloat16),
+        ],
+        out_specs=pl.BlockSpec((own, width), whole),
+        out_shape=jax.ShapeDtypeStruct((own, width), jnp.bfloat16),
         scratch_shapes=[
             pltpu.VMEM((width, q_rows), jnp.bfloat16),
             pltpu.VMEM((heads, 1, q_rows), jnp.float32),
@@ -161,7 +155,7 @@
             transcendentals=q_rows * k_rows * heads,
             bytes_accessed=k_rows * channels * 2 + q_rows * width * 8,
         ),
-    )(qt_own, qt_other, hidden_kv, qkv_weight, wvt, hidden, out_weight)
+    )(qt_own, qt_other, hidden_kv, qkv_weight, wvt)
 
 
 def finish_kernel(heads, head_size, o_ref, st_ref, og_ref, sg_ref, hid_ref, wo_ref, out_ref):
@@ -414,9 +408,11 @@
     scale_row = jnp.repeat(logit_scale / math.sqrt(head_size), head_size)[None, :]
 
     hidden_all, qt_own, wvt, qt_other = gather_rows(hidden, qkv_weight, scale_row, head_count, head_size, "zx")
-    return attend_partial(
-        qt_own, qt_other, hidden_all, qkv_weight, wvt, hidden, out_weight, head_count, head_size
-    )
+    attended = attend_partial(qt_own, qt_other, hidden_all, qkv_weight, wvt, head_count, head_size)
+    return (
+        hidden.astype(jnp.float32)
+        + jnp.dot(attended, out_weight, preferred_element_type=jnp.float32)
+    ).astype(jnp.bfloat16)
 
 
 def solution(mesh):

time: 98.4 us -> 98.1 us (level)
  matrix products: 3.19 us -> 5.26 us
  local copies, waits for them, and re-layouts: 7.52 us -> 5.86 us
    dot_general x0 -> x1, matrix products: none -> 2.07 us  [body(): jnp.dot(attended, out_weight, preferred_element_type=jnp.float32)]
    unnamed x5 -> x8, local copies, waits for them, and re-layouts: 6.12 us -> 4.36 us
where the time goes in v22:
time: 98.1 us; the launch traced here: 97.8 us
  Pallas kernels  75.7 us (77%)
  starting transfers between devices  6.43 us (7%)
  local copies, waits for them, and re-layouts  5.86 us (6%)
  matrix products  5.26 us (5%)
  waiting for transfers between devices  2.42 us (2%)
  other arithmetic  1.99 us (2%)
    pallas_call x1, Pallas kernels, gather_rows(): pl.pallas_call(functools.partial(ring_gather_kernel, side, heads, head_si...  45.8 us
    pallas_call x1, Pallas kernels, attend_partial(): pl.pallas_call(functools.partial(attend_kernel, heads, head_size, nk), gr...  24.9 us
    pallas_call x1, Pallas kernels, conv_gelu(): pl.pallas_call(functools.partial(conv_gelu_kernel, taps, rows, halo), gri...  5.06 us
    ppermute x1, starting transfers between devices, padded_2(): lax.ppermute(lax.slice_in_dim(block, block.shape[0] - width, None, axis=0...  4.51 us
    unnamed x8, local copies, waits for them, and re-layouts  4.36 us
    dot_general x4, matrix products, convolve(): jnp.dot(padded[offset:offset + row_count], weight[offset], preferred_elem...  2.71 us
    ppermute x1, waiting for transfers between devices, padded_2(): lax.ppermute(lax.slice_in_dim(block, 0, width, axis=0), SEQ_AXES, backward)  2.42 us
    dot_general x1, matrix products, body(): jnp.dot(attended, out_weight, preferred_element_type=jnp.float32)  2.07 us
  transfers between devices with their start and end apart: 2, of which 1 were waited for; matrix products, arithmetic and copies ran while one was open for 1% of the time, Pallas kernels for 0%

profile of v22, /device:TPU:1, one launch (start us, length us, event | category | flops | bytes accessed | tf_op | source)
XLA Modules:
  0.0 97.8 jit_solution(11823535814187063418)
XLA Ops:
  0.0 0.0 copy-start
  0.0 0.8 fusion.21
  0.8 4.5 %collective-permute-start = (bf16[4,1536]{1,0:T(4,128)(2,1)S(1)}, bf16[4,1536]{1,0:T(4,128)(2,1)S(1)}, u32[]{:S(2)}, u32[]{:S(2)}) collective-permute-start(bf16[4,1536]{1,0:T(4,128)(2,1)S(1)} %get-tuple-element.13), channel_id=1, source_target_pairs={{0,4},{4,8},{8,12},{12,16},{16,20},{20,24},{24,28},{28,32},{32,36}... | collective-permute-start | bytes 36872 | tf_op jit(solution)/shard_map/ppermute | solution.py:20
  5.4 1.9 %collective-permute-start.1 = (bf16[4,1536]{1,0:T(4,128)(2,1)S(1)}, bf16[4,1536]{1,0:T(4,128)(2,1)S(1)}, u32[]{:S(2)}, u32[]{:S(2)}) collective-permute-start(bf16[4,1536]{1,0:T(4,128)(2,1)S(1)} %get-tuple-element.14), channel_id=1, source_target_pairs={{4,0},{8,4},{12,8},{16,12},{20,16},{24,20},{28,24},{32,28},{36,32}... | collective-permute-start | bytes 36872 | tf_op jit(solution)/shard_map/ppermute | solution.py:21
  7.3 0.7 broadcast_multiply_fusion
  8.0 0.0 collective-permute-done
  8.0 2.4 %collective-permute-done.1 = bf16[4,1536]{1,0:T(4,128)(2,1)S(1)} collective-permute-done((bf16[4,1536]{1,0:T(4,128)(2,1)S(1)}, bf16[4,1536]{1,0:T(4,128)(2,1)S(1)}, u32[]{:S(2)}, u32[]{:S(2)}) %collective-permute-start.1) | collective-permute-done | bytes 12320 | tf_op jit(solution)/shard_map/ppermute | solution.py:21
  10.4 1.3 %pad_maximum_fusion.x_ref = bf16[264,1536]{1,0:T(8,128)(2,1)S(1)} fusion(bf16[4,1536]{1,0:T(4,128)(2,1)S(1)} %collective-permute-done.1, bf16[256,1536]{1,0:T(8,128)(2,1)} %param.6, bf16[4,1536]{1,0:T(4,128)(2,1)S(1)} %collective-permute-done), kind=kLoop, calls=%fused_computation.17 | loop fusion | flops 2433024 | bytes 1622016 | tf_op jit(solution)/shard_map/concatenate | solution.py:24
  11.7 0.0 copy-start.1
  11.7 4.3 %copy-done.1 = bf16[5,1536,768]{2,1,0:T(8,128)(2,1)S(1)} copy-done((bf16[5,1536,768]{2,1,0:T(8,128)(2,1)S(1)}, bf16[5,1536,768]{2,1,0:T(8,128)(2,1)}, u32[]{:S(2)}) %copy-start.1) | copy-done | bytes 11796504
  16.1 0.0 copy-start.3
  16.1 5.1 %shard_map.64 = bf16[260,768]{1,0:T(8,128)(2,1)S(1)} custom-call(bf16[264,1536]{1,0:T(8,128)(2,1)S(1)} %pad_maximum_fusion.x_ref, bf16[5,1536,768]{2,1,0:T(8,128)(2,1)S(1)} %copy-done.1), custom_call_target="tpu_custom_call" | custom-call | flops 3114270720 | bytes 13006848 | tf_op jit(solution)/shard_map/pallas_call | solution.py:377
  21.1 0.0 copy-done.3
  21.1 0.5 fusion.4
  21.6 0.5 convolution_add_fusion.4
  22.1 0.5 convolution_add_fusion.3
  22.6 0.5 convolution_add_fusion.2
  23.1 1.2 %add_convert_fusion.h_ref = bf16[256,768]{1,0:T(8,128)(2,1)} fusion(f32[256,768]{1,0:T(8,128)S(1)} %convolution_add_fusion.2, bf16[5,768,768]{2,1,0:T(8,128)(2,1)S(1)} %copy-done.3, bf16[260,768]{1,0:T(8,128)(2,1)S(1)} %shard_map.64), kind=kOutput, calls=%fused_computation.18 | convolution fusion | flops 302776320 | bytes 3145728 | tf_op jit(solution)/shard_map/dot_general | solution.py:30
  24.4 0.7 broadcast_in_dim.3
  25.0 45.8 %shard_map.65 = (bf16[16,2,128,768]{3,2,1,0:T(8,128)(2,1)}, bf16[512,256]{1,0:T(8,128)(2,1)}, bf16[512,768]{1,0:T(8,128)(2,1)}, bf16[512,256]{1,0:T(8,128)(2,1)}) custom-call(bf16[2,128,768]{2,1,0:T(8,128)(2,1)} %bitcast.22, bf16[256,768]{1,0:T(8,128)(2,1)} %add_convert_fusion.h_ref, bf16[768,1536]{1,0:T(8,128)(2,1)} %wk_ref.1, bf16[768,1536]{1,0:T(8,128)(2,1)} %wk_ref.1, ...), custom_call_target="tpu_custom_call" | custom-call | tf_op jit(solution)/shard_map/pallas_call | solution.py:315
  70.8 0.0 copy-start.2
  70.8 24.9 %shard_map.66 = bf16[256,512]{1,0:T(8,128)(2,1)} custom-call(bf16[512,256]{1,0:T(8,128)(2,1)} %get-tuple-element.9.qa_ref, bf16[512,256]{1,0:T(8,128)(2,1)} %get-tuple-element.10.qb_ref, bf16[4096,768]{1,0:T(8,128)(2,1)} %bitcast.24, bf16[768,1536]{1,0:T(8,128)(2,1)} %wk_ref.1, bf16[512,768]{1,0:T(8,128)(2,1)} %get-tuple-element.12.wvt_ref), custom_call_target="tpu_custom_call" | custom-call | flops 10737418240 | bytes 8388608 | tf_op jit(solution)/shard_map/pallas_call | solution.py:128
  95.7 0.0 copy-done
  95.7 0.0 copy-done.2
  95.7 2.1 %fusion = bf16[256,768]{1,0:T(8,128)(2,1)} fusion(bf16[256,512]{1,0:T(8,128)(2,1)} %shard_map.66, bf16[512,768]{1,0:T(8,128)(2,1)S(1)} %copy-done, bf16[256,768]{1,0:T(8,128)(2,1)S(1)} %copy-done.2), kind=kOutput, calls=%fused_computation.5 | convolution fusion | flops 201916416 | bytes 1835008 | tf_op jit(solution)/shard_map/dot_general | solution.py:414
Async XLA Ops:
  0.0 95.7 %copy-start = (bf16[512,768]{1,0:T(8,128)(2,1)S(1)}, bf16[512,768]{1,0:T(8,128)(2,1)}, u32[]{:S(2)}) copy-start(bf16[512,768]{1,0:T(8,128)(2,1)} %param.10) | copy-start | bytes 2359300
  0.8 7.1 %collective-permute-start = (bf16[4,1536]{1,0:T(4,128)(2,1)S(1)}, bf16[4,1536]{1,0:T(4,128)(2,1)S(1)}, u32[]{:S(2)}, u32[]{:S(2)}) collective-permute-start(bf16[4,1536]{1,0:T(4,128)(2,1)S(1)} %get-tuple-element.13), channel_id=1, source_target_pairs={{0,4},{4,8},{8,12},{12,16},{16,20},{20,24},{24,28},{28,32},{32,36}... | collective-permute-start | bytes 36872 | tf_op jit(solution)/shard_map/ppermute | solution.py:20
  5.4 5.0 %collective-permute-start.1 = (bf16[4,1536]{1,0:T(4,128)(2,1)S(1)}, bf16[4,1536]{1,0:T(4,128)(2,1)S(1)}, u32[]{:S(2)}, u32[]{:S(2)}) collective-permute-start(bf16[4,1536]{1,0:T(4,128)(2,1)S(1)} %get-tuple-element.14), channel_id=1, source_target_pairs={{4,0},{8,4},{12,8},{16,12},{20,16},{24,20},{28,24},{32,28},{36,32}... | collective-permute-start | bytes 36872 | tf_op jit(solution)/shard_map/ppermute | solution.py:21
  11.7 4.4 %copy-start.1 = (bf16[5,1536,768]{2,1,0:T(8,128)(2,1)S(1)}, bf16[5,1536,768]{2,1,0:T(8,128)(2,1)}, u32[]{:S(2)}) copy-start(bf16[5,1536,768]{2,1,0:T(8,128)(2,1)} %w_ref.1) | copy-start | bytes 35389444
  16.1 5.1 %copy-start.3 = (bf16[5,768,768]{2,1,0:T(8,128)(2,1)S(1)}, bf16[5,768,768]{2,1,0:T(8,128)(2,1)}, u32[]{:S(2)}) copy-start(bf16[5,768,768]{2,1,0:T(8,128)(2,1)} %param.8) | copy-start | bytes 17694724
  70.8 24.9 %copy-start.2 = (bf16[256,768]{1,0:T(8,128)(2,1)S(1)}, bf16[256,768]{1,0:T(8,128)(2,1)}, u32[]{:S(2)}) copy-start(bf16[256,768]{1,0:T(8,128)(2,1)} %add_convert_fusion.h_ref) | copy-start | bytes 1179652

commit v23 on v22

--- a/solution.py
+++ b/solution.py
@@ -278,13 +278,13 @@
             send((st, 4, 1, k), part(st, a0 + k, b0 - 1, 0), part(st, a0 + k, b0 - 1, 0), slot(st, a0, b0 + 1))
             send((st, 4, -1, k), part(st, a0 + k, b0 + 1, q), part(st, a0 + k, b0 + 1, q), slot(st, a0, b0 - 1))
     proj = jnp.dot(h_ref[...], wq_ref[...], preferred_element_type=jnp.float32)
-    scale = scale_ref[...]
     normed = []
     for h in range(heads):
         cols = slice(h * head_size, (h + 1) * head_size)
         part_q = proj[:, cols]
         mean_sq = jnp.mean(part_q * part_q, axis=1, keepdims=True)
-        normed.append(part_q * lax.rsqrt(mean_sq + 1e-06) * scale[:, cols])
+        scale = jnp.full((1, head_size), scale_ref[h], jnp.float32) / math.sqrt(head_size)
+        normed.append(part_q * lax.rsqrt(mean_sq + 1e-06) * scale)
     qt_ref[...] = jnp.concatenate(normed, axis=1).T.astype(qt_ref.dtype)
     wvt_ref[...] = wv_ref[...].astype(jnp.float32).T.astype(wvt_ref.dtype)
     pair = pltpu.make_async_remote_copy(
@@ -304,7 +304,7 @@
         copy.wait_send()
 
 
-def gather_rows(block, qkv_weight, scale_row, heads, head_size, axis):
+def gather_rows(block, qkv_weight, logit_scale, heads, head_size, axis):
     n = lax.axis_size(axis)
     side = math.isqrt(n)
     rows, width = block.shape
@@ -320,7 +320,7 @@
             pl.BlockSpec((rows, width), whole),
             pl.BlockSpec((channels, width_all), lambda i: (0, 0)),
             pl.BlockSpec((channels, width_all), lambda i: (0, 2)),
-            pl.BlockSpec((1, width_all), whole),
+            pl.BlockSpec(memory_space=pltpu.SMEM),
         ],
         out_specs=[
             pl.BlockSpec(memory_space=pl.ANY),
@@ -341,7 +341,7 @@
             pltpu.SemaphoreType.DMA((2,)),
         ],
         compiler_params=pltpu.CompilerParams(collective_id=0, has_side_effects=True),
-    )(block.reshape(2, rows // 2, width), block, qkv_weight, qkv_weight, scale_row)
+    )(block.reshape(2, rows // 2, width), block, qkv_weight, qkv_weight, logit_scale)
     return out.reshape(n * rows, width), qt, wvt, qo
 
 
@@ -405,9 +405,8 @@
     head_count = logit_scale.shape[0]
     width_all = qkv_weight.shape[1] // 3
     head_size = width_all // head_count
-    scale_row = jnp.repeat(logit_scale / math.sqrt(head_size), head_size)[None, :]
-
-    hidden_all, qt_own, wvt, qt_other = gather_rows(hidden, qkv_weight, scale_row, head_count, head_size, "zx")
+
+    hidden_all, qt_own, wvt, qt_other = gather_rows(hidden, qkv_weight, logit_scale, head_count, head_size, "zx")
     attended = attend_partial(qt_own, qt_other, hidden_all, qkv_weight, wvt, head_count, head_size)
     return (
         hidden.astype(jnp.float32)

time: 98.1 us -> 97.5 us (level)
  transfers between devices with their start and end apart: 2 -> 2, of which waited for: 1 -> 1; matrix products, arithmetic and copies ran while one was open for 1% -> 0% of each run, Pallas kernels for 0% -> 0%
where the time goes in v23:
time: 97.5 us; the launch traced here: 97.2 us
  Pallas kernels  75.8 us (78%)
  starting transfers between devices  6.43 us (7%)
  matrix products  5.26 us (5%)
  local copies, waits for them, and re-layouts  5.2 us (5%)
  waiting for transfers between devices  3.08 us (3%)
  other arithmetic  1.33 us (1%)
    pallas_call x1, Pallas kernels, gather_rows(): pl.pallas_call(functools.partial(ring_gather_kernel, side, heads, head_si...  45.8 us
    pallas_call x1, Pallas kernels, attend_partial(): pl.pallas_call(functools.partial(attend_kernel, heads, head_size, nk), gr...  24.9 us
    pallas_call x1, Pallas kernels, conv_gelu(): pl.pallas_call(functools.partial(conv_gelu_kernel, taps, rows, halo), gri...  5.06 us
    ppermute x1, starting transfers between devices, padded_2(): lax.ppermute(lax.slice_in_dim(block, block.shape[0] - width, None, axis=0...  4.51 us
    unnamed x8, local copies, waits for them, and re-layouts  4.36 us
    ppermute x1, waiting for transfers between devices, padded_2(): lax.ppermute(lax.slice_in_dim(block, 0, width, axis=0), SEQ_AXES, backward)  3.08 us
    dot_general x4, matrix products, convolve(): jnp.dot(padded[offset:offset + row_count], weight[offset], preferred_elem...  2.71 us
    dot_general x1, matrix products, body(): jnp.dot(attended, out_weight, preferred_element_type=jnp.float32)  2.07 us
  transfers between devices with their start and end apart: 2, of which 1 were waited for; matrix products, arithmetic and copies ran while one was open for 0% of the time, Pallas kernels for 0%

profile of v23, /device:TPU:1, one launch (start us, length us, event | category | flops | bytes accessed | tf_op | source)
XLA Modules:
  0.0 97.2 jit_solution(16245641308803225324)
XLA Ops:
  0.0 0.0 copy-start
  0.0 0.8 fusion.21
  0.8 4.5 %collective-permute-start = (bf16[4,1536]{1,0:T(4,128)(2,1)S(1)}, bf16[4,1536]{1,0:T(4,128)(2,1)S(1)}, u32[]{:S(2)}, u32[]{:S(2)}) collective-permute-start(bf16[4,1536]{1,0:T(4,128)(2,1)S(1)} %get-tuple-element.13), channel_id=1, source_target_pairs={{0,4},{4,8},{8,12},{12,16},{16,20},{20,24},{24,28},{28,32},{32,36}... | collective-permute-start | bytes 36872 | tf_op jit(solution)/shard_map/ppermute | solution.py:20
  5.4 1.9 %collective-permute-start.1 = (bf16[4,1536]{1,0:T(4,128)(2,1)S(1)}, bf16[4,1536]{1,0:T(4,128)(2,1)S(1)}, u32[]{:S(2)}, u32[]{:S(2)}) collective-permute-start(bf16[4,1536]{1,0:T(4,128)(2,1)S(1)} %get-tuple-element.14), channel_id=1, source_target_pairs={{4,0},{8,4},{12,8},{16,12},{20,16},{24,20},{28,24},{32,28},{36,32}... | collective-permute-start | bytes 36872 | tf_op jit(solution)/shard_map/ppermute | solution.py:21
  7.3 0.0 collective-permute-done
  7.3 3.1 %collective-permute-done.1 = bf16[4,1536]{1,0:T(4,128)(2,1)S(1)} collective-permute-done((bf16[4,1536]{1,0:T(4,128)(2,1)S(1)}, bf16[4,1536]{1,0:T(4,128)(2,1)S(1)}, u32[]{:S(2)}, u32[]{:S(2)}) %collective-permute-start.1) | collective-permute-done | bytes 12320 | tf_op jit(solution)/shard_map/ppermute | solution.py:21
  10.4 1.3 %pad_maximum_fusion.x_ref = bf16[264,1536]{1,0:T(8,128)(2,1)S(1)} fusion(bf16[4,1536]{1,0:T(4,128)(2,1)S(1)} %collective-permute-done.1, bf16[256,1536]{1,0:T(8,128)(2,1)} %param.6, bf16[4,1536]{1,0:T(4,128)(2,1)S(1)} %collective-permute-done), kind=kLoop, calls=%fused_computation.17 | loop fusion | flops 2433024 | bytes 1622016 | tf_op jit(solution)/shard_map/concatenate | solution.py:24
  11.7 0.0 copy-start.1
  11.7 4.3 %copy-done.1 = bf16[5,1536,768]{2,1,0:T(8,128)(2,1)S(1)} copy-done((bf16[5,1536,768]{2,1,0:T(8,128)(2,1)S(1)}, bf16[5,1536,768]{2,1,0:T(8,128)(2,1)}, u32[]{:S(2)}) %copy-start.1) | copy-done | bytes 11796504
  16.1 0.0 copy-start.3
  16.1 5.1 %shard_map.64 = bf16[260,768]{1,0:T(8,128)(2,1)S(1)} custom-call(bf16[264,1536]{1,0:T(8,128)(2,1)S(1)} %pad_maximum_fusion.x_ref, bf16[5,1536,768]{2,1,0:T(8,128)(2,1)S(1)} %copy-done.1), custom_call_target="tpu_custom_call" | custom-call | flops 3114270720 | bytes 13006848 | tf_op jit(solution)/shard_map/pallas_call | solution.py:377
  21.1 0.0 copy-done.3
  21.1 0.5 fusion.4
  21.6 0.5 convolution_add_fusion.4
  22.1 0.5 convolution_add_fusion.3
  22.6 0.5 convolution_add_fusion.2
  23.1 1.2 %add_convert_fusion.h_ref = bf16[256,768]{1,0:T(8,128)(2,1)} fusion(f32[256,768]{1,0:T(8,128)S(1)} %convolution_add_fusion.2, bf16[5,768,768]{2,1,0:T(8,128)(2,1)S(1)} %copy-done.3, bf16[260,768]{1,0:T(8,128)(2,1)S(1)} %shard_map.64), kind=kOutput, calls=%fused_computation.18 | convolution fusion | flops 302776320 | bytes 3145728 | tf_op jit(solution)/shard_map/dot_general | solution.py:30
  24.4 45.8 %shard_map.65 = (bf16[16,2,128,768]{3,2,1,0:T(8,128)(2,1)}, bf16[512,256]{1,0:T(8,128)(2,1)}, bf16[512,768]{1,0:T(8,128)(2,1)}, bf16[512,256]{1,0:T(8,128)(2,1)}) custom-call(bf16[2,128,768]{2,1,0:T(8,128)(2,1)} %bitcast.21, bf16[256,768]{1,0:T(8,128)(2,1)} %add_convert_fusion.h_ref, bf16[768,1536]{1,0:T(8,128)(2,1)} %wk_ref.1, bf16[768,1536]{1,0:T(8,128)(2,1)} %wk_ref.1, ...), custom_call_target="tpu_custom_call" | custom-call | tf_op jit(solution)/shard_map/pallas_call | solution.py:315
  70.2 0.0 copy-start.2
  70.2 24.9 %shard_map.66 = bf16[256,512]{1,0:T(8,128)(2,1)} custom-call(bf16[512,256]{1,0:T(8,128)(2,1)} %get-tuple-element.9.qa_ref, bf16[512,256]{1,0:T(8,128)(2,1)} %get-tuple-element.10.qb_ref, bf16[4096,768]{1,0:T(8,128)(2,1)} %bitcast.22, bf16[768,1536]{1,0:T(8,128)(2,1)} %wk_ref.1, bf16[512,768]{1,0:T(8,128)(2,1)} %get-tuple-element.12.wvt_ref), custom_call_target="tpu_custom_call" | custom-call | flops 10737418240 | bytes 8388608 | tf_op jit(solution)/shard_map/pallas_call | solution.py:128
  95.1 0.0 copy-done
  95.1 0.0 copy-done.2
  95.1 2.1 %fusion = bf16[256,768]{1,0:T(8,128)(2,1)} fusion(bf16[256,512]{1,0:T(8,128)(2,1)} %shard_map.66, bf16[512,768]{1,0:T(8,128)(2,1)S(1)} %copy-done, bf16[256,768]{1,0:T(8,128)(2,1)S(1)} %copy-done.2), kind=kOutput, calls=%fused_computation.5 | convolution fusion | flops 201916416 | bytes 1835008 | tf_op jit(solution)/shard_map/dot_general | solution.py:413
Async XLA Ops:
  0.0 95.1 %copy-start = (bf16[512,768]{1,0:T(8,128)(2,1)S(1)}, bf16[512,768]{1,0:T(8,128)(2,1)}, u32[]{:S(2)}) copy-start(bf16[512,768]{1,0:T(8,128)(2,1)} %param.10) | copy-start | bytes 2359300
  0.8 6.4 %collective-permute-start = (bf16[4,1536]{1,0:T(4,128)(2,1)S(1)}, bf16[4,1536]{1,0:T(4,128)(2,1)S(1)}, u32[]{:S(2)}, u32[]{:S(2)}) collective-permute-start(bf16[4,1536]{1,0:T(4,128)(2,1)S(1)} %get-tuple-element.13), channel_id=1, source_target_pairs={{0,4},{4,8},{8,12},{12,16},{16,20},{20,24},{24,28},{28,32},{32,36}... | collective-permute-start | bytes 36872 | tf_op jit(solution)/shard_map/ppermute | solution.py:20
  5.4 5.0 %collective-permute-start.1 = (bf16[4,1536]{1,0:T(4,128)(2,1)S(1)}, bf16[4,1536]{1,0:T(4,128)(2,1)S(1)}, u32[]{:S(2)}, u32[]{:S(2)}) collective-permute-start(bf16[4,1536]{1,0:T(4,128)(2,1)S(1)} %get-tuple-element.14), channel_id=1, source_target_pairs={{4,0},{8,4},{12,8},{16,12},{20,16},{24,20},{28,24},{32,28},{36,32}... | collective-permute-start | bytes 36872 | tf_op jit(solution)/shard_map/ppermute | solution.py:21
  11.7 4.4 %copy-start.1 = (bf16[5,1536,768]{2,1,0:T(8,128)(2,1)S(1)}, bf16[5,1536,768]{2,1,0:T(8,128)(2,1)}, u32[]{:S(2)}) copy-start(bf16[5,1536,768]{2,1,0:T(8,128)(2,1)} %w_ref.1) | copy-start | bytes 35389444
  16.1 5.1 %copy-start.3 = (bf16[5,768,768]{2,1,0:T(8,128)(2,1)S(1)}, bf16[5,768,768]{2,1,0:T(8,128)(2,1)}, u32[]{:S(2)}) copy-start(bf16[5,768,768]{2,1,0:T(8,128)(2,1)} %param.8) | copy-start | bytes 17694724
  70.2 24.9 %copy-start.2 = (bf16[256,768]{1,0:T(8,128)(2,1)S(1)}, bf16[256,768]{1,0:T(8,128)(2,1)}, u32[]{:S(2)}) copy-start(bf16[256,768]{1,0:T(8,128)(2,1)} %add_convert_fusion.h_ref) | copy-start | bytes 1179652

commit v24 on v23

--- a/solution.py
+++ b/solution.py
@@ -22,6 +22,15 @@
     extra = (-(block.shape[0] + 2 * width)) % align
     fill = jnp.zeros((extra, block.shape[1]), block.dtype)
     return jnp.concatenate([low, block, high, fill], axis=0)
+
+
+def halo_rows(block, width):
+    count = lax.axis_size(SEQ_AXES)
+    forward = [(i, i + 1) for i in range(count - 1)]
+    backward = [(target, source) for source, target in forward]
+    low = lax.ppermute(lax.slice_in_dim(block, block.shape[0] - width, None, axis=0), SEQ_AXES, forward)
+    high = lax.ppermute(lax.slice_in_dim(block, 0, width, axis=0), SEQ_AXES, backward)
+    return low, high
 
 
 def convolve(padded, weight, row_count):
@@ -345,8 +354,16 @@
     return out.reshape(n * rows, width), qt, wvt, qo
 
 
-def conv_gelu_kernel(taps, rows, halo, x_ref, w_ref, o_ref, acc_sc):
+def conv_gelu_kernel(taps, rows, halo, lo_ref, mid_ref, hi_ref, w_ref, o_ref, x_ref, acc_sc):
     j = pl.program_id(0)
+    edge = lo_ref.shape[0]
+
+    @pl.when(j == 0)
+    def _():
+        x_ref[:edge, :] = lo_ref[...]
+        x_ref[edge : edge + mid_ref.shape[0], :] = mid_ref[...]
+        x_ref[edge + mid_ref.shape[0] :, :] = hi_ref[...]
+
     product = jnp.dot(x_ref[...], w_ref[...], preferred_element_type=jnp.float32)
     for t in range(taps):
 
@@ -370,35 +387,38 @@
         o_ref[...] = jnp.where(outside, 0.0, value).astype(o_ref.dtype)
 
 
-def conv_gelu(padded, weight, halo):
+def conv_gelu(low, block, high, weight, halo):
     taps, channels, width = weight.shape
-    rows = padded.shape[0] - taps + 1
+    total = low.shape[0] + block.shape[0] + high.shape[0]
+    rows = total - taps + 1
     whole = lambda j: (0, 0)
     return pl.pallas_call(
         functools.partial(conv_gelu_kernel, taps, rows, halo),
         grid=(taps,),
         in_specs=[
-            pl.BlockSpec(padded.shape, whole),
+            pl.BlockSpec(low.shape, whole),
+            pl.BlockSpec(block.shape, whole),
+            pl.BlockSpec(high.shape, whole),
             pl.BlockSpec((None, channels, width), lambda j: (j, 0, 0)),
         ],
         out_specs=pl.BlockSpec((rows, width), whole),
         out_shape=jax.ShapeDtypeStruct((rows, width), jnp.bfloat16),
-        scratch_shapes=[pltpu.VMEM((rows, width), jnp.float32)],
+        scratch_shapes=[pltpu.VMEM((total, channels), block.dtype), pltpu.VMEM((rows, width), jnp.float32)],
         compiler_params=pltpu.CompilerParams(
             dimension_semantics=("arbitrary",), vmem_limit_bytes=24 * 1024 * 1024
         ),
         cost_estimate=pl.CostEstimate(
-            flops=2 * taps * padded.shape[0] * channels * width,
+            flops=2 * taps * total * channels * width,
             transcendentals=rows * width,
-            bytes_accessed=taps * channels * width * 2 + padded.size * 2 + rows * width * 2,
+            bytes_accessed=taps * channels * width * 2 + total * channels * 2 + rows * width * 2,
         ),
-    )(padded, weight)
+    )(low, block, high, weight)
 
 
 def body(sequence_input, conv_first, conv_second, qkv_weight, out_weight, logit_scale):
     row_count = sequence_input.shape[0]
-    padded_input = padded_2(sequence_input, 4)
-    padded_first = conv_gelu(padded_input, conv_first, 2)
+    low, high = halo_rows(sequence_input, 4)
+    padded_first = conv_gelu(low, sequence_input, high, conv_first, 2)
     first_out = padded_first[2 : 2 + row_count]
     second = convolve(padded_first, conv_second, row_count)
     hidden = (first_out.astype(jnp.float32) + second).astype(jnp.bfloat16)

time: 97.5 us -> 96 us (0.985)
  waiting for transfers between devices: 3.08 us -> 0.8 us
  other arithmetic: 1.33 us -> 0 us
  local copies, waits for them, and re-layouts: 5.2 us -> 6.34 us
    ppermute x2, waiting for transfers between devices: 3.08 us -> 0.8 us  [the longest x1 0.8 us: halo_rows(): lax.ppermute(lax.slice_in_dim(block, block.shape[0] - width, None, axis=0...]
    concatenate x1 -> x0, other arithmetic: 1.33 us -> none  [padded_2(): return jnp.concatenate([low, block, high, fill], axis=0)]
    unnamed x8 -> x10, local copies, waits for them, and re-layouts: 4.36 us -> 5.5 us
    pallas_call x1, Pallas kernels: 24.9 us -> 26 us  [attend_partial(): pl.pallas_call(functools.partial(attend_kernel, heads, head_size, nk), gr...]
where the time goes in v24:
time: 96 us; the launch traced here: 95.7 us
  Pallas kernels  76.7 us (80%)
  starting transfers between devices  6.43 us (7%)
  local copies, waits for them, and re-layouts  6.34 us (7%)
  matrix products  5.36 us (6%)
    pallas_call x1, Pallas kernels, gather_rows(): pl.pallas_call(functools.partial(ring_gather_kernel, side, heads, head_si...  45.5 us
    pallas_call x1, Pallas kernels, attend_partial(): pl.pallas_call(functools.partial(attend_kernel, heads, head_size, nk), gr...  26 us
    unnamed x10, local copies, waits for them, and re-layouts  5.5 us
    pallas_call x1, Pallas kernels, conv_gelu(): pl.pallas_call(functools.partial(conv_gelu_kernel, taps, rows, halo), gri...  5.17 us
    ppermute x1, starting transfers between devices, halo_rows(): lax.ppermute(lax.slice_in_dim(block, 0, width, axis=0), SEQ_AXES, backward)  3.33 us
    ppermute x1, starting transfers between devices, halo_rows(): lax.ppermute(lax.slice_in_dim(block, block.shape[0] - width, None, axis=0...  3.1 us
    dot_general x1, matrix products, body(): jnp.dot(attended, out_weight, preferred_element_type=jnp.float32)  2.07 us
    dot_general x4, matrix products, convolve(): jnp.dot(padded[offset:offset + row_count], weight[offset], preferred_elem...  1.93 us
  transfers between devices with their start and end apart: 2, of which 1 were waited for; matrix products, arithmetic and copies ran while one was open for 0% of the time, Pallas kernels for 0%

profile of v24, /device:TPU:1, one launch (start us, length us, event | category | flops | bytes accessed | tf_op | source)
XLA Modules:
  0.0 95.7 jit_solution(14066680587766585835)
XLA Ops:
  0.0 0.0 copy-start
  0.0 0.8 fusion.27
  0.8 3.3 %collective-permute-start.1 = (bf16[4,1536]{1,0:T(4,128)(2,1)S(1)}, bf16[4,1536]{1,0:T(4,128)(2,1)S(1)}, u32[]{:S(2)}, u32[]{:S(2)}) collective-permute-start(bf16[4,1536]{1,0:T(4,128)(2,1)S(1)} %get-tuple-element.13), channel_id=1, source_target_pairs={{4,0},{8,4},{12,8},{16,12},{20,16},{24,20},{28,24},{32,28},{36,32}... | collective-permute-start | bytes 36872 | tf_op jit(solution)/shard_map/ppermute | solution.py:32
  4.2 3.1 %collective-permute-start = (bf16[4,1536]{1,0:T(4,128)(2,1)S(1)}, bf16[4,1536]{1,0:T(4,128)(2,1)S(1)}, u32[]{:S(2)}, u32[]{:S(2)}) collective-permute-start(bf16[4,1536]{1,0:T(4,128)(2,1)S(1)} %get-tuple-element.14), channel_id=1, source_target_pairs={{0,4},{4,8},{8,12},{12,16},{16,20},{20,24},{24,28},{28,32},{32,36}... | collective-permute-start | bytes 36872 | tf_op jit(solution)/shard_map/ppermute | solution.py:31
  7.3 0.0 collective-permute-done.1.hi_ref
  7.3 0.8 collective-permute-done.lo_ref
  8.1 0.0 copy-start.1
  8.1 4.3 %copy-done.1 = bf16[5,1536,768]{2,1,0:T(8,128)(2,1)S(1)} copy-done((bf16[5,1536,768]{2,1,0:T(8,128)(2,1)S(1)}, bf16[5,1536,768]{2,1,0:T(8,128)(2,1)}, u32[]{:S(2)}) %copy-start.1) | copy-done | bytes 11796504
  12.5 0.0 copy-start.2
  12.5 1.1 %copy-done.2 = bf16[256,1536]{1,0:T(8,128)(2,1)S(1)} copy-done((bf16[256,1536]{1,0:T(8,128)(2,1)S(1)}, bf16[256,1536]{1,0:T(8,128)(2,1)}, u32[]{:S(2)}) %copy-start.2) | copy-done | bytes 786456
  13.6 0.0 copy-start.4
  13.6 5.2 %shard_map.64 = bf16[260,768]{1,0:T(8,128)(2,1)S(1)} custom-call(bf16[4,1536]{1,0:T(4,128)(2,1)S(1)} %collective-permute-done.lo_ref, bf16[256,1536]{1,0:T(8,128)(2,1)S(1)} %copy-done.2, bf16[4,1536]{1,0:T(4,128)(2,1)S(1)} %collective-permute-done.1.hi_ref, bf16[5,1536,768]{2,1,0:T(8,128)(2,1)S(1)} %copy-done.1), custom_call_target="tpu_custom_call" | custom-call | flops 3114270720 | bytes 13006848 | tf_op jit(solution)/shard_map/pallas_call | solution.py:395
  18.8 0.0 copy-done.4
  18.8 0.5 fusion.4
  19.3 0.5 fusion.6
  19.8 0.5 fusion.10
  20.3 0.5 fusion.8
  20.7 1.4 %add_convert_fusion.h_ref = bf16[256,768]{1,0:T(8,128)(2,1)} fusion(f32[256,768]{1,0:T(8,128)S(1)} %fusion.4, f32[256,768]{1,0:T(8,128)S(1)} %fusion.6, f32[256,768]{1,0:T(8,128)S(1)} %fusion.8, f32[256,768]{1,0:T(8,128)S(1)} %fusion.10, bf16[5,768,768]{2,1,0:T(8,128)(2,1)S(1)} %copy-done.4, bf16[260,768]{1,0:T(8,128)(2,1)S(1)} %shard_map.64), kind=kOutput, calls=%fused_computation.20 | convolution fusion | flops 303366144 | bytes 5505024 | tf_op jit(solution)/shard_map/dot_general | solution.py:37
  22.1 45.5 %shard_map.65 = (bf16[16,2,128,768]{3,2,1,0:T(8,128)(2,1)}, bf16[512,256]{1,0:T(8,128)(2,1)}, bf16[512,768]{1,0:T(8,128)(2,1)}, bf16[512,256]{1,0:T(8,128)(2,1)}) custom-call(bf16[2,128,768]{2,1,0:T(8,128)(2,1)} %bitcast.21, bf16[256,768]{1,0:T(8,128)(2,1)} %add_convert_fusion.h_ref, bf16[768,1536]{1,0:T(8,128)(2,1)} %wk_ref.1, bf16[768,1536]{1,0:T(8,128)(2,1)} %wk_ref.1, ...), custom_call_target="tpu_custom_call" | custom-call | tf_op jit(solution)/shard_map/pallas_call | solution.py:324
  67.6 0.0 copy-start.3
  67.7 26.0 %shard_map.66 = bf16[256,512]{1,0:T(8,128)(2,1)} custom-call(bf16[512,256]{1,0:T(8,128)(2,1)} %get-tuple-element.9.qa_ref, bf16[512,256]{1,0:T(8,128)(2,1)} %get-tuple-element.10.qb_ref, bf16[4096,768]{1,0:T(8,128)(2,1)} %bitcast.22, bf16[768,1536]{1,0:T(8,128)(2,1)} %wk_ref.1, bf16[512,768]{1,0:T(8,128)(2,1)} %get-tuple-element.12.wvt_ref), custom_call_target="tpu_custom_call" | custom-call | flops 10737418240 | bytes 8388608 | tf_op jit(solution)/shard_map/pallas_call | solution.py:137
  93.6 0.0 copy-done
  93.7 0.0 copy-done.3
  93.7 2.1 %fusion.3 = bf16[256,768]{1,0:T(8,128)(2,1)} fusion(bf16[256,512]{1,0:T(8,128)(2,1)} %shard_map.66, bf16[512,768]{1,0:T(8,128)(2,1)S(1)} %copy-done, bf16[256,768]{1,0:T(8,128)(2,1)S(1)} %copy-done.3), kind=kOutput, calls=%fused_computation.5 | convolution fusion | flops 201916416 | bytes 1835008 | tf_op jit(solution)/shard_map/dot_general | solution.py:433
Async XLA Ops:
  0.0 93.6 %copy-start = (bf16[512,768]{1,0:T(8,128)(2,1)S(1)}, bf16[512,768]{1,0:T(8,128)(2,1)}, u32[]{:S(2)}) copy-start(bf16[512,768]{1,0:T(8,128)(2,1)} %param.10) | copy-start | bytes 2359300
  0.8 6.4 %collective-permute-start.1 = (bf16[4,1536]{1,0:T(4,128)(2,1)S(1)}, bf16[4,1536]{1,0:T(4,128)(2,1)S(1)}, u32[]{:S(2)}, u32[]{:S(2)}) collective-permute-start(bf16[4,1536]{1,0:T(4,128)(2,1)S(1)} %get-tuple-element.13), channel_id=1, source_target_pairs={{4,0},{8,4},{12,8},{16,12},{20,16},{24,20},{28,24},{32,28},{36,32}... | collective-permute-start | bytes 36872 | tf_op jit(solution)/shard_map/ppermute | solution.py:32
  4.2 3.9 %collective-permute-start = (bf16[4,1536]{1,0:T(4,128)(2,1)S(1)}, bf16[4,1536]{1,0:T(4,128)(2,1)S(1)}, u32[]{:S(2)}, u32[]{:S(2)}) collective-permute-start(bf16[4,1536]{1,0:T(4,128)(2,1)S(1)} %get-tuple-element.14), channel_id=1, source_target_pairs={{0,4},{4,8},{8,12},{12,16},{16,20},{20,24},{24,28},{28,32},{32,36}... | collective-permute-start | bytes 36872 | tf_op jit(solution)/shard_map/ppermute | solution.py:31
  8.1 4.4 %copy-start.1 = (bf16[5,1536,768]{2,1,0:T(8,128)(2,1)S(1)}, bf16[5,1536,768]{2,1,0:T(8,128)(2,1)}, u32[]{:S(2)}) copy-start(bf16[5,1536,768]{2,1,0:T(8,128)(2,1)} %w_ref.1) | copy-start | bytes 35389444
  12.5 1.1 %copy-start.2 = (bf16[256,1536]{1,0:T(8,128)(2,1)S(1)}, bf16[256,1536]{1,0:T(8,128)(2,1)}, u32[]{:S(2)}) copy-start(bf16[256,1536]{1,0:T(8,128)(2,1)} %mid_ref.1) | copy-start | bytes 2359300
  13.6 5.2 %copy-start.4 = (bf16[5,768,768]{2,1,0:T(8,128)(2,1)S(1)}, bf16[5,768,768]{2,1,0:T(8,128)(2,1)}, u32[]{:S(2)}) copy-start(bf16[5,768,768]{2,1,0:T(8,128)(2,1)} %param.8) | copy-start | bytes 17694724
  67.6 26.0 %copy-start.3 = (bf16[256,768]{1,0:T(8,128)(2,1)S(1)}, bf16[256,768]{1,0:T(8,128)(2,1)}, u32[]{:S(2)}) copy-start(bf16[256,768]{1,0:T(8,128)(2,1)} %add_convert_fusion.h_ref) | copy-start | bytes 1179652

commit v25 on v24

--- a/solution.py
+++ b/solution.py
@@ -354,7 +354,7 @@
     return out.reshape(n * rows, width), qt, wvt, qo
 
 
-def conv_gelu_kernel(taps, rows, halo, lo_ref, mid_ref, hi_ref, w_ref, o_ref, x_ref, acc_sc):
+def conv_gelu_kernel(taps, rows, halo, lo_ref, mid_ref, hi_ref, w_ref, w2_ref, o_ref, x_ref, acc_sc):
     j = pl.program_id(0)
     edge = lo_ref.shape[0]
 
@@ -384,10 +384,18 @@
             jnp.logical_and(place == last, row >= rows - halo),
         )
         value = jax.nn.gelu(acc_sc[...])
-        o_ref[...] = jnp.where(outside, 0.0, value).astype(o_ref.dtype)
-
-
-def conv_gelu(low, block, high, weight, halo):
+        first = jnp.where(outside, 0.0, value).astype(jnp.bfloat16)
+        out_rows = o_ref.shape[0]
+        second = None
+        for t in range(taps):
+            product2 = jnp.dot(first, w2_ref[t], preferred_element_type=jnp.float32)
+            term = product2[t : t + out_rows]
+            second = term if second is None else second + term
+        residual = first.astype(jnp.float32)[halo : halo + out_rows]
+        o_ref[...] = (residual + second).astype(o_ref.dtype)
+
+
+def conv_block(low, block, high, weight, weight2, halo):
     taps, channels, width = weight.shape
     total = low.shape[0] + block.shape[0] + high.shape[0]
     rows = total - taps + 1
@@ -400,28 +408,26 @@
             pl.BlockSpec(block.shape, whole),
             pl.BlockSpec(high.shape, whole),
             pl.BlockSpec((None, channels, width), lambda j: (j, 0, 0)),
-        ],
-        out_specs=pl.BlockSpec((rows, width), whole),
-        out_shape=jax.ShapeDtypeStruct((rows, width), jnp.bfloat16),
+            pl.BlockSpec(weight2.shape, lambda j: (0, 0, 0)),
+        ],
+        out_specs=pl.BlockSpec(block.shape[:1] + (width,), whole),
+        out_shape=jax.ShapeDtypeStruct(block.shape[:1] + (width,), jnp.bfloat16),
         scratch_shapes=[pltpu.VMEM((total, channels), block.dtype), pltpu.VMEM((rows, width), jnp.float32)],
         compiler_params=pltpu.CompilerParams(
-            dimension_semantics=("arbitrary",), vmem_limit_bytes=24 * 1024 * 1024
+            dimension_semantics=("arbitrary",), vmem_limit_bytes=48 * 1024 * 1024
         ),
         cost_estimate=pl.CostEstimate(
             flops=2 * taps * total * channels * width,
             transcendentals=rows * width,
             bytes_accessed=taps * channels * width * 2 + total * channels * 2 + rows * width * 2,
         ),
-    )(low, block, high, weight)
+    )(low, block, high, weight, weight2)
 
 
 def body(sequence_input, conv_first, conv_second, qkv_weight, out_weight, logit_scale):
     row_count = sequence_input.shape[0]
     low, high = halo_rows(sequence_input, 4)
-    padded_first = conv_gelu(low, sequence_input, high, conv_first, 2)
-    first_out = padded_first[2 : 2 + row_count]
-    second = convolve(padded_first, conv_second, row_count)
-    hidden = (first_out.astype(jnp.float32) + second).astype(jnp.bfloat16)
+    hidden = conv_block(low, sequence_input, high, conv_first, conv_second, 2)
     head_count = logit_scale.shape[0]
     width_all = qkv_weight.shape[1] // 3
     head_size = width_all // head_count

time: 96 us -> 95.6 us (level)
  Pallas kernels: 76.7 us -> 83.1 us
  local copies, waits for them, and re-layouts: 6.34 us -> 2.72 us
  matrix products: 5.36 us -> 2.07 us
    pallas_call x1, Pallas kernels: 5.17 us -> 11.6 us  [conv_block(): pl.pallas_call(functools.partial(conv_gelu_kernel, taps, rows, halo), gri...]
    unnamed x10 -> x8, local copies, waits for them, and re-layouts: 5.5 us -> 1.88 us
    dot_general x5 -> x0, matrix products: 3.29 us -> none  [the longest x4 1.93 us: convolve(): jnp.dot(padded[offset:offset + row_count], weight[offset], preferred_elem...]
where the time goes in v25:
time: 95.6 us; the launch traced here: 95.3 us
  Pallas kernels  83.1 us (87%)
  starting transfers between devices  6.43 us (7%)
  local copies, waits for them, and re-layouts  2.72 us (3%)
  matrix products  2.07 us (2%)
    pallas_call x1, Pallas kernels, gather_rows(): pl.pallas_call(functools.partial(ring_gather_kernel, side, heads, head_si...  45.5 us
    pallas_call x1, Pallas kernels, attend_partial(): pl.pallas_call(functools.partial(attend_kernel, heads, head_size, nk), gr...  26 us
    pallas_call x1, Pallas kernels, conv_block(): pl.pallas_call(functools.partial(conv_gelu_kernel, taps, rows, halo), gri...  11.6 us
    ppermute x1, starting transfers between devices, halo_rows(): lax.ppermute(lax.slice_in_dim(block, 0, width, axis=0), SEQ_AXES, backward)  3.33 us
    ppermute x1, starting transfers between devices, halo_rows(): lax.ppermute(lax.slice_in_dim(block, block.shape[0] - width, None, axis=0...  3.1 us
    dot_general x1, matrix products, body(): jnp.dot(attended, out_weight, preferred_element_type=jnp.float32)  2.07 us
  transfers between devices with their start and end apart: 2, of which 1 were waited for; matrix products, arithmetic and copies ran while one was open for 0% of the time, Pallas kernels for 0%

profile of v25, /device:TPU:1, one launch (start us, length us, event | category | flops | bytes accessed | tf_op | source)
XLA Modules:
  0.0 95.3 jit_solution(16413165164632594214)
XLA Ops:
  0.0 0.0 copy-start
  0.0 0.8 fusion
  0.8 3.3 %collective-permute-start.1 = (bf16[4,1536]{1,0:T(4,128)(2,1)S(1)}, bf16[4,1536]{1,0:T(4,128)(2,1)S(1)}, u32[]{:S(2)}, u32[]{:S(2)}) collective-permute-start(bf16[4,1536]{1,0:T(4,128)(2,1)S(1)} %get-tuple-element.13), channel_id=1, source_target_pairs={{4,0},{8,4},{12,8},{16,12},{20,16},{24,20},{28,24},{32,28},{36,32}... | collective-permute-start | bytes 36872 | tf_op jit(solution)/shard_map/ppermute | solution.py:32
  4.2 3.1 %collective-permute-start = (bf16[4,1536]{1,0:T(4,128)(2,1)S(1)}, bf16[4,1536]{1,0:T(4,128)(2,1)S(1)}, u32[]{:S(2)}, u32[]{:S(2)}) collective-permute-start(bf16[4,1536]{1,0:T(4,128)(2,1)S(1)} %get-tuple-element.14), channel_id=1, source_target_pairs={{0,4},{4,8},{8,12},{12,16},{16,20},{20,24},{24,28},{28,32},{32,36}... | collective-permute-start | bytes 36872 | tf_op jit(solution)/shard_map/ppermute | solution.py:31
  7.3 0.0 collective-permute-done.1.hi_ref
  7.3 0.8 collective-permute-done.lo_ref
  8.1 0.0 copy-start.3
  8.1 1.1 %copy-done.3 = bf16[256,1536]{1,0:T(8,128)(2,1)S(1)} copy-done((bf16[256,1536]{1,0:T(8,128)(2,1)S(1)}, bf16[256,1536]{1,0:T(8,128)(2,1)}, u32[]{:S(2)}) %copy-start.3) | copy-done | bytes 786456
  9.2 11.6 %shard_map.64.h_ref = bf16[256,768]{1,0:T(8,128)(2,1)S(1)} custom-call(bf16[4,1536]{1,0:T(4,128)(2,1)S(1)} %collective-permute-done.lo_ref, bf16[256,1536]{1,0:T(8,128)(2,1)S(1)} %copy-done.3, bf16[4,1536]{1,0:T(4,128)(2,1)S(1)} %collective-permute-done.1.hi_ref, bf16[5,1536,768]{2,1,0:T(8,128)(2,1)} %w_ref.1, bf16[5,768,768]{2,1,0:T(8,128)(2,1)} %w2_ref.1), custom_call_target="tpu_custom_call" | custom-call | flops 3114270720 | bytes 13006848 | tf_op jit(solution)/shard_map/pallas_call | solution.py:403
  20.9 0.0 copy-start.1
  20.9 0.7 copy-done.1
  21.6 45.5 %shard_map.65 = (bf16[16,2,128,768]{3,2,1,0:T(8,128)(2,1)}, bf16[512,256]{1,0:T(8,128)(2,1)}, bf16[512,768]{1,0:T(8,128)(2,1)}, bf16[512,256]{1,0:T(8,128)(2,1)}) custom-call(bf16[2,128,768]{2,1,0:T(8,128)(2,1)} %bitcast.4, bf16[256,768]{1,0:T(8,128)(2,1)} %copy-done.1, bf16[768,1536]{1,0:T(8,128)(2,1)} %wk_ref.1, bf16[768,1536]{1,0:T(8,128)(2,1)} %wk_ref.1, ...), custom_call_target="tpu_custom_call" | custom-call | tf_op jit(solution)/shard_map/pallas_call | solution.py:324
  67.2 0.0 copy-start.2
  67.2 26.0 %shard_map.66 = bf16[256,512]{1,0:T(8,128)(2,1)} custom-call(bf16[512,256]{1,0:T(8,128)(2,1)} %get-tuple-element.9.qa_ref, bf16[512,256]{1,0:T(8,128)(2,1)} %get-tuple-element.10.qb_ref, bf16[4096,768]{1,0:T(8,128)(2,1)} %bitcast.5, bf16[768,1536]{1,0:T(8,128)(2,1)} %wk_ref.1, bf16[512,768]{1,0:T(8,128)(2,1)} %get-tuple-element.12.wvt_ref), custom_call_target="tpu_custom_call" | custom-call | flops 10737418240 | bytes 8388608 | tf_op jit(solution)/shard_map/pallas_call | solution.py:137
  93.2 0.0 copy-done
  93.2 0.0 copy-done.2
  93.2 2.1 %add_convert_fusion = bf16[256,768]{1,0:T(8,128)(2,1)} fusion(bf16[256,768]{1,0:T(8,128)(2,1)S(1)} %copy-done.2, bf16[256,512]{1,0:T(8,128)(2,1)} %shard_map.66, bf16[512,768]{1,0:T(8,128)(2,1)S(1)} %copy-done), kind=kOutput, calls=%fused_computation | convolution fusion | flops 201916416 | bytes 1835008 | tf_op jit(solution)/shard_map/dot_general | solution.py:439
Async XLA Ops:
  0.0 93.2 %copy-start = (bf16[512,768]{1,0:T(8,128)(2,1)S(1)}, bf16[512,768]{1,0:T(8,128)(2,1)}, u32[]{:S(2)}) copy-start(bf16[512,768]{1,0:T(8,128)(2,1)} %param.10) | copy-start | bytes 2359300
  0.8 6.4 %collective-permute-start.1 = (bf16[4,1536]{1,0:T(4,128)(2,1)S(1)}, bf16[4,1536]{1,0:T(4,128)(2,1)S(1)}, u32[]{:S(2)}, u32[]{:S(2)}) collective-permute-start(bf16[4,1536]{1,0:T(4,128)(2,1)S(1)} %get-tuple-element.13), channel_id=1, source_target_pairs={{4,0},{8,4},{12,8},{16,12},{20,16},{24,20},{28,24},{32,28},{36,32}... | collective-permute-start | bytes 36872 | tf_op jit(solution)/shard_map/ppermute | solution.py:32
  4.2 3.9 %collective-permute-start = (bf16[4,1536]{1,0:T(4,128)(2,1)S(1)}, bf16[4,1536]{1,0:T(4,128)(2,1)S(1)}, u32[]{:S(2)}, u32[]{:S(2)}) collective-permute-start(bf16[4,1536]{1,0:T(4,128)(2,1)S(1)} %get-tuple-element.14), channel_id=1, source_target_pairs={{0,4},{4,8},{8,12},{12,16},{16,20},{20,24},{24,28},{28,32},{32,36}... | collective-permute-start | bytes 36872 | tf_op jit(solution)/shard_map/ppermute | solution.py:31
  8.1 1.1 %copy-start.3 = (bf16[256,1536]{1,0:T(8,128)(2,1)S(1)}, bf16[256,1536]{1,0:T(8,128)(2,1)}, u32[]{:S(2)}) copy-start(bf16[256,1536]{1,0:T(8,128)(2,1)} %mid_ref.1) | copy-start | bytes 2359300
  20.9 0.7 copy-start.1
  67.2 26.0 %copy-start.2 = (bf16[256,768]{1,0:T(8,128)(2,1)S(1)}, bf16[256,768]{1,0:T(8,128)(2,1)}, u32[]{:S(2)}) copy-start(bf16[256,768]{1,0:T(8,128)(2,1)} %copy-done.1) | copy-start | bytes 1179652

commit v26 on v24

--- a/solution.py
+++ b/solution.py
@@ -128,7 +128,7 @@
         out_ref[...] = jnp.concatenate(mixed, axis=0).T.astype(out_ref.dtype)
 
 
-def attend_partial(qt_own, qt_other, hidden_kv, qkv_weight, wvt, heads, head_size, tk=2048):
+def attend_partial(qt_own, qt_other, hidden_kv, qkv_weight, wvt, heads, head_size, tk=4096):
     width, own = qt_own.shape
     q_rows = 2 * own
     k_rows, channels = hidden_kv.shape

time: 96 us -> 96.6 us (level)
  no operation moved by 1% of the time
where the time goes in v26:
time: 96.6 us; the launch traced here: 96.3 us
  Pallas kernels  77.3 us (80%)
  starting transfers between devices  6.43 us (7%)
  local copies, waits for them, and re-layouts  6.34 us (7%)
  matrix products  5.36 us (6%)
    pallas_call x1, Pallas kernels, gather_rows(): pl.pallas_call(functools.partial(ring_gather_kernel, side, heads, head_si...  45.5 us
    pallas_call x1, Pallas kernels, attend_partial(): pl.pallas_call(functools.partial(attend_kernel, heads, head_size, nk), gr...  26.6 us
    unnamed x10, local copies, waits for them, and re-layouts  5.5 us
    pallas_call x1, Pallas kernels, conv_gelu(): pl.pallas_call(functools.partial(conv_gelu_kernel, taps, rows, halo), gri...  5.17 us
    ppermute x1, starting transfers between devices, halo_rows(): lax.ppermute(lax.slice_in_dim(block, 0, width, axis=0), SEQ_AXES, backward)  3.33 us
    ppermute x1, starting transfers between devices, halo_rows(): lax.ppermute(lax.slice_in_dim(block, block.shape[0] - width, None, axis=0...  3.1 us
    dot_general x1, matrix products, body(): jnp.dot(attended, out_weight, preferred_element_type=jnp.float32)  2.07 us
    dot_general x4, matrix products, convolve(): jnp.dot(padded[offset:offset + row_count], weight[offset], preferred_elem...  1.93 us
  transfers between devices with their start and end apart: 2, of which 1 were waited for; matrix products, arithmetic and copies ran while one was open for 0% of the time, Pallas kernels for 0%

profile of v26, /device:TPU:1, one launch (start us, length us, event | category | flops | bytes accessed | tf_op | source)
XLA Modules:
  0.0 96.3 jit_solution(17343678596525558103)
XLA Ops:
  0.0 0.0 copy-start
  0.0 0.8 fusion.27
  0.8 3.3 %collective-permute-start.1 = (bf16[4,1536]{1,0:T(4,128)(2,1)S(1)}, bf16[4,1536]{1,0:T(4,128)(2,1)S(1)}, u32[]{:S(2)}, u32[]{:S(2)}) collective-permute-start(bf16[4,1536]{1,0:T(4,128)(2,1)S(1)} %get-tuple-element.13), channel_id=1, source_target_pairs={{4,0},{8,4},{12,8},{16,12},{20,16},{24,20},{28,24},{32,28},{36,32}... | collective-permute-start | bytes 36872 | tf_op jit(solution)/shard_map/ppermute | solution.py:32
  4.2 3.1 %collective-permute-start = (bf16[4,1536]{1,0:T(4,128)(2,1)S(1)}, bf16[4,1536]{1,0:T(4,128)(2,1)S(1)}, u32[]{:S(2)}, u32[]{:S(2)}) collective-permute-start(bf16[4,1536]{1,0:T(4,128)(2,1)S(1)} %get-tuple-element.14), channel_id=1, source_target_pairs={{0,4},{4,8},{8,12},{12,16},{16,20},{20,24},{24,28},{28,32},{32,36}... | collective-permute-start | bytes 36872 | tf_op jit(solution)/shard_map/ppermute | solution.py:31
  7.3 0.0 collective-permute-done.1.hi_ref
  7.3 0.8 collective-permute-done.lo_ref
  8.1 0.0 copy-start.1
  8.1 4.3 %copy-done.1 = bf16[5,1536,768]{2,1,0:T(8,128)(2,1)S(1)} copy-done((bf16[5,1536,768]{2,1,0:T(8,128)(2,1)S(1)}, bf16[5,1536,768]{2,1,0:T(8,128)(2,1)}, u32[]{:S(2)}) %copy-start.1) | copy-done | bytes 11796504
  12.5 0.0 copy-start.2
  12.5 1.1 %copy-done.2 = bf16[256,1536]{1,0:T(8,128)(2,1)S(1)} copy-done((bf16[256,1536]{1,0:T(8,128)(2,1)S(1)}, bf16[256,1536]{1,0:T(8,128)(2,1)}, u32[]{:S(2)}) %copy-start.2) | copy-done | bytes 786456
  13.6 0.0 copy-start.4
  13.6 5.2 %shard_map.64 = bf16[260,768]{1,0:T(8,128)(2,1)S(1)} custom-call(bf16[4,1536]{1,0:T(4,128)(2,1)S(1)} %collective-permute-done.lo_ref, bf16[256,1536]{1,0:T(8,128)(2,1)S(1)} %copy-done.2, bf16[4,1536]{1,0:T(4,128)(2,1)S(1)} %collective-permute-done.1.hi_ref, bf16[5,1536,768]{2,1,0:T(8,128)(2,1)S(1)} %copy-done.1), custom_call_target="tpu_custom_call" | custom-call | flops 3114270720 | bytes 13006848 | tf_op jit(solution)/shard_map/pallas_call | solution.py:395
  18.8 0.0 copy-done.4
  18.8 0.5 fusion.4
  19.3 0.5 fusion.6
  19.8 0.5 fusion.10
  20.3 0.5 fusion.8
  20.7 1.4 %add_convert_fusion.h_ref = bf16[256,768]{1,0:T(8,128)(2,1)} fusion(f32[256,768]{1,0:T(8,128)S(1)} %fusion.4, f32[256,768]{1,0:T(8,128)S(1)} %fusion.6, f32[256,768]{1,0:T(8,128)S(1)} %fusion.8, f32[256,768]{1,0:T(8,128)S(1)} %fusion.10, bf16[5,768,768]{2,1,0:T(8,128)(2,1)S(1)} %copy-done.4, bf16[260,768]{1,0:T(8,128)(2,1)S(1)} %shard_map.64), kind=kOutput, calls=%fused_computation.20 | convolution fusion | flops 303366144 | bytes 5505024 | tf_op jit(solution)/shard_map/dot_general | solution.py:37
  22.1 45.5 %shard_map.65 = (bf16[16,2,128,768]{3,2,1,0:T(8,128)(2,1)}, bf16[512,256]{1,0:T(8,128)(2,1)}, bf16[512,768]{1,0:T(8,128)(2,1)}, bf16[512,256]{1,0:T(8,128)(2,1)}) custom-call(bf16[2,128,768]{2,1,0:T(8,128)(2,1)} %bitcast.21, bf16[256,768]{1,0:T(8,128)(2,1)} %add_convert_fusion.h_ref, bf16[768,1536]{1,0:T(8,128)(2,1)} %wk_ref.1, bf16[768,1536]{1,0:T(8,128)(2,1)} %wk_ref.1, ...), custom_call_target="tpu_custom_call" | custom-call | tf_op jit(solution)/shard_map/pallas_call | solution.py:324
  67.6 0.0 copy-start.3
  67.7 26.6 %shard_map.66 = bf16[256,512]{1,0:T(8,128)(2,1)} custom-call(bf16[512,256]{1,0:T(8,128)(2,1)} %get-tuple-element.9.qa_ref, bf16[512,256]{1,0:T(8,128)(2,1)} %get-tuple-element.10.qb_ref, bf16[4096,768]{1,0:T(8,128)(2,1)} %bitcast.22, bf16[768,1536]{1,0:T(8,128)(2,1)} %wk_ref.1, bf16[512,768]{1,0:T(8,128)(2,1)} %get-tuple-element.12.wvt_ref), custom_call_target="tpu_custom_call" | custom-call | flops 10737418240 | bytes 8388608 | tf_op jit(solution)/shard_map/pallas_call | solution.py:137
  94.2 0.0 copy-done
  94.2 0.0 copy-done.3
  94.2 2.1 %fusion.3 = bf16[256,768]{1,0:T(8,128)(2,1)} fusion(bf16[256,512]{1,0:T(8,128)(2,1)} %shard_map.66, bf16[512,768]{1,0:T(8,128)(2,1)S(1)} %copy-done, bf16[256,768]{1,0:T(8,128)(2,1)S(1)} %copy-done.3), kind=kOutput, calls=%fused_computation.5 | convolution fusion | flops 201916416 | bytes 1835008 | tf_op jit(solution)/shard_map/dot_general | solution.py:433
Async XLA Ops:
  0.0 94.2 %copy-start = (bf16[512,768]{1,0:T(8,128)(2,1)S(1)}, bf16[512,768]{1,0:T(8,128)(2,1)}, u32[]{:S(2)}) copy-start(bf16[512,768]{1,0:T(8,128)(2,1)} %param.10) | copy-start | bytes 2359300
  0.8 6.4 %collective-permute-start.1 = (bf16[4,1536]{1,0:T(4,128)(2,1)S(1)}, bf16[4,1536]{1,0:T(4,128)(2,1)S(1)}, u32[]{:S(2)}, u32[]{:S(2)}) collective-permute-start(bf16[4,1536]{1,0:T(4,128)(2,1)S(1)} %get-tuple-element.13), channel_id=1, source_target_pairs={{4,0},{8,4},{12,8},{16,12},{20,16},{24,20},{28,24},{32,28},{36,32}... | collective-permute-start | bytes 36872 | tf_op jit(solution)/shard_map/ppermute | solution.py:32
  4.2 3.9 %collective-permute-start = (bf16[4,1536]{1,0:T(4,128)(2,1)S(1)}, bf16[4,1536]{1,0:T(4,128)(2,1)S(1)}, u32[]{:S(2)}, u32[]{:S(2)}) collective-permute-start(bf16[4,1536]{1,0:T(4,128)(2,1)S(1)} %get-tuple-element.14), channel_id=1, source_target_pairs={{0,4},{4,8},{8,12},{12,16},{16,20},{20,24},{24,28},{28,32},{32,36}... | collective-permute-start | bytes 36872 | tf_op jit(solution)/shard_map/ppermute | solution.py:31
  8.1 4.4 %copy-start.1 = (bf16[5,1536,768]{2,1,0:T(8,128)(2,1)S(1)}, bf16[5,1536,768]{2,1,0:T(8,128)(2,1)}, u32[]{:S(2)}) copy-start(bf16[5,1536,768]{2,1,0:T(8,128)(2,1)} %w_ref.1) | copy-start | bytes 35389444
  12.5 1.1 %copy-start.2 = (bf16[256,1536]{1,0:T(8,128)(2,1)S(1)}, bf16[256,1536]{1,0:T(8,128)(2,1)}, u32[]{:S(2)}) copy-start(bf16[256,1536]{1,0:T(8,128)(2,1)} %mid_ref.1) | copy-start | bytes 2359300
  13.6 5.2 %copy-start.4 = (bf16[5,768,768]{2,1,0:T(8,128)(2,1)S(1)}, bf16[5,768,768]{2,1,0:T(8,128)(2,1)}, u32[]{:S(2)}) copy-start(bf16[5,768,768]{2,1,0:T(8,128)(2,1)} %param.8) | copy-start | bytes 17694724
  67.6 26.6 %copy-start.3 = (bf16[256,768]{1,0:T(8,128)(2,1)S(1)}, bf16[256,768]{1,0:T(8,128)(2,1)}, u32[]{:S(2)}) copy-start(bf16[256,768]{1,0:T(8,128)(2,1)} %add_convert_fusion.h_ref) | copy-start | bytes 1179652

commit v27 on v24

--- a/solution.py
+++ b/solution.py
@@ -268,11 +268,11 @@
     for st in range(2):
         a0, b0 = own[st]
         recv((st, 1, 1), part(st, a0 - 1, b0), slot(st, a0 - 1, b0))
+        send((st, 2, 1), part(st, a0 - 1, b0, 0), part(st, a0 - 1, b0, 0), slot(st, a0 + 1, b0))
+        send_row(st, side - 1)
         recv((st, 1, -1), part(st, a0 + 1, b0), slot(st, a0 + 1, b0))
-        send((st, 2, 1), part(st, a0 - 1, b0, 0), part(st, a0 - 1, b0, 0), slot(st, a0 + 1, b0))
         send((st, 2, -1), part(st, a0 + 1, b0, q), part(st, a0 + 1, b0, q), slot(st, a0 - 1, b0))
         send_row(st, 1)
-        send_row(st, side - 1)
     for st in range(2):
         a0, b0 = own[st]
         recv((st, 2, 1), part(st, a0 - 2, b0, 0), slot(st, a0 - 1, b0))

time: 96 us -> 96.9 us (level)
    pallas_call x1, Pallas kernels: 26 us -> 27.1 us  [attend_partial(): pl.pallas_call(functools.partial(attend_kernel, heads, head_size, nk), gr...]
where the time goes in v27:
time: 96.9 us; the launch traced here: 96.6 us
  Pallas kernels  77.5 us (80%)
  starting transfers between devices  6.43 us (7%)
  local copies, waits for them, and re-layouts  6.34 us (7%)
  matrix products  5.36 us (6%)
    pallas_call x1, Pallas kernels, gather_rows(): pl.pallas_call(functools.partial(ring_gather_kernel, side, heads, head_si...  45.3 us
    pallas_call x1, Pallas kernels, attend_partial(): pl.pallas_call(functools.partial(attend_kernel, heads, head_size, nk), gr...  27.1 us
    unnamed x10, local copies, waits for them, and re-layouts  5.5 us
    pallas_call x1, Pallas kernels, conv_gelu(): pl.pallas_call(functools.partial(conv_gelu_kernel, taps, rows, halo), gri...  5.17 us
    ppermute x1, starting transfers between devices, halo_rows(): lax.ppermute(lax.slice_in_dim(block, 0, width, axis=0), SEQ_AXES, backward)  3.33 us
    ppermute x1, starting transfers between devices, halo_rows(): lax.ppermute(lax.slice_in_dim(block, block.shape[0] - width, None, axis=0...  3.1 us
    dot_general x1, matrix products, body(): jnp.dot(attended, out_weight, preferred_element_type=jnp.float32)  2.07 us
  transfers between devices with their start and end apart: 2, of which 1 were waited for; matrix products, arithmetic and copies ran while one was open for 0% of the time, Pallas kernels for 0%

profile of v27, /device:TPU:1, one launch (start us, length us, event | category | flops | bytes accessed | tf_op | source)
XLA Modules:
  0.0 96.6 jit_solution(3943401740798928013)
XLA Ops:
  0.0 0.0 copy-start
  0.0 0.8 fusion.27
  0.8 3.3 %collective-permute-start.1 = (bf16[4,1536]{1,0:T(4,128)(2,1)S(1)}, bf16[4,1536]{1,0:T(4,128)(2,1)S(1)}, u32[]{:S(2)}, u32[]{:S(2)}) collective-permute-start(bf16[4,1536]{1,0:T(4,128)(2,1)S(1)} %get-tuple-element.13), channel_id=1, source_target_pairs={{4,0},{8,4},{12,8},{16,12},{20,16},{24,20},{28,24},{32,28},{36,32}... | collective-permute-start | bytes 36872 | tf_op jit(solution)/shard_map/ppermute | solution.py:32
  4.2 3.1 %collective-permute-start = (bf16[4,1536]{1,0:T(4,128)(2,1)S(1)}, bf16[4,1536]{1,0:T(4,128)(2,1)S(1)}, u32[]{:S(2)}, u32[]{:S(2)}) collective-permute-start(bf16[4,1536]{1,0:T(4,128)(2,1)S(1)} %get-tuple-element.14), channel_id=1, source_target_pairs={{0,4},{4,8},{8,12},{12,16},{16,20},{20,24},{24,28},{28,32},{32,36}... | collective-permute-start | bytes 36872 | tf_op jit(solution)/shard_map/ppermute | solution.py:31
  7.3 0.0 collective-permute-done.1.hi_ref
  7.3 0.8 collective-permute-done.lo_ref
  8.1 0.0 copy-start.1
  8.1 4.3 %copy-done.1 = bf16[5,1536,768]{2,1,0:T(8,128)(2,1)S(1)} copy-done((bf16[5,1536,768]{2,1,0:T(8,128)(2,1)S(1)}, bf16[5,1536,768]{2,1,0:T(8,128)(2,1)}, u32[]{:S(2)}) %copy-start.1) | copy-done | bytes 11796504
  12.5 0.0 copy-start.2
  12.5 1.1 %copy-done.2 = bf16[256,1536]{1,0:T(8,128)(2,1)S(1)} copy-done((bf16[256,1536]{1,0:T(8,128)(2,1)S(1)}, bf16[256,1536]{1,0:T(8,128)(2,1)}, u32[]{:S(2)}) %copy-start.2) | copy-done | bytes 786456
  13.6 0.0 copy-start.4
  13.6 5.2 %shard_map.64 = bf16[260,768]{1,0:T(8,128)(2,1)S(1)} custom-call(bf16[4,1536]{1,0:T(4,128)(2,1)S(1)} %collective-permute-done.lo_ref, bf16[256,1536]{1,0:T(8,128)(2,1)S(1)} %copy-done.2, bf16[4,1536]{1,0:T(4,128)(2,1)S(1)} %collective-permute-done.1.hi_ref, bf16[5,1536,768]{2,1,0:T(8,128)(2,1)S(1)} %copy-done.1), custom_call_target="tpu_custom_call" | custom-call | flops 3114270720 | bytes 13006848 | tf_op jit(solution)/shard_map/pallas_call | solution.py:395
  18.8 0.0 copy-done.4
  18.8 0.5 fusion.4
  19.3 0.5 fusion.6
  19.8 0.5 fusion.10
  20.3 0.5 fusion.8
  20.7 1.4 %add_convert_fusion.h_ref = bf16[256,768]{1,0:T(8,128)(2,1)} fusion(f32[256,768]{1,0:T(8,128)S(1)} %fusion.4, f32[256,768]{1,0:T(8,128)S(1)} %fusion.6, f32[256,768]{1,0:T(8,128)S(1)} %fusion.8, f32[256,768]{1,0:T(8,128)S(1)} %fusion.10, bf16[5,768,768]{2,1,0:T(8,128)(2,1)S(1)} %copy-done.4, bf16[260,768]{1,0:T(8,128)(2,1)S(1)} %shard_map.64), kind=kOutput, calls=%fused_computation.20 | convolution fusion | flops 303366144 | bytes 5505024 | tf_op jit(solution)/shard_map/dot_general | solution.py:37
  22.1 45.3 %shard_map.65 = (bf16[16,2,128,768]{3,2,1,0:T(8,128)(2,1)}, bf16[512,256]{1,0:T(8,128)(2,1)}, bf16[512,768]{1,0:T(8,128)(2,1)}, bf16[512,256]{1,0:T(8,128)(2,1)}) custom-call(bf16[2,128,768]{2,1,0:T(8,128)(2,1)} %bitcast.21, bf16[256,768]{1,0:T(8,128)(2,1)} %add_convert_fusion.h_ref, bf16[768,1536]{1,0:T(8,128)(2,1)} %wk_ref.1, bf16[768,1536]{1,0:T(8,128)(2,1)} %wk_ref.1, ...), custom_call_target="tpu_custom_call" | custom-call | tf_op jit(solution)/shard_map/pallas_call | solution.py:324
  67.4 0.0 copy-start.3
  67.4 27.1 %shard_map.66 = bf16[256,512]{1,0:T(8,128)(2,1)} custom-call(bf16[512,256]{1,0:T(8,128)(2,1)} %get-tuple-element.9.qa_ref, bf16[512,256]{1,0:T(8,128)(2,1)} %get-tuple-element.10.qb_ref, bf16[4096,768]{1,0:T(8,128)(2,1)} %bitcast.22, bf16[768,1536]{1,0:T(8,128)(2,1)} %wk_ref.1, bf16[512,768]{1,0:T(8,128)(2,1)} %get-tuple-element.12.wvt_ref), custom_call_target="tpu_custom_call" | custom-call | flops 10737418240 | bytes 8388608 | tf_op jit(solution)/shard_map/pallas_call | solution.py:137
  94.5 0.0 copy-done
  94.5 0.0 copy-done.3
  94.5 2.1 %fusion.3 = bf16[256,768]{1,0:T(8,128)(2,1)} fusion(bf16[256,512]{1,0:T(8,128)(2,1)} %shard_map.66, bf16[512,768]{1,0:T(8,128)(2,1)S(1)} %copy-done, bf16[256,768]{1,0:T(8,128)(2,1)S(1)} %copy-done.3), kind=kOutput, calls=%fused_computation.5 | convolution fusion | flops 201916416 | bytes 1835008 | tf_op jit(solution)/shard_map/dot_general | solution.py:433
Async XLA Ops:
  0.0 94.5 %copy-start = (bf16[512,768]{1,0:T(8,128)(2,1)S(1)}, bf16[512,768]{1,0:T(8,128)(2,1)}, u32[]{:S(2)}) copy-start(bf16[512,768]{1,0:T(8,128)(2,1)} %param.10) | copy-start | bytes 2359300
  0.8 6.4 %collective-permute-start.1 = (bf16[4,1536]{1,0:T(4,128)(2,1)S(1)}, bf16[4,1536]{1,0:T(4,128)(2,1)S(1)}, u32[]{:S(2)}, u32[]{:S(2)}) collective-permute-start(bf16[4,1536]{1,0:T(4,128)(2,1)S(1)} %get-tuple-element.13), channel_id=1, source_target_pairs={{4,0},{8,4},{12,8},{16,12},{20,16},{24,20},{28,24},{32,28},{36,32}... | collective-permute-start | bytes 36872 | tf_op jit(solution)/shard_map/ppermute | solution.py:32
  4.2 3.9 %collective-permute-start = (bf16[4,1536]{1,0:T(4,128)(2,1)S(1)}, bf16[4,1536]{1,0:T(4,128)(2,1)S(1)}, u32[]{:S(2)}, u32[]{:S(2)}) collective-permute-start(bf16[4,1536]{1,0:T(4,128)(2,1)S(1)} %get-tuple-element.14), channel_id=1, source_target_pairs={{0,4},{4,8},{8,12},{12,16},{16,20},{20,24},{24,28},{28,32},{32,36}... | collective-permute-start | bytes 36872 | tf_op jit(solution)/shard_map/ppermute | solution.py:31
  8.1 4.4 %copy-start.1 = (bf16[5,1536,768]{2,1,0:T(8,128)(2,1)S(1)}, bf16[5,1536,768]{2,1,0:T(8,128)(2,1)}, u32[]{:S(2)}) copy-start(bf16[5,1536,768]{2,1,0:T(8,128)(2,1)} %w_ref.1) | copy-start | bytes 35389444
  12.5 1.1 %copy-start.2 = (bf16[256,1536]{1,0:T(8,128)(2,1)S(1)}, bf16[256,1536]{1,0:T(8,128)(2,1)}, u32[]{:S(2)}) copy-start(bf16[256,1536]{1,0:T(8,128)(2,1)} %mid_ref.1) | copy-start | bytes 2359300
  13.6 5.2 %copy-start.4 = (bf16[5,768,768]{2,1,0:T(8,128)(2,1)S(1)}, bf16[5,768,768]{2,1,0:T(8,128)(2,1)}, u32[]{:S(2)}) copy-start(bf16[5,768,768]{2,1,0:T(8,128)(2,1)} %param.8) | copy-start | bytes 17694724
  67.4 27.1 %copy-start.3 = (bf16[256,768]{1,0:T(8,128)(2,1)S(1)}, bf16[256,768]{1,0:T(8,128)(2,1)}, u32[]{:S(2)}) copy-start(bf16[256,768]{1,0:T(8,128)(2,1)} %add_convert_fusion.h_ref) | copy-start | bytes 1179652
